TPU v7x, 32 devices: a whole 2x2x4 slice. The times are simulated.
32 devices in a mesh: dp: 2 (over core), crow: 4 (over y, x), ccol: 4 (over z).
Axes of the slice: x: 2, y: 2, z: 4, core: 2. Of those that a mesh axis runs over, the one named last changes fastest.
Arguments:
- data: float32 [16, 16384], P(None, ('dp', 'crow')), may hold values from 0 to 1
- centres: float32 [16, 3072], P(None, 'ccol'), may hold values from 0 to 1
- scales: float32 [16], replicated, may hold values from 0.5 to 1.2
- factor: float32 [3072, 3072], P('crow', 'ccol'), may hold values from -1 to 1, as said below
- block_inv: float32 [12, 256, 256], P('crow'), may hold values from -1 to 2
- iterate: float32 [8, 3072], replicated, may hold values from -6 to 6
- residual: float32 [8, 3072], replicated, may hold values from -6 to 6
- direction: float32 [8, 3072], replicated, may hold values from -6 to 6
Outputs:
- new_iterate: float32 [8, 3072], replicated
- new_residual: float32 [8, 3072], replicated
- new_direction: float32 [8, 3072], replicated
Inputs may be any that keep to these rules, and one draw needn't show every extreme that they name: `factor`: blocks of 256 x 256 on and above the block diagonal are zero.
All inputs are finite; a program needn't handle non-finite values.
Results may differ from a plain program's by a relative error of at most 0.0001.
Values sent between devices are 32-bit elements; how exact they have to be, the bound alone decides.
No kernel may reach another device: no remote copies, remote signals or barrier semaphores. Data moves between devices by JAX's collectives and lax.ppermute only.
A program may use at most 64 MiB of HBM per device.

v0:
```python
import functools
import math

import jax
import jax.numpy as jnp
from jax import lax
from jax.experimental import pallas as pl
from jax.experimental.pallas import tpu as pltpu
from jax.sharding import PartitionSpec as P


ridge_weight = 0.2
LOG2E = 1.0 / math.log(2.0)
NN = (((1,), (0,)), ((), ()))
NT = (((1,), (1,)), ((), ()))
TN = (((0,), (0,)), ((), ()))


def pair(value):
    high = value.astype(jnp.bfloat16)
    low = (value - high.astype(jnp.float32)).astype(jnp.bfloat16)
    return high, low


def stacked(value):
    high, low = pair(value)
    return jnp.concatenate([high, low], axis=0)


def fold(product, rows):
    return product[:rows] + product[rows:]


def times_pair(rows, high, low, dims):
    both = stacked(rows)
    out = lax.dot_general(both, high, dims, preferred_element_type=jnp.float32)
    out = out + lax.dot_general(both, low, dims, preferred_element_type=jnp.float32)
    return fold(out, rows.shape[0])


def times(rows, matrix, dims):
    high, low = pair(matrix)
    return times_pair(rows, high, low, dims)


def blocks_of(held):
    return [(r, c) for r in range(1, held) for c in range(r)]


def lower(low_ref, order, r, c):
    at = r * (r - 1) // 2 + c
    return low_ref[:, at * order : (at + 1) * order]


def square(one, other):
    first, first_low = pair(one)
    second, second_low = pair(other)
    out = lax.dot_general(first, second, NN, preferred_element_type=jnp.float32)
    out = out + lax.dot_general(first, second_low, NN, preferred_element_type=jnp.float32)
    return out + lax.dot_general(first_low, second, NN, preferred_element_type=jnp.float32)


def cut(ref, at, width):
    return ref[:, pl.ds(pl.multiple_of(at * width, width), width)]


def back_apply(target, low_ref, inv_ref):
    held, order = inv_ref.shape[0], inv_ref.shape[1]
    parts = [target[:, n * order : (n + 1) * order] for n in range(held)]
    pieces = []
    for c in range(held):
        piece = times(parts[c], inv_ref[c], NN)
        for r in range(c + 1, held):
            piece = piece + times(parts[r], lower(low_ref, order, r, c), NN)
        pieces.append(piece)
    return jnp.concatenate(pieces, axis=1)


def fore_apply(source, high_ref, low_ref, order):
    pieces = []
    for end in range(order, source.shape[1] + 1, order):
        block = (slice(0, end), slice(end - order, end))
        pieces.append(times_pair(source[:, :end], high_ref[block], low_ref[block], NN))
    return jnp.concatenate(pieces, axis=1)


def store_turned(low, inv_ref, high_out, low_out):
    held, order = inv_ref.shape[0], inv_ref.shape[1]
    for r in range(held):
        for c in range(r + 1):
            at = r * (r - 1) // 2 + c
            block = inv_ref[r] if r == c else low[:, at * order : (at + 1) * order]
            place = (slice(c * order, (c + 1) * order), slice(r * order, (r + 1) * order))
            high_out[place], low_out[place] = pair(block.T)


def turn_kernel(low_ref, inv_ref, high_out, low_out):
    store_turned(low_ref[...], inv_ref, high_out, low_out)


def turn_factor_kernel(factor_ref, high_out, low_out):
    high_out[...], low_out[...] = pair(factor_ref[...].T)


def first_kernel(direction_ref, inv_ref, *refs):
    tri_refs, out_ref = refs[:-1], refs[-1]
    held, order = inv_ref.shape[0], inv_ref.shape[1]
    width = held * order
    tri = dict(zip(blocks_of(held), tri_refs))
    target = cut(direction_ref, lax.axis_index("crow"), width)
    pieces = [None] * held
    for number in reversed(range(held)):
        part = target[:, number * order : (number + 1) * order]
        for later in range(number + 1, held):
            part = part - times(pieces[later], tri[later, number][...], NN)
        pieces[number] = times(part, inv_ref[number], NN)
    out_ref[...] = jnp.concatenate(pieces, axis=1)


def lower_kernel(after_ref, inv_ref, *refs):
    tri_refs, out_ref = refs[:-1], refs[-1]
    held, order = inv_ref.shape[0], inv_ref.shape[1]
    tri = dict(zip(blocks_of(held), tri_refs))
    found = {(n, n): inv_ref[n] for n in range(held)}
    for r in range(1, held):
        for c in range(r):
            total = square(tri[r, c][...], found[c, c])
            for between in range(c + 1, r):
                total = total + square(tri[r, between][...], found[between, c])
            found[r, c] = -square(inv_ref[r], total)
            at = r * (r - 1) // 2 + c
            out_ref[:, at * order : (at + 1) * order] = found[r, c]


def pair_kernel(factor_ref, high_ref, low_ref):
    high, low = pair(factor_ref[...])
    high_ref[...] = high
    low_ref[...] = low


def spread_kernel(cols, lend, *refs):
    outs = refs[len(refs) - 1 - lend :]
    refs = refs[: len(refs) - 1 - lend]
    if lend:
        low_of, half = refs[-1], outs[1]
        tall = half.shape[0]
        at = lax.rem(lax.axis_index("dp"), 2) * tall
        half[...] = low_of[pl.ds(pl.multiple_of(at, tall), tall), :]
        refs = refs[:-1]
    extra = refs[: len(refs) - 2 - len(cols)]
    got_refs = refs[len(extra) : len(extra) + len(cols)]
    high_ref, low_ref = refs[-2:]
    col = lax.axis_index("ccol")
    piece = got_refs[0][...]
    for at, got in zip(cols[1:], got_refs[1:]):
        piece = jnp.where(col == at, got[...], piece)
    out = times_pair(piece, high_ref[...], low_ref[...], NN)
    for ref in extra:
        out = out + ref[...]
    outs[0][...] = out


def merge_kernel(mine_ref, other_ref, inv_ref, high_out, low_out):
    odd = lax.rem(lax.axis_index("dp"), 2) == 1
    mine, other = mine_ref[...], other_ref[...]
    low = jnp.concatenate([jnp.where(odd, other, mine), jnp.where(odd, mine, other)], axis=0)
    store_turned(low, inv_ref, high_out, low_out)


def solve_kernel(direction_ref, sub_ref, low_ref, inv_ref, out_ref):
    width = sub_ref.shape[1]
    target = cut(direction_ref, lax.axis_index("crow"), width) - sub_ref[...]
    out_ref[...] = back_apply(target, low_ref, inv_ref)


def pick_kernel(places, *refs):
    row, col = lax.axis_index("crow"), lax.axis_index("ccol")
    out = jnp.zeros_like(refs[0][...])
    for (r, c), ref in zip(places, refs[:-1]):
        out = jnp.where((row == r) & (col == c), ref[...], out)
    refs[-1][...] = out


def solve_pick_kernel(places, direction_ref, sub_ref, low_ref, inv_ref, *refs):
    width = sub_ref.shape[1]
    row, col = lax.axis_index("crow"), lax.axis_index("ccol")
    target = cut(direction_ref, row, width) - sub_ref[...]
    out = jnp.where((row == 0) & (col == 0), back_apply(target, low_ref, inv_ref), 0.0)
    for (r, c), ref in zip(places, refs[:-1]):
        out = jnp.where((row == r) & (col == c), ref[...], out)
    refs[-1][...] = out


def triple(value):
    high, middle = pair(value)
    rest = value - high.astype(jnp.float32) - middle.astype(jnp.float32)
    return high, middle, rest.astype(jnp.bfloat16)


def norm_rows(norm, inputs):
    row = lax.broadcasted_iota(jnp.int32, (inputs, norm.shape[1]), 0)
    wide = jnp.broadcast_to(norm, (inputs, norm.shape[1]))
    high, middle, low = (part.astype(jnp.float32) for part in triple(wide))
    rows = jnp.where(row == 0, high, jnp.where(row == 1, middle, jnp.where(row == 2, low, 0.0)))
    return rows.astype(jnp.bfloat16)


def ones_rows(norm, inputs):
    row = lax.broadcasted_iota(jnp.int32, (inputs, norm.shape[1]), 0)
    return jnp.where(row < 3, 1.0, 0.0).astype(jnp.bfloat16)


def scale_by(value, scales_ref):
    inputs = value.shape[0]
    row = lax.broadcasted_iota(jnp.int32, value.shape, 0)
    scales = jnp.full(value.shape, scales_ref[0], jnp.float32)
    for n in range(1, inputs):
        scales = jnp.where(row == n, scales_ref[n], scales)
    return value / scales


def tile_kernel(scales_ref, centres_ref, data_ref, high_ref, low_ref, right):
    inputs = data_ref.shape[0]

    @pl.when(pl.program_id(0) == 0)
    def _():
        scaled = scale_by(data_ref[...], scales_ref)
        norm = jnp.sum(scaled * scaled, axis=0, keepdims=True) * (-0.5 * LOG2E)
        high, middle, low = triple(scaled)
        right[...] = jnp.concatenate(
            [high, middle, high, middle, low, high, norm_rows(norm, inputs), ones_rows(norm, inputs)],
            axis=0,
        )

    scaled = scale_by(centres_ref[...], scales_ref)
    norm = jnp.sum(scaled * scaled, axis=0, keepdims=True) * (-0.5 * LOG2E)
    high, middle, low = triple(scaled * LOG2E)
    left = jnp.concatenate(
        [high, high, middle, middle, high, low, ones_rows(norm, inputs), norm_rows(norm, inputs)], axis=0
    )
    exponent = lax.dot_general(left, right[...], TN, preferred_element_type=jnp.float32)
    high, low = pair(jnp.exp2(exponent))
    high_ref[...] = high
    low_ref[...] = low


def image_kernel(*refs):
    part_refs = refs[:-6]
    high_ref, low_ref, half_ref, mine_ref, out_ref, half_out = refs[-6:]

    half_out[...] = half_ref[...]
    piece = part_refs[0][...]
    for ref in part_refs[1:]:
        piece = piece + ref[...]
    mine_ref[...] = piece
    out_ref[...] = times_pair(piece, high_ref[...], low_ref[...], NN)


def normal_kernel(*refs):
    part_refs = refs[:-3]
    high_ref, low_ref, out_ref = refs[-3:]
    piece = part_refs[0][...]
    for ref in part_refs[1:]:
        piece = piece + ref[...]
    both = stacked(piece)
    out = lax.dot_general(high_ref[...], both, NT, preferred_element_type=jnp.float32)
    out = out + lax.dot_general(low_ref[...], both, NT, preferred_element_type=jnp.float32)
    out_ref[...] = fold(out.T, piece.shape[0])


def source_kernel(scale, order, mine_ref, *refs):
    part_refs = refs[:-4]
    high_ref, low_ref, out_ref, image_ref = refs[-4:]
    total = part_refs[0][...]
    for ref in part_refs[1:]:
        total = total + ref[...]
    normal = total * scale + ridge_weight * mine_ref[...]
    out_ref[...] = normal
    image_ref[...] = fore_apply(normal, high_ref, low_ref, order)


def fore_kernel(order, sides, *refs):
    side_refs = refs[:sides]
    got_ref, source_ref, fh_ref, fl_ref, high_ref, low_ref, image_out = refs[sides:]
    left = source_ref[...] - times_pair(got_ref[...], fh_ref[...], fl_ref[...], NN)
    for ref in side_refs:
        left = left - ref[...]
    image_out[...] = fore_apply(left, high_ref, low_ref, order)


def side_kernel(rows, sides, *refs):
    side_refs = refs[:sides]
    got_refs = refs[sides : sides + len(rows)]
    fh_ref, fl_ref, side_out = refs[sides + len(rows) :]
    row = lax.axis_index("crow")
    piece = got_refs[0][...]
    for at, ref in zip(rows[1:], got_refs[1:]):
        piece = jnp.where(row == at, ref[...], piece)
    side = times_pair(piece, fh_ref[...], fl_ref[...], NN)
    for ref in side_refs:
        side = side + ref[...]
    side_out[...] = side


def sum_kernel(*refs):
    total = refs[0][...]
    for ref in refs[1:-1]:
        total = total + ref[...]
    refs[-1][...] = total


def final_kernel(iterate_ref, residual_ref, direction_ref, *refs):
    part_refs = refs[:-4]
    iterate_out, residual_out, direction_out, image_ref = refs[-4:]
    width = part_refs[0].shape[1]
    row = lax.axis_index("crow")
    for step, ref in enumerate(part_refs):
        at = row ^ step
        image_ref[:, pl.ds(pl.multiple_of(at * width, width), width)] = ref[...]
    residual = residual_ref[...]
    direction = direction_ref[...]
    image = image_ref[...]
    gamma = jnp.sum(residual * residual, axis=1, keepdims=True)
    curvature = jnp.sum(direction * image, axis=1, keepdims=True)
    alpha = gamma / curvature
    iterate_out[...] = iterate_ref[...] + alpha * direction
    new_residual = residual - alpha * image
    residual_out[...] = new_residual
    gamma_next = jnp.sum(new_residual * new_residual, axis=1, keepdims=True)
    direction_out[...] = new_residual + (gamma_next / gamma) * direction


def shaped(*shape):
    return jax.ShapeDtypeStruct(shape, jnp.float32)


def call(kernel, outs, *args, limit=12, cost=(10**6, 10**6), **options):
    return pl.pallas_call(
        kernel,
        out_shape=outs,
        compiler_params=pltpu.CompilerParams(vmem_limit_bytes=limit << 20),
        cost_estimate=pl.CostEstimate(flops=cost[0], bytes_accessed=cost[1], transcendentals=0),
        **options,
    )(*args)


def swap(size, one, other, still=False):
    to = list(range(size))
    to[one], to[other] = other, one
    if not still:
        rest = [n for n in range(size) if n not in (one, other)]
        for a, b in zip(rest[::2], rest[1::2]):
            to[a], to[b] = b, a
    return to


def keep(size):
    return list(range(size))


def step_of(data, centres, scales, factor, block_inv, iterate, residual, direction):
    dp, crow, ccol = lax.axis_size("dp"), lax.axis_size("crow"), lax.axis_size("ccol")
    held, order = block_inv.shape[0], block_inv.shape[1]
    width = factor.shape[0]
    rows, total = direction.shape
    assert factor.shape[1] == width and crow == ccol and crow in (4, 8) and dp % 2 == 0
    part = shaped(rows, width)
    last = crow - 1

    def spot(d, r, c):
        return (d * crow + r) * ccol + c

    def move(value, row_to, col_to, flip=1):
        perm = [
            (spot(d, r, c), spot(d ^ flip, row_to[r], col_to[c]))
            for d in range(dp)
            for r in range(crow)
            for c in range(ccol)
        ]
        return lax.ppermute(value, ("dp", "crow", "ccol"), perm)

    def shifts(value, axis, flip=1):
        out = []
        for step in range(1, lax.axis_size(axis)):
            other = [n ^ step for n in range(lax.axis_size(axis))]
            if axis == "crow":
                out.append(move(value, other, keep(ccol), flip))
            else:
                out.append(move(value, keep(crow), other, flip))
        return out

    def with_tri(kernel, outs, *args, limit=12):
        full = [pl.BlockSpec(a.shape, lambda i, n=a.ndim: (0,) * n) for a in args]
        tri = [pl.BlockSpec((order, order), lambda i, r=r, c=c: (r, c)) for r, c in blocks_of(held)]
        shape = outs.shape
        return call(
            kernel, outs, *args, *([factor] * len(tri)), grid=(1,), in_specs=full + tri,
            out_specs=pl.BlockSpec(shape, lambda i: (0, 0)), limit=limit,
        )

    piece = with_tri(first_kernel, part, direction, block_inv, limit=58)
    found = {last: piece}
    low = with_tri(lower_kernel, shaped(order, len(blocks_of(held)) * order), piece, block_inv)
    wide = jax.ShapeDtypeStruct((width, width), jnp.bfloat16)
    high_f, low_f = call(pair_kernel, [wide, wide], factor)
    turned_f = call(turn_factor_kernel, [wide, wide], factor)
    turned = call(turn_kernel, [wide, wide], low, block_inv)

    samples = data.shape[1]
    tile = order
    inputs = data.shape[0]
    kernel_shape = jax.ShapeDtypeStruct((width, samples), jnp.bfloat16)
    high_k, low_k = call(
        tile_kernel, [kernel_shape] * 2, scales, centres, data,
        grid=(width // tile,),
        in_specs=[
            pl.BlockSpec(memory_space=pltpu.SMEM),
            pl.BlockSpec((inputs, tile), lambda i: (0, i)),
            pl.BlockSpec((inputs, samples), lambda i: (0, 0)),
        ],
        out_specs=[pl.BlockSpec((tile, samples), lambda i: (i, 0))] * 2,
        scratch_shapes=[pltpu.VMEM((8 * inputs, samples), jnp.bfloat16)],
        limit=20,
    )

    def spread(cols, extra, got, lend=()):
        outs = [part, shaped(order // 2, low.shape[1])] if lend else [part]
        return call(
            functools.partial(spread_kernel, cols, len(lend)), outs, *extra, *got, high_f, low_f, *lend
        )

    sums = []
    for step in range(last, 0, -1):
        cols = list(range(step))[::-1]
        got = [move(piece, keep(crow), swap(ccol, step, c)) for c in cols]
        down = (swap(crow, step, step - 1), keep(ccol))
        if step == last:
            sub = move(spread(cols[:1], [], got[:1])[0], *down)
            sums = [move(spread(cols[1:], [], got[1:])[0], *down)]
        else:
            out, *halves = spread(cols, sums, got, [low] if step == 1 else [])
            sub = move(out, *down)
            sums = [sub]
        if step > 1:
            piece = call(solve_kernel, part, direction, sub, low, block_inv)
            found[step - 1] = piece
    pairs = [((n, n), (n, n - 1)) for n in range(1, crow)]
    perm = [
        (spot(d, *one), spot(d, *other))
        for d in range(dp)
        for a, b in pairs
        for one, other in ((a, b), (b, a))
    ]
    half = lax.ppermute(halves[0], ("dp", "crow", "ccol"), perm)
    places = [(n, n) for n in range(1, crow)]
    own = call(
        functools.partial(solve_pick_kernel, places), part, direction, sub, low, block_inv,
        *[found[n] for n in range(1, crow)],
    )

    parts = [own] + shifts(own, "crow")
    mine, images, half = call(
        image_kernel, [part, shaped(rows, samples), shaped(*half.shape)], *parts, high_k, low_k, half,
        limit=16,
    )
    images = [images] + shifts(images, "ccol", 0)
    near = call(merge_kernel, [wide, wide], half, move(half, keep(crow), keep(ccol)), block_inv)
    summed = call(normal_kernel, part, *images, high_k, low_k, limit=16)
    if dp == 2:
        summed = summed + lax.ppermute(summed, "dp", [(0, 1), (1, 0)])
    else:
        summed = lax.psum(summed, "dp")
    parts = [summed] + shifts(summed, "crow")
    scale = 1.0 / (samples * dp * crow)
    source, image = call(
        functools.partial(source_kernel, scale, order), [part, part], mine, *parts, *turned
    )
    done = [image]
    places = [(0, 0)]
    side = []
    for step in range(1, crow):
        before = max(step - 2, 0)
        cols = swap(ccol, before, step - 1, True) if step > 1 else keep(ccol)
        later = list(range(step + 1, crow))
        first = move(image, swap(crow, step - 1, step), cols)
        if step == 1:
            source = move(source, keep(crow), [(c - 1) % ccol for c in range(ccol)])
        if side:
            side = [move(side[0], keep(crow), swap(ccol, before, step - 1))]
        others = [move(image, swap(crow, step - 1, at), cols) for at in later]
        image = call(
            functools.partial(fore_kernel, order, len(side)), part,
            *side, first, source, *turned_f, *near,
        )
        if later:
            side = [
                call(
                    functools.partial(side_kernel, later, len(side)), part, *side, *others, *turned_f
                )
            ]
        done.append(image)
        places.append((step, step - 1))
    own = call(functools.partial(pick_kernel, places), part, *done)
    own = call(sum_kernel, part, own, *shifts(own, "ccol"))
    full = shaped(rows, total)
    return tuple(
        call(
            final_kernel, [full, full, full], iterate, residual, direction, own, *shifts(own, "crow"),
            scratch_shapes=[pltpu.VMEM((rows, total), jnp.float32)],
        )
    )


def solution(mesh):
    placed = (
        P(None, ("dp", "crow")),
        P(None, "ccol"),
        P(),
        P("crow", "ccol"),
        P("crow", None, None),
        P(),
        P(),
        P(),
    )
    return jax.shard_map(
        step_of, mesh=mesh, in_specs=placed, out_specs=(P(), P(), P()), check_vma=False
    )
```

profile of v0, /device:TPU:0, one launch (start us, length us, event | category | flops | bytes accessed | tf_op | source)
XLA Modules:
  0.0 97.2 jit_solution(6368089757490417994)
XLA Ops:
  0.6 3.0 %shard_map.103.after_ref.refs_2_ = f32[8,768]{1,0:T(8,128)} custom-call(f32[8,3072]{1,0:T(8,128)} %direction_ref.9, f32[3,256,256]{2,1,0:T(8,128)} %inv_ref.13, f32[768,768]{1,0:T(8,128)} %factor_ref.3, f32[768,768]{1,0:T(8,128)} %factor_ref.3, f32[768,768]{1,0:T(8,128)} %factor_ref.3), custom_call_target="tpu_custom_call" | custom-call | flops 1000000 | bytes 1000000 | tf_op jit(solution)/shard_map/pallas_call | solution.py:338
  3.6 2.5 %collective-permute-start.3 = (f32[8,768]{1,0:T(8,128)}, f32[8,768]{1,0:T(8,128)S(1)}, u32[]{:S(2)}, u32[]{:S(2)}) collective-permute-start(f32[8,768]{1,0:T(8,128)} %shard_map.103.after_ref.refs_2_), channel_id=1, source_target_pairs={{0,17},{1,16},{2,19},{3,18},{4,21},{5,20},{6,23},{7,22},{8,25},{9,... | collective-permute-start | bytes 73736 | tf_op jit(solution)/shard_map/ppermute | solution.py:380
  6.1 2.9 %collective-permute-start = (f32[8,768]{1,0:T(8,128)}, f32[8,768]{1,0:T(8,128)S(1)}, u32[]{:S(2)}, u32[]{:S(2)}) collective-permute-start(f32[8,768]{1,0:T(8,128)} %shard_map.103.after_ref.refs_2_), channel_id=1, source_target_pairs={{0,18},{1,19},{2,16},{3,17},{4,22},{5,23},{6,20},{7,21},{8,26},{9,... | collective-permute-start | bytes 73736 | tf_op jit(solution)/shard_map/ppermute | solution.py:380
  9.8 1.4 %collective-permute-start.4 = (f32[8,768]{1,0:T(8,128)S(1)}, f32[8,768]{1,0:T(8,128)S(1)}, u32[]{:S(2)}, u32[]{:S(2)}) collective-permute-start(f32[8,768]{1,0:T(8,128)S(1)} %shard_map.106), channel_id=1, source_target_pairs={{0,20},{1,21},{2,22},{3,23},{4,16},{5,17},{6,18},{7,19},{8,28},{9,... | collective-permute-start | bytes 73736 | tf_op jit(solution)/shard_map/ppermute | solution.py:380
  11.2 1.8 %shard_map.107.low_ref.refs_4_ = f32[256,768]{1,0:T(8,128)S(1)} custom-call(f32[8,768]{1,0:T(8,128)S(1)} %copy-done.3, f32[3,256,256]{2,1,0:T(8,128)S(1)} %copy-done.1, f32[768,768]{1,0:T(8,128)S(1)} %copy-done, f32[768,768]{1,0:T(8,128)S(1)} %copy-done, f32[768,768]{1,0:T(8,128)S(1)} %copy-done), custom_call_target="tpu_custom_call" | custom-call | flops 1000000 | bytes 1000000 | tf_op jit(solution)/shard_map/pallas_call | solution.py:338
  13.0 1.5 %collective-permute-done.1.refs_1_ = f32[8,768]{1,0:T(8,128)S(1)} collective-permute-done((f32[8,768]{1,0:T(8,128)}, f32[8,768]{1,0:T(8,128)S(1)}, u32[]{:S(2)}, u32[]{:S(2)}) %collective-permute-start.1) | collective-permute-done | bytes 24608 | tf_op jit(solution)/shard_map/ppermute | solution.py:380
  18.1 3.4 %collective-permute-done.5.refs_1_ = f32[8,768]{1,0:T(8,128)S(1)} collective-permute-done((f32[8,768]{1,0:T(8,128)S(1)}, f32[8,768]{1,0:T(8,128)S(1)}, u32[]{:S(2)}, u32[]{:S(2)}) %collective-permute-start.5) | collective-permute-done | bytes 24608 | tf_op jit(solution)/shard_map/ppermute | solution.py:380
  23.1 1.5 %collective-permute-start.7 = (f32[8,768]{1,0:T(8,128)S(1)}, f32[8,768]{1,0:T(8,128)S(1)}, u32[]{:S(2)}, u32[]{:S(2)}) collective-permute-start(f32[8,768]{1,0:T(8,128)S(1)} %shard_map.109), channel_id=1, source_target_pairs={{0,28},{1,29},{2,30},{3,31},{4,24},{5,25},{6,26},{7,27},{8,20},{9,... | collective-permute-start | bytes 73736 | tf_op jit(solution)/shard_map/ppermute | solution.py:380
  24.7 2.7 %collective-permute-done.7.sub_ref.refs_0_ = f32[8,768]{1,0:T(8,128)S(1)} collective-permute-done((f32[8,768]{1,0:T(8,128)S(1)}, f32[8,768]{1,0:T(8,128)S(1)}, u32[]{:S(2)}, u32[]{:S(2)}) %collective-permute-start.7) | collective-permute-done | bytes 24608 | tf_op jit(solution)/shard_map/ppermute | solution.py:380
  27.7 3.2 %collective-permute-done.8.refs_1_ = f32[8,768]{1,0:T(8,128)S(1)} collective-permute-done((f32[8,768]{1,0:T(8,128)S(1)}, f32[8,768]{1,0:T(8,128)S(1)}, u32[]{:S(2)}, u32[]{:S(2)}) %collective-permute-start.8) | collective-permute-done | bytes 24608 | tf_op jit(solution)/shard_map/ppermute | solution.py:380
  32.2 1.8 %collective-permute-start.9 = (f32[8,768]{1,0:T(8,128)S(1)}, f32[8,768]{1,0:T(8,128)S(1)}, u32[]{:S(2)}, u32[]{:S(2)}) collective-permute-start(f32[8,768]{1,0:T(8,128)S(1)} %get-tuple-element.22), channel_id=1, source_target_pairs={{0,20},{1,21},{2,22},{3,23},{4,16},{5,17},{6,18},{7,19},{8,28},{9,... | collective-permute-start | bytes 73736 | tf_op jit(solution)/shard_map/ppermute | solution.py:380
  34.0 1.5 %collective-permute-done.9.sub_ref = f32[8,768]{1,0:T(8,128)S(1)} collective-permute-done((f32[8,768]{1,0:T(8,128)S(1)}, f32[8,768]{1,0:T(8,128)S(1)}, u32[]{:S(2)}, u32[]{:S(2)}) %collective-permute-start.9) | collective-permute-done | bytes 24608 | tf_op jit(solution)/shard_map/ppermute | solution.py:380
  35.9 2.0 %collective-permute-start.10 = (f32[8,768]{1,0:T(8,128)S(1)}, f32[8,768]{1,0:T(8,128)S(1)}, u32[]{:S(2)}, u32[]{:S(2)}) collective-permute-start(f32[8,768]{1,0:T(8,128)S(1)} %shard_map.112.refs_0_), channel_id=1, source_target_pairs={{0,20},{1,21},{2,22},{3,23},{4,16},{5,17},{6,18},{7,19},{8,28},{9,... | collective-permute-start | bytes 73736 | tf_op jit(solution)/shard_map/ppermute | solution.py:380
  39.2 2.5 %shard_map.113 = (bf16[768,2048]{1,0:T(8,128)(2,1)S(1)}, bf16[768,2048]{1,0:T(8,128)(2,1)S(1)}) custom-call(f32[16]{0:T(128)S(1)} %copy-done.8, f32[16,768]{1,0:T(8,128)S(1)} %copy-done.7, f32[16,2048]{1,0:T(8,128)S(1)} %copy-done.4), custom_call_target="tpu_custom_call" | custom-call | flops 1000000 | bytes 1000000 | tf_op jit(solution)/shard_map/pallas_call | solution.py:338
  43.2 2.2 %collective-permute-start.14 = (f32[8,2048]{1,0:T(8,128)S(1)}, f32[8,2048]{1,0:T(8,128)S(1)}, u32[]{:S(2)}, u32[]{:S(2)}) collective-permute-start(f32[8,2048]{1,0:T(8,128)S(1)} %get-tuple-element.27.refs_0_), channel_id=1, source_target_pairs={{0,1},{1,0},{2,3},{3,2},{4,5},{5,4},{6,7},{7,6},{8,9},{9,8},{10,11... | collective-permute-start | bytes 196616 | tf_op jit(solution)/shard_map/ppermute | solution.py:380
  45.4 1.8 %collective-permute-start.15 = (f32[8,2048]{1,0:T(8,128)S(1)}, f32[8,2048]{1,0:T(8,128)S(1)}, u32[]{:S(2)}, u32[]{:S(2)}) collective-permute-start(f32[8,2048]{1,0:T(8,128)S(1)} %get-tuple-element.27.refs_0_), channel_id=1, source_target_pairs={{0,2},{1,3},{2,0},{3,1},{4,6},{5,7},{6,4},{7,5},{8,10},{9,11},{10,... | collective-permute-start | bytes 196616 | tf_op jit(solution)/shard_map/ppermute | solution.py:380
  47.2 1.4 %collective-permute-start.16 = (f32[8,2048]{1,0:T(8,128)S(1)}, f32[8,2048]{1,0:T(8,128)S(1)}, u32[]{:S(2)}, u32[]{:S(2)}) collective-permute-start(f32[8,2048]{1,0:T(8,128)S(1)} %get-tuple-element.27.refs_0_), channel_id=1, source_target_pairs={{0,3},{1,2},{2,1},{3,0},{4,7},{5,6},{6,5},{7,4},{8,11},{9,10},{10,... | collective-permute-start | bytes 196616 | tf_op jit(solution)/shard_map/ppermute | solution.py:380
  48.7 2.1 %collective-permute-done.15.refs_2_ = f32[8,2048]{1,0:T(8,128)S(1)} collective-permute-done((f32[8,2048]{1,0:T(8,128)S(1)}, f32[8,2048]{1,0:T(8,128)S(1)}, u32[]{:S(2)}, u32[]{:S(2)}) %collective-permute-start.15) | collective-permute-done | bytes 65568 | tf_op jit(solution)/shard_map/ppermute | solution.py:380
  50.7 3.2 %collective-permute-done.16.refs_3_ = f32[8,2048]{1,0:T(8,128)S(1)} collective-permute-done((f32[8,2048]{1,0:T(8,128)S(1)}, f32[8,2048]{1,0:T(8,128)S(1)}, u32[]{:S(2)}, u32[]{:S(2)}) %collective-permute-start.16) | collective-permute-done | bytes 65568 | tf_op jit(solution)/shard_map/ppermute | solution.py:380
  53.9 1.8 %shard_map.115 = f32[8,768]{1,0:T(8,128)S(1)} custom-call(f32[8,2048]{1,0:T(8,128)S(1)} %get-tuple-element.27.refs_0_, f32[8,2048]{1,0:T(8,128)S(1)} %collective-permute-done.14.refs_1_, f32[8,2048]{1,0:T(8,128)S(1)} %collective-permute-done.15.refs_2_, f32[8,2048]{1,0:T(8,128)S(1)} %collective-permute-done.16.refs_3_, ...), custom_call_target="tpu_custom_call" | custom-call | flops 1000000 | bytes 1000000 | tf_op jit(solution)/shard_map/pallas_call | solution.py:338
  61.4 1.9 %collective-permute-done.20.refs_3_ = f32[8,768]{1,0:T(8,128)S(1)} collective-permute-done((f32[8,768]{1,0:T(8,128)S(1)}, f32[8,768]{1,0:T(8,128)S(1)}, u32[]{:S(2)}, u32[]{:S(2)}) %collective-permute-start.20) | collective-permute-done | bytes 24608 | tf_op jit(solution)/shard_map/ppermute | solution.py:380
  64.4 1.6 %collective-permute-start.25 = (f32[8,768]{1,0:T(8,128)S(1)}, f32[8,768]{1,0:T(8,128)S(1)}, u32[]{:S(2)}, u32[]{:S(2)}) collective-permute-start(f32[8,768]{1,0:T(8,128)S(1)} %get-tuple-element.30.refs_0_), channel_id=1, source_target_pairs={{0,28},{1,29},{2,30},{3,31},{4,24},{5,25},{6,26},{7,27},{8,20},{9,... | collective-permute-start | bytes 73736 | tf_op jit(solution)/shard_map/ppermute | solution.py:380
  66.7 2.3 %collective-permute-start.22 = (f32[8,768]{1,0:T(8,128)S(1)}, f32[8,768]{1,0:T(8,128)S(1)}, u32[]{:S(2)}, u32[]{:S(2)}) collective-permute-start(f32[8,768]{1,0:T(8,128)S(1)} %get-tuple-element.31), channel_id=1, source_target_pairs={{0,19},{1,16},{2,17},{3,18},{4,23},{5,20},{6,21},{7,22},{8,27},{9,... | collective-permute-start | bytes 73736 | tf_op jit(solution)/shard_map/ppermute | solution.py:380
  71.4 1.3 %collective-permute-start.28 = (f32[8,768]{1,0:T(8,128)S(1)}, f32[8,768]{1,0:T(8,128)S(1)}, u32[]{:S(2)}, u32[]{:S(2)}) collective-permute-start(f32[8,768]{1,0:T(8,128)S(1)} %shard_map.120.refs_1_), channel_id=1, source_target_pairs={{0,25},{1,24},{2,26},{3,27},{4,29},{5,28},{6,30},{7,31},{8,17},{9,... | collective-permute-start | bytes 73736 | tf_op jit(solution)/shard_map/ppermute | solution.py:380
  72.7 1.7 %collective-permute-start.27 = (f32[8,768]{1,0:T(8,128)S(1)}, f32[8,768]{1,0:T(8,128)S(1)}, u32[]{:S(2)}, u32[]{:S(2)}) collective-permute-start(f32[8,768]{1,0:T(8,128)S(1)} %shard_map.120.refs_1_), channel_id=1, source_target_pairs={{0,29},{1,28},{2,30},{3,31},{4,25},{5,24},{6,26},{7,27},{8,21},{9,... | collective-permute-start | bytes 73736 | tf_op jit(solution)/shard_map/ppermute | solution.py:380
  76.0 2.5 %collective-permute-start.29 = (f32[8,768]{1,0:T(8,128)S(1)}, f32[8,768]{1,0:T(8,128)S(1)}, u32[]{:S(2)}, u32[]{:S(2)}) collective-permute-start(f32[8,768]{1,0:T(8,128)S(1)} %shard_map.123), channel_id=1, source_target_pairs={{0,19},{1,18},{2,17},{3,16},{4,23},{5,22},{6,21},{7,20},{8,27},{9,... | collective-permute-start | bytes 73736 | tf_op jit(solution)/shard_map/ppermute | solution.py:380
  79.6 1.5 %collective-permute-done.29.refs_0_ = f32[8,768]{1,0:T(8,128)S(1)} collective-permute-done((f32[8,768]{1,0:T(8,128)S(1)}, f32[8,768]{1,0:T(8,128)S(1)}, u32[]{:S(2)}, u32[]{:S(2)}) %collective-permute-start.29) | collective-permute-done | bytes 24608 | tf_op jit(solution)/shard_map/ppermute | solution.py:380
  81.1 1.3 %collective-permute-done.30.refs_1_ = f32[8,768]{1,0:T(8,128)S(1)} collective-permute-done((f32[8,768]{1,0:T(8,128)S(1)}, f32[8,768]{1,0:T(8,128)S(1)}, u32[]{:S(2)}, u32[]{:S(2)}) %collective-permute-start.30) | collective-permute-done | bytes 24608 | tf_op jit(solution)/shard_map/ppermute | solution.py:380
  84.6 2.4 %collective-permute-start.33 = (f32[8,768]{1,0:T(8,128)S(1)}, f32[8,768]{1,0:T(8,128)S(1)}, u32[]{:S(2)}, u32[]{:S(2)}) collective-permute-start(f32[8,768]{1,0:T(8,128)S(1)} %shard_map.125.refs_0_), channel_id=1, source_target_pairs={{0,19},{1,18},{2,17},{3,16},{4,23},{5,22},{6,21},{7,20},{8,27},{9,... | collective-permute-start | bytes 73736 | tf_op jit(solution)/shard_map/ppermute | solution.py:380
  87.0 1.7 %collective-permute-done.32.refs_2_ = f32[8,768]{1,0:T(8,128)S(1)} collective-permute-done((f32[8,768]{1,0:T(8,128)S(1)}, f32[8,768]{1,0:T(8,128)S(1)}, u32[]{:S(2)}, u32[]{:S(2)}) %collective-permute-start.32) | collective-permute-done | bytes 24608 | tf_op jit(solution)/shard_map/ppermute | solution.py:380
  90.9 1.3 %collective-permute-start.35 = (f32[8,768]{1,0:T(8,128)S(1)}, f32[8,768]{1,0:T(8,128)S(1)}, u32[]{:S(2)}, u32[]{:S(2)}) collective-permute-start(f32[8,768]{1,0:T(8,128)S(1)} %shard_map.126.refs_0_), channel_id=1, source_target_pairs={{0,24},{1,25},{2,26},{3,27},{4,28},{5,29},{6,30},{7,31},{8,16},{9,... | collective-permute-start | bytes 73736 | tf_op jit(solution)/shard_map/ppermute | solution.py:380
  94.1 2.2 %collective-permute-done.36.refs_3_ = f32[8,768]{1,0:T(8,128)S(1)} collective-permute-done((f32[8,768]{1,0:T(8,128)S(1)}, f32[8,768]{1,0:T(8,128)S(1)}, u32[]{:S(2)}, u32[]{:S(2)}) %collective-permute-start.36) | collective-permute-done | bytes 24608 | tf_op jit(solution)/shard_map/ppermute | solution.py:380
  (86 shorter events, 30.4 us)
Async XLA Ops:
  3.6 5.7 %collective-permute-start.3 = (f32[8,768]{1,0:T(8,128)}, f32[8,768]{1,0:T(8,128)S(1)}, u32[]{:S(2)}, u32[]{:S(2)}) collective-permute-start(f32[8,768]{1,0:T(8,128)} %shard_map.103.after_ref.refs_2_), channel_id=1, source_target_pairs={{0,17},{1,16},{2,19},{3,18},{4,21},{5,20},{6,23},{7,22},{8,25},{9,... | collective-permute-start | bytes 73736 | tf_op jit(solution)/shard_map/ppermute | solution.py:380
  6.1 6.9 %collective-permute-start = (f32[8,768]{1,0:T(8,128)}, f32[8,768]{1,0:T(8,128)S(1)}, u32[]{:S(2)}, u32[]{:S(2)}) collective-permute-start(f32[8,768]{1,0:T(8,128)} %shard_map.103.after_ref.refs_2_), channel_id=1, source_target_pairs={{0,18},{1,19},{2,16},{3,17},{4,22},{5,23},{6,20},{7,21},{8,26},{9,... | collective-permute-start | bytes 73736 | tf_op jit(solution)/shard_map/ppermute | solution.py:380
  9.0 5.5 %collective-permute-start.1 = (f32[8,768]{1,0:T(8,128)}, f32[8,768]{1,0:T(8,128)S(1)}, u32[]{:S(2)}, u32[]{:S(2)}) collective-permute-start(f32[8,768]{1,0:T(8,128)} %shard_map.103.after_ref.refs_2_), channel_id=1, source_target_pairs={{0,19},{1,18},{2,17},{3,16},{4,23},{5,22},{6,21},{7,20},{8,27},{9,... | collective-permute-start | bytes 73736 | tf_op jit(solution)/shard_map/ppermute | solution.py:380
  9.8 6.4 %collective-permute-start.4 = (f32[8,768]{1,0:T(8,128)S(1)}, f32[8,768]{1,0:T(8,128)S(1)}, u32[]{:S(2)}, u32[]{:S(2)}) collective-permute-start(f32[8,768]{1,0:T(8,128)S(1)} %shard_map.106), channel_id=1, source_target_pairs={{0,20},{1,21},{2,22},{3,23},{4,16},{5,17},{6,18},{7,19},{8,28},{9,... | collective-permute-start | bytes 73736 | tf_op jit(solution)/shard_map/ppermute | solution.py:380
  16.5 5.1 %collective-permute-start.5 = (f32[8,768]{1,0:T(8,128)S(1)}, f32[8,768]{1,0:T(8,128)S(1)}, u32[]{:S(2)}, u32[]{:S(2)}) collective-permute-start(f32[8,768]{1,0:T(8,128)S(1)} %shard_map.108.refs_1_), channel_id=1, source_target_pairs={{0,19},{1,18},{2,17},{3,16},{4,23},{5,22},{6,21},{7,20},{8,27},{9,... | collective-permute-start | bytes 73736 | tf_op jit(solution)/shard_map/ppermute | solution.py:380
  17.7 5.1 %collective-permute-start.6 = (f32[8,768]{1,0:T(8,128)S(1)}, f32[8,768]{1,0:T(8,128)S(1)}, u32[]{:S(2)}, u32[]{:S(2)}) collective-permute-start(f32[8,768]{1,0:T(8,128)S(1)} %shard_map.108.refs_1_), channel_id=1, source_target_pairs={{0,18},{1,19},{2,16},{3,17},{4,22},{5,23},{6,20},{7,21},{8,26},{9,... | collective-permute-start | bytes 73736 | tf_op jit(solution)/shard_map/ppermute | solution.py:380
  23.1 4.2 %collective-permute-start.7 = (f32[8,768]{1,0:T(8,128)S(1)}, f32[8,768]{1,0:T(8,128)S(1)}, u32[]{:S(2)}, u32[]{:S(2)}) collective-permute-start(f32[8,768]{1,0:T(8,128)S(1)} %shard_map.109), channel_id=1, source_target_pairs={{0,28},{1,29},{2,30},{3,31},{4,24},{5,25},{6,26},{7,27},{8,20},{9,... | collective-permute-start | bytes 73736 | tf_op jit(solution)/shard_map/ppermute | solution.py:380
  31.4 10.7 %collective-permute-start.13 = (f32[128,768]{1,0:T(8,128)S(1)}, f32[128,768]{1,0:T(8,128)S(1)}, u32[]{:S(2)}, u32[]{:S(2)}) collective-permute-start(f32[128,768]{1,0:T(8,128)S(1)} %get-tuple-element.25), channel_id=1, source_target_pairs={{5,4},{4,5},{10,9},{9,10},{15,14},{14,15},{21,20},{20,21},{26,25},... | collective-permute-start | bytes 1179656 | tf_op jit(solution)/shard_map/ppermute | solution.py:454
  32.2 3.4 %collective-permute-start.9 = (f32[8,768]{1,0:T(8,128)S(1)}, f32[8,768]{1,0:T(8,128)S(1)}, u32[]{:S(2)}, u32[]{:S(2)}) collective-permute-start(f32[8,768]{1,0:T(8,128)S(1)} %get-tuple-element.22), channel_id=1, source_target_pairs={{0,20},{1,21},{2,22},{3,23},{4,16},{5,17},{6,18},{7,19},{8,28},{9,... | collective-permute-start | bytes 73736 | tf_op jit(solution)/shard_map/ppermute | solution.py:380
  35.9 5.8 %collective-permute-start.10 = (f32[8,768]{1,0:T(8,128)S(1)}, f32[8,768]{1,0:T(8,128)S(1)}, u32[]{:S(2)}, u32[]{:S(2)}) collective-permute-start(f32[8,768]{1,0:T(8,128)S(1)} %shard_map.112.refs_0_), channel_id=1, source_target_pairs={{0,20},{1,21},{2,22},{3,23},{4,16},{5,17},{6,18},{7,19},{8,28},{9,... | collective-permute-start | bytes 73736 | tf_op jit(solution)/shard_map/ppermute | solution.py:380
  37.9 3.8 %collective-permute-start.11 = (f32[8,768]{1,0:T(8,128)S(1)}, f32[8,768]{1,0:T(8,128)S(1)}, u32[]{:S(2)}, u32[]{:S(2)}) collective-permute-start(f32[8,768]{1,0:T(8,128)S(1)} %shard_map.112.refs_0_), channel_id=1, source_target_pairs={{0,24},{1,25},{2,26},{3,27},{4,28},{5,29},{6,30},{7,31},{8,16},{9,... | collective-permute-start | bytes 73736 | tf_op jit(solution)/shard_map/ppermute | solution.py:380
  37.9 4.2 %collective-permute-start.12 = (f32[8,768]{1,0:T(8,128)S(1)}, f32[8,768]{1,0:T(8,128)S(1)}, u32[]{:S(2)}, u32[]{:S(2)}) collective-permute-start(f32[8,768]{1,0:T(8,128)S(1)} %shard_map.112.refs_0_), channel_id=1, source_target_pairs={{0,28},{1,29},{2,30},{3,31},{4,24},{5,25},{6,26},{7,27},{8,20},{9,... | collective-permute-start | bytes 73736 | tf_op jit(solution)/shard_map/ppermute | solution.py:380
  43.0 27.2 %collective-permute-start.23 = (f32[128,768]{1,0:T(8,128)S(1)}, f32[128,768]{1,0:T(8,128)S(1)}, u32[]{:S(2)}, u32[]{:S(2)}) collective-permute-start(f32[128,768]{1,0:T(8,128)S(1)} %get-tuple-element.34.mine_ref), channel_id=1, source_target_pairs={{0,16},{1,17},{2,18},{3,19},{4,20},{5,21},{6,22},{7,23},{8,24},{9,... | collective-permute-start | bytes 1179656 | tf_op jit(solution)/shard_map/ppermute | solution.py:380
  43.2 5.5 %collective-permute-start.14 = (f32[8,2048]{1,0:T(8,128)S(1)}, f32[8,2048]{1,0:T(8,128)S(1)}, u32[]{:S(2)}, u32[]{:S(2)}) collective-permute-start(f32[8,2048]{1,0:T(8,128)S(1)} %get-tuple-element.27.refs_0_), channel_id=1, source_target_pairs={{0,1},{1,0},{2,3},{3,2},{4,5},{5,4},{6,7},{7,6},{8,9},{9,8},{10,11... | collective-permute-start | bytes 196616 | tf_op jit(solution)/shard_map/ppermute | solution.py:380
  45.4 5.3 %collective-permute-start.15 = (f32[8,2048]{1,0:T(8,128)S(1)}, f32[8,2048]{1,0:T(8,128)S(1)}, u32[]{:S(2)}, u32[]{:S(2)}) collective-permute-start(f32[8,2048]{1,0:T(8,128)S(1)} %get-tuple-element.27.refs_0_), channel_id=1, source_target_pairs={{0,2},{1,3},{2,0},{3,1},{4,6},{5,7},{6,4},{7,5},{8,10},{9,11},{10,... | collective-permute-start | bytes 196616 | tf_op jit(solution)/shard_map/ppermute | solution.py:380
  47.2 6.7 %collective-permute-start.16 = (f32[8,2048]{1,0:T(8,128)S(1)}, f32[8,2048]{1,0:T(8,128)S(1)}, u32[]{:S(2)}, u32[]{:S(2)}) collective-permute-start(f32[8,2048]{1,0:T(8,128)S(1)} %get-tuple-element.27.refs_0_), channel_id=1, source_target_pairs={{0,3},{1,2},{2,1},{3,0},{4,7},{5,6},{6,5},{7,4},{8,11},{9,10},{10,... | collective-permute-start | bytes 196616 | tf_op jit(solution)/shard_map/ppermute | solution.py:380
  57.0 3.5 %collective-permute-start.18 = (f32[8,768]{1,0:T(8,128)S(1)}, f32[8,768]{1,0:T(8,128)S(1)}, u32[]{:S(2)}, u32[]{:S(2)}) collective-permute-start(f32[8,768]{1,0:T(8,128)S(1)} %add.3.refs_0_), channel_id=1, source_target_pairs={{0,20},{1,21},{2,22},{3,23},{4,16},{5,17},{6,18},{7,19},{8,28},{9,... | collective-permute-start | bytes 73736 | tf_op jit(solution)/shard_map/ppermute | solution.py:380
  59.2 4.2 %collective-permute-start.20 = (f32[8,768]{1,0:T(8,128)S(1)}, f32[8,768]{1,0:T(8,128)S(1)}, u32[]{:S(2)}, u32[]{:S(2)}) collective-permute-start(f32[8,768]{1,0:T(8,128)S(1)} %add.3.refs_0_), channel_id=1, source_target_pairs={{0,28},{1,29},{2,30},{3,31},{4,24},{5,25},{6,26},{7,27},{8,20},{9,... | collective-permute-start | bytes 73736 | tf_op jit(solution)/shard_map/ppermute | solution.py:380
  63.7 6.0 %collective-permute-start.24 = (f32[8,768]{1,0:T(8,128)S(1)}, f32[8,768]{1,0:T(8,128)S(1)}, u32[]{:S(2)}, u32[]{:S(2)}) collective-permute-start(f32[8,768]{1,0:T(8,128)S(1)} %get-tuple-element.30.refs_0_), channel_id=1, source_target_pairs={{0,24},{1,25},{2,26},{3,27},{4,28},{5,29},{6,30},{7,31},{8,16},{9,... | collective-permute-start | bytes 73736 | tf_op jit(solution)/shard_map/ppermute | solution.py:380
  64.4 5.3 %collective-permute-start.25 = (f32[8,768]{1,0:T(8,128)S(1)}, f32[8,768]{1,0:T(8,128)S(1)}, u32[]{:S(2)}, u32[]{:S(2)}) collective-permute-start(f32[8,768]{1,0:T(8,128)S(1)} %get-tuple-element.30.refs_0_), channel_id=1, source_target_pairs={{0,28},{1,29},{2,30},{3,31},{4,24},{5,25},{6,26},{7,27},{8,20},{9,... | collective-permute-start | bytes 73736 | tf_op jit(solution)/shard_map/ppermute | solution.py:380
  66.0 4.7 %collective-permute-start.21 = (f32[8,768]{1,0:T(8,128)S(1)}, f32[8,768]{1,0:T(8,128)S(1)}, u32[]{:S(2)}, u32[]{:S(2)}) collective-permute-start(f32[8,768]{1,0:T(8,128)S(1)} %get-tuple-element.30.refs_0_), channel_id=1, source_target_pairs={{0,20},{1,21},{2,22},{3,23},{4,16},{5,17},{6,18},{7,19},{8,28},{9,... | collective-permute-start | bytes 73736 | tf_op jit(solution)/shard_map/ppermute | solution.py:380
  66.7 4.0 %collective-permute-start.22 = (f32[8,768]{1,0:T(8,128)S(1)}, f32[8,768]{1,0:T(8,128)S(1)}, u32[]{:S(2)}, u32[]{:S(2)}) collective-permute-start(f32[8,768]{1,0:T(8,128)S(1)} %get-tuple-element.31), channel_id=1, source_target_pairs={{0,19},{1,16},{2,17},{3,18},{4,23},{5,20},{6,21},{7,22},{8,27},{9,... | collective-permute-start | bytes 73736 | tf_op jit(solution)/shard_map/ppermute | solution.py:380
  70.1 4.3 %collective-permute-start.26 = (f32[8,768]{1,0:T(8,128)S(1)}, f32[8,768]{1,0:T(8,128)S(1)}, u32[]{:S(2)}, u32[]{:S(2)}) collective-permute-start(f32[8,768]{1,0:T(8,128)S(1)} %shard_map.121), channel_id=1, source_target_pairs={{0,17},{1,16},{2,19},{3,18},{4,21},{5,20},{6,23},{7,22},{8,25},{9,... | collective-permute-start | bytes 73736 | tf_op jit(solution)/shard_map/ppermute | solution.py:380
  71.4 4.2 %collective-permute-start.28 = (f32[8,768]{1,0:T(8,128)S(1)}, f32[8,768]{1,0:T(8,128)S(1)}, u32[]{:S(2)}, u32[]{:S(2)}) collective-permute-start(f32[8,768]{1,0:T(8,128)S(1)} %shard_map.120.refs_1_), channel_id=1, source_target_pairs={{0,25},{1,24},{2,26},{3,27},{4,29},{5,28},{6,30},{7,31},{8,17},{9,... | collective-permute-start | bytes 73736 | tf_op jit(solution)/shard_map/ppermute | solution.py:380
  72.7 5.7 %collective-permute-start.27 = (f32[8,768]{1,0:T(8,128)S(1)}, f32[8,768]{1,0:T(8,128)S(1)}, u32[]{:S(2)}, u32[]{:S(2)}) collective-permute-start(f32[8,768]{1,0:T(8,128)S(1)} %shard_map.120.refs_1_), channel_id=1, source_target_pairs={{0,29},{1,28},{2,30},{3,31},{4,25},{5,24},{6,26},{7,27},{8,21},{9,... | collective-permute-start | bytes 73736 | tf_op jit(solution)/shard_map/ppermute | solution.py:380
  76.0 5.2 %collective-permute-start.29 = (f32[8,768]{1,0:T(8,128)S(1)}, f32[8,768]{1,0:T(8,128)S(1)}, u32[]{:S(2)}, u32[]{:S(2)}) collective-permute-start(f32[8,768]{1,0:T(8,128)S(1)} %shard_map.123), channel_id=1, source_target_pairs={{0,19},{1,18},{2,17},{3,16},{4,23},{5,22},{6,21},{7,20},{8,27},{9,... | collective-permute-start | bytes 73736 | tf_op jit(solution)/shard_map/ppermute | solution.py:380
  79.1 3.3 %collective-permute-start.30 = (f32[8,768]{1,0:T(8,128)S(1)}, f32[8,768]{1,0:T(8,128)S(1)}, u32[]{:S(2)}, u32[]{:S(2)}) collective-permute-start(f32[8,768]{1,0:T(8,128)S(1)} %shard_map.122.refs_2_), channel_id=1, source_target_pairs={{0,20},{1,22},{2,21},{3,23},{4,16},{5,18},{6,17},{7,19},{8,28},{9,... | collective-permute-start | bytes 73736 | tf_op jit(solution)/shard_map/ppermute | solution.py:380
  83.1 3.9 %collective-permute-start.31 = (f32[8,768]{1,0:T(8,128)S(1)}, f32[8,768]{1,0:T(8,128)S(1)}, u32[]{:S(2)}, u32[]{:S(2)}) collective-permute-start(f32[8,768]{1,0:T(8,128)S(1)} %shard_map.125.refs_0_), channel_id=1, source_target_pairs={{0,17},{1,16},{2,19},{3,18},{4,21},{5,20},{6,23},{7,22},{8,25},{9,... | collective-permute-start | bytes 73736 | tf_op jit(solution)/shard_map/ppermute | solution.py:380
  84.3 4.5 %collective-permute-start.32 = (f32[8,768]{1,0:T(8,128)S(1)}, f32[8,768]{1,0:T(8,128)S(1)}, u32[]{:S(2)}, u32[]{:S(2)}) collective-permute-start(f32[8,768]{1,0:T(8,128)S(1)} %shard_map.125.refs_0_), channel_id=1, source_target_pairs={{0,18},{1,19},{2,16},{3,17},{4,22},{5,23},{6,20},{7,21},{8,26},{9,... | collective-permute-start | bytes 73736 | tf_op jit(solution)/shard_map/ppermute | solution.py:380
  84.6 5.1 %collective-permute-start.33 = (f32[8,768]{1,0:T(8,128)S(1)}, f32[8,768]{1,0:T(8,128)S(1)}, u32[]{:S(2)}, u32[]{:S(2)}) collective-permute-start(f32[8,768]{1,0:T(8,128)S(1)} %shard_map.125.refs_0_), channel_id=1, source_target_pairs={{0,19},{1,18},{2,17},{3,16},{4,23},{5,22},{6,21},{7,20},{8,27},{9,... | collective-permute-start | bytes 73736 | tf_op jit(solution)/shard_map/ppermute | solution.py:380
  89.7 3.3 %collective-permute-start.34 = (f32[8,768]{1,0:T(8,128)S(1)}, f32[8,768]{1,0:T(8,128)S(1)}, u32[]{:S(2)}, u32[]{:S(2)}) collective-permute-start(f32[8,768]{1,0:T(8,128)S(1)} %shard_map.126.refs_0_), channel_id=1, source_target_pairs={{0,20},{1,21},{2,22},{3,23},{4,16},{5,17},{6,18},{7,19},{8,28},{9,... | collective-permute-start | bytes 73736 | tf_op jit(solution)/shard_map/ppermute | solution.py:380
  92.2 4.2 %collective-permute-start.36 = (f32[8,768]{1,0:T(8,128)S(1)}, f32[8,768]{1,0:T(8,128)S(1)}, u32[]{:S(2)}, u32[]{:S(2)}) collective-permute-start(f32[8,768]{1,0:T(8,128)S(1)} %shard_map.126.refs_0_), channel_id=1, source_target_pairs={{0,28},{1,29},{2,30},{3,31},{4,24},{5,25},{6,26},{7,27},{8,20},{9,... | collective-permute-start | bytes 73736 | tf_op jit(solution)/shard_map/ppermute | solution.py:380
  (14 other events, 87.5 us)
where the time goes:
time: 97.4 us; the launch traced here: 97.2 us
  starting transfers between devices  43.9 us (45%)
  waiting for transfers between devices  33.8 us (35%)
  Pallas kernels  18.7 us (19%)
    ppermute x35, starting transfers between devices, move(): return lax.ppermute(value, ('dp', 'crow', 'ccol'), perm)  43 us
    ppermute x35, waiting for transfers between devices, move(): return lax.ppermute(value, ('dp', 'crow', 'ccol'), perm)  32.6 us
    pallas_call x25, Pallas kernels, call(): pl.pallas_call(kernel, out_shape=outs, compiler_params=pltpu.CompilerPara...  18.7 us
  transfers between devices with their start and end apart: 37, of which 21 were waited for; matrix products, arithmetic and copies ran while one was open for 0% of the time, Pallas kernels for 12%

commit v1 on v0

--- a/solution.py
+++ b/solution.py
@@ -138,18 +138,10 @@
     low_ref[...] = low
 
 
-def spread_kernel(cols, lend, *refs):
-    outs = refs[len(refs) - 1 - lend :]
-    refs = refs[: len(refs) - 1 - lend]
-    if lend:
-        low_of, half = refs[-1], outs[1]
-        tall = half.shape[0]
-        at = lax.rem(lax.axis_index("dp"), 2) * tall
-        half[...] = low_of[pl.ds(pl.multiple_of(at, tall), tall), :]
-        refs = refs[:-1]
-    extra = refs[: len(refs) - 2 - len(cols)]
+def spread_kernel(cols, *refs):
+    extra = refs[: len(refs) - 3 - len(cols)]
     got_refs = refs[len(extra) : len(extra) + len(cols)]
-    high_ref, low_ref = refs[-2:]
+    high_ref, low_ref, out_ref = refs[-3:]
     col = lax.axis_index("ccol")
     piece = got_refs[0][...]
     for at, got in zip(cols[1:], got_refs[1:]):
@@ -157,13 +149,13 @@
     out = times_pair(piece, high_ref[...], low_ref[...], NN)
     for ref in extra:
         out = out + ref[...]
-    outs[0][...] = out
+    out_ref[...] = out
 
 
 def merge_kernel(mine_ref, other_ref, inv_ref, high_out, low_out):
     odd = lax.rem(lax.axis_index("dp"), 2) == 1
     mine, other = mine_ref[...], other_ref[...]
-    low = jnp.concatenate([jnp.where(odd, other, mine), jnp.where(odd, mine, other)], axis=0)
+    low = jnp.concatenate([jnp.where(odd, mine, other), jnp.where(odd, other, mine)], axis=0)
     store_turned(low, inv_ref, high_out, low_out)
 
 
@@ -245,10 +237,8 @@
 
 
 def image_kernel(*refs):
-    part_refs = refs[:-6]
-    high_ref, low_ref, half_ref, mine_ref, out_ref, half_out = refs[-6:]
-
-    half_out[...] = half_ref[...]
+    part_refs = refs[:-4]
+    high_ref, low_ref, mine_ref, out_ref = refs[-4:]
     piece = part_refs[0][...]
     for ref in part_refs[1:]:
         piece = piece + ref[...]
@@ -257,8 +247,11 @@
 
 
 def normal_kernel(*refs):
-    part_refs = refs[:-3]
-    high_ref, low_ref, out_ref = refs[-3:]
+    part_refs = refs[:-5]
+    high_ref, low_ref, lower_ref, out_ref, half_ref = refs[-5:]
+    tall = half_ref.shape[0]
+    at = lax.rem(lax.axis_index("dp"), 2) * tall
+    half_ref[...] = lower_ref[pl.ds(pl.multiple_of(at, tall), tall), :]
     piece = part_refs[0][...]
     for ref in part_refs[1:]:
         piece = piece + ref[...]
@@ -269,8 +262,9 @@
 
 
 def source_kernel(scale, order, mine_ref, *refs):
-    part_refs = refs[:-4]
-    high_ref, low_ref, out_ref, image_ref = refs[-4:]
+    part_refs = refs[:-6]
+    high_ref, low_ref, half_ref, out_ref, image_ref, half_out = refs[-6:]
+    half_out[...] = half_ref[...]
     total = part_refs[0][...]
     for ref in part_refs[1:]:
         total = total + ref[...]
@@ -344,20 +338,6 @@
     )(*args)
 
 
-def swap(size, one, other, still=False):
-    to = list(range(size))
-    to[one], to[other] = other, one
-    if not still:
-        rest = [n for n in range(size) if n not in (one, other)]
-        for a, b in zip(rest[::2], rest[1::2]):
-            to[a], to[b] = b, a
-    return to
-
-
-def keep(size):
-    return list(range(size))
-
-
 def step_of(data, centres, scales, factor, block_inv, iterate, residual, direction):
     dp, crow, ccol = lax.axis_size("dp"), lax.axis_size("crow"), lax.axis_size("ccol")
     held, order = block_inv.shape[0], block_inv.shape[1]
@@ -370,24 +350,25 @@
     def spot(d, r, c):
         return (d * crow + r) * ccol + c
 
-    def move(value, row_to, col_to, flip=1):
+    def permute(value, target):
         perm = [
-            (spot(d, r, c), spot(d ^ flip, row_to[r], col_to[c]))
+            (spot(d, r, c), spot(*target(d, r, c)))
             for d in range(dp)
             for r in range(crow)
             for c in range(ccol)
         ]
         return lax.ppermute(value, ("dp", "crow", "ccol"), perm)
 
+    def move(value, *pairs):
+        to = dict(pairs)
+        to.update((b, a) for a, b in pairs)
+        return permute(value, lambda d, r, c: (d ^ 1, *to.get((r, c), (r, c))))
+
     def shifts(value, axis, flip=1):
-        out = []
-        for step in range(1, lax.axis_size(axis)):
-            other = [n ^ step for n in range(lax.axis_size(axis))]
-            if axis == "crow":
-                out.append(move(value, other, keep(ccol), flip))
-            else:
-                out.append(move(value, keep(crow), other, flip))
-        return out
+        steps = range(1, lax.axis_size(axis))
+        if axis == "crow":
+            return [permute(value, lambda d, r, c: (d ^ flip, r ^ n, c)) for n in steps]
+        return [permute(value, lambda d, r, c: (d ^ flip, r, c ^ n)) for n in steps]
 
     def with_tri(kernel, outs, *args, limit=12):
         full = [pl.BlockSpec(a.shape, lambda i, n=a.ndim: (0,) * n) for a in args]
@@ -423,35 +404,23 @@
         limit=20,
     )
 
-    def spread(cols, extra, got, lend=()):
-        outs = [part, shaped(order // 2, low.shape[1])] if lend else [part]
-        return call(
-            functools.partial(spread_kernel, cols, len(lend)), outs, *extra, *got, high_f, low_f, *lend
-        )
+    def spread(cols, extra, got):
+        return call(functools.partial(spread_kernel, cols), part, *extra, *got, high_f, low_f)
 
     sums = []
     for step in range(last, 0, -1):
         cols = list(range(step))[::-1]
-        got = [move(piece, keep(crow), swap(ccol, step, c)) for c in cols]
-        down = (swap(crow, step, step - 1), keep(ccol))
+        got = [move(piece, ((step, step), (step, c))) for c in cols]
+        down = [((step, c), (step - 1, c)) for c in cols]
         if step == last:
-            sub = move(spread(cols[:1], [], got[:1])[0], *down)
-            sums = [move(spread(cols[1:], [], got[1:])[0], *down)]
+            sub = move(spread(cols[:1], [], got[:1]), down[0])
+            sums = [move(spread(cols[1:], [], got[1:]), *down[1:])]
         else:
-            out, *halves = spread(cols, sums, got, [low] if step == 1 else [])
-            sub = move(out, *down)
+            sub = move(spread(cols, sums, got), *down)
             sums = [sub]
         if step > 1:
             piece = call(solve_kernel, part, direction, sub, low, block_inv)
             found[step - 1] = piece
-    pairs = [((n, n), (n, n - 1)) for n in range(1, crow)]
-    perm = [
-        (spot(d, *one), spot(d, *other))
-        for d in range(dp)
-        for a, b in pairs
-        for one, other in ((a, b), (b, a))
-    ]
-    half = lax.ppermute(halves[0], ("dp", "crow", "ccol"), perm)
     places = [(n, n) for n in range(1, crow)]
     own = call(
         functools.partial(solve_pick_kernel, places), part, direction, sub, low, block_inv,
@@ -459,35 +428,35 @@
     )
 
     parts = [own] + shifts(own, "crow")
-    mine, images, half = call(
-        image_kernel, [part, shaped(rows, samples), shaped(*half.shape)], *parts, high_k, low_k, half,
-        limit=16,
-    )
+    mine, images = call(image_kernel, [part, shaped(rows, samples)], *parts, high_k, low_k, limit=16)
     images = [images] + shifts(images, "ccol", 0)
-    near = call(merge_kernel, [wide, wide], half, move(half, keep(crow), keep(ccol)), block_inv)
-    summed = call(normal_kernel, part, *images, high_k, low_k, limit=16)
+    half = shaped(order // 2, low.shape[1])
+    summed, half = call(normal_kernel, [part, half], *images, high_k, low_k, low, limit=16)
     if dp == 2:
-        summed = summed + lax.ppermute(summed, "dp", [(0, 1), (1, 0)])
+        summed = summed + permute(summed, lambda d, r, c: (d ^ 1, r, c))
     else:
         summed = lax.psum(summed, "dp")
     parts = [summed] + shifts(summed, "crow")
+    beside = [((n, n), (n, n - 1)) for n in range(1, crow)]
+    half = move(half, *beside)
     scale = 1.0 / (samples * dp * crow)
-    source, image = call(
-        functools.partial(source_kernel, scale, order), [part, part], mine, *parts, *turned
-    )
+    source, image, half = call(
+        functools.partial(source_kernel, scale, order), [part, part, shaped(*half.shape)],
+        mine, *parts, *turned, half,
+    )
+    near = call(merge_kernel, [wide, wide], half, move(half), block_inv)
     done = [image]
     places = [(0, 0)]
     side = []
     for step in range(1, crow):
-        before = max(step - 2, 0)
-        cols = swap(ccol, before, step - 1, True) if step > 1 else keep(ccol)
         later = list(range(step + 1, crow))
-        first = move(image, swap(crow, step - 1, step), cols)
+        first = move(image, (places[-1], (step, step - 1)))
         if step == 1:
-            source = move(source, keep(crow), [(c - 1) % ccol for c in range(ccol)])
+            source = move(source, *beside)
         if side:
-            side = [move(side[0], keep(crow), swap(ccol, before, step - 1))]
-        others = [move(image, swap(crow, step - 1, at), cols) for at in later]
+            shift = [((at, step - 2), (at, step - 1)) for at in range(step, crow)]
+            side = [move(side[0], *shift)]
+        others = [move(image, (places[-1], (at, step - 1))) for at in later]
         image = call(
             functools.partial(fore_kernel, order, len(side)), part,
             *side, first, source, *turned_f, *near,

time: 97.4 us -> 87.3 us (0.90)
  waiting for transfers between devices: 33.8 us -> 19.5 us
  starting transfers between devices: 43.9 us -> 47.4 us
    ppermute x37, waiting for transfers between devices: 33.8 us -> 19.5 us  [permute(): return lax.ppermute(value, ('dp', 'crow', 'ccol'), perm)]
    ppermute x37, starting transfers between devices: 43.9 us -> 47.4 us  [permute(): return lax.ppermute(value, ('dp', 'crow', 'ccol'), perm)]
  transfers between devices with their start and end apart: 37 -> 37, of which waited for: 21 -> 17; matrix products, arithmetic and copies ran while one was open for 0% -> 0% of each run, Pallas kernels for 12% -> 11%
where the time goes in v1:
time: 87.3 us; the launch traced here: 87.1 us
  starting transfers between devices  47.4 us (54%)
  waiting for transfers between devices  19.5 us (22%)
  Pallas kernels  18.8 us (22%)
    ppermute x37, starting transfers between devices, permute(): return lax.ppermute(value, ('dp', 'crow', 'ccol'), perm)  47.4 us
    ppermute x37, waiting for transfers between devices, permute(): return lax.ppermute(value, ('dp', 'crow', 'ccol'), perm)  19.5 us
    pallas_call x25, Pallas kernels, call(): pl.pallas_call(kernel, out_shape=outs, compiler_params=pltpu.CompilerPara...  18.8 us
  transfers between devices with their start and end apart: 37, of which 17 were waited for; matrix products, arithmetic and copies ran while one was open for 0% of the time, Pallas kernels for 11%

profile of v1, /device:TPU:0, one launch (start us, length us, event | category | flops | bytes accessed | tf_op | source)
XLA Modules:
  0.0 87.1 jit_solution(7989542951888634126)
XLA Ops:
  0.6 3.0 %shard_map.103.after_ref.refs_2_ = f32[8,768]{1,0:T(8,128)} custom-call(f32[8,3072]{1,0:T(8,128)} %direction_ref.9, f32[3,256,256]{2,1,0:T(8,128)} %inv_ref.13, f32[768,768]{1,0:T(8,128)} %factor_ref.3, f32[768,768]{1,0:T(8,128)} %factor_ref.3, f32[768,768]{1,0:T(8,128)} %factor_ref.3), custom_call_target="tpu_custom_call" | custom-call | flops 1000000 | bytes 1000000 | tf_op jit(solution)/shard_map/pallas_call | solution.py:332
  6.3 1.8 %shard_map.107.low_ref.refs_6_ = f32[256,768]{1,0:T(8,128)S(1)} custom-call(f32[8,768]{1,0:T(8,128)S(1)} %copy-done.3, f32[3,256,256]{2,1,0:T(8,128)S(1)} %copy-done.1, f32[768,768]{1,0:T(8,128)S(1)} %copy-done, f32[768,768]{1,0:T(8,128)S(1)} %copy-done, f32[768,768]{1,0:T(8,128)S(1)} %copy-done), custom_call_target="tpu_custom_call" | custom-call | flops 1000000 | bytes 1000000 | tf_op jit(solution)/shard_map/pallas_call | solution.py:332
  9.8 0.7 collective-permute-done.5.refs_1_
  11.4 1.0 %collective-permute-done.7.sub_ref.refs_0_ = f32[8,768]{1,0:T(8,128)S(1)} collective-permute-done((f32[8,768]{1,0:T(8,128)S(1)}, f32[8,768]{1,0:T(8,128)S(1)}, u32[]{:S(2)}, u32[]{:S(2)}) %collective-permute-start.7) | collective-permute-done | bytes 24608 | tf_op jit(solution)/shard_map/ppermute | solution.py:360
  13.0 1.0 %collective-permute-done.8.refs_1_ = f32[8,768]{1,0:T(8,128)S(1)} collective-permute-done((f32[8,768]{1,0:T(8,128)S(1)}, f32[8,768]{1,0:T(8,128)S(1)}, u32[]{:S(2)}, u32[]{:S(2)}) %collective-permute-start.8) | collective-permute-done | bytes 24608 | tf_op jit(solution)/shard_map/ppermute | solution.py:360
  14.5 13.0 %collective-permute-start.9 = (f32[8,768]{1,0:T(8,128)S(1)}, f32[8,768]{1,0:T(8,128)S(1)}, u32[]{:S(2)}, u32[]{:S(2)}) collective-permute-start(f32[8,768]{1,0:T(8,128)S(1)} %shard_map.111), channel_id=1, source_target_pairs={{0,20},{1,17},{2,18},{3,19},{4,16},{5,21},{6,22},{7,23},{8,24},{9,... | collective-permute-start | bytes 73736 | tf_op jit(solution)/shard_map/ppermute | solution.py:360
  27.5 1.5 %collective-permute-done.9.sub_ref = f32[8,768]{1,0:T(8,128)S(1)} collective-permute-done((f32[8,768]{1,0:T(8,128)S(1)}, f32[8,768]{1,0:T(8,128)S(1)}, u32[]{:S(2)}, u32[]{:S(2)}) %collective-permute-start.9) | collective-permute-done | bytes 24608 | tf_op jit(solution)/shard_map/ppermute | solution.py:360
  29.3 1.7 %collective-permute-start.10 = (f32[8,768]{1,0:T(8,128)S(1)}, f32[8,768]{1,0:T(8,128)S(1)}, u32[]{:S(2)}, u32[]{:S(2)}) collective-permute-start(f32[8,768]{1,0:T(8,128)S(1)} %shard_map.112.refs_0_), channel_id=1, source_target_pairs={{0,20},{1,21},{2,22},{3,23},{4,16},{5,17},{6,18},{7,19},{8,28},{9,... | collective-permute-start | bytes 73736 | tf_op jit(solution)/shard_map/ppermute | solution.py:360
  31.1 1.5 %collective-permute-start.12 = (f32[8,768]{1,0:T(8,128)S(1)}, f32[8,768]{1,0:T(8,128)S(1)}, u32[]{:S(2)}, u32[]{:S(2)}) collective-permute-start(f32[8,768]{1,0:T(8,128)S(1)} %shard_map.112.refs_0_), channel_id=1, source_target_pairs={{0,28},{1,29},{2,30},{3,31},{4,24},{5,25},{6,26},{7,27},{8,20},{9,... | collective-permute-start | bytes 73736 | tf_op jit(solution)/shard_map/ppermute | solution.py:360
  32.6 2.7 %shard_map.113 = (bf16[768,2048]{1,0:T(8,128)(2,1)S(1)}, bf16[768,2048]{1,0:T(8,128)(2,1)S(1)}) custom-call(f32[16]{0:T(128)S(1)} %copy-done.8, f32[16,768]{1,0:T(8,128)S(1)} %copy-done.7, f32[16,2048]{1,0:T(8,128)S(1)} %copy-done.4), custom_call_target="tpu_custom_call" | custom-call | flops 1000000 | bytes 1000000 | tf_op jit(solution)/shard_map/pallas_call | solution.py:332
  35.4 0.9 %shard_map.114 = (f32[8,768]{1,0:T(8,128)S(1)}, f32[8,2048]{1,0:T(8,128)S(1)}) custom-call(f32[8,768]{1,0:T(8,128)S(1)} %shard_map.112.refs_0_, f32[8,768]{1,0:T(8,128)S(1)} %collective-permute-done.10.refs_1_, f32[8,768]{1,0:T(8,128)S(1)} %collective-permute-done.11.refs_2_, f32[8,768]{1,0:T(8,128)S(1)} %collective-permute-done.12.refs_3_, ...), custom_call_target="tpu_custom_call" | custom-call | flops 1000000 | bytes 1000000 | tf_op jit(solution)/shard_map/pallas_call | solution.py:332
  36.3 4.3 %collective-permute-start.15 = (f32[8,2048]{1,0:T(8,128)S(1)}, f32[8,2048]{1,0:T(8,128)S(1)}, u32[]{:S(2)}, u32[]{:S(2)}) collective-permute-start(f32[8,2048]{1,0:T(8,128)S(1)} %get-tuple-element.25.refs_0_), channel_id=1, source_target_pairs={{0,3},{1,2},{2,1},{3,0},{4,7},{5,6},{6,5},{7,4},{8,11},{9,10},{10,... | collective-permute-start | bytes 196616 | tf_op jit(solution)/shard_map/ppermute | solution.py:360
  40.7 0.8 collective-permute-done.13.refs_1_
  41.5 3.5 %collective-permute-done.14.refs_2_ = f32[8,2048]{1,0:T(8,128)S(1)} collective-permute-done((f32[8,2048]{1,0:T(8,128)S(1)}, f32[8,2048]{1,0:T(8,128)S(1)}, u32[]{:S(2)}, u32[]{:S(2)}) %collective-permute-start.14) | collective-permute-done | bytes 65568 | tf_op jit(solution)/shard_map/ppermute | solution.py:360
  45.0 1.8 %shard_map.115 = (f32[8,768]{1,0:T(8,128)S(1)}, f32[128,768]{1,0:T(8,128)S(1)}) custom-call(f32[8,2048]{1,0:T(8,128)S(1)} %get-tuple-element.25.refs_0_, f32[8,2048]{1,0:T(8,128)S(1)} %collective-permute-done.13.refs_1_, f32[8,2048]{1,0:T(8,128)S(1)} %collective-permute-done.14.refs_2_, f32[8,2048]{1,0:T(8,128)S(1)} %collective-permute-done.15.refs_3_, ...), custom_call_target="tpu_custom_call" | custom-call | flops 1000000 | bytes 1000000 | tf_op jit(solution)/shard_map/pallas_call | solution.py:332
  47.3 1.2 %collective-permute-done.16 = f32[8,768]{1,0:T(8,128)S(1)} collective-permute-done((f32[8,768]{1,0:T(8,128)S(1)}, f32[8,768]{1,0:T(8,128)S(1)}, u32[]{:S(2)}, u32[]{:S(2)}) %collective-permute-start.16) | collective-permute-done | bytes 24608 | tf_op jit(solution)/shard_map/ppermute | solution.py:360
  48.6 2.2 %collective-permute-start.17 = (f32[8,768]{1,0:T(8,128)S(1)}, f32[8,768]{1,0:T(8,128)S(1)}, u32[]{:S(2)}, u32[]{:S(2)}) collective-permute-start(f32[8,768]{1,0:T(8,128)S(1)} %add.3.refs_0_), channel_id=1, source_target_pairs={{0,20},{1,21},{2,22},{3,23},{4,16},{5,17},{6,18},{7,19},{8,28},{9,... | collective-permute-start | bytes 73736 | tf_op jit(solution)/shard_map/ppermute | solution.py:360
  50.8 1.3 %collective-permute-start.19 = (f32[8,768]{1,0:T(8,128)S(1)}, f32[8,768]{1,0:T(8,128)S(1)}, u32[]{:S(2)}, u32[]{:S(2)}) collective-permute-start(f32[8,768]{1,0:T(8,128)S(1)} %add.3.refs_0_), channel_id=1, source_target_pairs={{0,28},{1,29},{2,30},{3,31},{4,24},{5,25},{6,26},{7,27},{8,20},{9,... | collective-permute-start | bytes 73736 | tf_op jit(solution)/shard_map/ppermute | solution.py:360
  52.6 1.5 %collective-permute-done.18.refs_2_ = f32[8,768]{1,0:T(8,128)S(1)} collective-permute-done((f32[8,768]{1,0:T(8,128)S(1)}, f32[8,768]{1,0:T(8,128)S(1)}, u32[]{:S(2)}, u32[]{:S(2)}) %collective-permute-start.18) | collective-permute-done | bytes 24608 | tf_op jit(solution)/shard_map/ppermute | solution.py:360
  54.1 0.9 %collective-permute-done.19.refs_3_ = f32[8,768]{1,0:T(8,128)S(1)} collective-permute-done((f32[8,768]{1,0:T(8,128)S(1)}, f32[8,768]{1,0:T(8,128)S(1)}, u32[]{:S(2)}, u32[]{:S(2)}) %collective-permute-start.19) | collective-permute-done | bytes 24608 | tf_op jit(solution)/shard_map/ppermute | solution.py:360
  55.5 1.7 %collective-permute-start.24 = (f32[8,768]{1,0:T(8,128)S(1)}, f32[8,768]{1,0:T(8,128)S(1)}, u32[]{:S(2)}, u32[]{:S(2)}) collective-permute-start(f32[8,768]{1,0:T(8,128)S(1)} %get-tuple-element.30.refs_0_), channel_id=1, source_target_pairs={{0,24},{1,17},{2,18},{3,19},{4,20},{5,21},{6,22},{7,23},{8,16},{9,... | collective-permute-start | bytes 73736 | tf_op jit(solution)/shard_map/ppermute | solution.py:360
  57.2 3.6 %collective-permute-start.21 = (f32[8,768]{1,0:T(8,128)S(1)}, f32[8,768]{1,0:T(8,128)S(1)}, u32[]{:S(2)}, u32[]{:S(2)}) collective-permute-start(f32[8,768]{1,0:T(8,128)S(1)} %get-tuple-element.30.refs_0_), channel_id=1, source_target_pairs={{0,20},{1,17},{2,18},{3,19},{4,16},{5,21},{6,22},{7,23},{8,24},{9,... | collective-permute-start | bytes 73736 | tf_op jit(solution)/shard_map/ppermute | solution.py:360
  60.9 0.7 shard_map.118
  64.2 0.7 collective-permute-done.28.refs_1_
  66.5 0.8 collective-permute-done.30.refs_1_
  68.2 4.0 %collective-permute-start.33 = (f32[8,768]{1,0:T(8,128)S(1)}, f32[8,768]{1,0:T(8,128)S(1)}, u32[]{:S(2)}, u32[]{:S(2)}) collective-permute-start(f32[8,768]{1,0:T(8,128)S(1)} %shard_map.125.refs_0_), channel_id=1, source_target_pairs={{0,19},{1,18},{2,17},{3,16},{4,23},{5,22},{6,21},{7,20},{8,27},{9,... | collective-permute-start | bytes 73736 | tf_op jit(solution)/shard_map/ppermute | solution.py:360
  72.4 1.8 %collective-permute-done.33.refs_3_ = f32[8,768]{1,0:T(8,128)S(1)} collective-permute-done((f32[8,768]{1,0:T(8,128)S(1)}, f32[8,768]{1,0:T(8,128)S(1)}, u32[]{:S(2)}, u32[]{:S(2)}) %collective-permute-start.33) | collective-permute-done | bytes 24608 | tf_op jit(solution)/shard_map/ppermute | solution.py:360
  74.2 4.3 %collective-permute-start.34 = (f32[8,768]{1,0:T(8,128)S(1)}, f32[8,768]{1,0:T(8,128)S(1)}, u32[]{:S(2)}, u32[]{:S(2)}) collective-permute-start(f32[8,768]{1,0:T(8,128)S(1)} %shard_map.126.refs_0_), channel_id=1, source_target_pairs={{0,20},{1,21},{2,22},{3,23},{4,16},{5,17},{6,18},{7,19},{8,28},{9,... | collective-permute-start | bytes 73736 | tf_op jit(solution)/shard_map/ppermute | solution.py:360
  78.5 3.6 %collective-permute-start.35 = (f32[8,768]{1,0:T(8,128)S(1)}, f32[8,768]{1,0:T(8,128)S(1)}, u32[]{:S(2)}, u32[]{:S(2)}) collective-permute-start(f32[8,768]{1,0:T(8,128)S(1)} %shard_map.126.refs_0_), channel_id=1, source_target_pairs={{0,24},{1,25},{2,26},{3,27},{4,28},{5,29},{6,30},{7,31},{8,16},{9,... | collective-permute-start | bytes 73736 | tf_op jit(solution)/shard_map/ppermute | solution.py:360
  82.1 0.9 %collective-permute-start.36 = (f32[8,768]{1,0:T(8,128)S(1)}, f32[8,768]{1,0:T(8,128)S(1)}, u32[]{:S(2)}, u32[]{:S(2)}) collective-permute-start(f32[8,768]{1,0:T(8,128)S(1)} %shard_map.126.refs_0_), channel_id=1, source_target_pairs={{0,28},{1,29},{2,30},{3,31},{4,24},{5,25},{6,26},{7,27},{8,20},{9,... | collective-permute-start | bytes 73736 | tf_op jit(solution)/shard_map/ppermute | solution.py:360
  83.6 2.6 %collective-permute-done.36.refs_3_ = f32[8,768]{1,0:T(8,128)S(1)} collective-permute-done((f32[8,768]{1,0:T(8,128)S(1)}, f32[8,768]{1,0:T(8,128)S(1)}, u32[]{:S(2)}, u32[]{:S(2)}) %collective-permute-start.36) | collective-permute-done | bytes 24608 | tf_op jit(solution)/shard_map/ppermute | solution.py:360
  86.2 0.9 %shard_map.127 = (f32[8,3072]{1,0:T(8,128)}, f32[8,3072]{1,0:T(8,128)}, f32[8,3072]{1,0:T(8,128)}) custom-call(f32[8,3072]{1,0:T(8,128)S(1)} %copy-done.5, f32[8,3072]{1,0:T(8,128)S(1)} %copy-done.6, f32[8,3072]{1,0:T(8,128)S(1)} %copy-done.2, f32[8,768]{1,0:T(8,128)S(1)} %shard_map.126.refs_0_, f32[8,768]{1,0:T(8,128)S(1)} %collective-permute-done.34.refs_1_, ...), custom_call_target="tpu_custom_call" | custom-call | flops 1000000 | bytes 1000000 | tf_op jit(solution)/shard_map/pallas_call | solution.py:332
  (86 shorter events, 14.2 us)
Async XLA Ops:
  3.6 1.6 %collective-permute-start.3 = (f32[8,768]{1,0:T(8,128)}, f32[8,768]{1,0:T(8,128)S(1)}, u32[]{:S(2)}, u32[]{:S(2)}) collective-permute-start(f32[8,768]{1,0:T(8,128)} %shard_map.103.after_ref.refs_2_), channel_id=1, source_target_pairs={{0,16},{1,17},{2,18},{3,19},{4,20},{5,21},{6,22},{7,23},{8,24},{9,... | collective-permute-start | bytes 73736 | tf_op jit(solution)/shard_map/ppermute | solution.py:360
  4.1 4.0 %collective-permute-start = (f32[8,768]{1,0:T(8,128)}, f32[8,768]{1,0:T(8,128)S(1)}, u32[]{:S(2)}, u32[]{:S(2)}) collective-permute-start(f32[8,768]{1,0:T(8,128)} %shard_map.103.after_ref.refs_2_), channel_id=1, source_target_pairs={{0,16},{1,17},{2,18},{3,19},{4,20},{5,21},{6,22},{7,23},{8,24},{9,... | collective-permute-start | bytes 73736 | tf_op jit(solution)/shard_map/ppermute | solution.py:360
  4.1 4.0 %collective-permute-start.1 = (f32[8,768]{1,0:T(8,128)}, f32[8,768]{1,0:T(8,128)S(1)}, u32[]{:S(2)}, u32[]{:S(2)}) collective-permute-start(f32[8,768]{1,0:T(8,128)} %shard_map.103.after_ref.refs_2_), channel_id=1, source_target_pairs={{0,16},{1,17},{2,18},{3,19},{4,20},{5,21},{6,22},{7,23},{8,24},{9,... | collective-permute-start | bytes 73736 | tf_op jit(solution)/shard_map/ppermute | solution.py:360
  5.6 3.3 %collective-permute-start.4 = (f32[8,768]{1,0:T(8,128)S(1)}, f32[8,768]{1,0:T(8,128)S(1)}, u32[]{:S(2)}, u32[]{:S(2)}) collective-permute-start(f32[8,768]{1,0:T(8,128)S(1)} %shard_map.106), channel_id=1, source_target_pairs={{0,16},{1,17},{2,18},{3,19},{4,20},{5,21},{6,22},{7,23},{8,24},{9,... | collective-permute-start | bytes 73736 | tf_op jit(solution)/shard_map/ppermute | solution.py:360
  8.5 1.3 %collective-permute-start.2 = (f32[8,768]{1,0:T(8,128)S(1)}, f32[8,768]{1,0:T(8,128)S(1)}, u32[]{:S(2)}, u32[]{:S(2)}) collective-permute-start(f32[8,768]{1,0:T(8,128)S(1)} %shard_map.105), channel_id=1, source_target_pairs={{0,16},{1,17},{2,18},{3,19},{4,20},{5,21},{6,22},{7,23},{8,28},{9,... | collective-permute-start | bytes 73736 | tf_op jit(solution)/shard_map/ppermute | solution.py:360
  14.5 14.5 %collective-permute-start.9 = (f32[8,768]{1,0:T(8,128)S(1)}, f32[8,768]{1,0:T(8,128)S(1)}, u32[]{:S(2)}, u32[]{:S(2)}) collective-permute-start(f32[8,768]{1,0:T(8,128)S(1)} %shard_map.111), channel_id=1, source_target_pairs={{0,20},{1,17},{2,18},{3,19},{4,16},{5,21},{6,22},{7,23},{8,24},{9,... | collective-permute-start | bytes 73736 | tf_op jit(solution)/shard_map/ppermute | solution.py:360
  29.3 6.0 %collective-permute-start.10 = (f32[8,768]{1,0:T(8,128)S(1)}, f32[8,768]{1,0:T(8,128)S(1)}, u32[]{:S(2)}, u32[]{:S(2)}) collective-permute-start(f32[8,768]{1,0:T(8,128)S(1)} %shard_map.112.refs_0_), channel_id=1, source_target_pairs={{0,20},{1,21},{2,22},{3,23},{4,16},{5,17},{6,18},{7,19},{8,28},{9,... | collective-permute-start | bytes 73736 | tf_op jit(solution)/shard_map/ppermute | solution.py:360
  31.1 4.3 %collective-permute-start.11 = (f32[8,768]{1,0:T(8,128)S(1)}, f32[8,768]{1,0:T(8,128)S(1)}, u32[]{:S(2)}, u32[]{:S(2)}) collective-permute-start(f32[8,768]{1,0:T(8,128)S(1)} %shard_map.112.refs_0_), channel_id=1, source_target_pairs={{0,24},{1,25},{2,26},{3,27},{4,28},{5,29},{6,30},{7,31},{8,16},{9,... | collective-permute-start | bytes 73736 | tf_op jit(solution)/shard_map/ppermute | solution.py:360
  31.1 4.3 %collective-permute-start.12 = (f32[8,768]{1,0:T(8,128)S(1)}, f32[8,768]{1,0:T(8,128)S(1)}, u32[]{:S(2)}, u32[]{:S(2)}) collective-permute-start(f32[8,768]{1,0:T(8,128)S(1)} %shard_map.112.refs_0_), channel_id=1, source_target_pairs={{0,28},{1,29},{2,30},{3,31},{4,24},{5,25},{6,26},{7,27},{8,20},{9,... | collective-permute-start | bytes 73736 | tf_op jit(solution)/shard_map/ppermute | solution.py:360
  36.3 5.3 %collective-permute-start.13 = (f32[8,2048]{1,0:T(8,128)S(1)}, f32[8,2048]{1,0:T(8,128)S(1)}, u32[]{:S(2)}, u32[]{:S(2)}) collective-permute-start(f32[8,2048]{1,0:T(8,128)S(1)} %get-tuple-element.25.refs_0_), channel_id=1, source_target_pairs={{0,1},{1,0},{2,3},{3,2},{4,5},{5,4},{6,7},{7,6},{8,9},{9,8},{10,11... | collective-permute-start | bytes 196616 | tf_op jit(solution)/shard_map/ppermute | solution.py:360
  36.3 8.7 %collective-permute-start.14 = (f32[8,2048]{1,0:T(8,128)S(1)}, f32[8,2048]{1,0:T(8,128)S(1)}, u32[]{:S(2)}, u32[]{:S(2)}) collective-permute-start(f32[8,2048]{1,0:T(8,128)S(1)} %get-tuple-element.25.refs_0_), channel_id=1, source_target_pairs={{0,2},{1,3},{2,0},{3,1},{4,6},{5,7},{6,4},{7,5},{8,10},{9,11},{10,... | collective-permute-start | bytes 196616 | tf_op jit(solution)/shard_map/ppermute | solution.py:360
  36.3 8.6 %collective-permute-start.15 = (f32[8,2048]{1,0:T(8,128)S(1)}, f32[8,2048]{1,0:T(8,128)S(1)}, u32[]{:S(2)}, u32[]{:S(2)}) collective-permute-start(f32[8,2048]{1,0:T(8,128)S(1)} %get-tuple-element.25.refs_0_), channel_id=1, source_target_pairs={{0,3},{1,2},{2,1},{3,0},{4,7},{5,6},{6,5},{7,4},{8,11},{9,10},{10,... | collective-permute-start | bytes 196616 | tf_op jit(solution)/shard_map/ppermute | solution.py:360
  46.8 8.2 %collective-permute-start.20 = (f32[128,768]{1,0:T(8,128)S(1)}, f32[128,768]{1,0:T(8,128)S(1)}, u32[]{:S(2)}, u32[]{:S(2)}) collective-permute-start(f32[128,768]{1,0:T(8,128)S(1)} %get-tuple-element.29), channel_id=1, source_target_pairs={{0,16},{1,17},{2,18},{3,19},{4,21},{5,20},{6,22},{7,23},{8,24},{9,... | collective-permute-start | bytes 1179656 | tf_op jit(solution)/shard_map/ppermute | solution.py:360
  46.8 1.7 %collective-permute-start.16 = (f32[8,768]{1,0:T(8,128)S(1)}, f32[8,768]{1,0:T(8,128)S(1)}, u32[]{:S(2)}, u32[]{:S(2)}) collective-permute-start(f32[8,768]{1,0:T(8,128)S(1)} %get-tuple-element.26), channel_id=1, source_target_pairs={{0,16},{1,17},{2,18},{3,19},{4,20},{5,21},{6,22},{7,23},{8,24},{9,... | collective-permute-start | bytes 73736 | tf_op jit(solution)/shard_map/ppermute | solution.py:360
  48.6 4.0 %collective-permute-start.17 = (f32[8,768]{1,0:T(8,128)S(1)}, f32[8,768]{1,0:T(8,128)S(1)}, u32[]{:S(2)}, u32[]{:S(2)}) collective-permute-start(f32[8,768]{1,0:T(8,128)S(1)} %add.3.refs_0_), channel_id=1, source_target_pairs={{0,20},{1,21},{2,22},{3,23},{4,16},{5,17},{6,18},{7,19},{8,28},{9,... | collective-permute-start | bytes 73736 | tf_op jit(solution)/shard_map/ppermute | solution.py:360
  50.8 3.3 %collective-permute-start.18 = (f32[8,768]{1,0:T(8,128)S(1)}, f32[8,768]{1,0:T(8,128)S(1)}, u32[]{:S(2)}, u32[]{:S(2)}) collective-permute-start(f32[8,768]{1,0:T(8,128)S(1)} %add.3.refs_0_), channel_id=1, source_target_pairs={{0,24},{1,25},{2,26},{3,27},{4,28},{5,29},{6,30},{7,31},{8,16},{9,... | collective-permute-start | bytes 73736 | tf_op jit(solution)/shard_map/ppermute | solution.py:360
  50.8 4.2 %collective-permute-start.19 = (f32[8,768]{1,0:T(8,128)S(1)}, f32[8,768]{1,0:T(8,128)S(1)}, u32[]{:S(2)}, u32[]{:S(2)}) collective-permute-start(f32[8,768]{1,0:T(8,128)S(1)} %add.3.refs_0_), channel_id=1, source_target_pairs={{0,28},{1,29},{2,30},{3,31},{4,24},{5,25},{6,26},{7,27},{8,20},{9,... | collective-permute-start | bytes 73736 | tf_op jit(solution)/shard_map/ppermute | solution.py:360
  55.3 7.2 %collective-permute-start.23 = (f32[128,768]{1,0:T(8,128)S(1)}, f32[128,768]{1,0:T(8,128)S(1)}, u32[]{:S(2)}, u32[]{:S(2)}) collective-permute-start(f32[128,768]{1,0:T(8,128)S(1)} %get-tuple-element.34.mine_ref), channel_id=1, source_target_pairs={{0,16},{1,17},{2,18},{3,19},{4,20},{5,21},{6,22},{7,23},{8,24},{9,... | collective-permute-start | bytes 1179656 | tf_op jit(solution)/shard_map/ppermute | solution.py:360
  55.5 6.1 %collective-permute-start.24 = (f32[8,768]{1,0:T(8,128)S(1)}, f32[8,768]{1,0:T(8,128)S(1)}, u32[]{:S(2)}, u32[]{:S(2)}) collective-permute-start(f32[8,768]{1,0:T(8,128)S(1)} %get-tuple-element.30.refs_0_), channel_id=1, source_target_pairs={{0,24},{1,17},{2,18},{3,19},{4,20},{5,21},{6,22},{7,23},{8,16},{9,... | collective-permute-start | bytes 73736 | tf_op jit(solution)/shard_map/ppermute | solution.py:360
  57.2 4.4 %collective-permute-start.25 = (f32[8,768]{1,0:T(8,128)S(1)}, f32[8,768]{1,0:T(8,128)S(1)}, u32[]{:S(2)}, u32[]{:S(2)}) collective-permute-start(f32[8,768]{1,0:T(8,128)S(1)} %get-tuple-element.30.refs_0_), channel_id=1, source_target_pairs={{0,28},{1,17},{2,18},{3,19},{4,20},{5,21},{6,22},{7,23},{8,24},{9,... | collective-permute-start | bytes 73736 | tf_op jit(solution)/shard_map/ppermute | solution.py:360
  57.2 5.7 %collective-permute-start.21 = (f32[8,768]{1,0:T(8,128)S(1)}, f32[8,768]{1,0:T(8,128)S(1)}, u32[]{:S(2)}, u32[]{:S(2)}) collective-permute-start(f32[8,768]{1,0:T(8,128)S(1)} %get-tuple-element.30.refs_0_), channel_id=1, source_target_pairs={{0,20},{1,17},{2,18},{3,19},{4,16},{5,21},{6,22},{7,23},{8,24},{9,... | collective-permute-start | bytes 73736 | tf_op jit(solution)/shard_map/ppermute | solution.py:360
  60.8 2.1 %collective-permute-start.22 = (f32[8,768]{1,0:T(8,128)S(1)}, f32[8,768]{1,0:T(8,128)S(1)}, u32[]{:S(2)}, u32[]{:S(2)}) collective-permute-start(f32[8,768]{1,0:T(8,128)S(1)} %get-tuple-element.31), channel_id=1, source_target_pairs={{0,16},{1,17},{2,18},{3,19},{4,21},{5,20},{6,22},{7,23},{8,24},{9,... | collective-permute-start | bytes 73736 | tf_op jit(solution)/shard_map/ppermute | solution.py:360
  62.0 2.2 %collective-permute-start.26 = (f32[8,768]{1,0:T(8,128)S(1)}, f32[8,768]{1,0:T(8,128)S(1)}, u32[]{:S(2)}, u32[]{:S(2)}) collective-permute-start(f32[8,768]{1,0:T(8,128)S(1)} %shard_map.121), channel_id=1, source_target_pairs={{0,16},{1,17},{2,18},{3,19},{4,20},{5,21},{6,22},{7,23},{8,25},{9,... | collective-permute-start | bytes 73736 | tf_op jit(solution)/shard_map/ppermute | solution.py:360
  63.7 1.7 %collective-permute-start.27 = (f32[8,768]{1,0:T(8,128)S(1)}, f32[8,768]{1,0:T(8,128)S(1)}, u32[]{:S(2)}, u32[]{:S(2)}) collective-permute-start(f32[8,768]{1,0:T(8,128)S(1)} %shard_map.120.refs_1_), channel_id=1, source_target_pairs={{0,16},{1,17},{2,18},{3,19},{4,25},{5,21},{6,22},{7,23},{8,24},{9,... | collective-permute-start | bytes 73736 | tf_op jit(solution)/shard_map/ppermute | solution.py:360
  65.3 1.2 %collective-permute-start.29 = (f32[8,768]{1,0:T(8,128)S(1)}, f32[8,768]{1,0:T(8,128)S(1)}, u32[]{:S(2)}, u32[]{:S(2)}) collective-permute-start(f32[8,768]{1,0:T(8,128)S(1)} %shard_map.123), channel_id=1, source_target_pairs={{0,16},{1,17},{2,18},{3,19},{4,20},{5,21},{6,22},{7,23},{8,24},{9,... | collective-permute-start | bytes 73736 | tf_op jit(solution)/shard_map/ppermute | solution.py:360
  66.1 1.2 %collective-permute-start.30 = (f32[8,768]{1,0:T(8,128)S(1)}, f32[8,768]{1,0:T(8,128)S(1)}, u32[]{:S(2)}, u32[]{:S(2)}) collective-permute-start(f32[8,768]{1,0:T(8,128)S(1)} %shard_map.122.refs_2_), channel_id=1, source_target_pairs={{0,16},{1,17},{2,18},{3,19},{4,20},{5,21},{6,22},{7,23},{8,24},{9,... | collective-permute-start | bytes 73736 | tf_op jit(solution)/shard_map/ppermute | solution.py:360
  68.1 4.1 %collective-permute-start.31 = (f32[8,768]{1,0:T(8,128)S(1)}, f32[8,768]{1,0:T(8,128)S(1)}, u32[]{:S(2)}, u32[]{:S(2)}) collective-permute-start(f32[8,768]{1,0:T(8,128)S(1)} %shard_map.125.refs_0_), channel_id=1, source_target_pairs={{0,17},{1,16},{2,19},{3,18},{4,21},{5,20},{6,23},{7,22},{8,25},{9,... | collective-permute-start | bytes 73736 | tf_op jit(solution)/shard_map/ppermute | solution.py:360
  68.2 4.2 %collective-permute-start.32 = (f32[8,768]{1,0:T(8,128)S(1)}, f32[8,768]{1,0:T(8,128)S(1)}, u32[]{:S(2)}, u32[]{:S(2)}) collective-permute-start(f32[8,768]{1,0:T(8,128)S(1)} %shard_map.125.refs_0_), channel_id=1, source_target_pairs={{0,18},{1,19},{2,16},{3,17},{4,22},{5,23},{6,20},{7,21},{8,26},{9,... | collective-permute-start | bytes 73736 | tf_op jit(solution)/shard_map/ppermute | solution.py:360
  68.2 5.9 %collective-permute-start.33 = (f32[8,768]{1,0:T(8,128)S(1)}, f32[8,768]{1,0:T(8,128)S(1)}, u32[]{:S(2)}, u32[]{:S(2)}) collective-permute-start(f32[8,768]{1,0:T(8,128)S(1)} %shard_map.125.refs_0_), channel_id=1, source_target_pairs={{0,19},{1,18},{2,17},{3,16},{4,23},{5,22},{6,21},{7,20},{8,27},{9,... | collective-permute-start | bytes 73736 | tf_op jit(solution)/shard_map/ppermute | solution.py:360
  74.2 8.8 %collective-permute-start.34 = (f32[8,768]{1,0:T(8,128)S(1)}, f32[8,768]{1,0:T(8,128)S(1)}, u32[]{:S(2)}, u32[]{:S(2)}) collective-permute-start(f32[8,768]{1,0:T(8,128)S(1)} %shard_map.126.refs_0_), channel_id=1, source_target_pairs={{0,20},{1,21},{2,22},{3,23},{4,16},{5,17},{6,18},{7,19},{8,28},{9,... | collective-permute-start | bytes 73736 | tf_op jit(solution)/shard_map/ppermute | solution.py:360
  78.5 5.1 %collective-permute-start.35 = (f32[8,768]{1,0:T(8,128)S(1)}, f32[8,768]{1,0:T(8,128)S(1)}, u32[]{:S(2)}, u32[]{:S(2)}) collective-permute-start(f32[8,768]{1,0:T(8,128)S(1)} %shard_map.126.refs_0_), channel_id=1, source_target_pairs={{0,24},{1,25},{2,26},{3,27},{4,28},{5,29},{6,30},{7,31},{8,16},{9,... | collective-permute-start | bytes 73736 | tf_op jit(solution)/shard_map/ppermute | solution.py:360
  82.1 4.2 %collective-permute-start.36 = (f32[8,768]{1,0:T(8,128)S(1)}, f32[8,768]{1,0:T(8,128)S(1)}, u32[]{:S(2)}, u32[]{:S(2)}) collective-permute-start(f32[8,768]{1,0:T(8,128)S(1)} %shard_map.126.refs_0_), channel_id=1, source_target_pairs={{0,28},{1,29},{2,30},{3,31},{4,24},{5,25},{6,26},{7,27},{8,20},{9,... | collective-permute-start | bytes 73736 | tf_op jit(solution)/shard_map/ppermute | solution.py:360
  (14 other events, 107.8 us)

commit v2 on v1

--- a/solution.py
+++ b/solution.py
@@ -117,8 +117,8 @@
     out_ref[...] = jnp.concatenate(pieces, axis=1)
 
 
-def lower_kernel(after_ref, inv_ref, *refs):
-    tri_refs, out_ref = refs[:-1], refs[-1]
+def lower_kernel(inv_ref, *refs):
+    tri_refs, out_ref, half_ref = refs[:-2], refs[-2], refs[-1]
     held, order = inv_ref.shape[0], inv_ref.shape[1]
     tri = dict(zip(blocks_of(held), tri_refs))
     found = {(n, n): inv_ref[n] for n in range(held)}
@@ -130,6 +130,9 @@
             found[r, c] = -square(inv_ref[r], total)
             at = r * (r - 1) // 2 + c
             out_ref[:, at * order : (at + 1) * order] = found[r, c]
+    tall = half_ref.shape[0]
+    at = lax.rem(lax.axis_index("dp"), 2) * tall
+    half_ref[...] = out_ref[pl.ds(pl.multiple_of(at, tall), tall), :]
 
 
 def pair_kernel(factor_ref, high_ref, low_ref):
@@ -247,11 +250,8 @@
 
 
 def normal_kernel(*refs):
-    part_refs = refs[:-5]
-    high_ref, low_ref, lower_ref, out_ref, half_ref = refs[-5:]
-    tall = half_ref.shape[0]
-    at = lax.rem(lax.axis_index("dp"), 2) * tall
-    half_ref[...] = lower_ref[pl.ds(pl.multiple_of(at, tall), tall), :]
+    part_refs = refs[:-3]
+    high_ref, low_ref, out_ref = refs[-3:]
     piece = part_refs[0][...]
     for ref in part_refs[1:]:
         piece = piece + ref[...]
@@ -262,9 +262,8 @@
 
 
 def source_kernel(scale, order, mine_ref, *refs):
-    part_refs = refs[:-6]
-    high_ref, low_ref, half_ref, out_ref, image_ref, half_out = refs[-6:]
-    half_out[...] = half_ref[...]
+    part_refs = refs[:-4]
+    high_ref, low_ref, out_ref, image_ref = refs[-4:]
     total = part_refs[0][...]
     for ref in part_refs[1:]:
         total = total + ref[...]
@@ -373,15 +372,15 @@
     def with_tri(kernel, outs, *args, limit=12):
         full = [pl.BlockSpec(a.shape, lambda i, n=a.ndim: (0,) * n) for a in args]
         tri = [pl.BlockSpec((order, order), lambda i, r=r, c=c: (r, c)) for r, c in blocks_of(held)]
-        shape = outs.shape
         return call(
             kernel, outs, *args, *([factor] * len(tri)), grid=(1,), in_specs=full + tri,
-            out_specs=pl.BlockSpec(shape, lambda i: (0, 0)), limit=limit,
+            out_specs=[pl.BlockSpec(out.shape, lambda i: (0, 0)) for out in outs], limit=limit,
         )
 
-    piece = with_tri(first_kernel, part, direction, block_inv, limit=58)
+    (piece,) = with_tri(first_kernel, [part], direction, block_inv, limit=58)
     found = {last: piece}
-    low = with_tri(lower_kernel, shaped(order, len(blocks_of(held)) * order), piece, block_inv)
+    spots = len(blocks_of(held)) * order
+    low, half = with_tri(lower_kernel, [shaped(order, spots), shaped(order // 2, spots)], block_inv)
     wide = jax.ShapeDtypeStruct((width, width), jnp.bfloat16)
     high_f, low_f = call(pair_kernel, [wide, wide], factor)
     turned_f = call(turn_factor_kernel, [wide, wide], factor)
@@ -430,8 +429,7 @@
     parts = [own] + shifts(own, "crow")
     mine, images = call(image_kernel, [part, shaped(rows, samples)], *parts, high_k, low_k, limit=16)
     images = [images] + shifts(images, "ccol", 0)
-    half = shaped(order // 2, low.shape[1])
-    summed, half = call(normal_kernel, [part, half], *images, high_k, low_k, low, limit=16)
+    summed = call(normal_kernel, part, *images, high_k, low_k, limit=16)
     if dp == 2:
         summed = summed + permute(summed, lambda d, r, c: (d ^ 1, r, c))
     else:
@@ -440,9 +438,8 @@
     beside = [((n, n), (n, n - 1)) for n in range(1, crow)]
     half = move(half, *beside)
     scale = 1.0 / (samples * dp * crow)
-    source, image, half = call(
-        functools.partial(source_kernel, scale, order), [part, part, shaped(*half.shape)],
-        mine, *parts, *turned, half,
+    source, image = call(
+        functools.partial(source_kernel, scale, order), [part, part], mine, *parts, *turned
     )
     near = call(merge_kernel, [wide, wide], half, move(half), block_inv)
     done = [image]

time: 87.3 us -> 101 us (1.16)
  starting transfers between devices: 47.4 us -> 54.4 us
  waiting for transfers between devices: 19.5 us -> 24.1 us
  local copies, waits for them, and re-layouts: 0.49 us -> 2.84 us
    ppermute x37, starting transfers between devices: 47.4 us -> 54.4 us  [permute(): return lax.ppermute(value, ('dp', 'crow', 'ccol'), perm)]
    ppermute x37, waiting for transfers between devices: 19.5 us -> 24.1 us  [permute(): return lax.ppermute(value, ('dp', 'crow', 'ccol'), perm)]
    unnamed x18 -> x22, local copies, waits for them, and re-layouts: 0.49 us -> 2.84 us
  transfers between devices with their start and end apart: 37 -> 37, of which waited for: 17 -> 21; matrix products, arithmetic and copies ran while one was open for 0% -> 0% of each run, Pallas kernels for 11% -> 15%
where the time goes in v2:
time: 101 us
  starting transfers between devices  54.4 us (54%)
  waiting for transfers between devices  24.1 us (24%)
  Pallas kernels  18.9 us (19%)
  local copies, waits for them, and re-layouts  2.84 us (3%)
    ppermute x37, starting transfers between devices, permute(): return lax.ppermute(value, ('dp', 'crow', 'ccol'), perm)  54.4 us
    ppermute x37, waiting for transfers between devices, permute(): return lax.ppermute(value, ('dp', 'crow', 'ccol'), perm)  24.1 us
    pallas_call x25, Pallas kernels, call(): pl.pallas_call(kernel, out_shape=outs, compiler_params=pltpu.CompilerPara...  18.9 us
    unnamed x22, local copies, waits for them, and re-layouts  2.84 us
  transfers between devices with their start and end apart: 37, of which 21 were waited for; matrix products, arithmetic and copies ran while one was open for 0% of the time, Pallas kernels for 15%

profile of v2, /device:TPU:0, one launch (start us, length us, event | category | flops | bytes accessed | tf_op | source)
XLA Modules:
  0.0 101.1 jit_solution(8646717369594847464)
XLA Ops:
  0.6 1.7 %copy-done = f32[768,768]{1,0:T(8,128)S(1)} copy-done((f32[768,768]{1,0:T(8,128)S(1)}, f32[768,768]{1,0:T(8,128)}, u32[]{:S(2)}) %copy-start) | copy-done | bytes 2359320
  2.3 1.1 %copy-done.2 = f32[3,256,256]{2,1,0:T(8,128)S(1)} copy-done((f32[3,256,256]{2,1,0:T(8,128)S(1)}, f32[3,256,256]{2,1,0:T(8,128)}, u32[]{:S(2)}) %copy-start.2) | copy-done | bytes 786456
  3.4 1.8 %shard_map.107 = (f32[256,768]{1,0:T(8,128)S(1)}, f32[128,768]{1,0:T(8,128)S(1)}) custom-call(f32[3,256,256]{2,1,0:T(8,128)S(1)} %copy-done.2, f32[768,768]{1,0:T(8,128)S(1)} %copy-done, f32[768,768]{1,0:T(8,128)S(1)} %copy-done, f32[768,768]{1,0:T(8,128)S(1)} %copy-done), custom_call_target="tpu_custom_call" | custom-call | flops 1000000 | bytes 1000000 | tf_op jit(solution)/shard_map/pallas_call | solution.py:331
  5.8 1.3 %collective-permute-done.22.mine_ref = f32[128,768]{1,0:T(8,128)S(1)} collective-permute-done((f32[128,768]{1,0:T(8,128)S(1)}, f32[128,768]{1,0:T(8,128)S(1)}, u32[]{:S(2)}, u32[]{:S(2)}) %collective-permute-start.22) | collective-permute-done | bytes 393248 | tf_op jit(solution)/shard_map/ppermute | solution.py:359
  7.6 3.0 %shard_map.103.refs_2_ = f32[8,768]{1,0:T(8,128)} custom-call(f32[8,3072]{1,0:T(8,128)} %direction_ref.9, f32[3,256,256]{2,1,0:T(8,128)} %inv_ref.13, f32[768,768]{1,0:T(8,128)} %factor_ref.3, f32[768,768]{1,0:T(8,128)} %factor_ref.3, f32[768,768]{1,0:T(8,128)} %factor_ref.3), custom_call_target="tpu_custom_call" | custom-call | flops 1000000 | bytes 1000000 | tf_op jit(solution)/shard_map/pallas_call | solution.py:331
  16.0 0.8 collective-permute-done.7.sub_ref.refs_0_
  17.6 0.8 collective-permute-done.8.refs_1_
  18.9 23.8 %collective-permute-start.9 = (f32[8,768]{1,0:T(8,128)S(1)}, f32[8,768]{1,0:T(8,128)S(1)}, u32[]{:S(2)}, u32[]{:S(2)}) collective-permute-start(f32[8,768]{1,0:T(8,128)S(1)} %shard_map.111), channel_id=1, source_target_pairs={{0,20},{1,17},{2,18},{3,19},{4,16},{5,21},{6,22},{7,23},{8,24},{9,... | collective-permute-start | bytes 73736 | tf_op jit(solution)/shard_map/ppermute | solution.py:359
  42.7 1.5 %collective-permute-done.9.sub_ref = f32[8,768]{1,0:T(8,128)S(1)} collective-permute-done((f32[8,768]{1,0:T(8,128)S(1)}, f32[8,768]{1,0:T(8,128)S(1)}, u32[]{:S(2)}, u32[]{:S(2)}) %collective-permute-start.9) | collective-permute-done | bytes 24608 | tf_op jit(solution)/shard_map/ppermute | solution.py:359
  44.6 1.7 %collective-permute-start.10 = (f32[8,768]{1,0:T(8,128)S(1)}, f32[8,768]{1,0:T(8,128)S(1)}, u32[]{:S(2)}, u32[]{:S(2)}) collective-permute-start(f32[8,768]{1,0:T(8,128)S(1)} %shard_map.112.refs_0_), channel_id=1, source_target_pairs={{0,20},{1,21},{2,22},{3,23},{4,16},{5,17},{6,18},{7,19},{8,28},{9,... | collective-permute-start | bytes 73736 | tf_op jit(solution)/shard_map/ppermute | solution.py:359
  46.3 1.5 %collective-permute-start.12 = (f32[8,768]{1,0:T(8,128)S(1)}, f32[8,768]{1,0:T(8,128)S(1)}, u32[]{:S(2)}, u32[]{:S(2)}) collective-permute-start(f32[8,768]{1,0:T(8,128)S(1)} %shard_map.112.refs_0_), channel_id=1, source_target_pairs={{0,28},{1,29},{2,30},{3,31},{4,24},{5,25},{6,26},{7,27},{8,20},{9,... | collective-permute-start | bytes 73736 | tf_op jit(solution)/shard_map/ppermute | solution.py:359
  47.9 2.7 %shard_map.113 = (bf16[768,2048]{1,0:T(8,128)(2,1)S(1)}, bf16[768,2048]{1,0:T(8,128)(2,1)S(1)}) custom-call(f32[16]{0:T(128)S(1)} %copy-done.10, f32[16,768]{1,0:T(8,128)S(1)} %copy-done.9, f32[16,2048]{1,0:T(8,128)S(1)} %copy-done.5), custom_call_target="tpu_custom_call" | custom-call | flops 1000000 | bytes 1000000 | tf_op jit(solution)/shard_map/pallas_call | solution.py:331
  50.6 0.9 shard_map.114
  51.6 4.3 %collective-permute-start.15 = (f32[8,2048]{1,0:T(8,128)S(1)}, f32[8,2048]{1,0:T(8,128)S(1)}, u32[]{:S(2)}, u32[]{:S(2)}) collective-permute-start(f32[8,2048]{1,0:T(8,128)S(1)} %get-tuple-element.25.refs_0_), channel_id=1, source_target_pairs={{0,3},{1,2},{2,1},{3,0},{4,7},{5,6},{6,5},{7,4},{8,11},{9,10},{10,... | collective-permute-start | bytes 196616 | tf_op jit(solution)/shard_map/ppermute | solution.py:359
  55.9 0.8 collective-permute-done.13.refs_1_
  56.8 3.5 %collective-permute-done.14.refs_2_ = f32[8,2048]{1,0:T(8,128)S(1)} collective-permute-done((f32[8,2048]{1,0:T(8,128)S(1)}, f32[8,2048]{1,0:T(8,128)S(1)}, u32[]{:S(2)}, u32[]{:S(2)}) %collective-permute-start.14) | collective-permute-done | bytes 65568 | tf_op jit(solution)/shard_map/ppermute | solution.py:359
  60.2 1.8 %shard_map.115 = f32[8,768]{1,0:T(8,128)S(1)} custom-call(f32[8,2048]{1,0:T(8,128)S(1)} %get-tuple-element.25.refs_0_, f32[8,2048]{1,0:T(8,128)S(1)} %collective-permute-done.13.refs_1_, f32[8,2048]{1,0:T(8,128)S(1)} %collective-permute-done.14.refs_2_, f32[8,2048]{1,0:T(8,128)S(1)} %collective-permute-done.15.refs_3_, ...), custom_call_target="tpu_custom_call" | custom-call | flops 1000000 | bytes 1000000 | tf_op jit(solution)/shard_map/pallas_call | solution.py:331
  62.1 1.2 %collective-permute-done.16 = f32[8,768]{1,0:T(8,128)S(1)} collective-permute-done((f32[8,768]{1,0:T(8,128)S(1)}, f32[8,768]{1,0:T(8,128)S(1)}, u32[]{:S(2)}, u32[]{:S(2)}) %collective-permute-start.16) | collective-permute-done | bytes 24608 | tf_op jit(solution)/shard_map/ppermute | solution.py:359
  63.3 1.4 %collective-permute-start.17 = (f32[8,768]{1,0:T(8,128)S(1)}, f32[8,768]{1,0:T(8,128)S(1)}, u32[]{:S(2)}, u32[]{:S(2)}) collective-permute-start(f32[8,768]{1,0:T(8,128)S(1)} %add.3.refs_0_), channel_id=1, source_target_pairs={{0,20},{1,21},{2,22},{3,23},{4,16},{5,17},{6,18},{7,19},{8,28},{9,... | collective-permute-start | bytes 73736 | tf_op jit(solution)/shard_map/ppermute | solution.py:359
  65.0 1.3 %collective-permute-start.19 = (f32[8,768]{1,0:T(8,128)S(1)}, f32[8,768]{1,0:T(8,128)S(1)}, u32[]{:S(2)}, u32[]{:S(2)}) collective-permute-start(f32[8,768]{1,0:T(8,128)S(1)} %add.3.refs_0_), channel_id=1, source_target_pairs={{0,28},{1,29},{2,30},{3,31},{4,24},{5,25},{6,26},{7,27},{8,20},{9,... | collective-permute-start | bytes 73736 | tf_op jit(solution)/shard_map/ppermute | solution.py:359
  66.8 1.2 %collective-permute-done.18.refs_2_ = f32[8,768]{1,0:T(8,128)S(1)} collective-permute-done((f32[8,768]{1,0:T(8,128)S(1)}, f32[8,768]{1,0:T(8,128)S(1)}, u32[]{:S(2)}, u32[]{:S(2)}) %collective-permute-start.18) | collective-permute-done | bytes 24608 | tf_op jit(solution)/shard_map/ppermute | solution.py:359
  68.0 1.1 %collective-permute-done.19.refs_3_ = f32[8,768]{1,0:T(8,128)S(1)} collective-permute-done((f32[8,768]{1,0:T(8,128)S(1)}, f32[8,768]{1,0:T(8,128)S(1)}, u32[]{:S(2)}, u32[]{:S(2)}) %collective-permute-start.19) | collective-permute-done | bytes 24608 | tf_op jit(solution)/shard_map/ppermute | solution.py:359
  69.4 1.5 %collective-permute-start.24 = (f32[8,768]{1,0:T(8,128)S(1)}, f32[8,768]{1,0:T(8,128)S(1)}, u32[]{:S(2)}, u32[]{:S(2)}) collective-permute-start(f32[8,768]{1,0:T(8,128)S(1)} %get-tuple-element.28.refs_0_), channel_id=1, source_target_pairs={{0,24},{1,17},{2,18},{3,19},{4,20},{5,21},{6,22},{7,23},{8,16},{9,... | collective-permute-start | bytes 73736 | tf_op jit(solution)/shard_map/ppermute | solution.py:359
  72.7 2.4 %collective-permute-done.25.refs_1_ = f32[8,768]{1,0:T(8,128)S(1)} collective-permute-done((f32[8,768]{1,0:T(8,128)S(1)}, f32[8,768]{1,0:T(8,128)S(1)}, u32[]{:S(2)}, u32[]{:S(2)}) %collective-permute-start.25) | collective-permute-done | bytes 24608 | tf_op jit(solution)/shard_map/ppermute | solution.py:359
  79.9 0.8 collective-permute-done.30.refs_1_
  81.6 4.0 %collective-permute-start.33 = (f32[8,768]{1,0:T(8,128)S(1)}, f32[8,768]{1,0:T(8,128)S(1)}, u32[]{:S(2)}, u32[]{:S(2)}) collective-permute-start(f32[8,768]{1,0:T(8,128)S(1)} %shard_map.125.refs_0_), channel_id=1, source_target_pairs={{0,19},{1,18},{2,17},{3,16},{4,23},{5,22},{6,21},{7,20},{8,27},{9,... | collective-permute-start | bytes 73736 | tf_op jit(solution)/shard_map/ppermute | solution.py:359
  85.8 1.8 %collective-permute-done.33.refs_3_ = f32[8,768]{1,0:T(8,128)S(1)} collective-permute-done((f32[8,768]{1,0:T(8,128)S(1)}, f32[8,768]{1,0:T(8,128)S(1)}, u32[]{:S(2)}, u32[]{:S(2)}) %collective-permute-start.33) | collective-permute-done | bytes 24608 | tf_op jit(solution)/shard_map/ppermute | solution.py:359
  87.6 4.8 %collective-permute-start.34 = (f32[8,768]{1,0:T(8,128)S(1)}, f32[8,768]{1,0:T(8,128)S(1)}, u32[]{:S(2)}, u32[]{:S(2)}) collective-permute-start(f32[8,768]{1,0:T(8,128)S(1)} %shard_map.126.refs_0_), channel_id=1, source_target_pairs={{0,20},{1,21},{2,22},{3,23},{4,16},{5,17},{6,18},{7,19},{8,28},{9,... | collective-permute-start | bytes 73736 | tf_op jit(solution)/shard_map/ppermute | solution.py:359
  92.4 3.7 %collective-permute-start.35 = (f32[8,768]{1,0:T(8,128)S(1)}, f32[8,768]{1,0:T(8,128)S(1)}, u32[]{:S(2)}, u32[]{:S(2)}) collective-permute-start(f32[8,768]{1,0:T(8,128)S(1)} %shard_map.126.refs_0_), channel_id=1, source_target_pairs={{0,24},{1,25},{2,26},{3,27},{4,28},{5,29},{6,30},{7,31},{8,16},{9,... | collective-permute-start | bytes 73736 | tf_op jit(solution)/shard_map/ppermute | solution.py:359
  96.1 1.5 %collective-permute-done.35.refs_2_ = f32[8,768]{1,0:T(8,128)S(1)} collective-permute-done((f32[8,768]{1,0:T(8,128)S(1)}, f32[8,768]{1,0:T(8,128)S(1)}, u32[]{:S(2)}, u32[]{:S(2)}) %collective-permute-start.35) | collective-permute-done | bytes 24608 | tf_op jit(solution)/shard_map/ppermute | solution.py:359
  97.6 2.6 %collective-permute-done.36.refs_3_ = f32[8,768]{1,0:T(8,128)S(1)} collective-permute-done((f32[8,768]{1,0:T(8,128)S(1)}, f32[8,768]{1,0:T(8,128)S(1)}, u32[]{:S(2)}, u32[]{:S(2)}) %collective-permute-start.36) | collective-permute-done | bytes 24608 | tf_op jit(solution)/shard_map/ppermute | solution.py:359
  100.2 0.9 shard_map.127
  (90 shorter events, 16.6 us)
Async XLA Ops:
  5.3 1.9 %collective-permute-start.22 = (f32[128,768]{1,0:T(8,128)S(1)}, f32[128,768]{1,0:T(8,128)S(1)}, u32[]{:S(2)}, u32[]{:S(2)}) collective-permute-start(f32[128,768]{1,0:T(8,128)S(1)} %get-tuple-element.32), channel_id=1, source_target_pairs={{0,16},{1,17},{2,18},{3,19},{4,21},{5,20},{6,22},{7,23},{8,24},{9,... | collective-permute-start | bytes 1179656 | tf_op jit(solution)/shard_map/ppermute | solution.py:359
  7.2 68.7 %collective-permute-start.23 = (f32[128,768]{1,0:T(8,128)S(1)}, f32[128,768]{1,0:T(8,128)S(1)}, u32[]{:S(2)}, u32[]{:S(2)}) collective-permute-start(f32[128,768]{1,0:T(8,128)S(1)} %collective-permute-done.22.mine_ref), channel_id=1, source_target_pairs={{0,16},{1,17},{2,18},{3,19},{4,20},{5,21},{6,22},{7,23},{8,24},{9,... | collective-permute-start | bytes 1179656 | tf_op jit(solution)/shard_map/ppermute | solution.py:359
  10.5 1.4 %collective-permute-start.3 = (f32[8,768]{1,0:T(8,128)}, f32[8,768]{1,0:T(8,128)S(1)}, u32[]{:S(2)}, u32[]{:S(2)}) collective-permute-start(f32[8,768]{1,0:T(8,128)} %shard_map.103.refs_2_), channel_id=1, source_target_pairs={{0,16},{1,17},{2,18},{3,19},{4,20},{5,21},{6,22},{7,23},{8,24},{9,... | collective-permute-start | bytes 73736 | tf_op jit(solution)/shard_map/ppermute | solution.py:359
  10.7 1.9 %collective-permute-start = (f32[8,768]{1,0:T(8,128)}, f32[8,768]{1,0:T(8,128)S(1)}, u32[]{:S(2)}, u32[]{:S(2)}) collective-permute-start(f32[8,768]{1,0:T(8,128)} %shard_map.103.refs_2_), channel_id=1, source_target_pairs={{0,16},{1,17},{2,18},{3,19},{4,20},{5,21},{6,22},{7,23},{8,24},{9,... | collective-permute-start | bytes 73736 | tf_op jit(solution)/shard_map/ppermute | solution.py:359
  11.0 1.5 %collective-permute-start.1 = (f32[8,768]{1,0:T(8,128)}, f32[8,768]{1,0:T(8,128)S(1)}, u32[]{:S(2)}, u32[]{:S(2)}) collective-permute-start(f32[8,768]{1,0:T(8,128)} %shard_map.103.refs_2_), channel_id=1, source_target_pairs={{0,16},{1,17},{2,18},{3,19},{4,20},{5,21},{6,22},{7,23},{8,24},{9,... | collective-permute-start | bytes 73736 | tf_op jit(solution)/shard_map/ppermute | solution.py:359
  12.9 1.5 %collective-permute-start.2 = (f32[8,768]{1,0:T(8,128)S(1)}, f32[8,768]{1,0:T(8,128)S(1)}, u32[]{:S(2)}, u32[]{:S(2)}) collective-permute-start(f32[8,768]{1,0:T(8,128)S(1)} %shard_map.105), channel_id=1, source_target_pairs={{0,16},{1,17},{2,18},{3,19},{4,20},{5,21},{6,22},{7,23},{8,28},{9,... | collective-permute-start | bytes 73736 | tf_op jit(solution)/shard_map/ppermute | solution.py:359
  18.9 25.3 %collective-permute-start.9 = (f32[8,768]{1,0:T(8,128)S(1)}, f32[8,768]{1,0:T(8,128)S(1)}, u32[]{:S(2)}, u32[]{:S(2)}) collective-permute-start(f32[8,768]{1,0:T(8,128)S(1)} %shard_map.111), channel_id=1, source_target_pairs={{0,20},{1,17},{2,18},{3,19},{4,16},{5,21},{6,22},{7,23},{8,24},{9,... | collective-permute-start | bytes 73736 | tf_op jit(solution)/shard_map/ppermute | solution.py:359
  44.6 6.0 %collective-permute-start.10 = (f32[8,768]{1,0:T(8,128)S(1)}, f32[8,768]{1,0:T(8,128)S(1)}, u32[]{:S(2)}, u32[]{:S(2)}) collective-permute-start(f32[8,768]{1,0:T(8,128)S(1)} %shard_map.112.refs_0_), channel_id=1, source_target_pairs={{0,20},{1,21},{2,22},{3,23},{4,16},{5,17},{6,18},{7,19},{8,28},{9,... | collective-permute-start | bytes 73736 | tf_op jit(solution)/shard_map/ppermute | solution.py:359
  46.3 4.3 %collective-permute-start.11 = (f32[8,768]{1,0:T(8,128)S(1)}, f32[8,768]{1,0:T(8,128)S(1)}, u32[]{:S(2)}, u32[]{:S(2)}) collective-permute-start(f32[8,768]{1,0:T(8,128)S(1)} %shard_map.112.refs_0_), channel_id=1, source_target_pairs={{0,24},{1,25},{2,26},{3,27},{4,28},{5,29},{6,30},{7,31},{8,16},{9,... | collective-permute-start | bytes 73736 | tf_op jit(solution)/shard_map/ppermute | solution.py:359
  46.3 4.3 %collective-permute-start.12 = (f32[8,768]{1,0:T(8,128)S(1)}, f32[8,768]{1,0:T(8,128)S(1)}, u32[]{:S(2)}, u32[]{:S(2)}) collective-permute-start(f32[8,768]{1,0:T(8,128)S(1)} %shard_map.112.refs_0_), channel_id=1, source_target_pairs={{0,28},{1,29},{2,30},{3,31},{4,24},{5,25},{6,26},{7,27},{8,20},{9,... | collective-permute-start | bytes 73736 | tf_op jit(solution)/shard_map/ppermute | solution.py:359
  51.5 5.3 %collective-permute-start.13 = (f32[8,2048]{1,0:T(8,128)S(1)}, f32[8,2048]{1,0:T(8,128)S(1)}, u32[]{:S(2)}, u32[]{:S(2)}) collective-permute-start(f32[8,2048]{1,0:T(8,128)S(1)} %get-tuple-element.25.refs_0_), channel_id=1, source_target_pairs={{0,1},{1,0},{2,3},{3,2},{4,5},{5,4},{6,7},{7,6},{8,9},{9,8},{10,11... | collective-permute-start | bytes 196616 | tf_op jit(solution)/shard_map/ppermute | solution.py:359
  51.5 8.7 %collective-permute-start.14 = (f32[8,2048]{1,0:T(8,128)S(1)}, f32[8,2048]{1,0:T(8,128)S(1)}, u32[]{:S(2)}, u32[]{:S(2)}) collective-permute-start(f32[8,2048]{1,0:T(8,128)S(1)} %get-tuple-element.25.refs_0_), channel_id=1, source_target_pairs={{0,2},{1,3},{2,0},{3,1},{4,6},{5,7},{6,4},{7,5},{8,10},{9,11},{10,... | collective-permute-start | bytes 196616 | tf_op jit(solution)/shard_map/ppermute | solution.py:359
  51.6 8.7 %collective-permute-start.15 = (f32[8,2048]{1,0:T(8,128)S(1)}, f32[8,2048]{1,0:T(8,128)S(1)}, u32[]{:S(2)}, u32[]{:S(2)}) collective-permute-start(f32[8,2048]{1,0:T(8,128)S(1)} %get-tuple-element.25.refs_0_), channel_id=1, source_target_pairs={{0,3},{1,2},{2,1},{3,0},{4,7},{5,6},{6,5},{7,4},{8,11},{9,10},{10,... | collective-permute-start | bytes 196616 | tf_op jit(solution)/shard_map/ppermute | solution.py:359
  62.1 1.2 %collective-permute-start.16 = (f32[8,768]{1,0:T(8,128)S(1)}, f32[8,768]{1,0:T(8,128)S(1)}, u32[]{:S(2)}, u32[]{:S(2)}) collective-permute-start(f32[8,768]{1,0:T(8,128)S(1)} %shard_map.115), channel_id=1, source_target_pairs={{0,16},{1,17},{2,18},{3,19},{4,20},{5,21},{6,22},{7,23},{8,24},{9,... | collective-permute-start | bytes 73736 | tf_op jit(solution)/shard_map/ppermute | solution.py:359
  63.3 3.5 %collective-permute-start.17 = (f32[8,768]{1,0:T(8,128)S(1)}, f32[8,768]{1,0:T(8,128)S(1)}, u32[]{:S(2)}, u32[]{:S(2)}) collective-permute-start(f32[8,768]{1,0:T(8,128)S(1)} %add.3.refs_0_), channel_id=1, source_target_pairs={{0,20},{1,21},{2,22},{3,23},{4,16},{5,17},{6,18},{7,19},{8,28},{9,... | collective-permute-start | bytes 73736 | tf_op jit(solution)/shard_map/ppermute | solution.py:359
  64.7 3.3 %collective-permute-start.18 = (f32[8,768]{1,0:T(8,128)S(1)}, f32[8,768]{1,0:T(8,128)S(1)}, u32[]{:S(2)}, u32[]{:S(2)}) collective-permute-start(f32[8,768]{1,0:T(8,128)S(1)} %add.3.refs_0_), channel_id=1, source_target_pairs={{0,24},{1,25},{2,26},{3,27},{4,28},{5,29},{6,30},{7,31},{8,16},{9,... | collective-permute-start | bytes 73736 | tf_op jit(solution)/shard_map/ppermute | solution.py:359
  65.0 4.2 %collective-permute-start.19 = (f32[8,768]{1,0:T(8,128)S(1)}, f32[8,768]{1,0:T(8,128)S(1)}, u32[]{:S(2)}, u32[]{:S(2)}) collective-permute-start(f32[8,768]{1,0:T(8,128)S(1)} %add.3.refs_0_), channel_id=1, source_target_pairs={{0,28},{1,29},{2,30},{3,31},{4,24},{5,25},{6,26},{7,27},{8,20},{9,... | collective-permute-start | bytes 73736 | tf_op jit(solution)/shard_map/ppermute | solution.py:359
  69.4 3.3 %collective-permute-start.24 = (f32[8,768]{1,0:T(8,128)S(1)}, f32[8,768]{1,0:T(8,128)S(1)}, u32[]{:S(2)}, u32[]{:S(2)}) collective-permute-start(f32[8,768]{1,0:T(8,128)S(1)} %get-tuple-element.28.refs_0_), channel_id=1, source_target_pairs={{0,24},{1,17},{2,18},{3,19},{4,20},{5,21},{6,22},{7,23},{8,16},{9,... | collective-permute-start | bytes 73736 | tf_op jit(solution)/shard_map/ppermute | solution.py:359
  71.0 4.2 %collective-permute-start.25 = (f32[8,768]{1,0:T(8,128)S(1)}, f32[8,768]{1,0:T(8,128)S(1)}, u32[]{:S(2)}, u32[]{:S(2)}) collective-permute-start(f32[8,768]{1,0:T(8,128)S(1)} %get-tuple-element.28.refs_0_), channel_id=1, source_target_pairs={{0,28},{1,17},{2,18},{3,19},{4,20},{5,21},{6,22},{7,23},{8,24},{9,... | collective-permute-start | bytes 73736 | tf_op jit(solution)/shard_map/ppermute | solution.py:359
  71.1 5.3 %collective-permute-start.20 = (f32[8,768]{1,0:T(8,128)S(1)}, f32[8,768]{1,0:T(8,128)S(1)}, u32[]{:S(2)}, u32[]{:S(2)}) collective-permute-start(f32[8,768]{1,0:T(8,128)S(1)} %get-tuple-element.28.refs_0_), channel_id=1, source_target_pairs={{0,20},{1,17},{2,18},{3,19},{4,16},{5,21},{6,22},{7,23},{8,24},{9,... | collective-permute-start | bytes 73736 | tf_op jit(solution)/shard_map/ppermute | solution.py:359
  71.5 4.8 %collective-permute-start.21 = (f32[8,768]{1,0:T(8,128)S(1)}, f32[8,768]{1,0:T(8,128)S(1)}, u32[]{:S(2)}, u32[]{:S(2)}) collective-permute-start(f32[8,768]{1,0:T(8,128)S(1)} %get-tuple-element.29), channel_id=1, source_target_pairs={{0,16},{1,17},{2,18},{3,19},{4,21},{5,20},{6,22},{7,23},{8,24},{9,... | collective-permute-start | bytes 73736 | tf_op jit(solution)/shard_map/ppermute | solution.py:359
  75.5 2.1 %collective-permute-start.26 = (f32[8,768]{1,0:T(8,128)S(1)}, f32[8,768]{1,0:T(8,128)S(1)}, u32[]{:S(2)}, u32[]{:S(2)}) collective-permute-start(f32[8,768]{1,0:T(8,128)S(1)} %shard_map.121), channel_id=1, source_target_pairs={{0,16},{1,17},{2,18},{3,19},{4,20},{5,21},{6,22},{7,23},{8,25},{9,... | collective-permute-start | bytes 73736 | tf_op jit(solution)/shard_map/ppermute | solution.py:359
  77.1 1.2 %collective-permute-start.28 = (f32[8,768]{1,0:T(8,128)S(1)}, f32[8,768]{1,0:T(8,128)S(1)}, u32[]{:S(2)}, u32[]{:S(2)}) collective-permute-start(f32[8,768]{1,0:T(8,128)S(1)} %shard_map.120.refs_1_), channel_id=1, source_target_pairs={{0,16},{1,17},{2,18},{3,19},{4,29},{5,21},{6,22},{7,23},{8,24},{9,... | collective-permute-start | bytes 73736 | tf_op jit(solution)/shard_map/ppermute | solution.py:359
  77.2 1.6 %collective-permute-start.27 = (f32[8,768]{1,0:T(8,128)S(1)}, f32[8,768]{1,0:T(8,128)S(1)}, u32[]{:S(2)}, u32[]{:S(2)}) collective-permute-start(f32[8,768]{1,0:T(8,128)S(1)} %shard_map.120.refs_1_), channel_id=1, source_target_pairs={{0,16},{1,17},{2,18},{3,19},{4,25},{5,21},{6,22},{7,23},{8,24},{9,... | collective-permute-start | bytes 73736 | tf_op jit(solution)/shard_map/ppermute | solution.py:359
  78.7 1.2 %collective-permute-start.29 = (f32[8,768]{1,0:T(8,128)S(1)}, f32[8,768]{1,0:T(8,128)S(1)}, u32[]{:S(2)}, u32[]{:S(2)}) collective-permute-start(f32[8,768]{1,0:T(8,128)S(1)} %shard_map.123), channel_id=1, source_target_pairs={{0,16},{1,17},{2,18},{3,19},{4,20},{5,21},{6,22},{7,23},{8,24},{9,... | collective-permute-start | bytes 73736 | tf_op jit(solution)/shard_map/ppermute | solution.py:359
  79.5 1.2 %collective-permute-start.30 = (f32[8,768]{1,0:T(8,128)S(1)}, f32[8,768]{1,0:T(8,128)S(1)}, u32[]{:S(2)}, u32[]{:S(2)}) collective-permute-start(f32[8,768]{1,0:T(8,128)S(1)} %shard_map.122.refs_2_), channel_id=1, source_target_pairs={{0,16},{1,17},{2,18},{3,19},{4,20},{5,21},{6,22},{7,23},{8,24},{9,... | collective-permute-start | bytes 73736 | tf_op jit(solution)/shard_map/ppermute | solution.py:359
  81.5 4.1 %collective-permute-start.31 = (f32[8,768]{1,0:T(8,128)S(1)}, f32[8,768]{1,0:T(8,128)S(1)}, u32[]{:S(2)}, u32[]{:S(2)}) collective-permute-start(f32[8,768]{1,0:T(8,128)S(1)} %shard_map.125.refs_0_), channel_id=1, source_target_pairs={{0,17},{1,16},{2,19},{3,18},{4,21},{5,20},{6,23},{7,22},{8,25},{9,... | collective-permute-start | bytes 73736 | tf_op jit(solution)/shard_map/ppermute | solution.py:359
  81.6 4.2 %collective-permute-start.32 = (f32[8,768]{1,0:T(8,128)S(1)}, f32[8,768]{1,0:T(8,128)S(1)}, u32[]{:S(2)}, u32[]{:S(2)}) collective-permute-start(f32[8,768]{1,0:T(8,128)S(1)} %shard_map.125.refs_0_), channel_id=1, source_target_pairs={{0,18},{1,19},{2,16},{3,17},{4,22},{5,23},{6,20},{7,21},{8,26},{9,... | collective-permute-start | bytes 73736 | tf_op jit(solution)/shard_map/ppermute | solution.py:359
  81.6 5.9 %collective-permute-start.33 = (f32[8,768]{1,0:T(8,128)S(1)}, f32[8,768]{1,0:T(8,128)S(1)}, u32[]{:S(2)}, u32[]{:S(2)}) collective-permute-start(f32[8,768]{1,0:T(8,128)S(1)} %shard_map.125.refs_0_), channel_id=1, source_target_pairs={{0,19},{1,18},{2,17},{3,16},{4,23},{5,22},{6,21},{7,20},{8,27},{9,... | collective-permute-start | bytes 73736 | tf_op jit(solution)/shard_map/ppermute | solution.py:359
  87.6 8.5 %collective-permute-start.34 = (f32[8,768]{1,0:T(8,128)S(1)}, f32[8,768]{1,0:T(8,128)S(1)}, u32[]{:S(2)}, u32[]{:S(2)}) collective-permute-start(f32[8,768]{1,0:T(8,128)S(1)} %shard_map.126.refs_0_), channel_id=1, source_target_pairs={{0,20},{1,21},{2,22},{3,23},{4,16},{5,17},{6,18},{7,19},{8,28},{9,... | collective-permute-start | bytes 73736 | tf_op jit(solution)/shard_map/ppermute | solution.py:359
  92.4 5.2 %collective-permute-start.35 = (f32[8,768]{1,0:T(8,128)S(1)}, f32[8,768]{1,0:T(8,128)S(1)}, u32[]{:S(2)}, u32[]{:S(2)}) collective-permute-start(f32[8,768]{1,0:T(8,128)S(1)} %shard_map.126.refs_0_), channel_id=1, source_target_pairs={{0,24},{1,25},{2,26},{3,27},{4,28},{5,29},{6,30},{7,31},{8,16},{9,... | collective-permute-start | bytes 73736 | tf_op jit(solution)/shard_map/ppermute | solution.py:359
  96.1 4.2 %collective-permute-start.36 = (f32[8,768]{1,0:T(8,128)S(1)}, f32[8,768]{1,0:T(8,128)S(1)}, u32[]{:S(2)}, u32[]{:S(2)}) collective-permute-start(f32[8,768]{1,0:T(8,128)S(1)} %shard_map.126.refs_0_), channel_id=1, source_target_pairs={{0,28},{1,29},{2,30},{3,31},{4,24},{5,25},{6,26},{7,27},{8,20},{9,... | collective-permute-start | bytes 73736 | tf_op jit(solution)/shard_map/ppermute | solution.py:359
  (16 other events, 170.3 us)

commit v3 on v2

--- a/solution.py
+++ b/solution.py
@@ -118,7 +118,7 @@
 
 
 def lower_kernel(inv_ref, *refs):
-    tri_refs, out_ref, half_ref = refs[:-2], refs[-2], refs[-1]
+    tri_refs, (out_ref, half_ref, rest_ref) = refs[:-3], refs[-3:]
     held, order = inv_ref.shape[0], inv_ref.shape[1]
     tri = dict(zip(blocks_of(held), tri_refs))
     found = {(n, n): inv_ref[n] for n in range(held)}
@@ -132,7 +132,9 @@
             out_ref[:, at * order : (at + 1) * order] = found[r, c]
     tall = half_ref.shape[0]
     at = lax.rem(lax.axis_index("dp"), 2) * tall
-    half_ref[...] = out_ref[pl.ds(pl.multiple_of(at, tall), tall), :]
+    split = half_ref.shape[1]
+    half_ref[...] = out_ref[pl.ds(pl.multiple_of(at, tall), tall), :split]
+    rest_ref[...] = out_ref[:, split:]
 
 
 def pair_kernel(factor_ref, high_ref, low_ref):
@@ -155,10 +157,11 @@
     out_ref[...] = out
 
 
-def merge_kernel(mine_ref, other_ref, inv_ref, high_out, low_out):
+def merge_kernel(mine_ref, other_ref, rest_ref, inv_ref, high_out, low_out):
     odd = lax.rem(lax.axis_index("dp"), 2) == 1
     mine, other = mine_ref[...], other_ref[...]
     low = jnp.concatenate([jnp.where(odd, mine, other), jnp.where(odd, other, mine)], axis=0)
+    low = jnp.concatenate([low, rest_ref[...]], axis=1)
     store_turned(low, inv_ref, high_out, low_out)
 
 
@@ -358,9 +361,15 @@
         ]
         return lax.ppermute(value, ("dp", "crow", "ccol"), perm)
 
-    def move(value, *pairs):
+    idle = [(r, c) for r in range(crow) for c in range(r + 1, ccol)]
+
+    def move(value, *pairs, direct=False):
         to = dict(pairs)
-        to.update((b, a) for a, b in pairs)
+        for (a, b), spare in zip(pairs, idle):
+            if direct:
+                to[b] = a
+            else:
+                to[b], to[spare] = spare, a
         return permute(value, lambda d, r, c: (d ^ 1, *to.get((r, c), (r, c))))
 
     def shifts(value, axis, flip=1):
@@ -380,7 +389,11 @@
     (piece,) = with_tri(first_kernel, [part], direction, block_inv, limit=58)
     found = {last: piece}
     spots = len(blocks_of(held)) * order
-    low, half = with_tri(lower_kernel, [shaped(order, spots), shaped(order // 2, spots)], block_inv)
+    low, half, rest = with_tri(
+        lower_kernel,
+        [shaped(order, spots), shaped(order // 2, spots - order), shaped(order, order)],
+        block_inv,
+    )
     wide = jax.ShapeDtypeStruct((width, width), jnp.bfloat16)
     high_f, low_f = call(pair_kernel, [wide, wide], factor)
     turned_f = call(turn_factor_kernel, [wide, wide], factor)
@@ -427,6 +440,8 @@
     )
 
     parts = [own] + shifts(own, "crow")
+    beside = [((n, n), (n, n - 1)) for n in range(1, crow)]
+    half = move(half, *beside, direct=True)
     mine, images = call(image_kernel, [part, shaped(rows, samples)], *parts, high_k, low_k, limit=16)
     images = [images] + shifts(images, "ccol", 0)
     summed = call(normal_kernel, part, *images, high_k, low_k, limit=16)
@@ -435,13 +450,12 @@
     else:
         summed = lax.psum(summed, "dp")
     parts = [summed] + shifts(summed, "crow")
-    beside = [((n, n), (n, n - 1)) for n in range(1, crow)]
-    half = move(half, *beside)
+    rest = move(rest, *beside, direct=True)
     scale = 1.0 / (samples * dp * crow)
     source, image = call(
         functools.partial(source_kernel, scale, order), [part, part], mine, *parts, *turned
     )
-    near = call(merge_kernel, [wide, wide], half, move(half), block_inv)
+    near = call(merge_kernel, [wide, wide], half, move(half), rest, block_inv)
     done = [image]
     places = [(0, 0)]
     side = []

time: 101 us -> 102 us (level)
  starting transfers between devices: 54.4 us -> 56.1 us
    ppermute x37 -> x38, starting transfers between devices: 54.4 us -> 56.1 us  [permute(): return lax.ppermute(value, ('dp', 'crow', 'ccol'), perm)]
    ppermute x37 -> x38, waiting for transfers between devices: 24.1 us -> 23.1 us  [permute(): return lax.ppermute(value, ('dp', 'crow', 'ccol'), perm)]
  transfers between devices with their start and end apart: 37 -> 38, of which waited for: 21 -> 19; matrix products, arithmetic and copies ran while one was open for 0% -> 0% of each run, Pallas kernels for 15% -> 15%
where the time goes in v3:
time: 102 us
  starting transfers between devices  56.1 us (55%)
  waiting for transfers between devices  23.1 us (23%)
  Pallas kernels  18.7 us (18%)
  local copies, waits for them, and re-layouts  2.84 us (3%)
    ppermute x38, starting transfers between devices, permute(): return lax.ppermute(value, ('dp', 'crow', 'ccol'), perm)  56.1 us
    ppermute x38, waiting for transfers between devices, permute(): return lax.ppermute(value, ('dp', 'crow', 'ccol'), perm)  23.1 us
    pallas_call x25, Pallas kernels, call(): pl.pallas_call(kernel, out_shape=outs, compiler_params=pltpu.CompilerPara...  18.7 us
    unnamed x22, local copies, waits for them, and re-layouts  2.84 us
  transfers between devices with their start and end apart: 38, of which 19 were waited for; matrix products, arithmetic and copies ran while one was open for 0% of the time, Pallas kernels for 15%

profile of v3, /device:TPU:0, one launch (start us, length us, event | category | flops | bytes accessed | tf_op | source)
XLA Modules:
  0.0 101.5 jit_solution(17680862135889248709)
XLA Ops:
  0.6 1.7 %copy-done = f32[768,768]{1,0:T(8,128)S(1)} copy-done((f32[768,768]{1,0:T(8,128)S(1)}, f32[768,768]{1,0:T(8,128)}, u32[]{:S(2)}) %copy-start) | copy-done | bytes 2359320
  2.3 1.1 %copy-done.2 = f32[3,256,256]{2,1,0:T(8,128)S(1)} copy-done((f32[3,256,256]{2,1,0:T(8,128)S(1)}, f32[3,256,256]{2,1,0:T(8,128)}, u32[]{:S(2)}) %copy-start.2) | copy-done | bytes 786456
  3.4 1.8 %shard_map.107 = (f32[256,768]{1,0:T(8,128)S(1)}, f32[128,512]{1,0:T(8,128)S(1)}, f32[256,256]{1,0:T(8,128)S(1)}) custom-call(f32[3,256,256]{2,1,0:T(8,128)S(1)} %copy-done.2, f32[768,768]{1,0:T(8,128)S(1)} %copy-done, f32[768,768]{1,0:T(8,128)S(1)} %copy-done, f32[768,768]{1,0:T(8,128)S(1)} %copy-done), custom_call_target="tpu_custom_call" | custom-call | flops 1000000 | bytes 1000000 | tf_op jit(solution)/shard_map/pallas_call | solution.py:334
  5.8 3.0 %shard_map.103.refs_2_ = f32[8,768]{1,0:T(8,128)} custom-call(f32[8,3072]{1,0:T(8,128)} %direction_ref.9, f32[3,256,256]{2,1,0:T(8,128)} %inv_ref.13, f32[768,768]{1,0:T(8,128)} %factor_ref.3, f32[768,768]{1,0:T(8,128)} %factor_ref.3, f32[768,768]{1,0:T(8,128)} %factor_ref.3), custom_call_target="tpu_custom_call" | custom-call | flops 1000000 | bytes 1000000 | tf_op jit(solution)/shard_map/pallas_call | solution.py:334
  12.7 0.7 collective-permute-done.5.refs_1_
  15.9 0.8 collective-permute-done.8.refs_1_
  17.1 21.4 %collective-permute-start.9 = (f32[8,768]{1,0:T(8,128)S(1)}, f32[8,768]{1,0:T(8,128)S(1)}, u32[]{:S(2)}, u32[]{:S(2)}) collective-permute-start(f32[8,768]{1,0:T(8,128)S(1)} %shard_map.111), channel_id=1, source_target_pairs={{0,17},{1,20},{2,18},{3,19},{4,16},{5,21},{6,22},{7,23},{8,24},{9,... | collective-permute-start | bytes 73736 | tf_op jit(solution)/shard_map/ppermute | solution.py:362
  38.6 1.5 %collective-permute-done.9.sub_ref = f32[8,768]{1,0:T(8,128)S(1)} collective-permute-done((f32[8,768]{1,0:T(8,128)S(1)}, f32[8,768]{1,0:T(8,128)S(1)}, u32[]{:S(2)}, u32[]{:S(2)}) %collective-permute-start.9) | collective-permute-done | bytes 24608 | tf_op jit(solution)/shard_map/ppermute | solution.py:362
  40.4 1.9 %collective-permute-start.10 = (f32[8,768]{1,0:T(8,128)S(1)}, f32[8,768]{1,0:T(8,128)S(1)}, u32[]{:S(2)}, u32[]{:S(2)}) collective-permute-start(f32[8,768]{1,0:T(8,128)S(1)} %shard_map.112.refs_0_), channel_id=1, source_target_pairs={{0,20},{1,21},{2,22},{3,23},{4,16},{5,17},{6,18},{7,19},{8,28},{9,... | collective-permute-start | bytes 73736 | tf_op jit(solution)/shard_map/ppermute | solution.py:362
  42.4 1.5 %collective-permute-start.12 = (f32[8,768]{1,0:T(8,128)S(1)}, f32[8,768]{1,0:T(8,128)S(1)}, u32[]{:S(2)}, u32[]{:S(2)}) collective-permute-start(f32[8,768]{1,0:T(8,128)S(1)} %shard_map.112.refs_0_), channel_id=1, source_target_pairs={{0,28},{1,29},{2,30},{3,31},{4,24},{5,25},{6,26},{7,27},{8,20},{9,... | collective-permute-start | bytes 73736 | tf_op jit(solution)/shard_map/ppermute | solution.py:362
  43.9 2.5 %shard_map.113 = (bf16[768,2048]{1,0:T(8,128)(2,1)S(1)}, bf16[768,2048]{1,0:T(8,128)(2,1)S(1)}) custom-call(f32[16]{0:T(128)S(1)} %copy-done.10, f32[16,768]{1,0:T(8,128)S(1)} %copy-done.9, f32[16,2048]{1,0:T(8,128)S(1)} %copy-done.5), custom_call_target="tpu_custom_call" | custom-call | flops 1000000 | bytes 1000000 | tf_op jit(solution)/shard_map/pallas_call | solution.py:334
  46.5 0.9 shard_map.114
  47.5 1.4 %collective-permute-start.13 = (f32[8,2048]{1,0:T(8,128)S(1)}, f32[8,2048]{1,0:T(8,128)S(1)}, u32[]{:S(2)}, u32[]{:S(2)}) collective-permute-start(f32[8,2048]{1,0:T(8,128)S(1)} %get-tuple-element.26.refs_0_), channel_id=1, source_target_pairs={{0,1},{1,0},{2,3},{3,2},{4,5},{5,4},{6,7},{7,6},{8,9},{9,8},{10,11... | collective-permute-start | bytes 196616 | tf_op jit(solution)/shard_map/ppermute | solution.py:362
  48.9 3.0 %collective-permute-start.15 = (f32[8,2048]{1,0:T(8,128)S(1)}, f32[8,2048]{1,0:T(8,128)S(1)}, u32[]{:S(2)}, u32[]{:S(2)}) collective-permute-start(f32[8,2048]{1,0:T(8,128)S(1)} %get-tuple-element.26.refs_0_), channel_id=1, source_target_pairs={{0,3},{1,2},{2,1},{3,0},{4,7},{5,6},{6,5},{7,4},{8,11},{9,10},{10,... | collective-permute-start | bytes 196616 | tf_op jit(solution)/shard_map/ppermute | solution.py:362
  51.9 5.0 %collective-permute-done.14.refs_2_ = f32[8,2048]{1,0:T(8,128)S(1)} collective-permute-done((f32[8,2048]{1,0:T(8,128)S(1)}, f32[8,2048]{1,0:T(8,128)S(1)}, u32[]{:S(2)}, u32[]{:S(2)}) %collective-permute-start.14) | collective-permute-done | bytes 65568 | tf_op jit(solution)/shard_map/ppermute | solution.py:362
  56.9 1.8 %shard_map.115 = f32[8,768]{1,0:T(8,128)S(1)} custom-call(f32[8,2048]{1,0:T(8,128)S(1)} %get-tuple-element.26.refs_0_, f32[8,2048]{1,0:T(8,128)S(1)} %collective-permute-done.13.refs_1_, f32[8,2048]{1,0:T(8,128)S(1)} %collective-permute-done.14.refs_2_, f32[8,2048]{1,0:T(8,128)S(1)} %collective-permute-done.15.refs_3_, ...), custom_call_target="tpu_custom_call" | custom-call | flops 1000000 | bytes 1000000 | tf_op jit(solution)/shard_map/pallas_call | solution.py:334
  58.7 1.2 %collective-permute-done.16 = f32[8,768]{1,0:T(8,128)S(1)} collective-permute-done((f32[8,768]{1,0:T(8,128)S(1)}, f32[8,768]{1,0:T(8,128)S(1)}, u32[]{:S(2)}, u32[]{:S(2)}) %collective-permute-start.16) | collective-permute-done | bytes 24608 | tf_op jit(solution)/shard_map/ppermute | solution.py:362
  59.9 0.9 collective-permute-start.17
  60.8 0.9 collective-permute-start.18
  61.7 1.2 %collective-permute-start.19 = (f32[8,768]{1,0:T(8,128)S(1)}, f32[8,768]{1,0:T(8,128)S(1)}, u32[]{:S(2)}, u32[]{:S(2)}) collective-permute-start(f32[8,768]{1,0:T(8,128)S(1)} %add.3.refs_0_), channel_id=1, source_target_pairs={{0,28},{1,29},{2,30},{3,31},{4,24},{5,25},{6,26},{7,27},{8,20},{9,... | collective-permute-start | bytes 73736 | tf_op jit(solution)/shard_map/ppermute | solution.py:362
  64.0 1.8 %collective-permute-done.19.refs_3_ = f32[8,768]{1,0:T(8,128)S(1)} collective-permute-done((f32[8,768]{1,0:T(8,128)S(1)}, f32[8,768]{1,0:T(8,128)S(1)}, u32[]{:S(2)}, u32[]{:S(2)}) %collective-permute-start.19) | collective-permute-done | bytes 24608 | tf_op jit(solution)/shard_map/ppermute | solution.py:362
  66.1 0.9 collective-permute-start.25
  67.0 0.7 collective-permute-start.26
  67.7 1.7 %collective-permute-done.25.refs_0_ = f32[8,768]{1,0:T(8,128)S(1)} collective-permute-done((f32[8,768]{1,0:T(8,128)S(1)}, f32[8,768]{1,0:T(8,128)S(1)}, u32[]{:S(2)}, u32[]{:S(2)}) %collective-permute-start.25) | collective-permute-done | bytes 24608 | tf_op jit(solution)/shard_map/ppermute | solution.py:362
  75.4 0.8 collective-permute-done.31.refs_1_
  77.0 11.0 %collective-permute-start.32 = (f32[8,768]{1,0:T(8,128)S(1)}, f32[8,768]{1,0:T(8,128)S(1)}, u32[]{:S(2)}, u32[]{:S(2)}) collective-permute-start(f32[8,768]{1,0:T(8,128)S(1)} %shard_map.125.refs_0_), channel_id=1, source_target_pairs={{0,17},{1,16},{2,19},{3,18},{4,21},{5,20},{6,23},{7,22},{8,25},{9,... | collective-permute-start | bytes 73736 | tf_op jit(solution)/shard_map/ppermute | solution.py:362
  88.0 2.4 %collective-permute-start.34 = (f32[8,768]{1,0:T(8,128)S(1)}, f32[8,768]{1,0:T(8,128)S(1)}, u32[]{:S(2)}, u32[]{:S(2)}) collective-permute-start(f32[8,768]{1,0:T(8,128)S(1)} %shard_map.125.refs_0_), channel_id=1, source_target_pairs={{0,19},{1,18},{2,17},{3,16},{4,23},{5,22},{6,21},{7,20},{8,27},{9,... | collective-permute-start | bytes 73736 | tf_op jit(solution)/shard_map/ppermute | solution.py:362
  90.4 2.0 %collective-permute-done.33.refs_2_ = f32[8,768]{1,0:T(8,128)S(1)} collective-permute-done((f32[8,768]{1,0:T(8,128)S(1)}, f32[8,768]{1,0:T(8,128)S(1)}, u32[]{:S(2)}, u32[]{:S(2)}) %collective-permute-start.33) | collective-permute-done | bytes 24608 | tf_op jit(solution)/shard_map/ppermute | solution.py:362
  93.2 3.3 %collective-permute-start.36 = (f32[8,768]{1,0:T(8,128)S(1)}, f32[8,768]{1,0:T(8,128)S(1)}, u32[]{:S(2)}, u32[]{:S(2)}) collective-permute-start(f32[8,768]{1,0:T(8,128)S(1)} %shard_map.126.refs_0_), channel_id=1, source_target_pairs={{0,24},{1,25},{2,26},{3,27},{4,28},{5,29},{6,30},{7,31},{8,16},{9,... | collective-permute-start | bytes 73736 | tf_op jit(solution)/shard_map/ppermute | solution.py:362
  96.5 1.5 %collective-permute-done.36.refs_2_ = f32[8,768]{1,0:T(8,128)S(1)} collective-permute-done((f32[8,768]{1,0:T(8,128)S(1)}, f32[8,768]{1,0:T(8,128)S(1)}, u32[]{:S(2)}, u32[]{:S(2)}) %collective-permute-start.36) | collective-permute-done | bytes 24608 | tf_op jit(solution)/shard_map/ppermute | solution.py:362
  98.0 2.6 %collective-permute-done.37.refs_3_ = f32[8,768]{1,0:T(8,128)S(1)} collective-permute-done((f32[8,768]{1,0:T(8,128)S(1)}, f32[8,768]{1,0:T(8,128)S(1)}, u32[]{:S(2)}, u32[]{:S(2)}) %collective-permute-start.37) | collective-permute-done | bytes 24608 | tf_op jit(solution)/shard_map/ppermute | solution.py:362
  100.6 0.9 shard_map.127
  (92 shorter events, 16.7 us)
Async XLA Ops:
  5.2 9.2 %collective-permute-start.22 = (f32[128,512]{1,0:T(8,128)S(1)}, f32[128,512]{1,0:T(8,128)S(1)}, u32[]{:S(2)}, u32[]{:S(2)}) collective-permute-start(f32[128,512]{1,0:T(8,128)S(1)} %get-tuple-element.33), channel_id=1, source_target_pairs={{0,16},{1,17},{2,18},{3,19},{4,21},{5,20},{6,22},{7,23},{8,24},{9,... | collective-permute-start | bytes 786440 | tf_op jit(solution)/shard_map/ppermute | solution.py:362
  8.8 1.4 %collective-permute-start.3 = (f32[8,768]{1,0:T(8,128)}, f32[8,768]{1,0:T(8,128)S(1)}, u32[]{:S(2)}, u32[]{:S(2)}) collective-permute-start(f32[8,768]{1,0:T(8,128)} %shard_map.103.refs_2_), channel_id=1, source_target_pairs={{0,16},{1,31},{2,18},{3,19},{4,20},{5,21},{6,22},{7,23},{8,24},{9,... | collective-permute-start | bytes 73736 | tf_op jit(solution)/shard_map/ppermute | solution.py:362
  8.8 2.0 %collective-permute-start = (f32[8,768]{1,0:T(8,128)}, f32[8,768]{1,0:T(8,128)S(1)}, u32[]{:S(2)}, u32[]{:S(2)}) collective-permute-start(f32[8,768]{1,0:T(8,128)} %shard_map.103.refs_2_), channel_id=1, source_target_pairs={{0,16},{1,31},{2,18},{3,19},{4,20},{5,21},{6,22},{7,23},{8,24},{9,... | collective-permute-start | bytes 73736 | tf_op jit(solution)/shard_map/ppermute | solution.py:362
  9.3 1.5 %collective-permute-start.1 = (f32[8,768]{1,0:T(8,128)}, f32[8,768]{1,0:T(8,128)S(1)}, u32[]{:S(2)}, u32[]{:S(2)}) collective-permute-start(f32[8,768]{1,0:T(8,128)} %shard_map.103.refs_2_), channel_id=1, source_target_pairs={{0,16},{1,31},{2,18},{3,19},{4,20},{5,21},{6,22},{7,23},{8,24},{9,... | collective-permute-start | bytes 73736 | tf_op jit(solution)/shard_map/ppermute | solution.py:362
  11.2 1.5 %collective-permute-start.2 = (f32[8,768]{1,0:T(8,128)S(1)}, f32[8,768]{1,0:T(8,128)S(1)}, u32[]{:S(2)}, u32[]{:S(2)}) collective-permute-start(f32[8,768]{1,0:T(8,128)S(1)} %shard_map.105), channel_id=1, source_target_pairs={{0,16},{1,29},{2,28},{3,19},{4,20},{5,21},{6,22},{7,23},{8,18},{9,... | collective-permute-start | bytes 73736 | tf_op jit(solution)/shard_map/ppermute | solution.py:362
  14.3 57.1 %collective-permute-start.24 = (f32[256,256]{1,0:T(8,128)S(1)}, f32[256,256]{1,0:T(8,128)S(1)}, u32[]{:S(2)}, u32[]{:S(2)}) collective-permute-start(f32[256,256]{1,0:T(8,128)S(1)} %get-tuple-element.34), channel_id=1, source_target_pairs={{0,16},{1,17},{2,18},{3,19},{4,21},{5,20},{6,22},{7,23},{8,24},{9,... | collective-permute-start | bytes 786440 | tf_op jit(solution)/shard_map/ppermute | solution.py:362
  14.5 56.9 %collective-permute-start.23 = (f32[128,512]{1,0:T(8,128)S(1)}, f32[128,512]{1,0:T(8,128)S(1)}, u32[]{:S(2)}, u32[]{:S(2)}) collective-permute-start(f32[128,512]{1,0:T(8,128)S(1)} %collective-permute-done.22.mine_ref), channel_id=1, source_target_pairs={{0,16},{1,17},{2,18},{3,19},{4,20},{5,21},{6,22},{7,23},{8,24},{9,... | collective-permute-start | bytes 786440 | tf_op jit(solution)/shard_map/ppermute | solution.py:362
  17.1 23.0 %collective-permute-start.9 = (f32[8,768]{1,0:T(8,128)S(1)}, f32[8,768]{1,0:T(8,128)S(1)}, u32[]{:S(2)}, u32[]{:S(2)}) collective-permute-start(f32[8,768]{1,0:T(8,128)S(1)} %shard_map.111), channel_id=1, source_target_pairs={{0,17},{1,20},{2,18},{3,19},{4,16},{5,21},{6,22},{7,23},{8,24},{9,... | collective-permute-start | bytes 73736 | tf_op jit(solution)/shard_map/ppermute | solution.py:362
  40.4 6.0 %collective-permute-start.10 = (f32[8,768]{1,0:T(8,128)S(1)}, f32[8,768]{1,0:T(8,128)S(1)}, u32[]{:S(2)}, u32[]{:S(2)}) collective-permute-start(f32[8,768]{1,0:T(8,128)S(1)} %shard_map.112.refs_0_), channel_id=1, source_target_pairs={{0,20},{1,21},{2,22},{3,23},{4,16},{5,17},{6,18},{7,19},{8,28},{9,... | collective-permute-start | bytes 73736 | tf_op jit(solution)/shard_map/ppermute | solution.py:362
  42.4 4.1 %collective-permute-start.11 = (f32[8,768]{1,0:T(8,128)S(1)}, f32[8,768]{1,0:T(8,128)S(1)}, u32[]{:S(2)}, u32[]{:S(2)}) collective-permute-start(f32[8,768]{1,0:T(8,128)S(1)} %shard_map.112.refs_0_), channel_id=1, source_target_pairs={{0,24},{1,25},{2,26},{3,27},{4,28},{5,29},{6,30},{7,31},{8,16},{9,... | collective-permute-start | bytes 73736 | tf_op jit(solution)/shard_map/ppermute | solution.py:362
  42.4 4.2 %collective-permute-start.12 = (f32[8,768]{1,0:T(8,128)S(1)}, f32[8,768]{1,0:T(8,128)S(1)}, u32[]{:S(2)}, u32[]{:S(2)}) collective-permute-start(f32[8,768]{1,0:T(8,128)S(1)} %shard_map.112.refs_0_), channel_id=1, source_target_pairs={{0,28},{1,29},{2,30},{3,31},{4,24},{5,25},{6,26},{7,27},{8,20},{9,... | collective-permute-start | bytes 73736 | tf_op jit(solution)/shard_map/ppermute | solution.py:362
  47.5 4.4 %collective-permute-start.13 = (f32[8,2048]{1,0:T(8,128)S(1)}, f32[8,2048]{1,0:T(8,128)S(1)}, u32[]{:S(2)}, u32[]{:S(2)}) collective-permute-start(f32[8,2048]{1,0:T(8,128)S(1)} %get-tuple-element.26.refs_0_), channel_id=1, source_target_pairs={{0,1},{1,0},{2,3},{3,2},{4,5},{5,4},{6,7},{7,6},{8,9},{9,8},{10,11... | collective-permute-start | bytes 196616 | tf_op jit(solution)/shard_map/ppermute | solution.py:362
  48.9 8.0 %collective-permute-start.14 = (f32[8,2048]{1,0:T(8,128)S(1)}, f32[8,2048]{1,0:T(8,128)S(1)}, u32[]{:S(2)}, u32[]{:S(2)}) collective-permute-start(f32[8,2048]{1,0:T(8,128)S(1)} %get-tuple-element.26.refs_0_), channel_id=1, source_target_pairs={{0,2},{1,3},{2,0},{3,1},{4,6},{5,7},{6,4},{7,5},{8,10},{9,11},{10,... | collective-permute-start | bytes 196616 | tf_op jit(solution)/shard_map/ppermute | solution.py:362
  48.9 8.0 %collective-permute-start.15 = (f32[8,2048]{1,0:T(8,128)S(1)}, f32[8,2048]{1,0:T(8,128)S(1)}, u32[]{:S(2)}, u32[]{:S(2)}) collective-permute-start(f32[8,2048]{1,0:T(8,128)S(1)} %get-tuple-element.26.refs_0_), channel_id=1, source_target_pairs={{0,3},{1,2},{2,1},{3,0},{4,7},{5,6},{6,5},{7,4},{8,11},{9,10},{10,... | collective-permute-start | bytes 196616 | tf_op jit(solution)/shard_map/ppermute | solution.py:362
  58.7 1.2 %collective-permute-start.16 = (f32[8,768]{1,0:T(8,128)S(1)}, f32[8,768]{1,0:T(8,128)S(1)}, u32[]{:S(2)}, u32[]{:S(2)}) collective-permute-start(f32[8,768]{1,0:T(8,128)S(1)} %shard_map.115), channel_id=1, source_target_pairs={{0,16},{1,17},{2,18},{3,19},{4,20},{5,21},{6,22},{7,23},{8,24},{9,... | collective-permute-start | bytes 73736 | tf_op jit(solution)/shard_map/ppermute | solution.py:362
  59.9 3.5 %collective-permute-start.17 = (f32[8,768]{1,0:T(8,128)S(1)}, f32[8,768]{1,0:T(8,128)S(1)}, u32[]{:S(2)}, u32[]{:S(2)}) collective-permute-start(f32[8,768]{1,0:T(8,128)S(1)} %add.3.refs_0_), channel_id=1, source_target_pairs={{0,20},{1,21},{2,22},{3,23},{4,16},{5,17},{6,18},{7,19},{8,28},{9,... | collective-permute-start | bytes 73736 | tf_op jit(solution)/shard_map/ppermute | solution.py:362
  60.8 3.3 %collective-permute-start.18 = (f32[8,768]{1,0:T(8,128)S(1)}, f32[8,768]{1,0:T(8,128)S(1)}, u32[]{:S(2)}, u32[]{:S(2)}) collective-permute-start(f32[8,768]{1,0:T(8,128)S(1)} %add.3.refs_0_), channel_id=1, source_target_pairs={{0,24},{1,25},{2,26},{3,27},{4,28},{5,29},{6,30},{7,31},{8,16},{9,... | collective-permute-start | bytes 73736 | tf_op jit(solution)/shard_map/ppermute | solution.py:362
  61.7 4.2 %collective-permute-start.19 = (f32[8,768]{1,0:T(8,128)S(1)}, f32[8,768]{1,0:T(8,128)S(1)}, u32[]{:S(2)}, u32[]{:S(2)}) collective-permute-start(f32[8,768]{1,0:T(8,128)S(1)} %add.3.refs_0_), channel_id=1, source_target_pairs={{0,28},{1,29},{2,30},{3,31},{4,24},{5,25},{6,26},{7,27},{8,20},{9,... | collective-permute-start | bytes 73736 | tf_op jit(solution)/shard_map/ppermute | solution.py:362
  66.1 3.3 %collective-permute-start.25 = (f32[8,768]{1,0:T(8,128)S(1)}, f32[8,768]{1,0:T(8,128)S(1)}, u32[]{:S(2)}, u32[]{:S(2)}) collective-permute-start(f32[8,768]{1,0:T(8,128)S(1)} %get-tuple-element.29.refs_0_), channel_id=1, source_target_pairs={{0,24},{1,16},{2,18},{3,19},{4,20},{5,21},{6,22},{7,23},{8,17},{9,... | collective-permute-start | bytes 73736 | tf_op jit(solution)/shard_map/ppermute | solution.py:362
  67.0 3.4 %collective-permute-start.26 = (f32[8,768]{1,0:T(8,128)S(1)}, f32[8,768]{1,0:T(8,128)S(1)}, u32[]{:S(2)}, u32[]{:S(2)}) collective-permute-start(f32[8,768]{1,0:T(8,128)S(1)} %get-tuple-element.29.refs_0_), channel_id=1, source_target_pairs={{0,28},{1,16},{2,18},{3,19},{4,20},{5,21},{6,22},{7,23},{8,24},{9,... | collective-permute-start | bytes 73736 | tf_op jit(solution)/shard_map/ppermute | solution.py:362
  67.7 4.2 %collective-permute-start.20 = (f32[8,768]{1,0:T(8,128)S(1)}, f32[8,768]{1,0:T(8,128)S(1)}, u32[]{:S(2)}, u32[]{:S(2)}) collective-permute-start(f32[8,768]{1,0:T(8,128)S(1)} %get-tuple-element.29.refs_0_), channel_id=1, source_target_pairs={{0,20},{1,16},{2,18},{3,19},{4,17},{5,21},{6,22},{7,23},{8,24},{9,... | collective-permute-start | bytes 73736 | tf_op jit(solution)/shard_map/ppermute | solution.py:362
  69.4 2.5 %collective-permute-start.21 = (f32[8,768]{1,0:T(8,128)S(1)}, f32[8,768]{1,0:T(8,128)S(1)}, u32[]{:S(2)}, u32[]{:S(2)}) collective-permute-start(f32[8,768]{1,0:T(8,128)S(1)} %get-tuple-element.30), channel_id=1, source_target_pairs={{0,16},{1,21},{2,26},{3,31},{4,17},{5,20},{6,22},{7,23},{8,24},{9,... | collective-permute-start | bytes 73736 | tf_op jit(solution)/shard_map/ppermute | solution.py:362
  70.8 2.3 %collective-permute-start.27 = (f32[8,768]{1,0:T(8,128)S(1)}, f32[8,768]{1,0:T(8,128)S(1)}, u32[]{:S(2)}, u32[]{:S(2)}) collective-permute-start(f32[8,768]{1,0:T(8,128)S(1)} %shard_map.121), channel_id=1, source_target_pairs={{0,16},{1,24},{2,28},{3,19},{4,20},{5,21},{6,22},{7,23},{8,25},{9,... | collective-permute-start | bytes 73736 | tf_op jit(solution)/shard_map/ppermute | solution.py:362
  72.6 1.8 %collective-permute-start.28 = (f32[8,768]{1,0:T(8,128)S(1)}, f32[8,768]{1,0:T(8,128)S(1)}, u32[]{:S(2)}, u32[]{:S(2)}) collective-permute-start(f32[8,768]{1,0:T(8,128)S(1)} %shard_map.120.refs_1_), channel_id=1, source_target_pairs={{0,16},{1,20},{2,18},{3,19},{4,25},{5,21},{6,22},{7,23},{8,24},{9,... | collective-permute-start | bytes 73736 | tf_op jit(solution)/shard_map/ppermute | solution.py:362
  74.2 1.2 %collective-permute-start.30 = (f32[8,768]{1,0:T(8,128)S(1)}, f32[8,768]{1,0:T(8,128)S(1)}, u32[]{:S(2)}, u32[]{:S(2)}) collective-permute-start(f32[8,768]{1,0:T(8,128)S(1)} %shard_map.123), channel_id=1, source_target_pairs={{0,16},{1,29},{2,18},{3,19},{4,20},{5,21},{6,22},{7,23},{8,24},{9,... | collective-permute-start | bytes 73736 | tf_op jit(solution)/shard_map/ppermute | solution.py:362
  75.0 1.2 %collective-permute-start.31 = (f32[8,768]{1,0:T(8,128)S(1)}, f32[8,768]{1,0:T(8,128)S(1)}, u32[]{:S(2)}, u32[]{:S(2)}) collective-permute-start(f32[8,768]{1,0:T(8,128)S(1)} %shard_map.122.refs_2_), channel_id=1, source_target_pairs={{0,16},{1,25},{2,18},{3,19},{4,20},{5,21},{6,22},{7,23},{8,24},{9,... | collective-permute-start | bytes 73736 | tf_op jit(solution)/shard_map/ppermute | solution.py:362
  77.0 13.5 %collective-permute-start.32 = (f32[8,768]{1,0:T(8,128)S(1)}, f32[8,768]{1,0:T(8,128)S(1)}, u32[]{:S(2)}, u32[]{:S(2)}) collective-permute-start(f32[8,768]{1,0:T(8,128)S(1)} %shard_map.125.refs_0_), channel_id=1, source_target_pairs={{0,17},{1,16},{2,19},{3,18},{4,21},{5,20},{6,23},{7,22},{8,25},{9,... | collective-permute-start | bytes 73736 | tf_op jit(solution)/shard_map/ppermute | solution.py:362
  88.0 4.5 %collective-permute-start.33 = (f32[8,768]{1,0:T(8,128)S(1)}, f32[8,768]{1,0:T(8,128)S(1)}, u32[]{:S(2)}, u32[]{:S(2)}) collective-permute-start(f32[8,768]{1,0:T(8,128)S(1)} %shard_map.125.refs_0_), channel_id=1, source_target_pairs={{0,18},{1,19},{2,16},{3,17},{4,22},{5,23},{6,20},{7,21},{8,26},{9,... | collective-permute-start | bytes 73736 | tf_op jit(solution)/shard_map/ppermute | solution.py:362
  88.0 5.1 %collective-permute-start.34 = (f32[8,768]{1,0:T(8,128)S(1)}, f32[8,768]{1,0:T(8,128)S(1)}, u32[]{:S(2)}, u32[]{:S(2)}) collective-permute-start(f32[8,768]{1,0:T(8,128)S(1)} %shard_map.125.refs_0_), channel_id=1, source_target_pairs={{0,19},{1,18},{2,17},{3,16},{4,23},{5,22},{6,21},{7,20},{8,27},{9,... | collective-permute-start | bytes 73736 | tf_op jit(solution)/shard_map/ppermute | solution.py:362
  93.1 3.3 %collective-permute-start.35 = (f32[8,768]{1,0:T(8,128)S(1)}, f32[8,768]{1,0:T(8,128)S(1)}, u32[]{:S(2)}, u32[]{:S(2)}) collective-permute-start(f32[8,768]{1,0:T(8,128)S(1)} %shard_map.126.refs_0_), channel_id=1, source_target_pairs={{0,20},{1,21},{2,22},{3,23},{4,16},{5,17},{6,18},{7,19},{8,28},{9,... | collective-permute-start | bytes 73736 | tf_op jit(solution)/shard_map/ppermute | solution.py:362
  93.2 4.8 %collective-permute-start.36 = (f32[8,768]{1,0:T(8,128)S(1)}, f32[8,768]{1,0:T(8,128)S(1)}, u32[]{:S(2)}, u32[]{:S(2)}) collective-permute-start(f32[8,768]{1,0:T(8,128)S(1)} %shard_map.126.refs_0_), channel_id=1, source_target_pairs={{0,24},{1,25},{2,26},{3,27},{4,28},{5,29},{6,30},{7,31},{8,16},{9,... | collective-permute-start | bytes 73736 | tf_op jit(solution)/shard_map/ppermute | solution.py:362
  96.5 4.2 %collective-permute-start.37 = (f32[8,768]{1,0:T(8,128)S(1)}, f32[8,768]{1,0:T(8,128)S(1)}, u32[]{:S(2)}, u32[]{:S(2)}) collective-permute-start(f32[8,768]{1,0:T(8,128)S(1)} %shard_map.126.refs_0_), channel_id=1, source_target_pairs={{0,28},{1,29},{2,30},{3,31},{4,24},{5,25},{6,26},{7,27},{8,20},{9,... | collective-permute-start | bytes 73736 | tf_op jit(solution)/shard_map/ppermute | solution.py:362
  (17 other events, 172.3 us)

commit v4 on v3

--- a/solution.py
+++ b/solution.py
@@ -1,4 +1,5 @@
 import functools
+import itertools
 import math
 
 import jax
@@ -361,14 +362,15 @@
         ]
         return lax.ppermute(value, ("dp", "crow", "ccol"), perm)
 
-    idle = [(r, c) for r in range(crow) for c in range(r + 1, ccol)]
+    idle = itertools.cycle([(r, c) for r in range(crow) for c in range(r + 1, ccol)])
 
     def move(value, *pairs, direct=False):
         to = dict(pairs)
-        for (a, b), spare in zip(pairs, idle):
+        for a, b in pairs:
             if direct:
                 to[b] = a
             else:
+                spare = next(idle)
                 to[b], to[spare] = spare, a
         return permute(value, lambda d, r, c: (d ^ 1, *to.get((r, c), (r, c))))
 

time: 102 us -> 97.3 us (0.954)
  starting transfers between devices: 56.1 us -> 46.1 us
  waiting for transfers between devices: 23.1 us -> 28.8 us
    ppermute x38, starting transfers between devices: 56.1 us -> 46.1 us  [permute(): return lax.ppermute(value, ('dp', 'crow', 'ccol'), perm)]
    ppermute x38, waiting for transfers between devices: 23.1 us -> 28.8 us  [permute(): return lax.ppermute(value, ('dp', 'crow', 'ccol'), perm)]
  transfers between devices with their start and end apart: 38 -> 38, of which waited for: 19 -> 21; matrix products, arithmetic and copies ran while one was open for 0% -> 0% of each run, Pallas kernels for 15% -> 16%
where the time goes in v4:
time: 97.3 us; the launch traced here: 97.1 us
  starting transfers between devices  46.1 us (47%)
  waiting for transfers between devices  28.8 us (30%)
  Pallas kernels  18.7 us (19%)
  local copies, waits for them, and re-layouts  2.84 us (3%)
    ppermute x38, starting transfers between devices, permute(): return lax.ppermute(value, ('dp', 'crow', 'ccol'), perm)  46.1 us
    ppermute x38, waiting for transfers between devices, permute(): return lax.ppermute(value, ('dp', 'crow', 'ccol'), perm)  28.8 us
    pallas_call x25, Pallas kernels, call(): pl.pallas_call(kernel, out_shape=outs, compiler_params=pltpu.CompilerPara...  18.7 us
    unnamed x22, local copies, waits for them, and re-layouts  2.84 us
  transfers between devices with their start and end apart: 38, of which 21 were waited for; matrix products, arithmetic and copies ran while one was open for 0% of the time, Pallas kernels for 16%

profile of v4, /device:TPU:0, one launch (start us, length us, event | category | flops | bytes accessed | tf_op | source)
XLA Modules:
  0.0 97.1 jit_solution(13303866451396433787)
XLA Ops:
  0.6 1.7 %copy-done = f32[768,768]{1,0:T(8,128)S(1)} copy-done((f32[768,768]{1,0:T(8,128)S(1)}, f32[768,768]{1,0:T(8,128)}, u32[]{:S(2)}) %copy-start) | copy-done | bytes 2359320
  2.3 1.1 %copy-done.2 = f32[3,256,256]{2,1,0:T(8,128)S(1)} copy-done((f32[3,256,256]{2,1,0:T(8,128)S(1)}, f32[3,256,256]{2,1,0:T(8,128)}, u32[]{:S(2)}) %copy-start.2) | copy-done | bytes 786456
  3.4 1.8 %shard_map.107 = (f32[256,768]{1,0:T(8,128)S(1)}, f32[128,512]{1,0:T(8,128)S(1)}, f32[256,256]{1,0:T(8,128)S(1)}) custom-call(f32[3,256,256]{2,1,0:T(8,128)S(1)} %copy-done.2, f32[768,768]{1,0:T(8,128)S(1)} %copy-done, f32[768,768]{1,0:T(8,128)S(1)} %copy-done, f32[768,768]{1,0:T(8,128)S(1)} %copy-done), custom_call_target="tpu_custom_call" | custom-call | flops 1000000 | bytes 1000000 | tf_op jit(solution)/shard_map/pallas_call | solution.py:335
  5.8 3.0 %shard_map.103.refs_2_ = f32[8,768]{1,0:T(8,128)} custom-call(f32[8,3072]{1,0:T(8,128)} %direction_ref.9, f32[3,256,256]{2,1,0:T(8,128)} %inv_ref.13, f32[768,768]{1,0:T(8,128)} %factor_ref.3, f32[768,768]{1,0:T(8,128)} %factor_ref.3, f32[768,768]{1,0:T(8,128)} %factor_ref.3), custom_call_target="tpu_custom_call" | custom-call | flops 1000000 | bytes 1000000 | tf_op jit(solution)/shard_map/pallas_call | solution.py:335
  15.8 0.8 collective-permute-done.8.refs_1_
  17.1 13.0 %collective-permute-start.9 = (f32[8,768]{1,0:T(8,128)S(1)}, f32[8,768]{1,0:T(8,128)S(1)}, u32[]{:S(2)}, u32[]{:S(2)}) collective-permute-start(f32[8,768]{1,0:T(8,128)S(1)} %shard_map.111), channel_id=1, source_target_pairs={{0,27},{1,17},{2,18},{3,19},{4,16},{5,21},{6,22},{7,23},{8,24},{9,... | collective-permute-start | bytes 73736 | tf_op jit(solution)/shard_map/ppermute | solution.py:363
  30.1 6.1 %collective-permute-done.9.sub_ref = f32[8,768]{1,0:T(8,128)S(1)} collective-permute-done((f32[8,768]{1,0:T(8,128)S(1)}, f32[8,768]{1,0:T(8,128)S(1)}, u32[]{:S(2)}, u32[]{:S(2)}) %collective-permute-start.9) | collective-permute-done | bytes 24608 | tf_op jit(solution)/shard_map/ppermute | solution.py:363
  36.6 5.3 %collective-permute-start.10 = (f32[8,768]{1,0:T(8,128)S(1)}, f32[8,768]{1,0:T(8,128)S(1)}, u32[]{:S(2)}, u32[]{:S(2)}) collective-permute-start(f32[8,768]{1,0:T(8,128)S(1)} %shard_map.112.refs_0_), channel_id=1, source_target_pairs={{0,20},{1,21},{2,22},{3,23},{4,16},{5,17},{6,18},{7,19},{8,28},{9,... | collective-permute-start | bytes 73736 | tf_op jit(solution)/shard_map/ppermute | solution.py:363
  41.9 1.5 %collective-permute-start.12 = (f32[8,768]{1,0:T(8,128)S(1)}, f32[8,768]{1,0:T(8,128)S(1)}, u32[]{:S(2)}, u32[]{:S(2)}) collective-permute-start(f32[8,768]{1,0:T(8,128)S(1)} %shard_map.112.refs_0_), channel_id=1, source_target_pairs={{0,28},{1,29},{2,30},{3,31},{4,24},{5,25},{6,26},{7,27},{8,20},{9,... | collective-permute-start | bytes 73736 | tf_op jit(solution)/shard_map/ppermute | solution.py:363
  43.4 2.5 %shard_map.113 = (bf16[768,2048]{1,0:T(8,128)(2,1)S(1)}, bf16[768,2048]{1,0:T(8,128)(2,1)S(1)}) custom-call(f32[16]{0:T(128)S(1)} %copy-done.10, f32[16,768]{1,0:T(8,128)S(1)} %copy-done.9, f32[16,2048]{1,0:T(8,128)S(1)} %copy-done.5), custom_call_target="tpu_custom_call" | custom-call | flops 1000000 | bytes 1000000 | tf_op jit(solution)/shard_map/pallas_call | solution.py:335
  46.1 0.9 shard_map.114
  47.1 4.3 %collective-permute-start.15 = (f32[8,2048]{1,0:T(8,128)S(1)}, f32[8,2048]{1,0:T(8,128)S(1)}, u32[]{:S(2)}, u32[]{:S(2)}) collective-permute-start(f32[8,2048]{1,0:T(8,128)S(1)} %get-tuple-element.26.refs_0_), channel_id=1, source_target_pairs={{0,3},{1,2},{2,1},{3,0},{4,7},{5,6},{6,5},{7,4},{8,11},{9,10},{10,... | collective-permute-start | bytes 196616 | tf_op jit(solution)/shard_map/ppermute | solution.py:363
  51.4 1.0 collective-permute-done.13.refs_1_
  52.4 3.3 %collective-permute-done.14.refs_2_ = f32[8,2048]{1,0:T(8,128)S(1)} collective-permute-done((f32[8,2048]{1,0:T(8,128)S(1)}, f32[8,2048]{1,0:T(8,128)S(1)}, u32[]{:S(2)}, u32[]{:S(2)}) %collective-permute-start.14) | collective-permute-done | bytes 65568 | tf_op jit(solution)/shard_map/ppermute | solution.py:363
  55.7 1.8 %shard_map.115 = f32[8,768]{1,0:T(8,128)S(1)} custom-call(f32[8,2048]{1,0:T(8,128)S(1)} %get-tuple-element.26.refs_0_, f32[8,2048]{1,0:T(8,128)S(1)} %collective-permute-done.13.refs_1_, f32[8,2048]{1,0:T(8,128)S(1)} %collective-permute-done.14.refs_2_, f32[8,2048]{1,0:T(8,128)S(1)} %collective-permute-done.15.refs_3_, ...), custom_call_target="tpu_custom_call" | custom-call | flops 1000000 | bytes 1000000 | tf_op jit(solution)/shard_map/pallas_call | solution.py:335
  57.6 1.2 %collective-permute-done.16 = f32[8,768]{1,0:T(8,128)S(1)} collective-permute-done((f32[8,768]{1,0:T(8,128)S(1)}, f32[8,768]{1,0:T(8,128)S(1)}, u32[]{:S(2)}, u32[]{:S(2)}) %collective-permute-start.16) | collective-permute-done | bytes 24608 | tf_op jit(solution)/shard_map/ppermute | solution.py:363
  58.8 1.4 %collective-permute-start.17 = (f32[8,768]{1,0:T(8,128)S(1)}, f32[8,768]{1,0:T(8,128)S(1)}, u32[]{:S(2)}, u32[]{:S(2)}) collective-permute-start(f32[8,768]{1,0:T(8,128)S(1)} %add.3.refs_0_), channel_id=1, source_target_pairs={{0,20},{1,21},{2,22},{3,23},{4,16},{5,17},{6,18},{7,19},{8,28},{9,... | collective-permute-start | bytes 73736 | tf_op jit(solution)/shard_map/ppermute | solution.py:363
  60.6 1.2 %collective-permute-start.19 = (f32[8,768]{1,0:T(8,128)S(1)}, f32[8,768]{1,0:T(8,128)S(1)}, u32[]{:S(2)}, u32[]{:S(2)}) collective-permute-start(f32[8,768]{1,0:T(8,128)S(1)} %add.3.refs_0_), channel_id=1, source_target_pairs={{0,28},{1,29},{2,30},{3,31},{4,24},{5,25},{6,26},{7,27},{8,20},{9,... | collective-permute-start | bytes 73736 | tf_op jit(solution)/shard_map/ppermute | solution.py:363
  62.3 1.1 %collective-permute-done.18.refs_2_ = f32[8,768]{1,0:T(8,128)S(1)} collective-permute-done((f32[8,768]{1,0:T(8,128)S(1)}, f32[8,768]{1,0:T(8,128)S(1)}, u32[]{:S(2)}, u32[]{:S(2)}) %collective-permute-start.18) | collective-permute-done | bytes 24608 | tf_op jit(solution)/shard_map/ppermute | solution.py:363
  63.4 1.3 %collective-permute-done.19.refs_3_ = f32[8,768]{1,0:T(8,128)S(1)} collective-permute-done((f32[8,768]{1,0:T(8,128)S(1)}, f32[8,768]{1,0:T(8,128)S(1)}, u32[]{:S(2)}, u32[]{:S(2)}) %collective-permute-start.19) | collective-permute-done | bytes 24608 | tf_op jit(solution)/shard_map/ppermute | solution.py:363
  65.1 1.3 %collective-permute-start.25 = (f32[8,768]{1,0:T(8,128)S(1)}, f32[8,768]{1,0:T(8,128)S(1)}, u32[]{:S(2)}, u32[]{:S(2)}) collective-permute-start(f32[8,768]{1,0:T(8,128)S(1)} %get-tuple-element.29.refs_0_), channel_id=1, source_target_pairs={{0,24},{1,17},{2,18},{3,19},{4,20},{5,21},{6,22},{7,16},{8,23},{9,... | collective-permute-start | bytes 73736 | tf_op jit(solution)/shard_map/ppermute | solution.py:363
  67.2 4.0 %collective-permute-done.25.refs_0_ = f32[8,768]{1,0:T(8,128)S(1)} collective-permute-done((f32[8,768]{1,0:T(8,128)S(1)}, f32[8,768]{1,0:T(8,128)S(1)}, u32[]{:S(2)}, u32[]{:S(2)}) %collective-permute-start.25) | collective-permute-done | bytes 24608 | tf_op jit(solution)/shard_map/ppermute | solution.py:363
  77.2 0.8 collective-permute-done.31.refs_1_
  78.7 1.4 %collective-permute-start.32 = (f32[8,768]{1,0:T(8,128)S(1)}, f32[8,768]{1,0:T(8,128)S(1)}, u32[]{:S(2)}, u32[]{:S(2)}) collective-permute-start(f32[8,768]{1,0:T(8,128)S(1)} %shard_map.125.refs_0_), channel_id=1, source_target_pairs={{0,17},{1,16},{2,19},{3,18},{4,21},{5,20},{6,23},{7,22},{8,25},{9,... | collective-permute-start | bytes 73736 | tf_op jit(solution)/shard_map/ppermute | solution.py:363
  80.6 2.2 %collective-permute-start.34 = (f32[8,768]{1,0:T(8,128)S(1)}, f32[8,768]{1,0:T(8,128)S(1)}, u32[]{:S(2)}, u32[]{:S(2)}) collective-permute-start(f32[8,768]{1,0:T(8,128)S(1)} %shard_map.125.refs_0_), channel_id=1, source_target_pairs={{0,19},{1,18},{2,17},{3,16},{4,23},{5,22},{6,21},{7,20},{8,27},{9,... | collective-permute-start | bytes 73736 | tf_op jit(solution)/shard_map/ppermute | solution.py:363
  82.8 2.1 %collective-permute-done.33.refs_2_ = f32[8,768]{1,0:T(8,128)S(1)} collective-permute-done((f32[8,768]{1,0:T(8,128)S(1)}, f32[8,768]{1,0:T(8,128)S(1)}, u32[]{:S(2)}, u32[]{:S(2)}) %collective-permute-start.33) | collective-permute-done | bytes 24608 | tf_op jit(solution)/shard_map/ppermute | solution.py:363
  84.9 0.8 collective-permute-done.34.refs_3_
  85.8 5.5 %collective-permute-start.35 = (f32[8,768]{1,0:T(8,128)S(1)}, f32[8,768]{1,0:T(8,128)S(1)}, u32[]{:S(2)}, u32[]{:S(2)}) collective-permute-start(f32[8,768]{1,0:T(8,128)S(1)} %shard_map.126.refs_0_), channel_id=1, source_target_pairs={{0,20},{1,21},{2,22},{3,23},{4,16},{5,17},{6,18},{7,19},{8,28},{9,... | collective-permute-start | bytes 73736 | tf_op jit(solution)/shard_map/ppermute | solution.py:363
  92.1 1.2 %collective-permute-start.37 = (f32[8,768]{1,0:T(8,128)S(1)}, f32[8,768]{1,0:T(8,128)S(1)}, u32[]{:S(2)}, u32[]{:S(2)}) collective-permute-start(f32[8,768]{1,0:T(8,128)S(1)} %shard_map.126.refs_0_), channel_id=1, source_target_pairs={{0,28},{1,29},{2,30},{3,31},{4,24},{5,25},{6,26},{7,27},{8,20},{9,... | collective-permute-start | bytes 73736 | tf_op jit(solution)/shard_map/ppermute | solution.py:363
  93.3 1.2 %collective-permute-done.36.refs_2_ = f32[8,768]{1,0:T(8,128)S(1)} collective-permute-done((f32[8,768]{1,0:T(8,128)S(1)}, f32[8,768]{1,0:T(8,128)S(1)}, u32[]{:S(2)}, u32[]{:S(2)}) %collective-permute-start.36) | collective-permute-done | bytes 24608 | tf_op jit(solution)/shard_map/ppermute | solution.py:363
  94.5 1.7 %collective-permute-done.37.refs_3_ = f32[8,768]{1,0:T(8,128)S(1)} collective-permute-done((f32[8,768]{1,0:T(8,128)S(1)}, f32[8,768]{1,0:T(8,128)S(1)}, u32[]{:S(2)}, u32[]{:S(2)}) %collective-permute-start.37) | collective-permute-done | bytes 24608 | tf_op jit(solution)/shard_map/ppermute | solution.py:363
  96.2 0.9 shard_map.127
  (92 shorter events, 18.6 us)
Async XLA Ops:
  5.2 9.2 %collective-permute-start.22 = (f32[128,512]{1,0:T(8,128)S(1)}, f32[128,512]{1,0:T(8,128)S(1)}, u32[]{:S(2)}, u32[]{:S(2)}) collective-permute-start(f32[128,512]{1,0:T(8,128)S(1)} %get-tuple-element.33), channel_id=1, source_target_pairs={{0,16},{1,17},{2,18},{3,19},{4,21},{5,20},{6,22},{7,23},{8,24},{9,... | collective-permute-start | bytes 786440 | tf_op jit(solution)/shard_map/ppermute | solution.py:363
  8.8 1.4 %collective-permute-start.3 = (f32[8,768]{1,0:T(8,128)}, f32[8,768]{1,0:T(8,128)S(1)}, u32[]{:S(2)}, u32[]{:S(2)}) collective-permute-start(f32[8,768]{1,0:T(8,128)} %shard_map.103.refs_2_), channel_id=1, source_target_pairs={{0,16},{1,31},{2,18},{3,19},{4,20},{5,21},{6,22},{7,23},{8,24},{9,... | collective-permute-start | bytes 73736 | tf_op jit(solution)/shard_map/ppermute | solution.py:363
  8.8 2.0 %collective-permute-start = (f32[8,768]{1,0:T(8,128)}, f32[8,768]{1,0:T(8,128)S(1)}, u32[]{:S(2)}, u32[]{:S(2)}) collective-permute-start(f32[8,768]{1,0:T(8,128)} %shard_map.103.refs_2_), channel_id=1, source_target_pairs={{0,16},{1,17},{2,31},{3,19},{4,20},{5,21},{6,22},{7,23},{8,24},{9,... | collective-permute-start | bytes 73736 | tf_op jit(solution)/shard_map/ppermute | solution.py:363
  9.3 1.5 %collective-permute-start.1 = (f32[8,768]{1,0:T(8,128)}, f32[8,768]{1,0:T(8,128)S(1)}, u32[]{:S(2)}, u32[]{:S(2)}) collective-permute-start(f32[8,768]{1,0:T(8,128)} %shard_map.103.refs_2_), channel_id=1, source_target_pairs={{0,16},{1,17},{2,18},{3,31},{4,20},{5,21},{6,22},{7,23},{8,24},{9,... | collective-permute-start | bytes 73736 | tf_op jit(solution)/shard_map/ppermute | solution.py:363
  11.2 1.5 %collective-permute-start.2 = (f32[8,768]{1,0:T(8,128)S(1)}, f32[8,768]{1,0:T(8,128)S(1)}, u32[]{:S(2)}, u32[]{:S(2)}) collective-permute-start(f32[8,768]{1,0:T(8,128)S(1)} %shard_map.105), channel_id=1, source_target_pairs={{0,16},{1,17},{2,18},{3,19},{4,20},{5,21},{6,22},{7,29},{8,27},{9,... | collective-permute-start | bytes 73736 | tf_op jit(solution)/shard_map/ppermute | solution.py:363
  14.3 58.8 %collective-permute-start.24 = (f32[256,256]{1,0:T(8,128)S(1)}, f32[256,256]{1,0:T(8,128)S(1)}, u32[]{:S(2)}, u32[]{:S(2)}) collective-permute-start(f32[256,256]{1,0:T(8,128)S(1)} %get-tuple-element.34), channel_id=1, source_target_pairs={{0,16},{1,17},{2,18},{3,19},{4,21},{5,20},{6,22},{7,23},{8,24},{9,... | collective-permute-start | bytes 786440 | tf_op jit(solution)/shard_map/ppermute | solution.py:363
  14.5 58.7 %collective-permute-start.23 = (f32[128,512]{1,0:T(8,128)S(1)}, f32[128,512]{1,0:T(8,128)S(1)}, u32[]{:S(2)}, u32[]{:S(2)}) collective-permute-start(f32[128,512]{1,0:T(8,128)S(1)} %collective-permute-done.22.mine_ref), channel_id=1, source_target_pairs={{0,16},{1,17},{2,18},{3,19},{4,20},{5,21},{6,22},{7,23},{8,24},{9,... | collective-permute-start | bytes 786440 | tf_op jit(solution)/shard_map/ppermute | solution.py:363
  17.1 19.1 %collective-permute-start.9 = (f32[8,768]{1,0:T(8,128)S(1)}, f32[8,768]{1,0:T(8,128)S(1)}, u32[]{:S(2)}, u32[]{:S(2)}) collective-permute-start(f32[8,768]{1,0:T(8,128)S(1)} %shard_map.111), channel_id=1, source_target_pairs={{0,27},{1,17},{2,18},{3,19},{4,16},{5,21},{6,22},{7,23},{8,24},{9,... | collective-permute-start | bytes 73736 | tf_op jit(solution)/shard_map/ppermute | solution.py:363
  36.6 9.4 %collective-permute-start.10 = (f32[8,768]{1,0:T(8,128)S(1)}, f32[8,768]{1,0:T(8,128)S(1)}, u32[]{:S(2)}, u32[]{:S(2)}) collective-permute-start(f32[8,768]{1,0:T(8,128)S(1)} %shard_map.112.refs_0_), channel_id=1, source_target_pairs={{0,20},{1,21},{2,22},{3,23},{4,16},{5,17},{6,18},{7,19},{8,28},{9,... | collective-permute-start | bytes 73736 | tf_op jit(solution)/shard_map/ppermute | solution.py:363
  41.9 4.0 %collective-permute-start.11 = (f32[8,768]{1,0:T(8,128)S(1)}, f32[8,768]{1,0:T(8,128)S(1)}, u32[]{:S(2)}, u32[]{:S(2)}) collective-permute-start(f32[8,768]{1,0:T(8,128)S(1)} %shard_map.112.refs_0_), channel_id=1, source_target_pairs={{0,24},{1,25},{2,26},{3,27},{4,28},{5,29},{6,30},{7,31},{8,16},{9,... | collective-permute-start | bytes 73736 | tf_op jit(solution)/shard_map/ppermute | solution.py:363
  41.9 4.2 %collective-permute-start.12 = (f32[8,768]{1,0:T(8,128)S(1)}, f32[8,768]{1,0:T(8,128)S(1)}, u32[]{:S(2)}, u32[]{:S(2)}) collective-permute-start(f32[8,768]{1,0:T(8,128)S(1)} %shard_map.112.refs_0_), channel_id=1, source_target_pairs={{0,28},{1,29},{2,30},{3,31},{4,24},{5,25},{6,26},{7,27},{8,20},{9,... | collective-permute-start | bytes 73736 | tf_op jit(solution)/shard_map/ppermute | solution.py:363
  47.0 5.4 %collective-permute-start.13 = (f32[8,2048]{1,0:T(8,128)S(1)}, f32[8,2048]{1,0:T(8,128)S(1)}, u32[]{:S(2)}, u32[]{:S(2)}) collective-permute-start(f32[8,2048]{1,0:T(8,128)S(1)} %get-tuple-element.26.refs_0_), channel_id=1, source_target_pairs={{0,1},{1,0},{2,3},{3,2},{4,5},{5,4},{6,7},{7,6},{8,9},{9,8},{10,11... | collective-permute-start | bytes 196616 | tf_op jit(solution)/shard_map/ppermute | solution.py:363
  47.0 8.7 %collective-permute-start.14 = (f32[8,2048]{1,0:T(8,128)S(1)}, f32[8,2048]{1,0:T(8,128)S(1)}, u32[]{:S(2)}, u32[]{:S(2)}) collective-permute-start(f32[8,2048]{1,0:T(8,128)S(1)} %get-tuple-element.26.refs_0_), channel_id=1, source_target_pairs={{0,2},{1,3},{2,0},{3,1},{4,6},{5,7},{6,4},{7,5},{8,10},{9,11},{10,... | collective-permute-start | bytes 196616 | tf_op jit(solution)/shard_map/ppermute | solution.py:363
  47.1 8.7 %collective-permute-start.15 = (f32[8,2048]{1,0:T(8,128)S(1)}, f32[8,2048]{1,0:T(8,128)S(1)}, u32[]{:S(2)}, u32[]{:S(2)}) collective-permute-start(f32[8,2048]{1,0:T(8,128)S(1)} %get-tuple-element.26.refs_0_), channel_id=1, source_target_pairs={{0,3},{1,2},{2,1},{3,0},{4,7},{5,6},{6,5},{7,4},{8,11},{9,10},{10,... | collective-permute-start | bytes 196616 | tf_op jit(solution)/shard_map/ppermute | solution.py:363
  57.5 1.2 %collective-permute-start.16 = (f32[8,768]{1,0:T(8,128)S(1)}, f32[8,768]{1,0:T(8,128)S(1)}, u32[]{:S(2)}, u32[]{:S(2)}) collective-permute-start(f32[8,768]{1,0:T(8,128)S(1)} %shard_map.115), channel_id=1, source_target_pairs={{0,16},{1,17},{2,18},{3,19},{4,20},{5,21},{6,22},{7,23},{8,24},{9,... | collective-permute-start | bytes 73736 | tf_op jit(solution)/shard_map/ppermute | solution.py:363
  58.8 3.5 %collective-permute-start.17 = (f32[8,768]{1,0:T(8,128)S(1)}, f32[8,768]{1,0:T(8,128)S(1)}, u32[]{:S(2)}, u32[]{:S(2)}) collective-permute-start(f32[8,768]{1,0:T(8,128)S(1)} %add.3.refs_0_), channel_id=1, source_target_pairs={{0,20},{1,21},{2,22},{3,23},{4,16},{5,17},{6,18},{7,19},{8,28},{9,... | collective-permute-start | bytes 73736 | tf_op jit(solution)/shard_map/ppermute | solution.py:363
  60.2 3.3 %collective-permute-start.18 = (f32[8,768]{1,0:T(8,128)S(1)}, f32[8,768]{1,0:T(8,128)S(1)}, u32[]{:S(2)}, u32[]{:S(2)}) collective-permute-start(f32[8,768]{1,0:T(8,128)S(1)} %add.3.refs_0_), channel_id=1, source_target_pairs={{0,24},{1,25},{2,26},{3,27},{4,28},{5,29},{6,30},{7,31},{8,16},{9,... | collective-permute-start | bytes 73736 | tf_op jit(solution)/shard_map/ppermute | solution.py:363
  60.6 4.2 %collective-permute-start.19 = (f32[8,768]{1,0:T(8,128)S(1)}, f32[8,768]{1,0:T(8,128)S(1)}, u32[]{:S(2)}, u32[]{:S(2)}) collective-permute-start(f32[8,768]{1,0:T(8,128)S(1)} %add.3.refs_0_), channel_id=1, source_target_pairs={{0,28},{1,29},{2,30},{3,31},{4,24},{5,25},{6,26},{7,27},{8,20},{9,... | collective-permute-start | bytes 73736 | tf_op jit(solution)/shard_map/ppermute | solution.py:363
  65.1 6.1 %collective-permute-start.25 = (f32[8,768]{1,0:T(8,128)S(1)}, f32[8,768]{1,0:T(8,128)S(1)}, u32[]{:S(2)}, u32[]{:S(2)}) collective-permute-start(f32[8,768]{1,0:T(8,128)S(1)} %get-tuple-element.29.refs_0_), channel_id=1, source_target_pairs={{0,24},{1,17},{2,18},{3,19},{4,20},{5,21},{6,22},{7,16},{8,23},{9,... | collective-permute-start | bytes 73736 | tf_op jit(solution)/shard_map/ppermute | solution.py:363
  66.4 5.9 %collective-permute-start.26 = (f32[8,768]{1,0:T(8,128)S(1)}, f32[8,768]{1,0:T(8,128)S(1)}, u32[]{:S(2)}, u32[]{:S(2)}) collective-permute-start(f32[8,768]{1,0:T(8,128)S(1)} %get-tuple-element.29.refs_0_), channel_id=1, source_target_pairs={{0,28},{1,17},{2,18},{3,19},{4,20},{5,21},{6,22},{7,23},{8,24},{9,... | collective-permute-start | bytes 73736 | tf_op jit(solution)/shard_map/ppermute | solution.py:363
  66.6 7.0 %collective-permute-start.20 = (f32[8,768]{1,0:T(8,128)S(1)}, f32[8,768]{1,0:T(8,128)S(1)}, u32[]{:S(2)}, u32[]{:S(2)}) collective-permute-start(f32[8,768]{1,0:T(8,128)S(1)} %get-tuple-element.29.refs_0_), channel_id=1, source_target_pairs={{0,20},{1,16},{2,18},{3,19},{4,17},{5,21},{6,22},{7,23},{8,24},{9,... | collective-permute-start | bytes 73736 | tf_op jit(solution)/shard_map/ppermute | solution.py:363
  71.1 2.5 %collective-permute-start.21 = (f32[8,768]{1,0:T(8,128)S(1)}, f32[8,768]{1,0:T(8,128)S(1)}, u32[]{:S(2)}, u32[]{:S(2)}) collective-permute-start(f32[8,768]{1,0:T(8,128)S(1)} %get-tuple-element.30), channel_id=1, source_target_pairs={{0,16},{1,17},{2,21},{3,26},{4,18},{5,20},{6,31},{7,23},{8,24},{9,... | collective-permute-start | bytes 73736 | tf_op jit(solution)/shard_map/ppermute | solution.py:363
  72.8 2.1 %collective-permute-start.27 = (f32[8,768]{1,0:T(8,128)S(1)}, f32[8,768]{1,0:T(8,128)S(1)}, u32[]{:S(2)}, u32[]{:S(2)}) collective-permute-start(f32[8,768]{1,0:T(8,128)S(1)} %shard_map.121), channel_id=1, source_target_pairs={{0,16},{1,17},{2,24},{3,28},{4,20},{5,21},{6,22},{7,23},{8,25},{9,... | collective-permute-start | bytes 73736 | tf_op jit(solution)/shard_map/ppermute | solution.py:363
  74.5 1.6 %collective-permute-start.28 = (f32[8,768]{1,0:T(8,128)S(1)}, f32[8,768]{1,0:T(8,128)S(1)}, u32[]{:S(2)}, u32[]{:S(2)}) collective-permute-start(f32[8,768]{1,0:T(8,128)S(1)} %shard_map.120.refs_1_), channel_id=1, source_target_pairs={{0,16},{1,20},{2,18},{3,19},{4,25},{5,21},{6,22},{7,23},{8,24},{9,... | collective-permute-start | bytes 73736 | tf_op jit(solution)/shard_map/ppermute | solution.py:363
  75.9 1.2 %collective-permute-start.30 = (f32[8,768]{1,0:T(8,128)S(1)}, f32[8,768]{1,0:T(8,128)S(1)}, u32[]{:S(2)}, u32[]{:S(2)}) collective-permute-start(f32[8,768]{1,0:T(8,128)S(1)} %shard_map.123), channel_id=1, source_target_pairs={{0,16},{1,17},{2,18},{3,19},{4,20},{5,21},{6,22},{7,23},{8,24},{9,... | collective-permute-start | bytes 73736 | tf_op jit(solution)/shard_map/ppermute | solution.py:363
  76.8 1.2 %collective-permute-start.31 = (f32[8,768]{1,0:T(8,128)S(1)}, f32[8,768]{1,0:T(8,128)S(1)}, u32[]{:S(2)}, u32[]{:S(2)}) collective-permute-start(f32[8,768]{1,0:T(8,128)S(1)} %shard_map.122.refs_2_), channel_id=1, source_target_pairs={{0,16},{1,17},{2,18},{3,19},{4,20},{5,21},{6,22},{7,25},{8,24},{9,... | collective-permute-start | bytes 73736 | tf_op jit(solution)/shard_map/ppermute | solution.py:363
  78.7 4.1 %collective-permute-start.32 = (f32[8,768]{1,0:T(8,128)S(1)}, f32[8,768]{1,0:T(8,128)S(1)}, u32[]{:S(2)}, u32[]{:S(2)}) collective-permute-start(f32[8,768]{1,0:T(8,128)S(1)} %shard_map.125.refs_0_), channel_id=1, source_target_pairs={{0,17},{1,16},{2,19},{3,18},{4,21},{5,20},{6,23},{7,22},{8,25},{9,... | collective-permute-start | bytes 73736 | tf_op jit(solution)/shard_map/ppermute | solution.py:363
  80.1 4.8 %collective-permute-start.33 = (f32[8,768]{1,0:T(8,128)S(1)}, f32[8,768]{1,0:T(8,128)S(1)}, u32[]{:S(2)}, u32[]{:S(2)}) collective-permute-start(f32[8,768]{1,0:T(8,128)S(1)} %shard_map.125.refs_0_), channel_id=1, source_target_pairs={{0,18},{1,19},{2,16},{3,17},{4,22},{5,23},{6,20},{7,21},{8,26},{9,... | collective-permute-start | bytes 73736 | tf_op jit(solution)/shard_map/ppermute | solution.py:363
  80.6 5.2 %collective-permute-start.34 = (f32[8,768]{1,0:T(8,128)S(1)}, f32[8,768]{1,0:T(8,128)S(1)}, u32[]{:S(2)}, u32[]{:S(2)}) collective-permute-start(f32[8,768]{1,0:T(8,128)S(1)} %shard_map.125.refs_0_), channel_id=1, source_target_pairs={{0,19},{1,18},{2,17},{3,16},{4,23},{5,22},{6,21},{7,20},{8,27},{9,... | collective-permute-start | bytes 73736 | tf_op jit(solution)/shard_map/ppermute | solution.py:363
  85.8 7.5 %collective-permute-start.35 = (f32[8,768]{1,0:T(8,128)S(1)}, f32[8,768]{1,0:T(8,128)S(1)}, u32[]{:S(2)}, u32[]{:S(2)}) collective-permute-start(f32[8,768]{1,0:T(8,128)S(1)} %shard_map.126.refs_0_), channel_id=1, source_target_pairs={{0,20},{1,21},{2,22},{3,23},{4,16},{5,17},{6,18},{7,19},{8,28},{9,... | collective-permute-start | bytes 73736 | tf_op jit(solution)/shard_map/ppermute | solution.py:363
  91.3 3.3 %collective-permute-start.36 = (f32[8,768]{1,0:T(8,128)S(1)}, f32[8,768]{1,0:T(8,128)S(1)}, u32[]{:S(2)}, u32[]{:S(2)}) collective-permute-start(f32[8,768]{1,0:T(8,128)S(1)} %shard_map.126.refs_0_), channel_id=1, source_target_pairs={{0,24},{1,25},{2,26},{3,27},{4,28},{5,29},{6,30},{7,31},{8,16},{9,... | collective-permute-start | bytes 73736 | tf_op jit(solution)/shard_map/ppermute | solution.py:363
  92.1 4.2 %collective-permute-start.37 = (f32[8,768]{1,0:T(8,128)S(1)}, f32[8,768]{1,0:T(8,128)S(1)}, u32[]{:S(2)}, u32[]{:S(2)}) collective-permute-start(f32[8,768]{1,0:T(8,128)S(1)} %shard_map.126.refs_0_), channel_id=1, source_target_pairs={{0,28},{1,29},{2,30},{3,31},{4,24},{5,25},{6,26},{7,27},{8,20},{9,... | collective-permute-start | bytes 73736 | tf_op jit(solution)/shard_map/ppermute | solution.py:363
  (17 other events, 154.7 us)

commit v5 on v4

--- a/solution.py
+++ b/solution.py
@@ -1,5 +1,5 @@
+import collections
 import functools
-import itertools
 import math
 
 import jax
@@ -362,16 +362,23 @@
         ]
         return lax.ppermute(value, ("dp", "crow", "ccol"), perm)
 
-    idle = itertools.cycle([(r, c) for r in range(crow) for c in range(r + 1, ccol)])
-
-    def move(value, *pairs, direct=False):
-        to = dict(pairs)
+    recent = collections.deque(maxlen=4)
+    cells = [(r, c) for r in range(crow) for c in range(ccol)]
+
+    def hops(a, b):
+        return (a[0] ^ b[0]).bit_count() + abs(a[1] - b[1])
+
+    def move(value, *pairs, idle=None):
+        to, taken = {}, {cell for two in pairs for cell in two}
         for a, b in pairs:
-            if direct:
-                to[b] = a
+            free = [cell for cell in cells if idle and idle(*cell) and cell not in taken]
+            if free:
+                spare = min(free, key=lambda cell: (cell in recent, hops(a, cell), hops(b, cell)))
+                taken.add(spare)
+                recent.append(spare)
+                to[a], to[b], to[spare] = b, spare, a
             else:
-                spare = next(idle)
-                to[b], to[spare] = spare, a
+                to[a], to[b] = b, a
         return permute(value, lambda d, r, c: (d ^ 1, *to.get((r, c), (r, c))))
 
     def shifts(value, axis, flip=1):
@@ -424,13 +431,14 @@
     sums = []
     for step in range(last, 0, -1):
         cols = list(range(step))[::-1]
-        got = [move(piece, ((step, step), (step, c))) for c in cols]
+        idle = lambda r, c, step=step: c > r or r > step
+        got = [move(piece, ((step, step), (step, c)), idle=idle) for c in cols]
         down = [((step, c), (step - 1, c)) for c in cols]
         if step == last:
-            sub = move(spread(cols[:1], [], got[:1]), down[0])
-            sums = [move(spread(cols[1:], [], got[1:]), *down[1:])]
+            sub = move(spread(cols[:1], [], got[:1]), down[0], idle=idle)
+            sums = [move(spread(cols[1:], [], got[1:]), *down[1:], idle=idle)]
         else:
-            sub = move(spread(cols, sums, got), *down)
+            sub = move(spread(cols, sums, got), *down, idle=idle)
             sums = [sub]
         if step > 1:
             piece = call(solve_kernel, part, direction, sub, low, block_inv)
@@ -443,7 +451,7 @@
 
     parts = [own] + shifts(own, "crow")
     beside = [((n, n), (n, n - 1)) for n in range(1, crow)]
-    half = move(half, *beside, direct=True)
+    half = move(half, *beside)
     mine, images = call(image_kernel, [part, shaped(rows, samples)], *parts, high_k, low_k, limit=16)
     images = [images] + shifts(images, "ccol", 0)
     summed = call(normal_kernel, part, *images, high_k, low_k, limit=16)
@@ -452,7 +460,7 @@
     else:
         summed = lax.psum(summed, "dp")
     parts = [summed] + shifts(summed, "crow")
-    rest = move(rest, *beside, direct=True)
+    rest = move(rest, *beside)
     scale = 1.0 / (samples * dp * crow)
     source, image = call(
         functools.partial(source_kernel, scale, order), [part, part], mine, *parts, *turned
@@ -463,13 +471,14 @@
     side = []
     for step in range(1, crow):
         later = list(range(step + 1, crow))
-        first = move(image, (places[-1], (step, step - 1)))
+        idle = lambda r, c, step=step: step > 1 and (c >= r or r < step - 1)
+        first = move(image, (places[-1], (step, step - 1)), idle=idle)
         if step == 1:
             source = move(source, *beside)
         if side:
             shift = [((at, step - 2), (at, step - 1)) for at in range(step, crow)]
-            side = [move(side[0], *shift)]
-        others = [move(image, (places[-1], (at, step - 1))) for at in later]
+            side = [move(side[0], *shift, idle=idle)]
+        others = [move(image, (places[-1], (at, step - 1)), idle=idle) for at in later]
         image = call(
             functools.partial(fore_kernel, order, len(side)), part,
             *side, first, source, *turned_f, *near,

time: 97.3 us -> 94.3 us (0.969)
  waiting for transfers between devices: 28.8 us -> 27 us
  starting transfers between devices: 46.1 us -> 44.7 us
    ppermute x38, waiting for transfers between devices: 28.8 us -> 27 us  [permute(): return lax.ppermute(value, ('dp', 'crow', 'ccol'), perm)]
    ppermute x38, starting transfers between devices: 46.1 us -> 44.7 us  [permute(): return lax.ppermute(value, ('dp', 'crow', 'ccol'), perm)]
where the time goes in v5:
time: 94.3 us; the launch traced here: 94.1 us
  starting transfers between devices  44.7 us (47%)
  waiting for transfers between devices  27 us (29%)
  Pallas kernels  18.7 us (20%)
  local copies, waits for them, and re-layouts  2.84 us (3%)
    ppermute x38, starting transfers between devices, permute(): return lax.ppermute(value, ('dp', 'crow', 'ccol'), perm)  44.7 us
    ppermute x38, waiting for transfers between devices, permute(): return lax.ppermute(value, ('dp', 'crow', 'ccol'), perm)  27 us
    pallas_call x25, Pallas kernels, call(): pl.pallas_call(kernel, out_shape=outs, compiler_params=pltpu.CompilerPara...  18.7 us
    unnamed x22, local copies, waits for them, and re-layouts  2.84 us
  transfers between devices with their start and end apart: 38, of which 21 were waited for; matrix products, arithmetic and copies ran while one was open for 0% of the time, Pallas kernels for 16%

profile of v5, /device:TPU:0, one launch (start us, length us, event | category | flops | bytes accessed | tf_op | source)
XLA Modules:
  0.0 94.1 jit_solution(6000743643298332958)
XLA Ops:
  0.6 1.7 %copy-done = f32[768,768]{1,0:T(8,128)S(1)} copy-done((f32[768,768]{1,0:T(8,128)S(1)}, f32[768,768]{1,0:T(8,128)}, u32[]{:S(2)}) %copy-start) | copy-done | bytes 2359320
  2.3 1.1 %copy-done.2 = f32[3,256,256]{2,1,0:T(8,128)S(1)} copy-done((f32[3,256,256]{2,1,0:T(8,128)S(1)}, f32[3,256,256]{2,1,0:T(8,128)}, u32[]{:S(2)}) %copy-start.2) | copy-done | bytes 786456
  3.4 1.8 %shard_map.107 = (f32[256,768]{1,0:T(8,128)S(1)}, f32[128,512]{1,0:T(8,128)S(1)}, f32[256,256]{1,0:T(8,128)S(1)}) custom-call(f32[3,256,256]{2,1,0:T(8,128)S(1)} %copy-done.2, f32[768,768]{1,0:T(8,128)S(1)} %copy-done, f32[768,768]{1,0:T(8,128)S(1)} %copy-done, f32[768,768]{1,0:T(8,128)S(1)} %copy-done), custom_call_target="tpu_custom_call" | custom-call | flops 1000000 | bytes 1000000 | tf_op jit(solution)/shard_map/pallas_call | solution.py:335
  5.8 3.0 %shard_map.103.refs_2_ = f32[8,768]{1,0:T(8,128)} custom-call(f32[8,3072]{1,0:T(8,128)} %direction_ref.9, f32[3,256,256]{2,1,0:T(8,128)} %inv_ref.13, f32[768,768]{1,0:T(8,128)} %factor_ref.3, f32[768,768]{1,0:T(8,128)} %factor_ref.3, f32[768,768]{1,0:T(8,128)} %factor_ref.3), custom_call_target="tpu_custom_call" | custom-call | flops 1000000 | bytes 1000000 | tf_op jit(solution)/shard_map/pallas_call | solution.py:335
  15.9 0.8 collective-permute-done.8.refs_1_
  17.1 17.6 %collective-permute-start.9 = (f32[8,768]{1,0:T(8,128)S(1)}, f32[8,768]{1,0:T(8,128)S(1)}, u32[]{:S(2)}, u32[]{:S(2)}) collective-permute-start(f32[8,768]{1,0:T(8,128)S(1)} %shard_map.111), channel_id=1, source_target_pairs={{0,24},{1,17},{2,18},{3,19},{4,16},{5,21},{6,22},{7,23},{8,20},{9,... | collective-permute-start | bytes 73736 | tf_op jit(solution)/shard_map/ppermute | solution.py:363
  34.7 4.2 %collective-permute-done.9.sub_ref = f32[8,768]{1,0:T(8,128)S(1)} collective-permute-done((f32[8,768]{1,0:T(8,128)S(1)}, f32[8,768]{1,0:T(8,128)S(1)}, u32[]{:S(2)}, u32[]{:S(2)}) %collective-permute-start.9) | collective-permute-done | bytes 24608 | tf_op jit(solution)/shard_map/ppermute | solution.py:363
  39.3 2.6 %collective-permute-start.10 = (f32[8,768]{1,0:T(8,128)S(1)}, f32[8,768]{1,0:T(8,128)S(1)}, u32[]{:S(2)}, u32[]{:S(2)}) collective-permute-start(f32[8,768]{1,0:T(8,128)S(1)} %shard_map.112.refs_0_), channel_id=1, source_target_pairs={{0,20},{1,21},{2,22},{3,23},{4,16},{5,17},{6,18},{7,19},{8,28},{9,... | collective-permute-start | bytes 73736 | tf_op jit(solution)/shard_map/ppermute | solution.py:363
  42.0 1.3 %collective-permute-start.12 = (f32[8,768]{1,0:T(8,128)S(1)}, f32[8,768]{1,0:T(8,128)S(1)}, u32[]{:S(2)}, u32[]{:S(2)}) collective-permute-start(f32[8,768]{1,0:T(8,128)S(1)} %shard_map.112.refs_0_), channel_id=1, source_target_pairs={{0,28},{1,29},{2,30},{3,31},{4,24},{5,25},{6,26},{7,27},{8,20},{9,... | collective-permute-start | bytes 73736 | tf_op jit(solution)/shard_map/ppermute | solution.py:363
  43.3 2.5 %shard_map.113 = (bf16[768,2048]{1,0:T(8,128)(2,1)S(1)}, bf16[768,2048]{1,0:T(8,128)(2,1)S(1)}) custom-call(f32[16]{0:T(128)S(1)} %copy-done.10, f32[16,768]{1,0:T(8,128)S(1)} %copy-done.9, f32[16,2048]{1,0:T(8,128)S(1)} %copy-done.5), custom_call_target="tpu_custom_call" | custom-call | flops 1000000 | bytes 1000000 | tf_op jit(solution)/shard_map/pallas_call | solution.py:335
  46.1 0.9 shard_map.114
  47.1 4.3 %collective-permute-start.15 = (f32[8,2048]{1,0:T(8,128)S(1)}, f32[8,2048]{1,0:T(8,128)S(1)}, u32[]{:S(2)}, u32[]{:S(2)}) collective-permute-start(f32[8,2048]{1,0:T(8,128)S(1)} %get-tuple-element.26.refs_0_), channel_id=1, source_target_pairs={{0,3},{1,2},{2,1},{3,0},{4,7},{5,6},{6,5},{7,4},{8,11},{9,10},{10,... | collective-permute-start | bytes 196616 | tf_op jit(solution)/shard_map/ppermute | solution.py:363
  52.2 3.4 %collective-permute-done.14.refs_2_ = f32[8,2048]{1,0:T(8,128)S(1)} collective-permute-done((f32[8,2048]{1,0:T(8,128)S(1)}, f32[8,2048]{1,0:T(8,128)S(1)}, u32[]{:S(2)}, u32[]{:S(2)}) %collective-permute-start.14) | collective-permute-done | bytes 65568 | tf_op jit(solution)/shard_map/ppermute | solution.py:363
  55.6 1.8 %shard_map.115 = f32[8,768]{1,0:T(8,128)S(1)} custom-call(f32[8,2048]{1,0:T(8,128)S(1)} %get-tuple-element.26.refs_0_, f32[8,2048]{1,0:T(8,128)S(1)} %collective-permute-done.13.refs_1_, f32[8,2048]{1,0:T(8,128)S(1)} %collective-permute-done.14.refs_2_, f32[8,2048]{1,0:T(8,128)S(1)} %collective-permute-done.15.refs_3_, ...), custom_call_target="tpu_custom_call" | custom-call | flops 1000000 | bytes 1000000 | tf_op jit(solution)/shard_map/pallas_call | solution.py:335
  57.5 1.2 %collective-permute-done.16 = f32[8,768]{1,0:T(8,128)S(1)} collective-permute-done((f32[8,768]{1,0:T(8,128)S(1)}, f32[8,768]{1,0:T(8,128)S(1)}, u32[]{:S(2)}, u32[]{:S(2)}) %collective-permute-start.16) | collective-permute-done | bytes 24608 | tf_op jit(solution)/shard_map/ppermute | solution.py:363
  58.7 1.4 %collective-permute-start.17 = (f32[8,768]{1,0:T(8,128)S(1)}, f32[8,768]{1,0:T(8,128)S(1)}, u32[]{:S(2)}, u32[]{:S(2)}) collective-permute-start(f32[8,768]{1,0:T(8,128)S(1)} %add.3.refs_0_), channel_id=1, source_target_pairs={{0,20},{1,21},{2,22},{3,23},{4,16},{5,17},{6,18},{7,19},{8,28},{9,... | collective-permute-start | bytes 73736 | tf_op jit(solution)/shard_map/ppermute | solution.py:363
  60.5 1.3 %collective-permute-start.19 = (f32[8,768]{1,0:T(8,128)S(1)}, f32[8,768]{1,0:T(8,128)S(1)}, u32[]{:S(2)}, u32[]{:S(2)}) collective-permute-start(f32[8,768]{1,0:T(8,128)S(1)} %add.3.refs_0_), channel_id=1, source_target_pairs={{0,28},{1,29},{2,30},{3,31},{4,24},{5,25},{6,26},{7,27},{8,20},{9,... | collective-permute-start | bytes 73736 | tf_op jit(solution)/shard_map/ppermute | solution.py:363
  62.2 1.1 %collective-permute-done.18.refs_2_ = f32[8,768]{1,0:T(8,128)S(1)} collective-permute-done((f32[8,768]{1,0:T(8,128)S(1)}, f32[8,768]{1,0:T(8,128)S(1)}, u32[]{:S(2)}, u32[]{:S(2)}) %collective-permute-start.18) | collective-permute-done | bytes 24608 | tf_op jit(solution)/shard_map/ppermute | solution.py:363
  63.3 1.3 %collective-permute-done.19.refs_3_ = f32[8,768]{1,0:T(8,128)S(1)} collective-permute-done((f32[8,768]{1,0:T(8,128)S(1)}, f32[8,768]{1,0:T(8,128)S(1)}, u32[]{:S(2)}, u32[]{:S(2)}) %collective-permute-start.19) | collective-permute-done | bytes 24608 | tf_op jit(solution)/shard_map/ppermute | solution.py:363
  65.0 1.3 %collective-permute-start.25 = (f32[8,768]{1,0:T(8,128)S(1)}, f32[8,768]{1,0:T(8,128)S(1)}, u32[]{:S(2)}, u32[]{:S(2)}) collective-permute-start(f32[8,768]{1,0:T(8,128)S(1)} %get-tuple-element.29.refs_0_), channel_id=1, source_target_pairs={{0,24},{1,17},{2,18},{3,19},{4,20},{5,21},{6,22},{7,23},{8,16},{9,... | collective-permute-start | bytes 73736 | tf_op jit(solution)/shard_map/ppermute | solution.py:363
  67.1 1.2 %collective-permute-done.25.refs_0_ = f32[8,768]{1,0:T(8,128)S(1)} collective-permute-done((f32[8,768]{1,0:T(8,128)S(1)}, f32[8,768]{1,0:T(8,128)S(1)}, u32[]{:S(2)}, u32[]{:S(2)}) %collective-permute-start.25) | collective-permute-done | bytes 24608 | tf_op jit(solution)/shard_map/ppermute | solution.py:363
  69.2 1.3 %collective-permute-done.26.refs_1_ = f32[8,768]{1,0:T(8,128)S(1)} collective-permute-done((f32[8,768]{1,0:T(8,128)S(1)}, f32[8,768]{1,0:T(8,128)S(1)}, u32[]{:S(2)}, u32[]{:S(2)}) %collective-permute-start.26) | collective-permute-done | bytes 24608 | tf_op jit(solution)/shard_map/ppermute | solution.py:363
  72.6 1.0 %collective-permute-start.28 = (f32[8,768]{1,0:T(8,128)S(1)}, f32[8,768]{1,0:T(8,128)S(1)}, u32[]{:S(2)}, u32[]{:S(2)}) collective-permute-start(f32[8,768]{1,0:T(8,128)S(1)} %shard_map.120.refs_1_), channel_id=1, source_target_pairs={{0,20},{1,17},{2,18},{3,19},{4,25},{5,21},{6,22},{7,23},{8,24},{9,... | collective-permute-start | bytes 73736 | tf_op jit(solution)/shard_map/ppermute | solution.py:363
  74.3 2.4 %collective-permute-done.28.refs_1_ = f32[8,768]{1,0:T(8,128)S(1)} collective-permute-done((f32[8,768]{1,0:T(8,128)S(1)}, f32[8,768]{1,0:T(8,128)S(1)}, u32[]{:S(2)}, u32[]{:S(2)}) %collective-permute-start.28) | collective-permute-done | bytes 24608 | tf_op jit(solution)/shard_map/ppermute | solution.py:363
  77.8 0.8 collective-permute-done.31.refs_1_
  79.4 2.1 %collective-permute-start.33 = (f32[8,768]{1,0:T(8,128)S(1)}, f32[8,768]{1,0:T(8,128)S(1)}, u32[]{:S(2)}, u32[]{:S(2)}) collective-permute-start(f32[8,768]{1,0:T(8,128)S(1)} %shard_map.125.refs_0_), channel_id=1, source_target_pairs={{0,18},{1,19},{2,16},{3,17},{4,22},{5,23},{6,20},{7,21},{8,26},{9,... | collective-permute-start | bytes 73736 | tf_op jit(solution)/shard_map/ppermute | solution.py:363
  81.5 1.9 %collective-permute-start.34 = (f32[8,768]{1,0:T(8,128)S(1)}, f32[8,768]{1,0:T(8,128)S(1)}, u32[]{:S(2)}, u32[]{:S(2)}) collective-permute-start(f32[8,768]{1,0:T(8,128)S(1)} %shard_map.125.refs_0_), channel_id=1, source_target_pairs={{0,19},{1,18},{2,17},{3,16},{4,23},{5,22},{6,21},{7,20},{8,27},{9,... | collective-permute-start | bytes 73736 | tf_op jit(solution)/shard_map/ppermute | solution.py:363
  83.6 3.0 %collective-permute-done.34.refs_3_ = f32[8,768]{1,0:T(8,128)S(1)} collective-permute-done((f32[8,768]{1,0:T(8,128)S(1)}, f32[8,768]{1,0:T(8,128)S(1)}, u32[]{:S(2)}, u32[]{:S(2)}) %collective-permute-start.34) | collective-permute-done | bytes 24608 | tf_op jit(solution)/shard_map/ppermute | solution.py:363
  87.5 1.6 %collective-permute-start.36 = (f32[8,768]{1,0:T(8,128)S(1)}, f32[8,768]{1,0:T(8,128)S(1)}, u32[]{:S(2)}, u32[]{:S(2)}) collective-permute-start(f32[8,768]{1,0:T(8,128)S(1)} %shard_map.126.refs_0_), channel_id=1, source_target_pairs={{0,24},{1,25},{2,26},{3,27},{4,28},{5,29},{6,30},{7,31},{8,16},{9,... | collective-permute-start | bytes 73736 | tf_op jit(solution)/shard_map/ppermute | solution.py:363
  89.1 1.2 %collective-permute-start.37 = (f32[8,768]{1,0:T(8,128)S(1)}, f32[8,768]{1,0:T(8,128)S(1)}, u32[]{:S(2)}, u32[]{:S(2)}) collective-permute-start(f32[8,768]{1,0:T(8,128)S(1)} %shard_map.126.refs_0_), channel_id=1, source_target_pairs={{0,28},{1,29},{2,30},{3,31},{4,24},{5,25},{6,26},{7,27},{8,20},{9,... | collective-permute-start | bytes 73736 | tf_op jit(solution)/shard_map/ppermute | solution.py:363
  90.7 2.5 %collective-permute-done.37.refs_3_ = f32[8,768]{1,0:T(8,128)S(1)} collective-permute-done((f32[8,768]{1,0:T(8,128)S(1)}, f32[8,768]{1,0:T(8,128)S(1)}, u32[]{:S(2)}, u32[]{:S(2)}) %collective-permute-start.37) | collective-permute-done | bytes 24608 | tf_op jit(solution)/shard_map/ppermute | solution.py:363
  93.2 0.9 shard_map.127
  (92 shorter events, 18.6 us)
Async XLA Ops:
  5.2 9.2 %collective-permute-start.22 = (f32[128,512]{1,0:T(8,128)S(1)}, f32[128,512]{1,0:T(8,128)S(1)}, u32[]{:S(2)}, u32[]{:S(2)}) collective-permute-start(f32[128,512]{1,0:T(8,128)S(1)} %get-tuple-element.33), channel_id=1, source_target_pairs={{0,16},{1,17},{2,18},{3,19},{4,21},{5,20},{6,22},{7,23},{8,24},{9,... | collective-permute-start | bytes 786440 | tf_op jit(solution)/shard_map/ppermute | solution.py:363
  8.8 1.4 %collective-permute-start.3 = (f32[8,768]{1,0:T(8,128)}, f32[8,768]{1,0:T(8,128)S(1)}, u32[]{:S(2)}, u32[]{:S(2)}) collective-permute-start(f32[8,768]{1,0:T(8,128)} %shard_map.103.refs_2_), channel_id=1, source_target_pairs={{0,16},{1,17},{2,18},{3,19},{4,20},{5,21},{6,22},{7,31},{8,24},{9,... | collective-permute-start | bytes 73736 | tf_op jit(solution)/shard_map/ppermute | solution.py:363
  8.8 2.0 %collective-permute-start = (f32[8,768]{1,0:T(8,128)}, f32[8,768]{1,0:T(8,128)S(1)}, u32[]{:S(2)}, u32[]{:S(2)}) collective-permute-start(f32[8,768]{1,0:T(8,128)} %shard_map.103.refs_2_), channel_id=1, source_target_pairs={{0,16},{1,17},{2,18},{3,19},{4,20},{5,21},{6,22},{7,23},{8,24},{9,... | collective-permute-start | bytes 73736 | tf_op jit(solution)/shard_map/ppermute | solution.py:363
  9.3 1.5 %collective-permute-start.1 = (f32[8,768]{1,0:T(8,128)}, f32[8,768]{1,0:T(8,128)S(1)}, u32[]{:S(2)}, u32[]{:S(2)}) collective-permute-start(f32[8,768]{1,0:T(8,128)} %shard_map.103.refs_2_), channel_id=1, source_target_pairs={{0,16},{1,17},{2,18},{3,19},{4,20},{5,21},{6,31},{7,23},{8,24},{9,... | collective-permute-start | bytes 73736 | tf_op jit(solution)/shard_map/ppermute | solution.py:363
  11.2 1.5 %collective-permute-start.2 = (f32[8,768]{1,0:T(8,128)S(1)}, f32[8,768]{1,0:T(8,128)S(1)}, u32[]{:S(2)}, u32[]{:S(2)}) collective-permute-start(f32[8,768]{1,0:T(8,128)S(1)} %shard_map.105), channel_id=1, source_target_pairs={{0,16},{1,29},{2,18},{3,19},{4,20},{5,21},{6,22},{7,28},{8,23},{9,... | collective-permute-start | bytes 73736 | tf_op jit(solution)/shard_map/ppermute | solution.py:363
  14.3 56.9 %collective-permute-start.24 = (f32[256,256]{1,0:T(8,128)S(1)}, f32[256,256]{1,0:T(8,128)S(1)}, u32[]{:S(2)}, u32[]{:S(2)}) collective-permute-start(f32[256,256]{1,0:T(8,128)S(1)} %get-tuple-element.34), channel_id=1, source_target_pairs={{0,16},{1,17},{2,18},{3,19},{4,21},{5,20},{6,22},{7,23},{8,24},{9,... | collective-permute-start | bytes 786440 | tf_op jit(solution)/shard_map/ppermute | solution.py:363
  14.5 56.8 %collective-permute-start.23 = (f32[128,512]{1,0:T(8,128)S(1)}, f32[128,512]{1,0:T(8,128)S(1)}, u32[]{:S(2)}, u32[]{:S(2)}) collective-permute-start(f32[128,512]{1,0:T(8,128)S(1)} %collective-permute-done.22.mine_ref), channel_id=1, source_target_pairs={{0,16},{1,17},{2,18},{3,19},{4,20},{5,21},{6,22},{7,23},{8,24},{9,... | collective-permute-start | bytes 786440 | tf_op jit(solution)/shard_map/ppermute | solution.py:363
  17.1 21.8 %collective-permute-start.9 = (f32[8,768]{1,0:T(8,128)S(1)}, f32[8,768]{1,0:T(8,128)S(1)}, u32[]{:S(2)}, u32[]{:S(2)}) collective-permute-start(f32[8,768]{1,0:T(8,128)S(1)} %shard_map.111), channel_id=1, source_target_pairs={{0,24},{1,17},{2,18},{3,19},{4,16},{5,21},{6,22},{7,23},{8,20},{9,... | collective-permute-start | bytes 73736 | tf_op jit(solution)/shard_map/ppermute | solution.py:363
  39.3 6.5 %collective-permute-start.10 = (f32[8,768]{1,0:T(8,128)S(1)}, f32[8,768]{1,0:T(8,128)S(1)}, u32[]{:S(2)}, u32[]{:S(2)}) collective-permute-start(f32[8,768]{1,0:T(8,128)S(1)} %shard_map.112.refs_0_), channel_id=1, source_target_pairs={{0,20},{1,21},{2,22},{3,23},{4,16},{5,17},{6,18},{7,19},{8,28},{9,... | collective-permute-start | bytes 73736 | tf_op jit(solution)/shard_map/ppermute | solution.py:363
  42.0 3.8 %collective-permute-start.11 = (f32[8,768]{1,0:T(8,128)S(1)}, f32[8,768]{1,0:T(8,128)S(1)}, u32[]{:S(2)}, u32[]{:S(2)}) collective-permute-start(f32[8,768]{1,0:T(8,128)S(1)} %shard_map.112.refs_0_), channel_id=1, source_target_pairs={{0,24},{1,25},{2,26},{3,27},{4,28},{5,29},{6,30},{7,31},{8,16},{9,... | collective-permute-start | bytes 73736 | tf_op jit(solution)/shard_map/ppermute | solution.py:363
  42.0 4.2 %collective-permute-start.12 = (f32[8,768]{1,0:T(8,128)S(1)}, f32[8,768]{1,0:T(8,128)S(1)}, u32[]{:S(2)}, u32[]{:S(2)}) collective-permute-start(f32[8,768]{1,0:T(8,128)S(1)} %shard_map.112.refs_0_), channel_id=1, source_target_pairs={{0,28},{1,29},{2,30},{3,31},{4,24},{5,25},{6,26},{7,27},{8,20},{9,... | collective-permute-start | bytes 73736 | tf_op jit(solution)/shard_map/ppermute | solution.py:363
  47.1 5.2 %collective-permute-start.13 = (f32[8,2048]{1,0:T(8,128)S(1)}, f32[8,2048]{1,0:T(8,128)S(1)}, u32[]{:S(2)}, u32[]{:S(2)}) collective-permute-start(f32[8,2048]{1,0:T(8,128)S(1)} %get-tuple-element.26.refs_0_), channel_id=1, source_target_pairs={{0,1},{1,0},{2,3},{3,2},{4,5},{5,4},{6,7},{7,6},{8,9},{9,8},{10,11... | collective-permute-start | bytes 196616 | tf_op jit(solution)/shard_map/ppermute | solution.py:363
  47.1 8.6 %collective-permute-start.14 = (f32[8,2048]{1,0:T(8,128)S(1)}, f32[8,2048]{1,0:T(8,128)S(1)}, u32[]{:S(2)}, u32[]{:S(2)}) collective-permute-start(f32[8,2048]{1,0:T(8,128)S(1)} %get-tuple-element.26.refs_0_), channel_id=1, source_target_pairs={{0,2},{1,3},{2,0},{3,1},{4,6},{5,7},{6,4},{7,5},{8,10},{9,11},{10,... | collective-permute-start | bytes 196616 | tf_op jit(solution)/shard_map/ppermute | solution.py:363
  47.1 8.5 %collective-permute-start.15 = (f32[8,2048]{1,0:T(8,128)S(1)}, f32[8,2048]{1,0:T(8,128)S(1)}, u32[]{:S(2)}, u32[]{:S(2)}) collective-permute-start(f32[8,2048]{1,0:T(8,128)S(1)} %get-tuple-element.26.refs_0_), channel_id=1, source_target_pairs={{0,3},{1,2},{2,1},{3,0},{4,7},{5,6},{6,5},{7,4},{8,11},{9,10},{10,... | collective-permute-start | bytes 196616 | tf_op jit(solution)/shard_map/ppermute | solution.py:363
  57.4 1.2 %collective-permute-start.16 = (f32[8,768]{1,0:T(8,128)S(1)}, f32[8,768]{1,0:T(8,128)S(1)}, u32[]{:S(2)}, u32[]{:S(2)}) collective-permute-start(f32[8,768]{1,0:T(8,128)S(1)} %shard_map.115), channel_id=1, source_target_pairs={{0,16},{1,17},{2,18},{3,19},{4,20},{5,21},{6,22},{7,23},{8,24},{9,... | collective-permute-start | bytes 73736 | tf_op jit(solution)/shard_map/ppermute | solution.py:363
  58.7 3.6 %collective-permute-start.17 = (f32[8,768]{1,0:T(8,128)S(1)}, f32[8,768]{1,0:T(8,128)S(1)}, u32[]{:S(2)}, u32[]{:S(2)}) collective-permute-start(f32[8,768]{1,0:T(8,128)S(1)} %add.3.refs_0_), channel_id=1, source_target_pairs={{0,20},{1,21},{2,22},{3,23},{4,16},{5,17},{6,18},{7,19},{8,28},{9,... | collective-permute-start | bytes 73736 | tf_op jit(solution)/shard_map/ppermute | solution.py:363
  60.1 3.3 %collective-permute-start.18 = (f32[8,768]{1,0:T(8,128)S(1)}, f32[8,768]{1,0:T(8,128)S(1)}, u32[]{:S(2)}, u32[]{:S(2)}) collective-permute-start(f32[8,768]{1,0:T(8,128)S(1)} %add.3.refs_0_), channel_id=1, source_target_pairs={{0,24},{1,25},{2,26},{3,27},{4,28},{5,29},{6,30},{7,31},{8,16},{9,... | collective-permute-start | bytes 73736 | tf_op jit(solution)/shard_map/ppermute | solution.py:363
  60.5 4.2 %collective-permute-start.19 = (f32[8,768]{1,0:T(8,128)S(1)}, f32[8,768]{1,0:T(8,128)S(1)}, u32[]{:S(2)}, u32[]{:S(2)}) collective-permute-start(f32[8,768]{1,0:T(8,128)S(1)} %add.3.refs_0_), channel_id=1, source_target_pairs={{0,28},{1,29},{2,30},{3,31},{4,24},{5,25},{6,26},{7,27},{8,20},{9,... | collective-permute-start | bytes 73736 | tf_op jit(solution)/shard_map/ppermute | solution.py:363
  65.0 3.3 %collective-permute-start.25 = (f32[8,768]{1,0:T(8,128)S(1)}, f32[8,768]{1,0:T(8,128)S(1)}, u32[]{:S(2)}, u32[]{:S(2)}) collective-permute-start(f32[8,768]{1,0:T(8,128)S(1)} %get-tuple-element.29.refs_0_), channel_id=1, source_target_pairs={{0,24},{1,17},{2,18},{3,19},{4,20},{5,21},{6,22},{7,23},{8,16},{9,... | collective-permute-start | bytes 73736 | tf_op jit(solution)/shard_map/ppermute | solution.py:363
  66.3 4.2 %collective-permute-start.26 = (f32[8,768]{1,0:T(8,128)S(1)}, f32[8,768]{1,0:T(8,128)S(1)}, u32[]{:S(2)}, u32[]{:S(2)}) collective-permute-start(f32[8,768]{1,0:T(8,128)S(1)} %get-tuple-element.29.refs_0_), channel_id=1, source_target_pairs={{0,28},{1,17},{2,18},{3,19},{4,20},{5,21},{6,22},{7,23},{8,24},{9,... | collective-permute-start | bytes 73736 | tf_op jit(solution)/shard_map/ppermute | solution.py:363
  66.5 5.2 %collective-permute-start.20 = (f32[8,768]{1,0:T(8,128)S(1)}, f32[8,768]{1,0:T(8,128)S(1)}, u32[]{:S(2)}, u32[]{:S(2)}) collective-permute-start(f32[8,768]{1,0:T(8,128)S(1)} %get-tuple-element.29.refs_0_), channel_id=1, source_target_pairs={{0,20},{1,17},{2,18},{3,19},{4,16},{5,21},{6,22},{7,23},{8,24},{9,... | collective-permute-start | bytes 73736 | tf_op jit(solution)/shard_map/ppermute | solution.py:363
  68.2 3.5 %collective-permute-start.21 = (f32[8,768]{1,0:T(8,128)S(1)}, f32[8,768]{1,0:T(8,128)S(1)}, u32[]{:S(2)}, u32[]{:S(2)}) collective-permute-start(f32[8,768]{1,0:T(8,128)S(1)} %get-tuple-element.30), channel_id=1, source_target_pairs={{0,16},{1,17},{2,18},{3,19},{4,21},{5,20},{6,22},{7,23},{8,24},{9,... | collective-permute-start | bytes 73736 | tf_op jit(solution)/shard_map/ppermute | solution.py:363
  70.9 2.8 %collective-permute-start.27 = (f32[8,768]{1,0:T(8,128)S(1)}, f32[8,768]{1,0:T(8,128)S(1)}, u32[]{:S(2)}, u32[]{:S(2)}) collective-permute-start(f32[8,768]{1,0:T(8,128)S(1)} %shard_map.121), channel_id=1, source_target_pairs={{0,16},{1,17},{2,18},{3,19},{4,20},{5,28},{6,22},{7,23},{8,25},{9,... | collective-permute-start | bytes 73736 | tf_op jit(solution)/shard_map/ppermute | solution.py:363
  72.4 1.2 %collective-permute-start.29 = (f32[8,768]{1,0:T(8,128)S(1)}, f32[8,768]{1,0:T(8,128)S(1)}, u32[]{:S(2)}, u32[]{:S(2)}) collective-permute-start(f32[8,768]{1,0:T(8,128)S(1)} %shard_map.120.refs_1_), channel_id=1, source_target_pairs={{0,16},{1,20},{2,18},{3,19},{4,29},{5,21},{6,22},{7,23},{8,24},{9,... | collective-permute-start | bytes 73736 | tf_op jit(solution)/shard_map/ppermute | solution.py:363
  72.6 4.2 %collective-permute-start.28 = (f32[8,768]{1,0:T(8,128)S(1)}, f32[8,768]{1,0:T(8,128)S(1)}, u32[]{:S(2)}, u32[]{:S(2)}) collective-permute-start(f32[8,768]{1,0:T(8,128)S(1)} %shard_map.120.refs_1_), channel_id=1, source_target_pairs={{0,20},{1,17},{2,18},{3,19},{4,25},{5,21},{6,22},{7,23},{8,24},{9,... | collective-permute-start | bytes 73736 | tf_op jit(solution)/shard_map/ppermute | solution.py:363
  74.0 3.7 %collective-permute-start.30 = (f32[8,768]{1,0:T(8,128)S(1)}, f32[8,768]{1,0:T(8,128)S(1)}, u32[]{:S(2)}, u32[]{:S(2)}) collective-permute-start(f32[8,768]{1,0:T(8,128)S(1)} %shard_map.123), channel_id=1, source_target_pairs={{0,16},{1,17},{2,18},{3,19},{4,20},{5,21},{6,29},{7,23},{8,24},{9,... | collective-permute-start | bytes 73736 | tf_op jit(solution)/shard_map/ppermute | solution.py:363
  79.3 4.1 %collective-permute-start.32 = (f32[8,768]{1,0:T(8,128)S(1)}, f32[8,768]{1,0:T(8,128)S(1)}, u32[]{:S(2)}, u32[]{:S(2)}) collective-permute-start(f32[8,768]{1,0:T(8,128)S(1)} %shard_map.125.refs_0_), channel_id=1, source_target_pairs={{0,17},{1,16},{2,19},{3,18},{4,21},{5,20},{6,23},{7,22},{8,25},{9,... | collective-permute-start | bytes 73736 | tf_op jit(solution)/shard_map/ppermute | solution.py:363
  79.4 4.2 %collective-permute-start.33 = (f32[8,768]{1,0:T(8,128)S(1)}, f32[8,768]{1,0:T(8,128)S(1)}, u32[]{:S(2)}, u32[]{:S(2)}) collective-permute-start(f32[8,768]{1,0:T(8,128)S(1)} %shard_map.125.refs_0_), channel_id=1, source_target_pairs={{0,18},{1,19},{2,16},{3,17},{4,22},{5,23},{6,20},{7,21},{8,26},{9,... | collective-permute-start | bytes 73736 | tf_op jit(solution)/shard_map/ppermute | solution.py:363
  81.5 5.2 %collective-permute-start.34 = (f32[8,768]{1,0:T(8,128)S(1)}, f32[8,768]{1,0:T(8,128)S(1)}, u32[]{:S(2)}, u32[]{:S(2)}) collective-permute-start(f32[8,768]{1,0:T(8,128)S(1)} %shard_map.125.refs_0_), channel_id=1, source_target_pairs={{0,19},{1,18},{2,17},{3,16},{4,23},{5,22},{6,21},{7,20},{8,27},{9,... | collective-permute-start | bytes 73736 | tf_op jit(solution)/shard_map/ppermute | solution.py:363
  86.7 3.6 %collective-permute-start.35 = (f32[8,768]{1,0:T(8,128)S(1)}, f32[8,768]{1,0:T(8,128)S(1)}, u32[]{:S(2)}, u32[]{:S(2)}) collective-permute-start(f32[8,768]{1,0:T(8,128)S(1)} %shard_map.126.refs_0_), channel_id=1, source_target_pairs={{0,20},{1,21},{2,22},{3,23},{4,16},{5,17},{6,18},{7,19},{8,28},{9,... | collective-permute-start | bytes 73736 | tf_op jit(solution)/shard_map/ppermute | solution.py:363
  87.5 3.3 %collective-permute-start.36 = (f32[8,768]{1,0:T(8,128)S(1)}, f32[8,768]{1,0:T(8,128)S(1)}, u32[]{:S(2)}, u32[]{:S(2)}) collective-permute-start(f32[8,768]{1,0:T(8,128)S(1)} %shard_map.126.refs_0_), channel_id=1, source_target_pairs={{0,24},{1,25},{2,26},{3,27},{4,28},{5,29},{6,30},{7,31},{8,16},{9,... | collective-permute-start | bytes 73736 | tf_op jit(solution)/shard_map/ppermute | solution.py:363
  89.1 4.2 %collective-permute-start.37 = (f32[8,768]{1,0:T(8,128)S(1)}, f32[8,768]{1,0:T(8,128)S(1)}, u32[]{:S(2)}, u32[]{:S(2)}) collective-permute-start(f32[8,768]{1,0:T(8,128)S(1)} %shard_map.126.refs_0_), channel_id=1, source_target_pairs={{0,28},{1,29},{2,30},{3,31},{4,24},{5,25},{6,26},{7,27},{8,20},{9,... | collective-permute-start | bytes 73736 | tf_op jit(solution)/shard_map/ppermute | solution.py:363
  (17 other events, 149.5 us)

commit v6 on v5

--- a/solution.py
+++ b/solution.py
@@ -362,7 +362,7 @@
         ]
         return lax.ppermute(value, ("dp", "crow", "ccol"), perm)
 
-    recent = collections.deque(maxlen=4)
+    recent = collections.deque(maxlen=5)
     cells = [(r, c) for r in range(crow) for c in range(ccol)]
 
     def hops(a, b):
@@ -431,8 +431,9 @@
     sums = []
     for step in range(last, 0, -1):
         cols = list(range(step))[::-1]
-        idle = lambda r, c, step=step: c > r or r > step
-        got = [move(piece, ((step, step), (step, c)), idle=idle) for c in cols]
+        idle = (lambda r, c: c > r) if step > 1 else None
+        near_idle = lambda r, c: c > r
+        got = [move(piece, ((step, step), (step, c)), idle=near_idle) for c in cols]
         down = [((step, c), (step - 1, c)) for c in cols]
         if step == last:
             sub = move(spread(cols[:1], [], got[:1]), down[0], idle=idle)
@@ -477,7 +478,7 @@
             source = move(source, *beside)
         if side:
             shift = [((at, step - 2), (at, step - 1)) for at in range(step, crow)]
-            side = [move(side[0], *shift, idle=idle)]
+            side = [move(side[0], *shift, idle=idle if step < last else None)]
         others = [move(image, (places[-1], (at, step - 1)), idle=idle) for at in later]
         image = call(
             functools.partial(fore_kernel, order, len(side)), part,

time: 94.3 us -> 93 us (0.986)
  transfers between devices with their start and end apart: 38 -> 38, of which waited for: 21 -> 22; matrix products, arithmetic and copies ran while one was open for 0% -> 0% of each run, Pallas kernels for 16% -> 16%
where the time goes in v6:
time: 93 us; the launch traced here: 92.8 us
  starting transfers between devices  44.1 us (47%)
  waiting for transfers between devices  26.3 us (28%)
  Pallas kernels  18.7 us (20%)
  local copies, waits for them, and re-layouts  2.84 us (3%)
    ppermute x38, starting transfers between devices, permute(): return lax.ppermute(value, ('dp', 'crow', 'ccol'), perm)  44.1 us
    ppermute x38, waiting for transfers between devices, permute(): return lax.ppermute(value, ('dp', 'crow', 'ccol'), perm)  26.3 us
    pallas_call x25, Pallas kernels, call(): pl.pallas_call(kernel, out_shape=outs, compiler_params=pltpu.CompilerPara...  18.7 us
    unnamed x22, local copies, waits for them, and re-layouts  2.84 us
  transfers between devices with their start and end apart: 38, of which 22 were waited for; matrix products, arithmetic and copies ran while one was open for 0% of the time, Pallas kernels for 16%

profile of v6, /device:TPU:0, one launch (start us, length us, event | category | flops | bytes accessed | tf_op | source)
XLA Modules:
  0.0 92.8 jit_solution(14652495434767026757)
XLA Ops:
  0.6 1.7 %copy-done = f32[768,768]{1,0:T(8,128)S(1)} copy-done((f32[768,768]{1,0:T(8,128)S(1)}, f32[768,768]{1,0:T(8,128)}, u32[]{:S(2)}) %copy-start) | copy-done | bytes 2359320
  2.3 1.1 %copy-done.2 = f32[3,256,256]{2,1,0:T(8,128)S(1)} copy-done((f32[3,256,256]{2,1,0:T(8,128)S(1)}, f32[3,256,256]{2,1,0:T(8,128)}, u32[]{:S(2)}) %copy-start.2) | copy-done | bytes 786456
  3.4 1.8 %shard_map.107 = (f32[256,768]{1,0:T(8,128)S(1)}, f32[128,512]{1,0:T(8,128)S(1)}, f32[256,256]{1,0:T(8,128)S(1)}) custom-call(f32[3,256,256]{2,1,0:T(8,128)S(1)} %copy-done.2, f32[768,768]{1,0:T(8,128)S(1)} %copy-done, f32[768,768]{1,0:T(8,128)S(1)} %copy-done, f32[768,768]{1,0:T(8,128)S(1)} %copy-done), custom_call_target="tpu_custom_call" | custom-call | flops 1000000 | bytes 1000000 | tf_op jit(solution)/shard_map/pallas_call | solution.py:335
  5.8 3.0 %shard_map.103.refs_2_ = f32[8,768]{1,0:T(8,128)} custom-call(f32[8,3072]{1,0:T(8,128)} %direction_ref.9, f32[3,256,256]{2,1,0:T(8,128)} %inv_ref.13, f32[768,768]{1,0:T(8,128)} %factor_ref.3, f32[768,768]{1,0:T(8,128)} %factor_ref.3, f32[768,768]{1,0:T(8,128)} %factor_ref.3), custom_call_target="tpu_custom_call" | custom-call | flops 1000000 | bytes 1000000 | tf_op jit(solution)/shard_map/pallas_call | solution.py:335
  15.9 0.8 collective-permute-done.8.refs_1_
  17.1 18.0 %collective-permute-start.9 = (f32[8,768]{1,0:T(8,128)S(1)}, f32[8,768]{1,0:T(8,128)S(1)}, u32[]{:S(2)}, u32[]{:S(2)}) collective-permute-start(f32[8,768]{1,0:T(8,128)S(1)} %shard_map.111), channel_id=1, source_target_pairs={{0,20},{1,17},{2,18},{3,19},{4,16},{5,21},{6,22},{7,23},{8,24},{9,... | collective-permute-start | bytes 73736 | tf_op jit(solution)/shard_map/ppermute | solution.py:363
  35.1 1.5 %collective-permute-done.9.sub_ref = f32[8,768]{1,0:T(8,128)S(1)} collective-permute-done((f32[8,768]{1,0:T(8,128)S(1)}, f32[8,768]{1,0:T(8,128)S(1)}, u32[]{:S(2)}, u32[]{:S(2)}) %collective-permute-start.9) | collective-permute-done | bytes 24608 | tf_op jit(solution)/shard_map/ppermute | solution.py:363
  37.0 1.7 %collective-permute-start.10 = (f32[8,768]{1,0:T(8,128)S(1)}, f32[8,768]{1,0:T(8,128)S(1)}, u32[]{:S(2)}, u32[]{:S(2)}) collective-permute-start(f32[8,768]{1,0:T(8,128)S(1)} %shard_map.112.refs_0_), channel_id=1, source_target_pairs={{0,20},{1,21},{2,22},{3,23},{4,16},{5,17},{6,18},{7,19},{8,28},{9,... | collective-permute-start | bytes 73736 | tf_op jit(solution)/shard_map/ppermute | solution.py:363
  38.7 1.5 %collective-permute-start.12 = (f32[8,768]{1,0:T(8,128)S(1)}, f32[8,768]{1,0:T(8,128)S(1)}, u32[]{:S(2)}, u32[]{:S(2)}) collective-permute-start(f32[8,768]{1,0:T(8,128)S(1)} %shard_map.112.refs_0_), channel_id=1, source_target_pairs={{0,28},{1,29},{2,30},{3,31},{4,24},{5,25},{6,26},{7,27},{8,20},{9,... | collective-permute-start | bytes 73736 | tf_op jit(solution)/shard_map/ppermute | solution.py:363
  40.2 2.5 %shard_map.113 = (bf16[768,2048]{1,0:T(8,128)(2,1)S(1)}, bf16[768,2048]{1,0:T(8,128)(2,1)S(1)}) custom-call(f32[16]{0:T(128)S(1)} %copy-done.10, f32[16,768]{1,0:T(8,128)S(1)} %copy-done.9, f32[16,2048]{1,0:T(8,128)S(1)} %copy-done.5), custom_call_target="tpu_custom_call" | custom-call | flops 1000000 | bytes 1000000 | tf_op jit(solution)/shard_map/pallas_call | solution.py:335
  42.9 0.9 shard_map.114
  43.9 4.3 %collective-permute-start.15 = (f32[8,2048]{1,0:T(8,128)S(1)}, f32[8,2048]{1,0:T(8,128)S(1)}, u32[]{:S(2)}, u32[]{:S(2)}) collective-permute-start(f32[8,2048]{1,0:T(8,128)S(1)} %get-tuple-element.26.refs_0_), channel_id=1, source_target_pairs={{0,3},{1,2},{2,1},{3,0},{4,7},{5,6},{6,5},{7,4},{8,11},{9,10},{10,... | collective-permute-start | bytes 196616 | tf_op jit(solution)/shard_map/ppermute | solution.py:363
  48.2 1.0 %collective-permute-done.13.refs_1_ = f32[8,2048]{1,0:T(8,128)S(1)} collective-permute-done((f32[8,2048]{1,0:T(8,128)S(1)}, f32[8,2048]{1,0:T(8,128)S(1)}, u32[]{:S(2)}, u32[]{:S(2)}) %collective-permute-start.13) | collective-permute-done | bytes 65568 | tf_op jit(solution)/shard_map/ppermute | solution.py:363
  49.2 3.4 %collective-permute-done.14.refs_2_ = f32[8,2048]{1,0:T(8,128)S(1)} collective-permute-done((f32[8,2048]{1,0:T(8,128)S(1)}, f32[8,2048]{1,0:T(8,128)S(1)}, u32[]{:S(2)}, u32[]{:S(2)}) %collective-permute-start.14) | collective-permute-done | bytes 65568 | tf_op jit(solution)/shard_map/ppermute | solution.py:363
  52.5 1.8 %shard_map.115 = f32[8,768]{1,0:T(8,128)S(1)} custom-call(f32[8,2048]{1,0:T(8,128)S(1)} %get-tuple-element.26.refs_0_, f32[8,2048]{1,0:T(8,128)S(1)} %collective-permute-done.13.refs_1_, f32[8,2048]{1,0:T(8,128)S(1)} %collective-permute-done.14.refs_2_, f32[8,2048]{1,0:T(8,128)S(1)} %collective-permute-done.15.refs_3_, ...), custom_call_target="tpu_custom_call" | custom-call | flops 1000000 | bytes 1000000 | tf_op jit(solution)/shard_map/pallas_call | solution.py:335
  54.4 1.2 %collective-permute-done.16 = f32[8,768]{1,0:T(8,128)S(1)} collective-permute-done((f32[8,768]{1,0:T(8,128)S(1)}, f32[8,768]{1,0:T(8,128)S(1)}, u32[]{:S(2)}, u32[]{:S(2)}) %collective-permute-start.16) | collective-permute-done | bytes 24608 | tf_op jit(solution)/shard_map/ppermute | solution.py:363
  55.6 1.4 %collective-permute-start.17 = (f32[8,768]{1,0:T(8,128)S(1)}, f32[8,768]{1,0:T(8,128)S(1)}, u32[]{:S(2)}, u32[]{:S(2)}) collective-permute-start(f32[8,768]{1,0:T(8,128)S(1)} %add.3.refs_0_), channel_id=1, source_target_pairs={{0,20},{1,21},{2,22},{3,23},{4,16},{5,17},{6,18},{7,19},{8,28},{9,... | collective-permute-start | bytes 73736 | tf_op jit(solution)/shard_map/ppermute | solution.py:363
  57.4 1.2 %collective-permute-start.19 = (f32[8,768]{1,0:T(8,128)S(1)}, f32[8,768]{1,0:T(8,128)S(1)}, u32[]{:S(2)}, u32[]{:S(2)}) collective-permute-start(f32[8,768]{1,0:T(8,128)S(1)} %add.3.refs_0_), channel_id=1, source_target_pairs={{0,28},{1,29},{2,30},{3,31},{4,24},{5,25},{6,26},{7,27},{8,20},{9,... | collective-permute-start | bytes 73736 | tf_op jit(solution)/shard_map/ppermute | solution.py:363
  59.1 1.1 %collective-permute-done.18.refs_2_ = f32[8,768]{1,0:T(8,128)S(1)} collective-permute-done((f32[8,768]{1,0:T(8,128)S(1)}, f32[8,768]{1,0:T(8,128)S(1)}, u32[]{:S(2)}, u32[]{:S(2)}) %collective-permute-start.18) | collective-permute-done | bytes 24608 | tf_op jit(solution)/shard_map/ppermute | solution.py:363
  60.2 1.3 %collective-permute-done.19.refs_3_ = f32[8,768]{1,0:T(8,128)S(1)} collective-permute-done((f32[8,768]{1,0:T(8,128)S(1)}, f32[8,768]{1,0:T(8,128)S(1)}, u32[]{:S(2)}, u32[]{:S(2)}) %collective-permute-start.19) | collective-permute-done | bytes 24608 | tf_op jit(solution)/shard_map/ppermute | solution.py:363
  61.9 1.3 %collective-permute-start.25 = (f32[8,768]{1,0:T(8,128)S(1)}, f32[8,768]{1,0:T(8,128)S(1)}, u32[]{:S(2)}, u32[]{:S(2)}) collective-permute-start(f32[8,768]{1,0:T(8,128)S(1)} %get-tuple-element.29.refs_0_), channel_id=1, source_target_pairs={{0,24},{1,17},{2,18},{3,19},{4,20},{5,21},{6,22},{7,23},{8,16},{9,... | collective-permute-start | bytes 73736 | tf_op jit(solution)/shard_map/ppermute | solution.py:363
  64.0 1.2 %collective-permute-done.25.refs_0_ = f32[8,768]{1,0:T(8,128)S(1)} collective-permute-done((f32[8,768]{1,0:T(8,128)S(1)}, f32[8,768]{1,0:T(8,128)S(1)}, u32[]{:S(2)}, u32[]{:S(2)}) %collective-permute-start.25) | collective-permute-done | bytes 24608 | tf_op jit(solution)/shard_map/ppermute | solution.py:363
  66.0 1.3 %collective-permute-done.26.refs_1_ = f32[8,768]{1,0:T(8,128)S(1)} collective-permute-done((f32[8,768]{1,0:T(8,128)S(1)}, f32[8,768]{1,0:T(8,128)S(1)}, u32[]{:S(2)}, u32[]{:S(2)}) %collective-permute-start.26) | collective-permute-done | bytes 24608 | tf_op jit(solution)/shard_map/ppermute | solution.py:363
  69.5 1.0 %collective-permute-start.28 = (f32[8,768]{1,0:T(8,128)S(1)}, f32[8,768]{1,0:T(8,128)S(1)}, u32[]{:S(2)}, u32[]{:S(2)}) collective-permute-start(f32[8,768]{1,0:T(8,128)S(1)} %shard_map.120.refs_1_), channel_id=1, source_target_pairs={{0,20},{1,17},{2,18},{3,19},{4,25},{5,21},{6,22},{7,23},{8,24},{9,... | collective-permute-start | bytes 73736 | tf_op jit(solution)/shard_map/ppermute | solution.py:363
  71.2 2.4 %collective-permute-done.28.refs_1_ = f32[8,768]{1,0:T(8,128)S(1)} collective-permute-done((f32[8,768]{1,0:T(8,128)S(1)}, f32[8,768]{1,0:T(8,128)S(1)}, u32[]{:S(2)}, u32[]{:S(2)}) %collective-permute-start.28) | collective-permute-done | bytes 24608 | tf_op jit(solution)/shard_map/ppermute | solution.py:363
  76.3 3.3 %collective-permute-start.33 = (f32[8,768]{1,0:T(8,128)S(1)}, f32[8,768]{1,0:T(8,128)S(1)}, u32[]{:S(2)}, u32[]{:S(2)}) collective-permute-start(f32[8,768]{1,0:T(8,128)S(1)} %shard_map.125.refs_0_), channel_id=1, source_target_pairs={{0,18},{1,19},{2,16},{3,17},{4,22},{5,23},{6,20},{7,21},{8,26},{9,... | collective-permute-start | bytes 73736 | tf_op jit(solution)/shard_map/ppermute | solution.py:363
  79.6 1.1 %collective-permute-start.34 = (f32[8,768]{1,0:T(8,128)S(1)}, f32[8,768]{1,0:T(8,128)S(1)}, u32[]{:S(2)}, u32[]{:S(2)}) collective-permute-start(f32[8,768]{1,0:T(8,128)S(1)} %shard_map.125.refs_0_), channel_id=1, source_target_pairs={{0,19},{1,18},{2,17},{3,16},{4,23},{5,22},{6,21},{7,20},{8,27},{9,... | collective-permute-start | bytes 73736 | tf_op jit(solution)/shard_map/ppermute | solution.py:363
  81.1 3.6 %collective-permute-done.34.refs_3_ = f32[8,768]{1,0:T(8,128)S(1)} collective-permute-done((f32[8,768]{1,0:T(8,128)S(1)}, f32[8,768]{1,0:T(8,128)S(1)}, u32[]{:S(2)}, u32[]{:S(2)}) %collective-permute-start.34) | collective-permute-done | bytes 24608 | tf_op jit(solution)/shard_map/ppermute | solution.py:363
  84.8 2.9 %collective-permute-start.36 = (f32[8,768]{1,0:T(8,128)S(1)}, f32[8,768]{1,0:T(8,128)S(1)}, u32[]{:S(2)}, u32[]{:S(2)}) collective-permute-start(f32[8,768]{1,0:T(8,128)S(1)} %shard_map.126.refs_0_), channel_id=1, source_target_pairs={{0,24},{1,25},{2,26},{3,27},{4,28},{5,29},{6,30},{7,31},{8,16},{9,... | collective-permute-start | bytes 73736 | tf_op jit(solution)/shard_map/ppermute | solution.py:363
  88.1 1.2 %collective-permute-done.36.refs_2_ = f32[8,768]{1,0:T(8,128)S(1)} collective-permute-done((f32[8,768]{1,0:T(8,128)S(1)}, f32[8,768]{1,0:T(8,128)S(1)}, u32[]{:S(2)}, u32[]{:S(2)}) %collective-permute-start.36) | collective-permute-done | bytes 24608 | tf_op jit(solution)/shard_map/ppermute | solution.py:363
  89.3 2.6 %collective-permute-done.37.refs_3_ = f32[8,768]{1,0:T(8,128)S(1)} collective-permute-done((f32[8,768]{1,0:T(8,128)S(1)}, f32[8,768]{1,0:T(8,128)S(1)}, u32[]{:S(2)}, u32[]{:S(2)}) %collective-permute-start.37) | collective-permute-done | bytes 24608 | tf_op jit(solution)/shard_map/ppermute | solution.py:363
  91.9 0.9 shard_map.127
  (92 shorter events, 17.8 us)
Async XLA Ops:
  5.2 9.2 %collective-permute-start.22 = (f32[128,512]{1,0:T(8,128)S(1)}, f32[128,512]{1,0:T(8,128)S(1)}, u32[]{:S(2)}, u32[]{:S(2)}) collective-permute-start(f32[128,512]{1,0:T(8,128)S(1)} %get-tuple-element.33), channel_id=1, source_target_pairs={{0,16},{1,17},{2,18},{3,19},{4,21},{5,20},{6,22},{7,23},{8,24},{9,... | collective-permute-start | bytes 786440 | tf_op jit(solution)/shard_map/ppermute | solution.py:363
  8.8 1.4 %collective-permute-start.3 = (f32[8,768]{1,0:T(8,128)}, f32[8,768]{1,0:T(8,128)S(1)}, u32[]{:S(2)}, u32[]{:S(2)}) collective-permute-start(f32[8,768]{1,0:T(8,128)} %shard_map.103.refs_2_), channel_id=1, source_target_pairs={{0,16},{1,17},{2,18},{3,19},{4,20},{5,21},{6,22},{7,31},{8,24},{9,... | collective-permute-start | bytes 73736 | tf_op jit(solution)/shard_map/ppermute | solution.py:363
  8.8 2.0 %collective-permute-start = (f32[8,768]{1,0:T(8,128)}, f32[8,768]{1,0:T(8,128)S(1)}, u32[]{:S(2)}, u32[]{:S(2)}) collective-permute-start(f32[8,768]{1,0:T(8,128)} %shard_map.103.refs_2_), channel_id=1, source_target_pairs={{0,16},{1,17},{2,18},{3,19},{4,20},{5,21},{6,22},{7,23},{8,24},{9,... | collective-permute-start | bytes 73736 | tf_op jit(solution)/shard_map/ppermute | solution.py:363
  9.3 1.5 %collective-permute-start.1 = (f32[8,768]{1,0:T(8,128)}, f32[8,768]{1,0:T(8,128)S(1)}, u32[]{:S(2)}, u32[]{:S(2)}) collective-permute-start(f32[8,768]{1,0:T(8,128)} %shard_map.103.refs_2_), channel_id=1, source_target_pairs={{0,16},{1,17},{2,18},{3,19},{4,20},{5,21},{6,31},{7,23},{8,24},{9,... | collective-permute-start | bytes 73736 | tf_op jit(solution)/shard_map/ppermute | solution.py:363
  11.2 1.5 %collective-permute-start.2 = (f32[8,768]{1,0:T(8,128)S(1)}, f32[8,768]{1,0:T(8,128)S(1)}, u32[]{:S(2)}, u32[]{:S(2)}) collective-permute-start(f32[8,768]{1,0:T(8,128)S(1)} %shard_map.105), channel_id=1, source_target_pairs={{0,16},{1,29},{2,18},{3,28},{4,20},{5,21},{6,22},{7,23},{8,19},{9,... | collective-permute-start | bytes 73736 | tf_op jit(solution)/shard_map/ppermute | solution.py:363
  14.3 53.8 %collective-permute-start.24 = (f32[256,256]{1,0:T(8,128)S(1)}, f32[256,256]{1,0:T(8,128)S(1)}, u32[]{:S(2)}, u32[]{:S(2)}) collective-permute-start(f32[256,256]{1,0:T(8,128)S(1)} %get-tuple-element.34), channel_id=1, source_target_pairs={{0,16},{1,17},{2,18},{3,19},{4,21},{5,20},{6,22},{7,23},{8,24},{9,... | collective-permute-start | bytes 786440 | tf_op jit(solution)/shard_map/ppermute | solution.py:363
  14.5 53.7 %collective-permute-start.23 = (f32[128,512]{1,0:T(8,128)S(1)}, f32[128,512]{1,0:T(8,128)S(1)}, u32[]{:S(2)}, u32[]{:S(2)}) collective-permute-start(f32[128,512]{1,0:T(8,128)S(1)} %collective-permute-done.22.mine_ref), channel_id=1, source_target_pairs={{0,16},{1,17},{2,18},{3,19},{4,20},{5,21},{6,22},{7,23},{8,24},{9,... | collective-permute-start | bytes 786440 | tf_op jit(solution)/shard_map/ppermute | solution.py:363
  17.1 19.5 %collective-permute-start.9 = (f32[8,768]{1,0:T(8,128)S(1)}, f32[8,768]{1,0:T(8,128)S(1)}, u32[]{:S(2)}, u32[]{:S(2)}) collective-permute-start(f32[8,768]{1,0:T(8,128)S(1)} %shard_map.111), channel_id=1, source_target_pairs={{0,20},{1,17},{2,18},{3,19},{4,16},{5,21},{6,22},{7,23},{8,24},{9,... | collective-permute-start | bytes 73736 | tf_op jit(solution)/shard_map/ppermute | solution.py:363
  37.0 5.8 %collective-permute-start.10 = (f32[8,768]{1,0:T(8,128)S(1)}, f32[8,768]{1,0:T(8,128)S(1)}, u32[]{:S(2)}, u32[]{:S(2)}) collective-permute-start(f32[8,768]{1,0:T(8,128)S(1)} %shard_map.112.refs_0_), channel_id=1, source_target_pairs={{0,20},{1,21},{2,22},{3,23},{4,16},{5,17},{6,18},{7,19},{8,28},{9,... | collective-permute-start | bytes 73736 | tf_op jit(solution)/shard_map/ppermute | solution.py:363
  38.7 4.0 %collective-permute-start.11 = (f32[8,768]{1,0:T(8,128)S(1)}, f32[8,768]{1,0:T(8,128)S(1)}, u32[]{:S(2)}, u32[]{:S(2)}) collective-permute-start(f32[8,768]{1,0:T(8,128)S(1)} %shard_map.112.refs_0_), channel_id=1, source_target_pairs={{0,24},{1,25},{2,26},{3,27},{4,28},{5,29},{6,30},{7,31},{8,16},{9,... | collective-permute-start | bytes 73736 | tf_op jit(solution)/shard_map/ppermute | solution.py:363
  38.7 4.2 %collective-permute-start.12 = (f32[8,768]{1,0:T(8,128)S(1)}, f32[8,768]{1,0:T(8,128)S(1)}, u32[]{:S(2)}, u32[]{:S(2)}) collective-permute-start(f32[8,768]{1,0:T(8,128)S(1)} %shard_map.112.refs_0_), channel_id=1, source_target_pairs={{0,28},{1,29},{2,30},{3,31},{4,24},{5,25},{6,26},{7,27},{8,20},{9,... | collective-permute-start | bytes 73736 | tf_op jit(solution)/shard_map/ppermute | solution.py:363
  43.8 5.4 %collective-permute-start.13 = (f32[8,2048]{1,0:T(8,128)S(1)}, f32[8,2048]{1,0:T(8,128)S(1)}, u32[]{:S(2)}, u32[]{:S(2)}) collective-permute-start(f32[8,2048]{1,0:T(8,128)S(1)} %get-tuple-element.26.refs_0_), channel_id=1, source_target_pairs={{0,1},{1,0},{2,3},{3,2},{4,5},{5,4},{6,7},{7,6},{8,9},{9,8},{10,11... | collective-permute-start | bytes 196616 | tf_op jit(solution)/shard_map/ppermute | solution.py:363
  43.8 8.7 %collective-permute-start.14 = (f32[8,2048]{1,0:T(8,128)S(1)}, f32[8,2048]{1,0:T(8,128)S(1)}, u32[]{:S(2)}, u32[]{:S(2)}) collective-permute-start(f32[8,2048]{1,0:T(8,128)S(1)} %get-tuple-element.26.refs_0_), channel_id=1, source_target_pairs={{0,2},{1,3},{2,0},{3,1},{4,6},{5,7},{6,4},{7,5},{8,10},{9,11},{10,... | collective-permute-start | bytes 196616 | tf_op jit(solution)/shard_map/ppermute | solution.py:363
  43.9 8.7 %collective-permute-start.15 = (f32[8,2048]{1,0:T(8,128)S(1)}, f32[8,2048]{1,0:T(8,128)S(1)}, u32[]{:S(2)}, u32[]{:S(2)}) collective-permute-start(f32[8,2048]{1,0:T(8,128)S(1)} %get-tuple-element.26.refs_0_), channel_id=1, source_target_pairs={{0,3},{1,2},{2,1},{3,0},{4,7},{5,6},{6,5},{7,4},{8,11},{9,10},{10,... | collective-permute-start | bytes 196616 | tf_op jit(solution)/shard_map/ppermute | solution.py:363
  54.3 1.2 %collective-permute-start.16 = (f32[8,768]{1,0:T(8,128)S(1)}, f32[8,768]{1,0:T(8,128)S(1)}, u32[]{:S(2)}, u32[]{:S(2)}) collective-permute-start(f32[8,768]{1,0:T(8,128)S(1)} %shard_map.115), channel_id=1, source_target_pairs={{0,16},{1,17},{2,18},{3,19},{4,20},{5,21},{6,22},{7,23},{8,24},{9,... | collective-permute-start | bytes 73736 | tf_op jit(solution)/shard_map/ppermute | solution.py:363
  55.6 3.5 %collective-permute-start.17 = (f32[8,768]{1,0:T(8,128)S(1)}, f32[8,768]{1,0:T(8,128)S(1)}, u32[]{:S(2)}, u32[]{:S(2)}) collective-permute-start(f32[8,768]{1,0:T(8,128)S(1)} %add.3.refs_0_), channel_id=1, source_target_pairs={{0,20},{1,21},{2,22},{3,23},{4,16},{5,17},{6,18},{7,19},{8,28},{9,... | collective-permute-start | bytes 73736 | tf_op jit(solution)/shard_map/ppermute | solution.py:363
  57.0 3.3 %collective-permute-start.18 = (f32[8,768]{1,0:T(8,128)S(1)}, f32[8,768]{1,0:T(8,128)S(1)}, u32[]{:S(2)}, u32[]{:S(2)}) collective-permute-start(f32[8,768]{1,0:T(8,128)S(1)} %add.3.refs_0_), channel_id=1, source_target_pairs={{0,24},{1,25},{2,26},{3,27},{4,28},{5,29},{6,30},{7,31},{8,16},{9,... | collective-permute-start | bytes 73736 | tf_op jit(solution)/shard_map/ppermute | solution.py:363
  57.4 4.2 %collective-permute-start.19 = (f32[8,768]{1,0:T(8,128)S(1)}, f32[8,768]{1,0:T(8,128)S(1)}, u32[]{:S(2)}, u32[]{:S(2)}) collective-permute-start(f32[8,768]{1,0:T(8,128)S(1)} %add.3.refs_0_), channel_id=1, source_target_pairs={{0,28},{1,29},{2,30},{3,31},{4,24},{5,25},{6,26},{7,27},{8,20},{9,... | collective-permute-start | bytes 73736 | tf_op jit(solution)/shard_map/ppermute | solution.py:363
  61.9 3.3 %collective-permute-start.25 = (f32[8,768]{1,0:T(8,128)S(1)}, f32[8,768]{1,0:T(8,128)S(1)}, u32[]{:S(2)}, u32[]{:S(2)}) collective-permute-start(f32[8,768]{1,0:T(8,128)S(1)} %get-tuple-element.29.refs_0_), channel_id=1, source_target_pairs={{0,24},{1,17},{2,18},{3,19},{4,20},{5,21},{6,22},{7,23},{8,16},{9,... | collective-permute-start | bytes 73736 | tf_op jit(solution)/shard_map/ppermute | solution.py:363
  63.2 4.2 %collective-permute-start.26 = (f32[8,768]{1,0:T(8,128)S(1)}, f32[8,768]{1,0:T(8,128)S(1)}, u32[]{:S(2)}, u32[]{:S(2)}) collective-permute-start(f32[8,768]{1,0:T(8,128)S(1)} %get-tuple-element.29.refs_0_), channel_id=1, source_target_pairs={{0,28},{1,17},{2,18},{3,19},{4,20},{5,21},{6,22},{7,23},{8,24},{9,... | collective-permute-start | bytes 73736 | tf_op jit(solution)/shard_map/ppermute | solution.py:363
  63.4 5.2 %collective-permute-start.20 = (f32[8,768]{1,0:T(8,128)S(1)}, f32[8,768]{1,0:T(8,128)S(1)}, u32[]{:S(2)}, u32[]{:S(2)}) collective-permute-start(f32[8,768]{1,0:T(8,128)S(1)} %get-tuple-element.29.refs_0_), channel_id=1, source_target_pairs={{0,20},{1,17},{2,18},{3,19},{4,16},{5,21},{6,22},{7,23},{8,24},{9,... | collective-permute-start | bytes 73736 | tf_op jit(solution)/shard_map/ppermute | solution.py:363
  65.1 3.5 %collective-permute-start.21 = (f32[8,768]{1,0:T(8,128)S(1)}, f32[8,768]{1,0:T(8,128)S(1)}, u32[]{:S(2)}, u32[]{:S(2)}) collective-permute-start(f32[8,768]{1,0:T(8,128)S(1)} %get-tuple-element.30), channel_id=1, source_target_pairs={{0,16},{1,17},{2,18},{3,19},{4,21},{5,20},{6,22},{7,23},{8,24},{9,... | collective-permute-start | bytes 73736 | tf_op jit(solution)/shard_map/ppermute | solution.py:363
  67.8 2.7 %collective-permute-start.27 = (f32[8,768]{1,0:T(8,128)S(1)}, f32[8,768]{1,0:T(8,128)S(1)}, u32[]{:S(2)}, u32[]{:S(2)}) collective-permute-start(f32[8,768]{1,0:T(8,128)S(1)} %shard_map.121), channel_id=1, source_target_pairs={{0,16},{1,17},{2,18},{3,19},{4,20},{5,28},{6,22},{7,23},{8,25},{9,... | collective-permute-start | bytes 73736 | tf_op jit(solution)/shard_map/ppermute | solution.py:363
  69.5 4.2 %collective-permute-start.28 = (f32[8,768]{1,0:T(8,128)S(1)}, f32[8,768]{1,0:T(8,128)S(1)}, u32[]{:S(2)}, u32[]{:S(2)}) collective-permute-start(f32[8,768]{1,0:T(8,128)S(1)} %shard_map.120.refs_1_), channel_id=1, source_target_pairs={{0,20},{1,17},{2,18},{3,19},{4,25},{5,21},{6,22},{7,23},{8,24},{9,... | collective-permute-start | bytes 73736 | tf_op jit(solution)/shard_map/ppermute | solution.py:363
  70.9 3.8 %collective-permute-start.30 = (f32[8,768]{1,0:T(8,128)S(1)}, f32[8,768]{1,0:T(8,128)S(1)}, u32[]{:S(2)}, u32[]{:S(2)}) collective-permute-start(f32[8,768]{1,0:T(8,128)S(1)} %shard_map.123), channel_id=1, source_target_pairs={{0,16},{1,17},{2,18},{3,19},{4,20},{5,21},{6,22},{7,23},{8,24},{9,... | collective-permute-start | bytes 73736 | tf_op jit(solution)/shard_map/ppermute | solution.py:363
  74.3 1.2 %collective-permute-start.31 = (f32[8,768]{1,0:T(8,128)S(1)}, f32[8,768]{1,0:T(8,128)S(1)}, u32[]{:S(2)}, u32[]{:S(2)}) collective-permute-start(f32[8,768]{1,0:T(8,128)S(1)} %shard_map.122.refs_2_), channel_id=1, source_target_pairs={{0,16},{1,17},{2,25},{3,19},{4,20},{5,21},{6,22},{7,23},{8,24},{9,... | collective-permute-start | bytes 73736 | tf_op jit(solution)/shard_map/ppermute | solution.py:363
  76.2 4.5 %collective-permute-start.32 = (f32[8,768]{1,0:T(8,128)S(1)}, f32[8,768]{1,0:T(8,128)S(1)}, u32[]{:S(2)}, u32[]{:S(2)}) collective-permute-start(f32[8,768]{1,0:T(8,128)S(1)} %shard_map.125.refs_0_), channel_id=1, source_target_pairs={{0,17},{1,16},{2,19},{3,18},{4,21},{5,20},{6,23},{7,22},{8,25},{9,... | collective-permute-start | bytes 73736 | tf_op jit(solution)/shard_map/ppermute | solution.py:363
  76.3 4.8 %collective-permute-start.33 = (f32[8,768]{1,0:T(8,128)S(1)}, f32[8,768]{1,0:T(8,128)S(1)}, u32[]{:S(2)}, u32[]{:S(2)}) collective-permute-start(f32[8,768]{1,0:T(8,128)S(1)} %shard_map.125.refs_0_), channel_id=1, source_target_pairs={{0,18},{1,19},{2,16},{3,17},{4,22},{5,23},{6,20},{7,21},{8,26},{9,... | collective-permute-start | bytes 73736 | tf_op jit(solution)/shard_map/ppermute | solution.py:363
  79.6 5.2 %collective-permute-start.34 = (f32[8,768]{1,0:T(8,128)S(1)}, f32[8,768]{1,0:T(8,128)S(1)}, u32[]{:S(2)}, u32[]{:S(2)}) collective-permute-start(f32[8,768]{1,0:T(8,128)S(1)} %shard_map.125.refs_0_), channel_id=1, source_target_pairs={{0,19},{1,18},{2,17},{3,16},{4,23},{5,22},{6,21},{7,20},{8,27},{9,... | collective-permute-start | bytes 73736 | tf_op jit(solution)/shard_map/ppermute | solution.py:363
  84.8 3.3 %collective-permute-start.35 = (f32[8,768]{1,0:T(8,128)S(1)}, f32[8,768]{1,0:T(8,128)S(1)}, u32[]{:S(2)}, u32[]{:S(2)}) collective-permute-start(f32[8,768]{1,0:T(8,128)S(1)} %shard_map.126.refs_0_), channel_id=1, source_target_pairs={{0,20},{1,21},{2,22},{3,23},{4,16},{5,17},{6,18},{7,19},{8,28},{9,... | collective-permute-start | bytes 73736 | tf_op jit(solution)/shard_map/ppermute | solution.py:363
  84.8 4.4 %collective-permute-start.36 = (f32[8,768]{1,0:T(8,128)S(1)}, f32[8,768]{1,0:T(8,128)S(1)}, u32[]{:S(2)}, u32[]{:S(2)}) collective-permute-start(f32[8,768]{1,0:T(8,128)S(1)} %shard_map.126.refs_0_), channel_id=1, source_target_pairs={{0,24},{1,25},{2,26},{3,27},{4,28},{5,29},{6,30},{7,31},{8,16},{9,... | collective-permute-start | bytes 73736 | tf_op jit(solution)/shard_map/ppermute | solution.py:363
  87.7 4.2 %collective-permute-start.37 = (f32[8,768]{1,0:T(8,128)S(1)}, f32[8,768]{1,0:T(8,128)S(1)}, u32[]{:S(2)}, u32[]{:S(2)}) collective-permute-start(f32[8,768]{1,0:T(8,128)S(1)} %shard_map.126.refs_0_), channel_id=1, source_target_pairs={{0,28},{1,29},{2,30},{3,31},{4,24},{5,25},{6,26},{7,27},{8,20},{9,... | collective-permute-start | bytes 73736 | tf_op jit(solution)/shard_map/ppermute | solution.py:363
  (17 other events, 141.7 us)

commit v7 on v3

--- a/solution.py
+++ b/solution.py
@@ -361,15 +361,9 @@
         ]
         return lax.ppermute(value, ("dp", "crow", "ccol"), perm)
 
-    idle = [(r, c) for r in range(crow) for c in range(r + 1, ccol)]
-
-    def move(value, *pairs, direct=False):
+    def move(value, *pairs):
         to = dict(pairs)
-        for (a, b), spare in zip(pairs, idle):
-            if direct:
-                to[b] = a
-            else:
-                to[b], to[spare] = spare, a
+        to.update((b, a) for a, b in pairs)
         return permute(value, lambda d, r, c: (d ^ 1, *to.get((r, c), (r, c))))
 
     def shifts(value, axis, flip=1):
@@ -441,7 +435,7 @@
 
     parts = [own] + shifts(own, "crow")
     beside = [((n, n), (n, n - 1)) for n in range(1, crow)]
-    half = move(half, *beside, direct=True)
+    half = move(half, *beside)
     mine, images = call(image_kernel, [part, shaped(rows, samples)], *parts, high_k, low_k, limit=16)
     images = [images] + shifts(images, "ccol", 0)
     summed = call(normal_kernel, part, *images, high_k, low_k, limit=16)
@@ -450,7 +444,7 @@
     else:
         summed = lax.psum(summed, "dp")
     parts = [summed] + shifts(summed, "crow")
-    rest = move(rest, *beside, direct=True)
+    rest = move(rest, *beside)
     scale = 1.0 / (samples * dp * crow)
     source, image = call(
         functools.partial(source_kernel, scale, order), [part, part], mine, *parts, *turned

time: 102 us -> 96.1 us (0.942)
  starting transfers between devices: 56.1 us -> 50.8 us
    ppermute x38, starting transfers between devices: 56.1 us -> 50.8 us  [permute(): return lax.ppermute(value, ('dp', 'crow', 'ccol'), perm)]
  transfers between devices with their start and end apart: 38 -> 38, of which waited for: 19 -> 21; matrix products, arithmetic and copies ran while one was open for 0% -> 0% of each run, Pallas kernels for 15% -> 16%
where the time goes in v7:
time: 96.1 us; the launch traced here: 95.9 us
  starting transfers between devices  50.8 us (53%)
  waiting for transfers between devices  22.6 us (24%)
  Pallas kernels  18.9 us (20%)
  local copies, waits for them, and re-layouts  2.84 us (3%)
    ppermute x38, starting transfers between devices, permute(): return lax.ppermute(value, ('dp', 'crow', 'ccol'), perm)  50.8 us
    ppermute x38, waiting for transfers between devices, permute(): return lax.ppermute(value, ('dp', 'crow', 'ccol'), perm)  22.6 us
    pallas_call x25, Pallas kernels, call(): pl.pallas_call(kernel, out_shape=outs, compiler_params=pltpu.CompilerPara...  18.9 us
    unnamed x22, local copies, waits for them, and re-layouts  2.84 us
  transfers between devices with their start and end apart: 38, of which 21 were waited for; matrix products, arithmetic and copies ran while one was open for 0% of the time, Pallas kernels for 16%

profile of v7, /device:TPU:0, one launch (start us, length us, event | category | flops | bytes accessed | tf_op | source)
XLA Modules:
  0.0 95.9 jit_solution(6286952504102285910)
XLA Ops:
  0.6 1.7 %copy-done = f32[768,768]{1,0:T(8,128)S(1)} copy-done((f32[768,768]{1,0:T(8,128)S(1)}, f32[768,768]{1,0:T(8,128)}, u32[]{:S(2)}) %copy-start) | copy-done | bytes 2359320
  2.3 1.1 %copy-done.2 = f32[3,256,256]{2,1,0:T(8,128)S(1)} copy-done((f32[3,256,256]{2,1,0:T(8,128)S(1)}, f32[3,256,256]{2,1,0:T(8,128)}, u32[]{:S(2)}) %copy-start.2) | copy-done | bytes 786456
  3.4 1.8 %shard_map.107 = (f32[256,768]{1,0:T(8,128)S(1)}, f32[128,512]{1,0:T(8,128)S(1)}, f32[256,256]{1,0:T(8,128)S(1)}) custom-call(f32[3,256,256]{2,1,0:T(8,128)S(1)} %copy-done.2, f32[768,768]{1,0:T(8,128)S(1)} %copy-done, f32[768,768]{1,0:T(8,128)S(1)} %copy-done, f32[768,768]{1,0:T(8,128)S(1)} %copy-done), custom_call_target="tpu_custom_call" | custom-call | flops 1000000 | bytes 1000000 | tf_op jit(solution)/shard_map/pallas_call | solution.py:334
  5.8 3.0 %shard_map.103.refs_2_ = f32[8,768]{1,0:T(8,128)} custom-call(f32[8,3072]{1,0:T(8,128)} %direction_ref.9, f32[3,256,256]{2,1,0:T(8,128)} %inv_ref.13, f32[768,768]{1,0:T(8,128)} %factor_ref.3, f32[768,768]{1,0:T(8,128)} %factor_ref.3, f32[768,768]{1,0:T(8,128)} %factor_ref.3), custom_call_target="tpu_custom_call" | custom-call | flops 1000000 | bytes 1000000 | tf_op jit(solution)/shard_map/pallas_call | solution.py:334
  12.7 0.7 collective-permute-done.5.refs_1_
  15.8 0.8 collective-permute-done.8.refs_1_
  17.1 20.5 %collective-permute-start.9 = (f32[8,768]{1,0:T(8,128)S(1)}, f32[8,768]{1,0:T(8,128)S(1)}, u32[]{:S(2)}, u32[]{:S(2)}) collective-permute-start(f32[8,768]{1,0:T(8,128)S(1)} %shard_map.111), channel_id=1, source_target_pairs={{0,20},{1,17},{2,18},{3,19},{4,16},{5,21},{6,22},{7,23},{8,24},{9,... | collective-permute-start | bytes 73736 | tf_op jit(solution)/shard_map/ppermute | solution.py:362
  37.6 1.5 %collective-permute-done.9.sub_ref = f32[8,768]{1,0:T(8,128)S(1)} collective-permute-done((f32[8,768]{1,0:T(8,128)S(1)}, f32[8,768]{1,0:T(8,128)S(1)}, u32[]{:S(2)}, u32[]{:S(2)}) %collective-permute-start.9) | collective-permute-done | bytes 24608 | tf_op jit(solution)/shard_map/ppermute | solution.py:362
  39.5 1.7 %collective-permute-start.10 = (f32[8,768]{1,0:T(8,128)S(1)}, f32[8,768]{1,0:T(8,128)S(1)}, u32[]{:S(2)}, u32[]{:S(2)}) collective-permute-start(f32[8,768]{1,0:T(8,128)S(1)} %shard_map.112.refs_0_), channel_id=1, source_target_pairs={{0,20},{1,21},{2,22},{3,23},{4,16},{5,17},{6,18},{7,19},{8,28},{9,... | collective-permute-start | bytes 73736 | tf_op jit(solution)/shard_map/ppermute | solution.py:362
  41.2 1.3 %collective-permute-start.12 = (f32[8,768]{1,0:T(8,128)S(1)}, f32[8,768]{1,0:T(8,128)S(1)}, u32[]{:S(2)}, u32[]{:S(2)}) collective-permute-start(f32[8,768]{1,0:T(8,128)S(1)} %shard_map.112.refs_0_), channel_id=1, source_target_pairs={{0,28},{1,29},{2,30},{3,31},{4,24},{5,25},{6,26},{7,27},{8,20},{9,... | collective-permute-start | bytes 73736 | tf_op jit(solution)/shard_map/ppermute | solution.py:362
  42.5 2.7 %shard_map.113 = (bf16[768,2048]{1,0:T(8,128)(2,1)S(1)}, bf16[768,2048]{1,0:T(8,128)(2,1)S(1)}) custom-call(f32[16]{0:T(128)S(1)} %copy-done.10, f32[16,768]{1,0:T(8,128)S(1)} %copy-done.9, f32[16,2048]{1,0:T(8,128)S(1)} %copy-done.5), custom_call_target="tpu_custom_call" | custom-call | flops 1000000 | bytes 1000000 | tf_op jit(solution)/shard_map/pallas_call | solution.py:334
  45.4 0.9 shard_map.114
  46.4 4.3 %collective-permute-start.15 = (f32[8,2048]{1,0:T(8,128)S(1)}, f32[8,2048]{1,0:T(8,128)S(1)}, u32[]{:S(2)}, u32[]{:S(2)}) collective-permute-start(f32[8,2048]{1,0:T(8,128)S(1)} %get-tuple-element.26.refs_0_), channel_id=1, source_target_pairs={{0,3},{1,2},{2,1},{3,0},{4,7},{5,6},{6,5},{7,4},{8,11},{9,10},{10,... | collective-permute-start | bytes 196616 | tf_op jit(solution)/shard_map/ppermute | solution.py:362
  50.7 0.8 collective-permute-done.13.refs_1_
  51.5 3.5 %collective-permute-done.14.refs_2_ = f32[8,2048]{1,0:T(8,128)S(1)} collective-permute-done((f32[8,2048]{1,0:T(8,128)S(1)}, f32[8,2048]{1,0:T(8,128)S(1)}, u32[]{:S(2)}, u32[]{:S(2)}) %collective-permute-start.14) | collective-permute-done | bytes 65568 | tf_op jit(solution)/shard_map/ppermute | solution.py:362
  55.0 1.8 %shard_map.115 = f32[8,768]{1,0:T(8,128)S(1)} custom-call(f32[8,2048]{1,0:T(8,128)S(1)} %get-tuple-element.26.refs_0_, f32[8,2048]{1,0:T(8,128)S(1)} %collective-permute-done.13.refs_1_, f32[8,2048]{1,0:T(8,128)S(1)} %collective-permute-done.14.refs_2_, f32[8,2048]{1,0:T(8,128)S(1)} %collective-permute-done.15.refs_3_, ...), custom_call_target="tpu_custom_call" | custom-call | flops 1000000 | bytes 1000000 | tf_op jit(solution)/shard_map/pallas_call | solution.py:334
  56.9 1.2 %collective-permute-done.16 = f32[8,768]{1,0:T(8,128)S(1)} collective-permute-done((f32[8,768]{1,0:T(8,128)S(1)}, f32[8,768]{1,0:T(8,128)S(1)}, u32[]{:S(2)}, u32[]{:S(2)}) %collective-permute-start.16) | collective-permute-done | bytes 24608 | tf_op jit(solution)/shard_map/ppermute | solution.py:362
  58.1 1.4 %collective-permute-start.17 = (f32[8,768]{1,0:T(8,128)S(1)}, f32[8,768]{1,0:T(8,128)S(1)}, u32[]{:S(2)}, u32[]{:S(2)}) collective-permute-start(f32[8,768]{1,0:T(8,128)S(1)} %add.3.refs_0_), channel_id=1, source_target_pairs={{0,20},{1,21},{2,22},{3,23},{4,16},{5,17},{6,18},{7,19},{8,28},{9,... | collective-permute-start | bytes 73736 | tf_op jit(solution)/shard_map/ppermute | solution.py:362
  59.7 1.3 %collective-permute-start.19 = (f32[8,768]{1,0:T(8,128)S(1)}, f32[8,768]{1,0:T(8,128)S(1)}, u32[]{:S(2)}, u32[]{:S(2)}) collective-permute-start(f32[8,768]{1,0:T(8,128)S(1)} %add.3.refs_0_), channel_id=1, source_target_pairs={{0,28},{1,29},{2,30},{3,31},{4,24},{5,25},{6,26},{7,27},{8,20},{9,... | collective-permute-start | bytes 73736 | tf_op jit(solution)/shard_map/ppermute | solution.py:362
  61.5 1.2 %collective-permute-done.18.refs_2_ = f32[8,768]{1,0:T(8,128)S(1)} collective-permute-done((f32[8,768]{1,0:T(8,128)S(1)}, f32[8,768]{1,0:T(8,128)S(1)}, u32[]{:S(2)}, u32[]{:S(2)}) %collective-permute-start.18) | collective-permute-done | bytes 24608 | tf_op jit(solution)/shard_map/ppermute | solution.py:362
  62.7 1.1 %collective-permute-done.19.refs_3_ = f32[8,768]{1,0:T(8,128)S(1)} collective-permute-done((f32[8,768]{1,0:T(8,128)S(1)}, f32[8,768]{1,0:T(8,128)S(1)}, u32[]{:S(2)}, u32[]{:S(2)}) %collective-permute-start.19) | collective-permute-done | bytes 24608 | tf_op jit(solution)/shard_map/ppermute | solution.py:362
  64.2 1.5 %collective-permute-start.25 = (f32[8,768]{1,0:T(8,128)S(1)}, f32[8,768]{1,0:T(8,128)S(1)}, u32[]{:S(2)}, u32[]{:S(2)}) collective-permute-start(f32[8,768]{1,0:T(8,128)S(1)} %get-tuple-element.29.refs_0_), channel_id=1, source_target_pairs={{0,24},{1,17},{2,18},{3,19},{4,20},{5,21},{6,22},{7,23},{8,16},{9,... | collective-permute-start | bytes 73736 | tf_op jit(solution)/shard_map/ppermute | solution.py:362
  66.3 1.2 %collective-permute-done.25.refs_0_ = f32[8,768]{1,0:T(8,128)S(1)} collective-permute-done((f32[8,768]{1,0:T(8,128)S(1)}, f32[8,768]{1,0:T(8,128)S(1)}, u32[]{:S(2)}, u32[]{:S(2)}) %collective-permute-start.25) | collective-permute-done | bytes 24608 | tf_op jit(solution)/shard_map/ppermute | solution.py:362
  68.4 1.5 %collective-permute-done.26.refs_1_ = f32[8,768]{1,0:T(8,128)S(1)} collective-permute-done((f32[8,768]{1,0:T(8,128)S(1)}, f32[8,768]{1,0:T(8,128)S(1)}, u32[]{:S(2)}, u32[]{:S(2)}) %collective-permute-start.26) | collective-permute-done | bytes 24608 | tf_op jit(solution)/shard_map/ppermute | solution.py:362
  74.7 0.8 collective-permute-done.31.refs_1_
  76.4 4.0 %collective-permute-start.34 = (f32[8,768]{1,0:T(8,128)S(1)}, f32[8,768]{1,0:T(8,128)S(1)}, u32[]{:S(2)}, u32[]{:S(2)}) collective-permute-start(f32[8,768]{1,0:T(8,128)S(1)} %shard_map.125.refs_0_), channel_id=1, source_target_pairs={{0,19},{1,18},{2,17},{3,16},{4,23},{5,22},{6,21},{7,20},{8,27},{9,... | collective-permute-start | bytes 73736 | tf_op jit(solution)/shard_map/ppermute | solution.py:362
  80.5 1.8 %collective-permute-done.34.refs_3_ = f32[8,768]{1,0:T(8,128)S(1)} collective-permute-done((f32[8,768]{1,0:T(8,128)S(1)}, f32[8,768]{1,0:T(8,128)S(1)}, u32[]{:S(2)}, u32[]{:S(2)}) %collective-permute-start.34) | collective-permute-done | bytes 24608 | tf_op jit(solution)/shard_map/ppermute | solution.py:362
  82.3 4.8 %collective-permute-start.35 = (f32[8,768]{1,0:T(8,128)S(1)}, f32[8,768]{1,0:T(8,128)S(1)}, u32[]{:S(2)}, u32[]{:S(2)}) collective-permute-start(f32[8,768]{1,0:T(8,128)S(1)} %shard_map.126.refs_0_), channel_id=1, source_target_pairs={{0,20},{1,21},{2,22},{3,23},{4,16},{5,17},{6,18},{7,19},{8,28},{9,... | collective-permute-start | bytes 73736 | tf_op jit(solution)/shard_map/ppermute | solution.py:362
  87.2 3.6 %collective-permute-start.36 = (f32[8,768]{1,0:T(8,128)S(1)}, f32[8,768]{1,0:T(8,128)S(1)}, u32[]{:S(2)}, u32[]{:S(2)}) collective-permute-start(f32[8,768]{1,0:T(8,128)S(1)} %shard_map.126.refs_0_), channel_id=1, source_target_pairs={{0,24},{1,25},{2,26},{3,27},{4,28},{5,29},{6,30},{7,31},{8,16},{9,... | collective-permute-start | bytes 73736 | tf_op jit(solution)/shard_map/ppermute | solution.py:362
  90.9 1.5 %collective-permute-done.36.refs_2_ = f32[8,768]{1,0:T(8,128)S(1)} collective-permute-done((f32[8,768]{1,0:T(8,128)S(1)}, f32[8,768]{1,0:T(8,128)S(1)}, u32[]{:S(2)}, u32[]{:S(2)}) %collective-permute-start.36) | collective-permute-done | bytes 24608 | tf_op jit(solution)/shard_map/ppermute | solution.py:362
  92.3 2.6 %collective-permute-done.37.refs_3_ = f32[8,768]{1,0:T(8,128)S(1)} collective-permute-done((f32[8,768]{1,0:T(8,128)S(1)}, f32[8,768]{1,0:T(8,128)S(1)}, u32[]{:S(2)}, u32[]{:S(2)}) %collective-permute-start.37) | collective-permute-done | bytes 24608 | tf_op jit(solution)/shard_map/ppermute | solution.py:362
  95.0 0.9 shard_map.127
  (92 shorter events, 16.4 us)
Async XLA Ops:
  5.2 9.2 %collective-permute-start.22 = (f32[128,512]{1,0:T(8,128)S(1)}, f32[128,512]{1,0:T(8,128)S(1)}, u32[]{:S(2)}, u32[]{:S(2)}) collective-permute-start(f32[128,512]{1,0:T(8,128)S(1)} %get-tuple-element.33), channel_id=1, source_target_pairs={{0,16},{1,17},{2,18},{3,19},{4,21},{5,20},{6,22},{7,23},{8,24},{9,... | collective-permute-start | bytes 786440 | tf_op jit(solution)/shard_map/ppermute | solution.py:362
  8.8 1.4 %collective-permute-start.3 = (f32[8,768]{1,0:T(8,128)}, f32[8,768]{1,0:T(8,128)S(1)}, u32[]{:S(2)}, u32[]{:S(2)}) collective-permute-start(f32[8,768]{1,0:T(8,128)} %shard_map.103.refs_2_), channel_id=1, source_target_pairs={{0,16},{1,17},{2,18},{3,19},{4,20},{5,21},{6,22},{7,23},{8,24},{9,... | collective-permute-start | bytes 73736 | tf_op jit(solution)/shard_map/ppermute | solution.py:362
  8.8 2.0 %collective-permute-start = (f32[8,768]{1,0:T(8,128)}, f32[8,768]{1,0:T(8,128)S(1)}, u32[]{:S(2)}, u32[]{:S(2)}) collective-permute-start(f32[8,768]{1,0:T(8,128)} %shard_map.103.refs_2_), channel_id=1, source_target_pairs={{0,16},{1,17},{2,18},{3,19},{4,20},{5,21},{6,22},{7,23},{8,24},{9,... | collective-permute-start | bytes 73736 | tf_op jit(solution)/shard_map/ppermute | solution.py:362
  9.3 1.5 %collective-permute-start.1 = (f32[8,768]{1,0:T(8,128)}, f32[8,768]{1,0:T(8,128)S(1)}, u32[]{:S(2)}, u32[]{:S(2)}) collective-permute-start(f32[8,768]{1,0:T(8,128)} %shard_map.103.refs_2_), channel_id=1, source_target_pairs={{0,16},{1,17},{2,18},{3,19},{4,20},{5,21},{6,22},{7,23},{8,24},{9,... | collective-permute-start | bytes 73736 | tf_op jit(solution)/shard_map/ppermute | solution.py:362
  11.2 1.5 %collective-permute-start.2 = (f32[8,768]{1,0:T(8,128)S(1)}, f32[8,768]{1,0:T(8,128)S(1)}, u32[]{:S(2)}, u32[]{:S(2)}) collective-permute-start(f32[8,768]{1,0:T(8,128)S(1)} %shard_map.105), channel_id=1, source_target_pairs={{0,16},{1,17},{2,18},{3,19},{4,20},{5,21},{6,22},{7,23},{8,28},{9,... | collective-permute-start | bytes 73736 | tf_op jit(solution)/shard_map/ppermute | solution.py:362
  14.3 56.4 %collective-permute-start.24 = (f32[256,256]{1,0:T(8,128)S(1)}, f32[256,256]{1,0:T(8,128)S(1)}, u32[]{:S(2)}, u32[]{:S(2)}) collective-permute-start(f32[256,256]{1,0:T(8,128)S(1)} %get-tuple-element.34), channel_id=1, source_target_pairs={{0,16},{1,17},{2,18},{3,19},{4,21},{5,20},{6,22},{7,23},{8,24},{9,... | collective-permute-start | bytes 786440 | tf_op jit(solution)/shard_map/ppermute | solution.py:362
  14.5 56.2 %collective-permute-start.23 = (f32[128,512]{1,0:T(8,128)S(1)}, f32[128,512]{1,0:T(8,128)S(1)}, u32[]{:S(2)}, u32[]{:S(2)}) collective-permute-start(f32[128,512]{1,0:T(8,128)S(1)} %collective-permute-done.22.mine_ref), channel_id=1, source_target_pairs={{0,16},{1,17},{2,18},{3,19},{4,20},{5,21},{6,22},{7,23},{8,24},{9,... | collective-permute-start | bytes 786440 | tf_op jit(solution)/shard_map/ppermute | solution.py:362
  17.1 22.0 %collective-permute-start.9 = (f32[8,768]{1,0:T(8,128)S(1)}, f32[8,768]{1,0:T(8,128)S(1)}, u32[]{:S(2)}, u32[]{:S(2)}) collective-permute-start(f32[8,768]{1,0:T(8,128)S(1)} %shard_map.111), channel_id=1, source_target_pairs={{0,20},{1,17},{2,18},{3,19},{4,16},{5,21},{6,22},{7,23},{8,24},{9,... | collective-permute-start | bytes 73736 | tf_op jit(solution)/shard_map/ppermute | solution.py:362
  39.5 5.7 %collective-permute-start.10 = (f32[8,768]{1,0:T(8,128)S(1)}, f32[8,768]{1,0:T(8,128)S(1)}, u32[]{:S(2)}, u32[]{:S(2)}) collective-permute-start(f32[8,768]{1,0:T(8,128)S(1)} %shard_map.112.refs_0_), channel_id=1, source_target_pairs={{0,20},{1,21},{2,22},{3,23},{4,16},{5,17},{6,18},{7,19},{8,28},{9,... | collective-permute-start | bytes 73736 | tf_op jit(solution)/shard_map/ppermute | solution.py:362
  41.2 4.0 %collective-permute-start.11 = (f32[8,768]{1,0:T(8,128)S(1)}, f32[8,768]{1,0:T(8,128)S(1)}, u32[]{:S(2)}, u32[]{:S(2)}) collective-permute-start(f32[8,768]{1,0:T(8,128)S(1)} %shard_map.112.refs_0_), channel_id=1, source_target_pairs={{0,24},{1,25},{2,26},{3,27},{4,28},{5,29},{6,30},{7,31},{8,16},{9,... | collective-permute-start | bytes 73736 | tf_op jit(solution)/shard_map/ppermute | solution.py:362
  41.2 4.2 %collective-permute-start.12 = (f32[8,768]{1,0:T(8,128)S(1)}, f32[8,768]{1,0:T(8,128)S(1)}, u32[]{:S(2)}, u32[]{:S(2)}) collective-permute-start(f32[8,768]{1,0:T(8,128)S(1)} %shard_map.112.refs_0_), channel_id=1, source_target_pairs={{0,28},{1,29},{2,30},{3,31},{4,24},{5,25},{6,26},{7,27},{8,20},{9,... | collective-permute-start | bytes 73736 | tf_op jit(solution)/shard_map/ppermute | solution.py:362
  46.3 5.3 %collective-permute-start.13 = (f32[8,2048]{1,0:T(8,128)S(1)}, f32[8,2048]{1,0:T(8,128)S(1)}, u32[]{:S(2)}, u32[]{:S(2)}) collective-permute-start(f32[8,2048]{1,0:T(8,128)S(1)} %get-tuple-element.26.refs_0_), channel_id=1, source_target_pairs={{0,1},{1,0},{2,3},{3,2},{4,5},{5,4},{6,7},{7,6},{8,9},{9,8},{10,11... | collective-permute-start | bytes 196616 | tf_op jit(solution)/shard_map/ppermute | solution.py:362
  46.3 8.7 %collective-permute-start.14 = (f32[8,2048]{1,0:T(8,128)S(1)}, f32[8,2048]{1,0:T(8,128)S(1)}, u32[]{:S(2)}, u32[]{:S(2)}) collective-permute-start(f32[8,2048]{1,0:T(8,128)S(1)} %get-tuple-element.26.refs_0_), channel_id=1, source_target_pairs={{0,2},{1,3},{2,0},{3,1},{4,6},{5,7},{6,4},{7,5},{8,10},{9,11},{10,... | collective-permute-start | bytes 196616 | tf_op jit(solution)/shard_map/ppermute | solution.py:362
  46.4 8.7 %collective-permute-start.15 = (f32[8,2048]{1,0:T(8,128)S(1)}, f32[8,2048]{1,0:T(8,128)S(1)}, u32[]{:S(2)}, u32[]{:S(2)}) collective-permute-start(f32[8,2048]{1,0:T(8,128)S(1)} %get-tuple-element.26.refs_0_), channel_id=1, source_target_pairs={{0,3},{1,2},{2,1},{3,0},{4,7},{5,6},{6,5},{7,4},{8,11},{9,10},{10,... | collective-permute-start | bytes 196616 | tf_op jit(solution)/shard_map/ppermute | solution.py:362
  56.8 1.2 %collective-permute-start.16 = (f32[8,768]{1,0:T(8,128)S(1)}, f32[8,768]{1,0:T(8,128)S(1)}, u32[]{:S(2)}, u32[]{:S(2)}) collective-permute-start(f32[8,768]{1,0:T(8,128)S(1)} %shard_map.115), channel_id=1, source_target_pairs={{0,16},{1,17},{2,18},{3,19},{4,20},{5,21},{6,22},{7,23},{8,24},{9,... | collective-permute-start | bytes 73736 | tf_op jit(solution)/shard_map/ppermute | solution.py:362
  58.1 3.5 %collective-permute-start.17 = (f32[8,768]{1,0:T(8,128)S(1)}, f32[8,768]{1,0:T(8,128)S(1)}, u32[]{:S(2)}, u32[]{:S(2)}) collective-permute-start(f32[8,768]{1,0:T(8,128)S(1)} %add.3.refs_0_), channel_id=1, source_target_pairs={{0,20},{1,21},{2,22},{3,23},{4,16},{5,17},{6,18},{7,19},{8,28},{9,... | collective-permute-start | bytes 73736 | tf_op jit(solution)/shard_map/ppermute | solution.py:362
  59.5 3.3 %collective-permute-start.18 = (f32[8,768]{1,0:T(8,128)S(1)}, f32[8,768]{1,0:T(8,128)S(1)}, u32[]{:S(2)}, u32[]{:S(2)}) collective-permute-start(f32[8,768]{1,0:T(8,128)S(1)} %add.3.refs_0_), channel_id=1, source_target_pairs={{0,24},{1,25},{2,26},{3,27},{4,28},{5,29},{6,30},{7,31},{8,16},{9,... | collective-permute-start | bytes 73736 | tf_op jit(solution)/shard_map/ppermute | solution.py:362
  59.7 4.2 %collective-permute-start.19 = (f32[8,768]{1,0:T(8,128)S(1)}, f32[8,768]{1,0:T(8,128)S(1)}, u32[]{:S(2)}, u32[]{:S(2)}) collective-permute-start(f32[8,768]{1,0:T(8,128)S(1)} %add.3.refs_0_), channel_id=1, source_target_pairs={{0,28},{1,29},{2,30},{3,31},{4,24},{5,25},{6,26},{7,27},{8,20},{9,... | collective-permute-start | bytes 73736 | tf_op jit(solution)/shard_map/ppermute | solution.py:362
  64.2 3.3 %collective-permute-start.25 = (f32[8,768]{1,0:T(8,128)S(1)}, f32[8,768]{1,0:T(8,128)S(1)}, u32[]{:S(2)}, u32[]{:S(2)}) collective-permute-start(f32[8,768]{1,0:T(8,128)S(1)} %get-tuple-element.29.refs_0_), channel_id=1, source_target_pairs={{0,24},{1,17},{2,18},{3,19},{4,20},{5,21},{6,22},{7,23},{8,16},{9,... | collective-permute-start | bytes 73736 | tf_op jit(solution)/shard_map/ppermute | solution.py:362
  65.7 4.2 %collective-permute-start.26 = (f32[8,768]{1,0:T(8,128)S(1)}, f32[8,768]{1,0:T(8,128)S(1)}, u32[]{:S(2)}, u32[]{:S(2)}) collective-permute-start(f32[8,768]{1,0:T(8,128)S(1)} %get-tuple-element.29.refs_0_), channel_id=1, source_target_pairs={{0,28},{1,17},{2,18},{3,19},{4,20},{5,21},{6,22},{7,23},{8,24},{9,... | collective-permute-start | bytes 73736 | tf_op jit(solution)/shard_map/ppermute | solution.py:362
  65.9 5.3 %collective-permute-start.20 = (f32[8,768]{1,0:T(8,128)S(1)}, f32[8,768]{1,0:T(8,128)S(1)}, u32[]{:S(2)}, u32[]{:S(2)}) collective-permute-start(f32[8,768]{1,0:T(8,128)S(1)} %get-tuple-element.29.refs_0_), channel_id=1, source_target_pairs={{0,20},{1,17},{2,18},{3,19},{4,16},{5,21},{6,22},{7,23},{8,24},{9,... | collective-permute-start | bytes 73736 | tf_op jit(solution)/shard_map/ppermute | solution.py:362
  67.5 3.7 %collective-permute-start.21 = (f32[8,768]{1,0:T(8,128)S(1)}, f32[8,768]{1,0:T(8,128)S(1)}, u32[]{:S(2)}, u32[]{:S(2)}) collective-permute-start(f32[8,768]{1,0:T(8,128)S(1)} %get-tuple-element.30), channel_id=1, source_target_pairs={{0,16},{1,17},{2,18},{3,19},{4,21},{5,20},{6,22},{7,23},{8,24},{9,... | collective-permute-start | bytes 73736 | tf_op jit(solution)/shard_map/ppermute | solution.py:362
  70.3 2.1 %collective-permute-start.27 = (f32[8,768]{1,0:T(8,128)S(1)}, f32[8,768]{1,0:T(8,128)S(1)}, u32[]{:S(2)}, u32[]{:S(2)}) collective-permute-start(f32[8,768]{1,0:T(8,128)S(1)} %shard_map.121), channel_id=1, source_target_pairs={{0,16},{1,17},{2,18},{3,19},{4,20},{5,21},{6,22},{7,23},{8,25},{9,... | collective-permute-start | bytes 73736 | tf_op jit(solution)/shard_map/ppermute | solution.py:362
  72.0 1.6 %collective-permute-start.28 = (f32[8,768]{1,0:T(8,128)S(1)}, f32[8,768]{1,0:T(8,128)S(1)}, u32[]{:S(2)}, u32[]{:S(2)}) collective-permute-start(f32[8,768]{1,0:T(8,128)S(1)} %shard_map.120.refs_1_), channel_id=1, source_target_pairs={{0,16},{1,17},{2,18},{3,19},{4,25},{5,21},{6,22},{7,23},{8,24},{9,... | collective-permute-start | bytes 73736 | tf_op jit(solution)/shard_map/ppermute | solution.py:362
  73.4 1.2 %collective-permute-start.30 = (f32[8,768]{1,0:T(8,128)S(1)}, f32[8,768]{1,0:T(8,128)S(1)}, u32[]{:S(2)}, u32[]{:S(2)}) collective-permute-start(f32[8,768]{1,0:T(8,128)S(1)} %shard_map.123), channel_id=1, source_target_pairs={{0,16},{1,17},{2,18},{3,19},{4,20},{5,21},{6,22},{7,23},{8,24},{9,... | collective-permute-start | bytes 73736 | tf_op jit(solution)/shard_map/ppermute | solution.py:362
  74.3 1.2 %collective-permute-start.31 = (f32[8,768]{1,0:T(8,128)S(1)}, f32[8,768]{1,0:T(8,128)S(1)}, u32[]{:S(2)}, u32[]{:S(2)}) collective-permute-start(f32[8,768]{1,0:T(8,128)S(1)} %shard_map.122.refs_2_), channel_id=1, source_target_pairs={{0,16},{1,17},{2,18},{3,19},{4,20},{5,21},{6,22},{7,23},{8,24},{9,... | collective-permute-start | bytes 73736 | tf_op jit(solution)/shard_map/ppermute | solution.py:362
  76.2 4.1 %collective-permute-start.32 = (f32[8,768]{1,0:T(8,128)S(1)}, f32[8,768]{1,0:T(8,128)S(1)}, u32[]{:S(2)}, u32[]{:S(2)}) collective-permute-start(f32[8,768]{1,0:T(8,128)S(1)} %shard_map.125.refs_0_), channel_id=1, source_target_pairs={{0,17},{1,16},{2,19},{3,18},{4,21},{5,20},{6,23},{7,22},{8,25},{9,... | collective-permute-start | bytes 73736 | tf_op jit(solution)/shard_map/ppermute | solution.py:362
  76.3 4.2 %collective-permute-start.33 = (f32[8,768]{1,0:T(8,128)S(1)}, f32[8,768]{1,0:T(8,128)S(1)}, u32[]{:S(2)}, u32[]{:S(2)}) collective-permute-start(f32[8,768]{1,0:T(8,128)S(1)} %shard_map.125.refs_0_), channel_id=1, source_target_pairs={{0,18},{1,19},{2,16},{3,17},{4,22},{5,23},{6,20},{7,21},{8,26},{9,... | collective-permute-start | bytes 73736 | tf_op jit(solution)/shard_map/ppermute | solution.py:362
  76.4 5.9 %collective-permute-start.34 = (f32[8,768]{1,0:T(8,128)S(1)}, f32[8,768]{1,0:T(8,128)S(1)}, u32[]{:S(2)}, u32[]{:S(2)}) collective-permute-start(f32[8,768]{1,0:T(8,128)S(1)} %shard_map.125.refs_0_), channel_id=1, source_target_pairs={{0,19},{1,18},{2,17},{3,16},{4,23},{5,22},{6,21},{7,20},{8,27},{9,... | collective-permute-start | bytes 73736 | tf_op jit(solution)/shard_map/ppermute | solution.py:362
  82.3 8.6 %collective-permute-start.35 = (f32[8,768]{1,0:T(8,128)S(1)}, f32[8,768]{1,0:T(8,128)S(1)}, u32[]{:S(2)}, u32[]{:S(2)}) collective-permute-start(f32[8,768]{1,0:T(8,128)S(1)} %shard_map.126.refs_0_), channel_id=1, source_target_pairs={{0,20},{1,21},{2,22},{3,23},{4,16},{5,17},{6,18},{7,19},{8,28},{9,... | collective-permute-start | bytes 73736 | tf_op jit(solution)/shard_map/ppermute | solution.py:362
  87.2 5.2 %collective-permute-start.36 = (f32[8,768]{1,0:T(8,128)S(1)}, f32[8,768]{1,0:T(8,128)S(1)}, u32[]{:S(2)}, u32[]{:S(2)}) collective-permute-start(f32[8,768]{1,0:T(8,128)S(1)} %shard_map.126.refs_0_), channel_id=1, source_target_pairs={{0,24},{1,25},{2,26},{3,27},{4,28},{5,29},{6,30},{7,31},{8,16},{9,... | collective-permute-start | bytes 73736 | tf_op jit(solution)/shard_map/ppermute | solution.py:362
  90.8 4.2 %collective-permute-start.37 = (f32[8,768]{1,0:T(8,128)S(1)}, f32[8,768]{1,0:T(8,128)S(1)}, u32[]{:S(2)}, u32[]{:S(2)}) collective-permute-start(f32[8,768]{1,0:T(8,128)S(1)} %shard_map.126.refs_0_), channel_id=1, source_target_pairs={{0,28},{1,29},{2,30},{3,31},{4,24},{5,25},{6,26},{7,27},{8,20},{9,... | collective-permute-start | bytes 73736 | tf_op jit(solution)/shard_map/ppermute | solution.py:362
  (17 other events, 157.1 us)

commit v8 on v6

--- a/solution.py
+++ b/solution.py
@@ -119,7 +119,7 @@
 
 
 def lower_kernel(inv_ref, *refs):
-    tri_refs, (out_ref, half_ref, rest_ref) = refs[:-3], refs[-3:]
+    tri_refs, out_ref, half_ref = refs[:-2], refs[-2], refs[-1]
     held, order = inv_ref.shape[0], inv_ref.shape[1]
     tri = dict(zip(blocks_of(held), tri_refs))
     found = {(n, n): inv_ref[n] for n in range(held)}
@@ -133,9 +133,7 @@
             out_ref[:, at * order : (at + 1) * order] = found[r, c]
     tall = half_ref.shape[0]
     at = lax.rem(lax.axis_index("dp"), 2) * tall
-    split = half_ref.shape[1]
-    half_ref[...] = out_ref[pl.ds(pl.multiple_of(at, tall), tall), :split]
-    rest_ref[...] = out_ref[:, split:]
+    half_ref[...] = out_ref[pl.ds(pl.multiple_of(at, tall), tall), :]
 
 
 def pair_kernel(factor_ref, high_ref, low_ref):
@@ -158,11 +156,14 @@
     out_ref[...] = out
 
 
-def merge_kernel(mine_ref, other_ref, rest_ref, inv_ref, high_out, low_out):
+def join_kernel(at, one_ref, other_ref, out_ref):
+    out_ref[...] = jnp.where(lax.axis_index("crow") == at, other_ref[...], one_ref[...])
+
+
+def merge_kernel(mine_ref, other_ref, inv_ref, high_out, low_out):
     odd = lax.rem(lax.axis_index("dp"), 2) == 1
     mine, other = mine_ref[...], other_ref[...]
     low = jnp.concatenate([jnp.where(odd, mine, other), jnp.where(odd, other, mine)], axis=0)
-    low = jnp.concatenate([low, rest_ref[...]], axis=1)
     store_turned(low, inv_ref, high_out, low_out)
 
 
@@ -398,11 +399,7 @@
     (piece,) = with_tri(first_kernel, [part], direction, block_inv, limit=58)
     found = {last: piece}
     spots = len(blocks_of(held)) * order
-    low, half, rest = with_tri(
-        lower_kernel,
-        [shaped(order, spots), shaped(order // 2, spots - order), shaped(order, order)],
-        block_inv,
-    )
+    low, half = with_tri(lower_kernel, [shaped(order, spots), shaped(order // 2, spots)], block_inv)
     wide = jax.ShapeDtypeStruct((width, width), jnp.bfloat16)
     high_f, low_f = call(pair_kernel, [wide, wide], factor)
     turned_f = call(turn_factor_kernel, [wide, wide], factor)
@@ -452,7 +449,9 @@
 
     parts = [own] + shifts(own, "crow")
     beside = [((n, n), (n, n - 1)) for n in range(1, crow)]
-    half = move(half, *beside)
+    early = move(half, *beside[: last - 2], beside[last - 1])
+    late = move(half, beside[last - 2])
+    half = call(functools.partial(join_kernel, last - 1), shaped(*half.shape), early, late)
     mine, images = call(image_kernel, [part, shaped(rows, samples)], *parts, high_k, low_k, limit=16)
     images = [images] + shifts(images, "ccol", 0)
     summed = call(normal_kernel, part, *images, high_k, low_k, limit=16)
@@ -461,12 +460,11 @@
     else:
         summed = lax.psum(summed, "dp")
     parts = [summed] + shifts(summed, "crow")
-    rest = move(rest, *beside)
     scale = 1.0 / (samples * dp * crow)
     source, image = call(
         functools.partial(source_kernel, scale, order), [part, part], mine, *parts, *turned
     )
-    near = call(merge_kernel, [wide, wide], half, move(half), rest, block_inv)
+    near = call(merge_kernel, [wide, wide], half, move(half), block_inv)
     done = [image]
     places = [(0, 0)]
     side = []
@@ -514,6 +512,4 @@
         P(),
         P(),
     )
-    return jax.shard_map(
-        step_of, mesh=mesh, in_specs=placed, out_specs=(P(), P(), P()), check_vma=False
-    )
+    return jax.shard_map(step_of, mesh=mesh, in_specs=placed, out_specs=(P(), P(), P()), check_vma=False)

time: 93 us -> 99.7 us (1.072)
  starting transfers between devices: 44.1 us -> 48.7 us
  waiting for transfers between devices: 26.3 us -> 28.4 us
    ppermute x38, starting transfers between devices: 44.1 us -> 48.7 us  [permute(): return lax.ppermute(value, ('dp', 'crow', 'ccol'), perm)]
    ppermute x38, waiting for transfers between devices: 26.3 us -> 28.4 us  [permute(): return lax.ppermute(value, ('dp', 'crow', 'ccol'), perm)]
    pallas_call x25 -> x26, Pallas kernels: 18.7 us -> 18.7 us  [call(): pl.pallas_call(kernel, out_shape=outs, compiler_params=pltpu.CompilerPara...]
  transfers between devices with their start and end apart: 38 -> 38, of which waited for: 22 -> 24; matrix products, arithmetic and copies ran while one was open for 0% -> 0% of each run, Pallas kernels for 16% -> 15%
where the time goes in v8:
time: 99.7 us; the launch traced here: 99.5 us
  starting transfers between devices  48.7 us (49%)
  waiting for transfers between devices  28.4 us (28%)
  Pallas kernels  18.7 us (19%)
  local copies, waits for them, and re-layouts  2.84 us (3%)
    ppermute x38, starting transfers between devices, permute(): return lax.ppermute(value, ('dp', 'crow', 'ccol'), perm)  48.7 us
    ppermute x38, waiting for transfers between devices, permute(): return lax.ppermute(value, ('dp', 'crow', 'ccol'), perm)  28.4 us
    pallas_call x26, Pallas kernels, call(): pl.pallas_call(kernel, out_shape=outs, compiler_params=pltpu.CompilerPara...  18.7 us
    unnamed x22, local copies, waits for them, and re-layouts  2.84 us
  transfers between devices with their start and end apart: 38, of which 24 were waited for; matrix products, arithmetic and copies ran while one was open for 0% of the time, Pallas kernels for 15%

profile of v8, /device:TPU:0, one launch (start us, length us, event | category | flops | bytes accessed | tf_op | source)
XLA Modules:
  0.0 99.5 jit_solution(8895001902399589758)
XLA Ops:
  0.6 1.7 %copy-done = f32[768,768]{1,0:T(8,128)S(1)} copy-done((f32[768,768]{1,0:T(8,128)S(1)}, f32[768,768]{1,0:T(8,128)}, u32[]{:S(2)}) %copy-start) | copy-done | bytes 2359320
  2.3 1.1 %copy-done.2 = f32[3,256,256]{2,1,0:T(8,128)S(1)} copy-done((f32[3,256,256]{2,1,0:T(8,128)S(1)}, f32[3,256,256]{2,1,0:T(8,128)}, u32[]{:S(2)}) %copy-start.2) | copy-done | bytes 786456
  3.4 1.8 %shard_map.107 = (f32[256,768]{1,0:T(8,128)S(1)}, f32[128,768]{1,0:T(8,128)S(1)}) custom-call(f32[3,256,256]{2,1,0:T(8,128)S(1)} %copy-done.2, f32[768,768]{1,0:T(8,128)S(1)} %copy-done, f32[768,768]{1,0:T(8,128)S(1)} %copy-done, f32[768,768]{1,0:T(8,128)S(1)} %copy-done), custom_call_target="tpu_custom_call" | custom-call | flops 1000000 | bytes 1000000 | tf_op jit(solution)/shard_map/pallas_call | solution.py:336
  5.9 1.3 %collective-permute-done.22.one_ref = f32[128,768]{1,0:T(8,128)S(1)} collective-permute-done((f32[128,768]{1,0:T(8,128)S(1)}, f32[128,768]{1,0:T(8,128)S(1)}, u32[]{:S(2)}, u32[]{:S(2)}) %collective-permute-start.22) | collective-permute-done | bytes 393248 | tf_op jit(solution)/shard_map/ppermute | solution.py:364
  8.2 3.0 %shard_map.103.refs_2_ = f32[8,768]{1,0:T(8,128)} custom-call(f32[8,3072]{1,0:T(8,128)} %direction_ref.9, f32[3,256,256]{2,1,0:T(8,128)} %inv_ref.13, f32[768,768]{1,0:T(8,128)} %factor_ref.3, f32[768,768]{1,0:T(8,128)} %factor_ref.3, f32[768,768]{1,0:T(8,128)} %factor_ref.3), custom_call_target="tpu_custom_call" | custom-call | flops 1000000 | bytes 1000000 | tf_op jit(solution)/shard_map/pallas_call | solution.py:336
  16.7 0.8 collective-permute-done.7.sub_ref.refs_0_
  19.6 22.3 %collective-permute-start.9 = (f32[8,768]{1,0:T(8,128)S(1)}, f32[8,768]{1,0:T(8,128)S(1)}, u32[]{:S(2)}, u32[]{:S(2)}) collective-permute-start(f32[8,768]{1,0:T(8,128)S(1)} %shard_map.111), channel_id=1, source_target_pairs={{0,20},{1,17},{2,18},{3,19},{4,16},{5,21},{6,22},{7,23},{8,24},{9,... | collective-permute-start | bytes 73736 | tf_op jit(solution)/shard_map/ppermute | solution.py:364
  41.8 1.5 %collective-permute-done.9.sub_ref = f32[8,768]{1,0:T(8,128)S(1)} collective-permute-done((f32[8,768]{1,0:T(8,128)S(1)}, f32[8,768]{1,0:T(8,128)S(1)}, u32[]{:S(2)}, u32[]{:S(2)}) %collective-permute-start.9) | collective-permute-done | bytes 24608 | tf_op jit(solution)/shard_map/ppermute | solution.py:364
  43.7 1.7 %collective-permute-start.10 = (f32[8,768]{1,0:T(8,128)S(1)}, f32[8,768]{1,0:T(8,128)S(1)}, u32[]{:S(2)}, u32[]{:S(2)}) collective-permute-start(f32[8,768]{1,0:T(8,128)S(1)} %shard_map.112.refs_0_), channel_id=1, source_target_pairs={{0,20},{1,21},{2,22},{3,23},{4,16},{5,17},{6,18},{7,19},{8,28},{9,... | collective-permute-start | bytes 73736 | tf_op jit(solution)/shard_map/ppermute | solution.py:364
  45.5 1.5 %collective-permute-start.12 = (f32[8,768]{1,0:T(8,128)S(1)}, f32[8,768]{1,0:T(8,128)S(1)}, u32[]{:S(2)}, u32[]{:S(2)}) collective-permute-start(f32[8,768]{1,0:T(8,128)S(1)} %shard_map.112.refs_0_), channel_id=1, source_target_pairs={{0,28},{1,29},{2,30},{3,31},{4,24},{5,25},{6,26},{7,27},{8,20},{9,... | collective-permute-start | bytes 73736 | tf_op jit(solution)/shard_map/ppermute | solution.py:364
  47.0 2.5 %shard_map.113 = (bf16[768,2048]{1,0:T(8,128)(2,1)S(1)}, bf16[768,2048]{1,0:T(8,128)(2,1)S(1)}) custom-call(f32[16]{0:T(128)S(1)} %copy-done.10, f32[16,768]{1,0:T(8,128)S(1)} %copy-done.9, f32[16,2048]{1,0:T(8,128)S(1)} %copy-done.5), custom_call_target="tpu_custom_call" | custom-call | flops 1000000 | bytes 1000000 | tf_op jit(solution)/shard_map/pallas_call | solution.py:336
  49.6 0.9 shard_map.114
  50.6 4.3 %collective-permute-start.15 = (f32[8,2048]{1,0:T(8,128)S(1)}, f32[8,2048]{1,0:T(8,128)S(1)}, u32[]{:S(2)}, u32[]{:S(2)}) collective-permute-start(f32[8,2048]{1,0:T(8,128)S(1)} %get-tuple-element.25.refs_0_), channel_id=1, source_target_pairs={{0,3},{1,2},{2,1},{3,0},{4,7},{5,6},{6,5},{7,4},{8,11},{9,10},{10,... | collective-permute-start | bytes 196616 | tf_op jit(solution)/shard_map/ppermute | solution.py:364
  54.9 1.0 %collective-permute-done.13.refs_1_ = f32[8,2048]{1,0:T(8,128)S(1)} collective-permute-done((f32[8,2048]{1,0:T(8,128)S(1)}, f32[8,2048]{1,0:T(8,128)S(1)}, u32[]{:S(2)}, u32[]{:S(2)}) %collective-permute-start.13) | collective-permute-done | bytes 65568 | tf_op jit(solution)/shard_map/ppermute | solution.py:364
  55.9 3.3 %collective-permute-done.14.refs_2_ = f32[8,2048]{1,0:T(8,128)S(1)} collective-permute-done((f32[8,2048]{1,0:T(8,128)S(1)}, f32[8,2048]{1,0:T(8,128)S(1)}, u32[]{:S(2)}, u32[]{:S(2)}) %collective-permute-start.14) | collective-permute-done | bytes 65568 | tf_op jit(solution)/shard_map/ppermute | solution.py:364
  59.3 1.8 %shard_map.115 = f32[8,768]{1,0:T(8,128)S(1)} custom-call(f32[8,2048]{1,0:T(8,128)S(1)} %get-tuple-element.25.refs_0_, f32[8,2048]{1,0:T(8,128)S(1)} %collective-permute-done.13.refs_1_, f32[8,2048]{1,0:T(8,128)S(1)} %collective-permute-done.14.refs_2_, f32[8,2048]{1,0:T(8,128)S(1)} %collective-permute-done.15.refs_3_, ...), custom_call_target="tpu_custom_call" | custom-call | flops 1000000 | bytes 1000000 | tf_op jit(solution)/shard_map/pallas_call | solution.py:336
  61.1 1.2 %collective-permute-done.16 = f32[8,768]{1,0:T(8,128)S(1)} collective-permute-done((f32[8,768]{1,0:T(8,128)S(1)}, f32[8,768]{1,0:T(8,128)S(1)}, u32[]{:S(2)}, u32[]{:S(2)}) %collective-permute-start.16) | collective-permute-done | bytes 24608 | tf_op jit(solution)/shard_map/ppermute | solution.py:364
  62.3 1.4 %collective-permute-start.17 = (f32[8,768]{1,0:T(8,128)S(1)}, f32[8,768]{1,0:T(8,128)S(1)}, u32[]{:S(2)}, u32[]{:S(2)}) collective-permute-start(f32[8,768]{1,0:T(8,128)S(1)} %add.3.refs_0_), channel_id=1, source_target_pairs={{0,20},{1,21},{2,22},{3,23},{4,16},{5,17},{6,18},{7,19},{8,28},{9,... | collective-permute-start | bytes 73736 | tf_op jit(solution)/shard_map/ppermute | solution.py:364
  64.1 1.2 %collective-permute-start.19 = (f32[8,768]{1,0:T(8,128)S(1)}, f32[8,768]{1,0:T(8,128)S(1)}, u32[]{:S(2)}, u32[]{:S(2)}) collective-permute-start(f32[8,768]{1,0:T(8,128)S(1)} %add.3.refs_0_), channel_id=1, source_target_pairs={{0,28},{1,29},{2,30},{3,31},{4,24},{5,25},{6,26},{7,27},{8,20},{9,... | collective-permute-start | bytes 73736 | tf_op jit(solution)/shard_map/ppermute | solution.py:364
  65.8 1.1 %collective-permute-done.18.refs_2_ = f32[8,768]{1,0:T(8,128)S(1)} collective-permute-done((f32[8,768]{1,0:T(8,128)S(1)}, f32[8,768]{1,0:T(8,128)S(1)}, u32[]{:S(2)}, u32[]{:S(2)}) %collective-permute-start.18) | collective-permute-done | bytes 24608 | tf_op jit(solution)/shard_map/ppermute | solution.py:364
  66.9 1.3 %collective-permute-done.19.refs_3_ = f32[8,768]{1,0:T(8,128)S(1)} collective-permute-done((f32[8,768]{1,0:T(8,128)S(1)}, f32[8,768]{1,0:T(8,128)S(1)}, u32[]{:S(2)}, u32[]{:S(2)}) %collective-permute-start.19) | collective-permute-done | bytes 24608 | tf_op jit(solution)/shard_map/ppermute | solution.py:364
  68.6 1.3 %collective-permute-start.25 = (f32[8,768]{1,0:T(8,128)S(1)}, f32[8,768]{1,0:T(8,128)S(1)}, u32[]{:S(2)}, u32[]{:S(2)}) collective-permute-start(f32[8,768]{1,0:T(8,128)S(1)} %get-tuple-element.28.refs_0_), channel_id=1, source_target_pairs={{0,24},{1,17},{2,18},{3,19},{4,20},{5,21},{6,22},{7,23},{8,16},{9,... | collective-permute-start | bytes 73736 | tf_op jit(solution)/shard_map/ppermute | solution.py:364
  71.8 2.2 %collective-permute-done.26.refs_1_ = f32[8,768]{1,0:T(8,128)S(1)} collective-permute-done((f32[8,768]{1,0:T(8,128)S(1)}, f32[8,768]{1,0:T(8,128)S(1)}, u32[]{:S(2)}, u32[]{:S(2)}) %collective-permute-start.26) | collective-permute-done | bytes 24608 | tf_op jit(solution)/shard_map/ppermute | solution.py:364
  76.2 1.0 %collective-permute-start.28 = (f32[8,768]{1,0:T(8,128)S(1)}, f32[8,768]{1,0:T(8,128)S(1)}, u32[]{:S(2)}, u32[]{:S(2)}) collective-permute-start(f32[8,768]{1,0:T(8,128)S(1)} %shard_map.121.refs_1_), channel_id=1, source_target_pairs={{0,20},{1,17},{2,18},{3,19},{4,25},{5,21},{6,22},{7,23},{8,24},{9,... | collective-permute-start | bytes 73736 | tf_op jit(solution)/shard_map/ppermute | solution.py:364
  77.9 2.4 %collective-permute-done.28.refs_1_ = f32[8,768]{1,0:T(8,128)S(1)} collective-permute-done((f32[8,768]{1,0:T(8,128)S(1)}, f32[8,768]{1,0:T(8,128)S(1)}, u32[]{:S(2)}, u32[]{:S(2)}) %collective-permute-start.28) | collective-permute-done | bytes 24608 | tf_op jit(solution)/shard_map/ppermute | solution.py:364
  83.0 3.2 %collective-permute-start.33 = (f32[8,768]{1,0:T(8,128)S(1)}, f32[8,768]{1,0:T(8,128)S(1)}, u32[]{:S(2)}, u32[]{:S(2)}) collective-permute-start(f32[8,768]{1,0:T(8,128)S(1)} %shard_map.126.refs_0_), channel_id=1, source_target_pairs={{0,18},{1,19},{2,16},{3,17},{4,22},{5,23},{6,20},{7,21},{8,26},{9,... | collective-permute-start | bytes 73736 | tf_op jit(solution)/shard_map/ppermute | solution.py:364
  86.3 1.2 %collective-permute-start.34 = (f32[8,768]{1,0:T(8,128)S(1)}, f32[8,768]{1,0:T(8,128)S(1)}, u32[]{:S(2)}, u32[]{:S(2)}) collective-permute-start(f32[8,768]{1,0:T(8,128)S(1)} %shard_map.126.refs_0_), channel_id=1, source_target_pairs={{0,19},{1,18},{2,17},{3,16},{4,23},{5,22},{6,21},{7,20},{8,27},{9,... | collective-permute-start | bytes 73736 | tf_op jit(solution)/shard_map/ppermute | solution.py:364
  87.8 3.6 %collective-permute-done.34.refs_3_ = f32[8,768]{1,0:T(8,128)S(1)} collective-permute-done((f32[8,768]{1,0:T(8,128)S(1)}, f32[8,768]{1,0:T(8,128)S(1)}, u32[]{:S(2)}, u32[]{:S(2)}) %collective-permute-start.34) | collective-permute-done | bytes 24608 | tf_op jit(solution)/shard_map/ppermute | solution.py:364
  91.5 3.0 %collective-permute-start.36 = (f32[8,768]{1,0:T(8,128)S(1)}, f32[8,768]{1,0:T(8,128)S(1)}, u32[]{:S(2)}, u32[]{:S(2)}) collective-permute-start(f32[8,768]{1,0:T(8,128)S(1)} %shard_map.127.refs_0_), channel_id=1, source_target_pairs={{0,24},{1,25},{2,26},{3,27},{4,28},{5,29},{6,30},{7,31},{8,16},{9,... | collective-permute-start | bytes 73736 | tf_op jit(solution)/shard_map/ppermute | solution.py:364
  94.7 1.2 %collective-permute-done.36.refs_2_ = f32[8,768]{1,0:T(8,128)S(1)} collective-permute-done((f32[8,768]{1,0:T(8,128)S(1)}, f32[8,768]{1,0:T(8,128)S(1)}, u32[]{:S(2)}, u32[]{:S(2)}) %collective-permute-start.36) | collective-permute-done | bytes 24608 | tf_op jit(solution)/shard_map/ppermute | solution.py:364
  96.0 2.6 %collective-permute-done.37.refs_3_ = f32[8,768]{1,0:T(8,128)S(1)} collective-permute-done((f32[8,768]{1,0:T(8,128)S(1)}, f32[8,768]{1,0:T(8,128)S(1)}, u32[]{:S(2)}, u32[]{:S(2)}) %collective-permute-start.37) | collective-permute-done | bytes 24608 | tf_op jit(solution)/shard_map/ppermute | solution.py:364
  98.6 0.9 shard_map.128
  (93 shorter events, 19.1 us)
Async XLA Ops:
  5.3 1.9 %collective-permute-start.22 = (f32[128,768]{1,0:T(8,128)S(1)}, f32[128,768]{1,0:T(8,128)S(1)}, u32[]{:S(2)}, u32[]{:S(2)}) collective-permute-start(f32[128,768]{1,0:T(8,128)S(1)} %get-tuple-element.32), channel_id=1, source_target_pairs={{0,16},{1,17},{2,18},{3,19},{4,21},{5,20},{6,22},{7,23},{8,24},{9,... | collective-permute-start | bytes 1179656 | tf_op jit(solution)/shard_map/ppermute | solution.py:364
  5.8 1.9 %collective-permute-start.23 = (f32[128,768]{1,0:T(8,128)S(1)}, f32[128,768]{1,0:T(8,128)S(1)}, u32[]{:S(2)}, u32[]{:S(2)}) collective-permute-start(f32[128,768]{1,0:T(8,128)S(1)} %get-tuple-element.32), channel_id=1, source_target_pairs={{0,16},{1,17},{2,18},{3,19},{4,20},{5,21},{6,22},{7,23},{8,24},{9,... | collective-permute-start | bytes 1179656 | tf_op jit(solution)/shard_map/ppermute | solution.py:364
  7.8 67.0 %collective-permute-start.24 = (f32[128,768]{1,0:T(8,128)S(1)}, f32[128,768]{1,0:T(8,128)S(1)}, u32[]{:S(2)}, u32[]{:S(2)}) collective-permute-start(f32[128,768]{1,0:T(8,128)S(1)} %shard_map.119.mine_ref), channel_id=1, source_target_pairs={{0,16},{1,17},{2,18},{3,19},{4,20},{5,21},{6,22},{7,23},{8,24},{9,... | collective-permute-start | bytes 1179656 | tf_op jit(solution)/shard_map/ppermute | solution.py:364
  11.2 1.4 %collective-permute-start.3 = (f32[8,768]{1,0:T(8,128)}, f32[8,768]{1,0:T(8,128)S(1)}, u32[]{:S(2)}, u32[]{:S(2)}) collective-permute-start(f32[8,768]{1,0:T(8,128)} %shard_map.103.refs_2_), channel_id=1, source_target_pairs={{0,16},{1,17},{2,18},{3,19},{4,20},{5,21},{6,22},{7,31},{8,24},{9,... | collective-permute-start | bytes 73736 | tf_op jit(solution)/shard_map/ppermute | solution.py:364
  11.3 1.9 %collective-permute-start = (f32[8,768]{1,0:T(8,128)}, f32[8,768]{1,0:T(8,128)S(1)}, u32[]{:S(2)}, u32[]{:S(2)}) collective-permute-start(f32[8,768]{1,0:T(8,128)} %shard_map.103.refs_2_), channel_id=1, source_target_pairs={{0,16},{1,17},{2,18},{3,19},{4,20},{5,21},{6,22},{7,23},{8,24},{9,... | collective-permute-start | bytes 73736 | tf_op jit(solution)/shard_map/ppermute | solution.py:364
  11.7 1.5 %collective-permute-start.1 = (f32[8,768]{1,0:T(8,128)}, f32[8,768]{1,0:T(8,128)S(1)}, u32[]{:S(2)}, u32[]{:S(2)}) collective-permute-start(f32[8,768]{1,0:T(8,128)} %shard_map.103.refs_2_), channel_id=1, source_target_pairs={{0,16},{1,17},{2,18},{3,19},{4,20},{5,21},{6,31},{7,23},{8,24},{9,... | collective-permute-start | bytes 73736 | tf_op jit(solution)/shard_map/ppermute | solution.py:364
  13.6 1.5 %collective-permute-start.2 = (f32[8,768]{1,0:T(8,128)S(1)}, f32[8,768]{1,0:T(8,128)S(1)}, u32[]{:S(2)}, u32[]{:S(2)}) collective-permute-start(f32[8,768]{1,0:T(8,128)S(1)} %shard_map.105), channel_id=1, source_target_pairs={{0,16},{1,29},{2,18},{3,28},{4,20},{5,21},{6,22},{7,23},{8,19},{9,... | collective-permute-start | bytes 73736 | tf_op jit(solution)/shard_map/ppermute | solution.py:364
  19.6 23.8 %collective-permute-start.9 = (f32[8,768]{1,0:T(8,128)S(1)}, f32[8,768]{1,0:T(8,128)S(1)}, u32[]{:S(2)}, u32[]{:S(2)}) collective-permute-start(f32[8,768]{1,0:T(8,128)S(1)} %shard_map.111), channel_id=1, source_target_pairs={{0,20},{1,17},{2,18},{3,19},{4,16},{5,21},{6,22},{7,23},{8,24},{9,... | collective-permute-start | bytes 73736 | tf_op jit(solution)/shard_map/ppermute | solution.py:364
  43.7 5.8 %collective-permute-start.10 = (f32[8,768]{1,0:T(8,128)S(1)}, f32[8,768]{1,0:T(8,128)S(1)}, u32[]{:S(2)}, u32[]{:S(2)}) collective-permute-start(f32[8,768]{1,0:T(8,128)S(1)} %shard_map.112.refs_0_), channel_id=1, source_target_pairs={{0,20},{1,21},{2,22},{3,23},{4,16},{5,17},{6,18},{7,19},{8,28},{9,... | collective-permute-start | bytes 73736 | tf_op jit(solution)/shard_map/ppermute | solution.py:364
  45.5 4.1 %collective-permute-start.11 = (f32[8,768]{1,0:T(8,128)S(1)}, f32[8,768]{1,0:T(8,128)S(1)}, u32[]{:S(2)}, u32[]{:S(2)}) collective-permute-start(f32[8,768]{1,0:T(8,128)S(1)} %shard_map.112.refs_0_), channel_id=1, source_target_pairs={{0,24},{1,25},{2,26},{3,27},{4,28},{5,29},{6,30},{7,31},{8,16},{9,... | collective-permute-start | bytes 73736 | tf_op jit(solution)/shard_map/ppermute | solution.py:364
  45.5 4.2 %collective-permute-start.12 = (f32[8,768]{1,0:T(8,128)S(1)}, f32[8,768]{1,0:T(8,128)S(1)}, u32[]{:S(2)}, u32[]{:S(2)}) collective-permute-start(f32[8,768]{1,0:T(8,128)S(1)} %shard_map.112.refs_0_), channel_id=1, source_target_pairs={{0,28},{1,29},{2,30},{3,31},{4,24},{5,25},{6,26},{7,27},{8,20},{9,... | collective-permute-start | bytes 73736 | tf_op jit(solution)/shard_map/ppermute | solution.py:364
  50.5 5.4 %collective-permute-start.13 = (f32[8,2048]{1,0:T(8,128)S(1)}, f32[8,2048]{1,0:T(8,128)S(1)}, u32[]{:S(2)}, u32[]{:S(2)}) collective-permute-start(f32[8,2048]{1,0:T(8,128)S(1)} %get-tuple-element.25.refs_0_), channel_id=1, source_target_pairs={{0,1},{1,0},{2,3},{3,2},{4,5},{5,4},{6,7},{7,6},{8,9},{9,8},{10,11... | collective-permute-start | bytes 196616 | tf_op jit(solution)/shard_map/ppermute | solution.py:364
  50.5 8.7 %collective-permute-start.14 = (f32[8,2048]{1,0:T(8,128)S(1)}, f32[8,2048]{1,0:T(8,128)S(1)}, u32[]{:S(2)}, u32[]{:S(2)}) collective-permute-start(f32[8,2048]{1,0:T(8,128)S(1)} %get-tuple-element.25.refs_0_), channel_id=1, source_target_pairs={{0,2},{1,3},{2,0},{3,1},{4,6},{5,7},{6,4},{7,5},{8,10},{9,11},{10,... | collective-permute-start | bytes 196616 | tf_op jit(solution)/shard_map/ppermute | solution.py:364
  50.6 8.7 %collective-permute-start.15 = (f32[8,2048]{1,0:T(8,128)S(1)}, f32[8,2048]{1,0:T(8,128)S(1)}, u32[]{:S(2)}, u32[]{:S(2)}) collective-permute-start(f32[8,2048]{1,0:T(8,128)S(1)} %get-tuple-element.25.refs_0_), channel_id=1, source_target_pairs={{0,3},{1,2},{2,1},{3,0},{4,7},{5,6},{6,5},{7,4},{8,11},{9,10},{10,... | collective-permute-start | bytes 196616 | tf_op jit(solution)/shard_map/ppermute | solution.py:364
  61.1 1.2 %collective-permute-start.16 = (f32[8,768]{1,0:T(8,128)S(1)}, f32[8,768]{1,0:T(8,128)S(1)}, u32[]{:S(2)}, u32[]{:S(2)}) collective-permute-start(f32[8,768]{1,0:T(8,128)S(1)} %shard_map.115), channel_id=1, source_target_pairs={{0,16},{1,17},{2,18},{3,19},{4,20},{5,21},{6,22},{7,23},{8,24},{9,... | collective-permute-start | bytes 73736 | tf_op jit(solution)/shard_map/ppermute | solution.py:364
  62.3 3.5 %collective-permute-start.17 = (f32[8,768]{1,0:T(8,128)S(1)}, f32[8,768]{1,0:T(8,128)S(1)}, u32[]{:S(2)}, u32[]{:S(2)}) collective-permute-start(f32[8,768]{1,0:T(8,128)S(1)} %add.3.refs_0_), channel_id=1, source_target_pairs={{0,20},{1,21},{2,22},{3,23},{4,16},{5,17},{6,18},{7,19},{8,28},{9,... | collective-permute-start | bytes 73736 | tf_op jit(solution)/shard_map/ppermute | solution.py:364
  63.7 3.3 %collective-permute-start.18 = (f32[8,768]{1,0:T(8,128)S(1)}, f32[8,768]{1,0:T(8,128)S(1)}, u32[]{:S(2)}, u32[]{:S(2)}) collective-permute-start(f32[8,768]{1,0:T(8,128)S(1)} %add.3.refs_0_), channel_id=1, source_target_pairs={{0,24},{1,25},{2,26},{3,27},{4,28},{5,29},{6,30},{7,31},{8,16},{9,... | collective-permute-start | bytes 73736 | tf_op jit(solution)/shard_map/ppermute | solution.py:364
  64.1 4.2 %collective-permute-start.19 = (f32[8,768]{1,0:T(8,128)S(1)}, f32[8,768]{1,0:T(8,128)S(1)}, u32[]{:S(2)}, u32[]{:S(2)}) collective-permute-start(f32[8,768]{1,0:T(8,128)S(1)} %add.3.refs_0_), channel_id=1, source_target_pairs={{0,28},{1,29},{2,30},{3,31},{4,24},{5,25},{6,26},{7,27},{8,20},{9,... | collective-permute-start | bytes 73736 | tf_op jit(solution)/shard_map/ppermute | solution.py:364
  68.6 3.3 %collective-permute-start.25 = (f32[8,768]{1,0:T(8,128)S(1)}, f32[8,768]{1,0:T(8,128)S(1)}, u32[]{:S(2)}, u32[]{:S(2)}) collective-permute-start(f32[8,768]{1,0:T(8,128)S(1)} %get-tuple-element.28.refs_0_), channel_id=1, source_target_pairs={{0,24},{1,17},{2,18},{3,19},{4,20},{5,21},{6,22},{7,23},{8,16},{9,... | collective-permute-start | bytes 73736 | tf_op jit(solution)/shard_map/ppermute | solution.py:364
  69.9 4.2 %collective-permute-start.26 = (f32[8,768]{1,0:T(8,128)S(1)}, f32[8,768]{1,0:T(8,128)S(1)}, u32[]{:S(2)}, u32[]{:S(2)}) collective-permute-start(f32[8,768]{1,0:T(8,128)S(1)} %get-tuple-element.28.refs_0_), channel_id=1, source_target_pairs={{0,28},{1,17},{2,18},{3,19},{4,20},{5,21},{6,22},{7,23},{8,24},{9,... | collective-permute-start | bytes 73736 | tf_op jit(solution)/shard_map/ppermute | solution.py:364
  70.1 5.2 %collective-permute-start.20 = (f32[8,768]{1,0:T(8,128)S(1)}, f32[8,768]{1,0:T(8,128)S(1)}, u32[]{:S(2)}, u32[]{:S(2)}) collective-permute-start(f32[8,768]{1,0:T(8,128)S(1)} %get-tuple-element.28.refs_0_), channel_id=1, source_target_pairs={{0,20},{1,17},{2,18},{3,19},{4,16},{5,21},{6,22},{7,23},{8,24},{9,... | collective-permute-start | bytes 73736 | tf_op jit(solution)/shard_map/ppermute | solution.py:364
  70.7 4.7 %collective-permute-start.21 = (f32[8,768]{1,0:T(8,128)S(1)}, f32[8,768]{1,0:T(8,128)S(1)}, u32[]{:S(2)}, u32[]{:S(2)}) collective-permute-start(f32[8,768]{1,0:T(8,128)S(1)} %get-tuple-element.29), channel_id=1, source_target_pairs={{0,16},{1,17},{2,18},{3,19},{4,21},{5,20},{6,22},{7,23},{8,24},{9,... | collective-permute-start | bytes 73736 | tf_op jit(solution)/shard_map/ppermute | solution.py:364
  74.5 2.8 %collective-permute-start.27 = (f32[8,768]{1,0:T(8,128)S(1)}, f32[8,768]{1,0:T(8,128)S(1)}, u32[]{:S(2)}, u32[]{:S(2)}) collective-permute-start(f32[8,768]{1,0:T(8,128)S(1)} %shard_map.122), channel_id=1, source_target_pairs={{0,16},{1,17},{2,18},{3,19},{4,20},{5,28},{6,22},{7,23},{8,25},{9,... | collective-permute-start | bytes 73736 | tf_op jit(solution)/shard_map/ppermute | solution.py:364
  76.2 4.2 %collective-permute-start.28 = (f32[8,768]{1,0:T(8,128)S(1)}, f32[8,768]{1,0:T(8,128)S(1)}, u32[]{:S(2)}, u32[]{:S(2)}) collective-permute-start(f32[8,768]{1,0:T(8,128)S(1)} %shard_map.121.refs_1_), channel_id=1, source_target_pairs={{0,20},{1,17},{2,18},{3,19},{4,25},{5,21},{6,22},{7,23},{8,24},{9,... | collective-permute-start | bytes 73736 | tf_op jit(solution)/shard_map/ppermute | solution.py:364
  77.6 3.8 %collective-permute-start.30 = (f32[8,768]{1,0:T(8,128)S(1)}, f32[8,768]{1,0:T(8,128)S(1)}, u32[]{:S(2)}, u32[]{:S(2)}) collective-permute-start(f32[8,768]{1,0:T(8,128)S(1)} %shard_map.124), channel_id=1, source_target_pairs={{0,16},{1,17},{2,18},{3,19},{4,20},{5,21},{6,22},{7,23},{8,24},{9,... | collective-permute-start | bytes 73736 | tf_op jit(solution)/shard_map/ppermute | solution.py:364
  81.0 1.2 %collective-permute-start.31 = (f32[8,768]{1,0:T(8,128)S(1)}, f32[8,768]{1,0:T(8,128)S(1)}, u32[]{:S(2)}, u32[]{:S(2)}) collective-permute-start(f32[8,768]{1,0:T(8,128)S(1)} %shard_map.123.refs_2_), channel_id=1, source_target_pairs={{0,16},{1,17},{2,25},{3,19},{4,20},{5,21},{6,22},{7,23},{8,24},{9,... | collective-permute-start | bytes 73736 | tf_op jit(solution)/shard_map/ppermute | solution.py:364
  82.9 4.5 %collective-permute-start.32 = (f32[8,768]{1,0:T(8,128)S(1)}, f32[8,768]{1,0:T(8,128)S(1)}, u32[]{:S(2)}, u32[]{:S(2)}) collective-permute-start(f32[8,768]{1,0:T(8,128)S(1)} %shard_map.126.refs_0_), channel_id=1, source_target_pairs={{0,17},{1,16},{2,19},{3,18},{4,21},{5,20},{6,23},{7,22},{8,25},{9,... | collective-permute-start | bytes 73736 | tf_op jit(solution)/shard_map/ppermute | solution.py:364
  83.0 4.8 %collective-permute-start.33 = (f32[8,768]{1,0:T(8,128)S(1)}, f32[8,768]{1,0:T(8,128)S(1)}, u32[]{:S(2)}, u32[]{:S(2)}) collective-permute-start(f32[8,768]{1,0:T(8,128)S(1)} %shard_map.126.refs_0_), channel_id=1, source_target_pairs={{0,18},{1,19},{2,16},{3,17},{4,22},{5,23},{6,20},{7,21},{8,26},{9,... | collective-permute-start | bytes 73736 | tf_op jit(solution)/shard_map/ppermute | solution.py:364
  86.3 5.2 %collective-permute-start.34 = (f32[8,768]{1,0:T(8,128)S(1)}, f32[8,768]{1,0:T(8,128)S(1)}, u32[]{:S(2)}, u32[]{:S(2)}) collective-permute-start(f32[8,768]{1,0:T(8,128)S(1)} %shard_map.126.refs_0_), channel_id=1, source_target_pairs={{0,19},{1,18},{2,17},{3,16},{4,23},{5,22},{6,21},{7,20},{8,27},{9,... | collective-permute-start | bytes 73736 | tf_op jit(solution)/shard_map/ppermute | solution.py:364
  91.4 3.3 %collective-permute-start.35 = (f32[8,768]{1,0:T(8,128)S(1)}, f32[8,768]{1,0:T(8,128)S(1)}, u32[]{:S(2)}, u32[]{:S(2)}) collective-permute-start(f32[8,768]{1,0:T(8,128)S(1)} %shard_map.127.refs_0_), channel_id=1, source_target_pairs={{0,20},{1,21},{2,22},{3,23},{4,16},{5,17},{6,18},{7,19},{8,28},{9,... | collective-permute-start | bytes 73736 | tf_op jit(solution)/shard_map/ppermute | solution.py:364
  91.5 4.5 %collective-permute-start.36 = (f32[8,768]{1,0:T(8,128)S(1)}, f32[8,768]{1,0:T(8,128)S(1)}, u32[]{:S(2)}, u32[]{:S(2)}) collective-permute-start(f32[8,768]{1,0:T(8,128)S(1)} %shard_map.127.refs_0_), channel_id=1, source_target_pairs={{0,24},{1,25},{2,26},{3,27},{4,28},{5,29},{6,30},{7,31},{8,16},{9,... | collective-permute-start | bytes 73736 | tf_op jit(solution)/shard_map/ppermute | solution.py:364
  94.5 4.2 %collective-permute-start.37 = (f32[8,768]{1,0:T(8,128)S(1)}, f32[8,768]{1,0:T(8,128)S(1)}, u32[]{:S(2)}, u32[]{:S(2)}) collective-permute-start(f32[8,768]{1,0:T(8,128)S(1)} %shard_map.127.refs_0_), channel_id=1, source_target_pairs={{0,28},{1,29},{2,30},{3,31},{4,24},{5,25},{6,26},{7,27},{8,20},{9,... | collective-permute-start | bytes 73736 | tf_op jit(solution)/shard_map/ppermute | solution.py:364
  (17 other events, 159.1 us)

commit v9 on v8

--- a/solution.py
+++ b/solution.py
@@ -428,15 +428,13 @@
     sums = []
     for step in range(last, 0, -1):
         cols = list(range(step))[::-1]
-        idle = (lambda r, c: c > r) if step > 1 else None
-        near_idle = lambda r, c: c > r
-        got = [move(piece, ((step, step), (step, c)), idle=near_idle) for c in cols]
+        got = [move(piece, ((step, step), (step, c))) for c in cols]
         down = [((step, c), (step - 1, c)) for c in cols]
         if step == last:
-            sub = move(spread(cols[:1], [], got[:1]), down[0], idle=idle)
-            sums = [move(spread(cols[1:], [], got[1:]), *down[1:], idle=idle)]
+            sub = move(spread(cols[:1], [], got[:1]), down[0])
+            sums = [move(spread(cols[1:], [], got[1:]), *down[1:])]
         else:
-            sub = move(spread(cols, sums, got), *down, idle=idle)
+            sub = move(spread(cols, sums, got), *down)
             sums = [sub]
         if step > 1:
             piece = call(solve_kernel, part, direction, sub, low, block_inv)
@@ -512,4 +510,6 @@
         P(),
         P(),
     )
-    return jax.shard_map(step_of, mesh=mesh, in_specs=placed, out_specs=(P(), P(), P()), check_vma=False)
+    return jax.shard_map(
+        step_of, mesh=mesh, in_specs=placed, out_specs=(P(), P(), P()), check_vma=False
+    )

time: 99.7 us -> 101 us (1.013)
  starting transfers between devices: 48.7 us -> 51.8 us
  waiting for transfers between devices: 28.4 us -> 26.3 us
    ppermute x38, starting transfers between devices: 48.7 us -> 51.8 us  [permute(): return lax.ppermute(value, ('dp', 'crow', 'ccol'), perm)]
    ppermute x38, waiting for transfers between devices: 28.4 us -> 26.3 us  [permute(): return lax.ppermute(value, ('dp', 'crow', 'ccol'), perm)]
  transfers between devices with their start and end apart: 38 -> 38, of which waited for: 24 -> 23; matrix products, arithmetic and copies ran while one was open for 0% -> 0% of each run, Pallas kernels for 15% -> 15%
where the time goes in v9:
time: 101 us
  starting transfers between devices  51.8 us (51%)
  waiting for transfers between devices  26.3 us (26%)
  Pallas kernels  18.7 us (19%)
  local copies, waits for them, and re-layouts  2.84 us (3%)
    ppermute x38, starting transfers between devices, permute(): return lax.ppermute(value, ('dp', 'crow', 'ccol'), perm)  51.8 us
    ppermute x38, waiting for transfers between devices, permute(): return lax.ppermute(value, ('dp', 'crow', 'ccol'), perm)  26.3 us
    pallas_call x26, Pallas kernels, call(): pl.pallas_call(kernel, out_shape=outs, compiler_params=pltpu.CompilerPara...  18.7 us
    unnamed x22, local copies, waits for them, and re-layouts  2.84 us
  transfers between devices with their start and end apart: 38, of which 23 were waited for; matrix products, arithmetic and copies ran while one was open for 0% of the time, Pallas kernels for 15%

profile of v9, /device:TPU:0, one launch (start us, length us, event | category | flops | bytes accessed | tf_op | source)
XLA Modules:
  0.0 100.5 jit_solution(5193763746372355801)
XLA Ops:
  0.6 1.7 %copy-done = f32[768,768]{1,0:T(8,128)S(1)} copy-done((f32[768,768]{1,0:T(8,128)S(1)}, f32[768,768]{1,0:T(8,128)}, u32[]{:S(2)}) %copy-start) | copy-done | bytes 2359320
  2.3 1.1 %copy-done.2 = f32[3,256,256]{2,1,0:T(8,128)S(1)} copy-done((f32[3,256,256]{2,1,0:T(8,128)S(1)}, f32[3,256,256]{2,1,0:T(8,128)}, u32[]{:S(2)}) %copy-start.2) | copy-done | bytes 786456
  3.4 1.8 %shard_map.107 = (f32[256,768]{1,0:T(8,128)S(1)}, f32[128,768]{1,0:T(8,128)S(1)}) custom-call(f32[3,256,256]{2,1,0:T(8,128)S(1)} %copy-done.2, f32[768,768]{1,0:T(8,128)S(1)} %copy-done, f32[768,768]{1,0:T(8,128)S(1)} %copy-done, f32[768,768]{1,0:T(8,128)S(1)} %copy-done), custom_call_target="tpu_custom_call" | custom-call | flops 1000000 | bytes 1000000 | tf_op jit(solution)/shard_map/pallas_call | solution.py:336
  5.9 1.3 %collective-permute-done.22.one_ref = f32[128,768]{1,0:T(8,128)S(1)} collective-permute-done((f32[128,768]{1,0:T(8,128)S(1)}, f32[128,768]{1,0:T(8,128)S(1)}, u32[]{:S(2)}, u32[]{:S(2)}) %collective-permute-start.22) | collective-permute-done | bytes 393248 | tf_op jit(solution)/shard_map/ppermute | solution.py:364
  8.2 3.0 %shard_map.103.refs_2_ = f32[8,768]{1,0:T(8,128)} custom-call(f32[8,3072]{1,0:T(8,128)} %direction_ref.9, f32[3,256,256]{2,1,0:T(8,128)} %inv_ref.13, f32[768,768]{1,0:T(8,128)} %factor_ref.3, f32[768,768]{1,0:T(8,128)} %factor_ref.3, f32[768,768]{1,0:T(8,128)} %factor_ref.3), custom_call_target="tpu_custom_call" | custom-call | flops 1000000 | bytes 1000000 | tf_op jit(solution)/shard_map/pallas_call | solution.py:336
  16.7 0.8 collective-permute-done.7.sub_ref.refs_0_
  18.3 0.8 collective-permute-done.8.refs_1_
  19.6 23.3 %collective-permute-start.9 = (f32[8,768]{1,0:T(8,128)S(1)}, f32[8,768]{1,0:T(8,128)S(1)}, u32[]{:S(2)}, u32[]{:S(2)}) collective-permute-start(f32[8,768]{1,0:T(8,128)S(1)} %shard_map.111), channel_id=1, source_target_pairs={{0,20},{1,17},{2,18},{3,19},{4,16},{5,21},{6,22},{7,23},{8,24},{9,... | collective-permute-start | bytes 73736 | tf_op jit(solution)/shard_map/ppermute | solution.py:364
  42.8 1.5 %collective-permute-done.9.sub_ref = f32[8,768]{1,0:T(8,128)S(1)} collective-permute-done((f32[8,768]{1,0:T(8,128)S(1)}, f32[8,768]{1,0:T(8,128)S(1)}, u32[]{:S(2)}, u32[]{:S(2)}) %collective-permute-start.9) | collective-permute-done | bytes 24608 | tf_op jit(solution)/shard_map/ppermute | solution.py:364
  44.7 1.7 %collective-permute-start.10 = (f32[8,768]{1,0:T(8,128)S(1)}, f32[8,768]{1,0:T(8,128)S(1)}, u32[]{:S(2)}, u32[]{:S(2)}) collective-permute-start(f32[8,768]{1,0:T(8,128)S(1)} %shard_map.112.refs_0_), channel_id=1, source_target_pairs={{0,20},{1,21},{2,22},{3,23},{4,16},{5,17},{6,18},{7,19},{8,28},{9,... | collective-permute-start | bytes 73736 | tf_op jit(solution)/shard_map/ppermute | solution.py:364
  46.4 1.5 %collective-permute-start.12 = (f32[8,768]{1,0:T(8,128)S(1)}, f32[8,768]{1,0:T(8,128)S(1)}, u32[]{:S(2)}, u32[]{:S(2)}) collective-permute-start(f32[8,768]{1,0:T(8,128)S(1)} %shard_map.112.refs_0_), channel_id=1, source_target_pairs={{0,28},{1,29},{2,30},{3,31},{4,24},{5,25},{6,26},{7,27},{8,20},{9,... | collective-permute-start | bytes 73736 | tf_op jit(solution)/shard_map/ppermute | solution.py:364
  48.0 2.5 %shard_map.113 = (bf16[768,2048]{1,0:T(8,128)(2,1)S(1)}, bf16[768,2048]{1,0:T(8,128)(2,1)S(1)}) custom-call(f32[16]{0:T(128)S(1)} %copy-done.10, f32[16,768]{1,0:T(8,128)S(1)} %copy-done.9, f32[16,2048]{1,0:T(8,128)S(1)} %copy-done.5), custom_call_target="tpu_custom_call" | custom-call | flops 1000000 | bytes 1000000 | tf_op jit(solution)/shard_map/pallas_call | solution.py:336
  50.6 0.9 shard_map.114
  51.6 4.3 %collective-permute-start.15 = (f32[8,2048]{1,0:T(8,128)S(1)}, f32[8,2048]{1,0:T(8,128)S(1)}, u32[]{:S(2)}, u32[]{:S(2)}) collective-permute-start(f32[8,2048]{1,0:T(8,128)S(1)} %get-tuple-element.25.refs_0_), channel_id=1, source_target_pairs={{0,3},{1,2},{2,1},{3,0},{4,7},{5,6},{6,5},{7,4},{8,11},{9,10},{10,... | collective-permute-start | bytes 196616 | tf_op jit(solution)/shard_map/ppermute | solution.py:364
  55.9 1.0 %collective-permute-done.13.refs_1_ = f32[8,2048]{1,0:T(8,128)S(1)} collective-permute-done((f32[8,2048]{1,0:T(8,128)S(1)}, f32[8,2048]{1,0:T(8,128)S(1)}, u32[]{:S(2)}, u32[]{:S(2)}) %collective-permute-start.13) | collective-permute-done | bytes 65568 | tf_op jit(solution)/shard_map/ppermute | solution.py:364
  57.0 3.3 %collective-permute-done.14.refs_2_ = f32[8,2048]{1,0:T(8,128)S(1)} collective-permute-done((f32[8,2048]{1,0:T(8,128)S(1)}, f32[8,2048]{1,0:T(8,128)S(1)}, u32[]{:S(2)}, u32[]{:S(2)}) %collective-permute-start.14) | collective-permute-done | bytes 65568 | tf_op jit(solution)/shard_map/ppermute | solution.py:364
  60.2 1.8 %shard_map.115 = f32[8,768]{1,0:T(8,128)S(1)} custom-call(f32[8,2048]{1,0:T(8,128)S(1)} %get-tuple-element.25.refs_0_, f32[8,2048]{1,0:T(8,128)S(1)} %collective-permute-done.13.refs_1_, f32[8,2048]{1,0:T(8,128)S(1)} %collective-permute-done.14.refs_2_, f32[8,2048]{1,0:T(8,128)S(1)} %collective-permute-done.15.refs_3_, ...), custom_call_target="tpu_custom_call" | custom-call | flops 1000000 | bytes 1000000 | tf_op jit(solution)/shard_map/pallas_call | solution.py:336
  62.1 1.2 %collective-permute-done.16 = f32[8,768]{1,0:T(8,128)S(1)} collective-permute-done((f32[8,768]{1,0:T(8,128)S(1)}, f32[8,768]{1,0:T(8,128)S(1)}, u32[]{:S(2)}, u32[]{:S(2)}) %collective-permute-start.16) | collective-permute-done | bytes 24608 | tf_op jit(solution)/shard_map/ppermute | solution.py:364
  63.3 1.4 %collective-permute-start.17 = (f32[8,768]{1,0:T(8,128)S(1)}, f32[8,768]{1,0:T(8,128)S(1)}, u32[]{:S(2)}, u32[]{:S(2)}) collective-permute-start(f32[8,768]{1,0:T(8,128)S(1)} %add.3.refs_0_), channel_id=1, source_target_pairs={{0,20},{1,21},{2,22},{3,23},{4,16},{5,17},{6,18},{7,19},{8,28},{9,... | collective-permute-start | bytes 73736 | tf_op jit(solution)/shard_map/ppermute | solution.py:364
  65.1 1.2 %collective-permute-start.19 = (f32[8,768]{1,0:T(8,128)S(1)}, f32[8,768]{1,0:T(8,128)S(1)}, u32[]{:S(2)}, u32[]{:S(2)}) collective-permute-start(f32[8,768]{1,0:T(8,128)S(1)} %add.3.refs_0_), channel_id=1, source_target_pairs={{0,28},{1,29},{2,30},{3,31},{4,24},{5,25},{6,26},{7,27},{8,20},{9,... | collective-permute-start | bytes 73736 | tf_op jit(solution)/shard_map/ppermute | solution.py:364
  66.8 1.1 %collective-permute-done.18.refs_2_ = f32[8,768]{1,0:T(8,128)S(1)} collective-permute-done((f32[8,768]{1,0:T(8,128)S(1)}, f32[8,768]{1,0:T(8,128)S(1)}, u32[]{:S(2)}, u32[]{:S(2)}) %collective-permute-start.18) | collective-permute-done | bytes 24608 | tf_op jit(solution)/shard_map/ppermute | solution.py:364
  67.9 1.3 %collective-permute-done.19.refs_3_ = f32[8,768]{1,0:T(8,128)S(1)} collective-permute-done((f32[8,768]{1,0:T(8,128)S(1)}, f32[8,768]{1,0:T(8,128)S(1)}, u32[]{:S(2)}, u32[]{:S(2)}) %collective-permute-start.19) | collective-permute-done | bytes 24608 | tf_op jit(solution)/shard_map/ppermute | solution.py:364
  69.6 1.3 %collective-permute-start.25 = (f32[8,768]{1,0:T(8,128)S(1)}, f32[8,768]{1,0:T(8,128)S(1)}, u32[]{:S(2)}, u32[]{:S(2)}) collective-permute-start(f32[8,768]{1,0:T(8,128)S(1)} %get-tuple-element.28.refs_0_), channel_id=1, source_target_pairs={{0,24},{1,17},{2,18},{3,19},{4,20},{5,21},{6,22},{7,23},{8,16},{9,... | collective-permute-start | bytes 73736 | tf_op jit(solution)/shard_map/ppermute | solution.py:364
  72.8 2.2 %collective-permute-done.26.refs_1_ = f32[8,768]{1,0:T(8,128)S(1)} collective-permute-done((f32[8,768]{1,0:T(8,128)S(1)}, f32[8,768]{1,0:T(8,128)S(1)}, u32[]{:S(2)}, u32[]{:S(2)}) %collective-permute-start.26) | collective-permute-done | bytes 24608 | tf_op jit(solution)/shard_map/ppermute | solution.py:364
  77.2 1.0 %collective-permute-start.28 = (f32[8,768]{1,0:T(8,128)S(1)}, f32[8,768]{1,0:T(8,128)S(1)}, u32[]{:S(2)}, u32[]{:S(2)}) collective-permute-start(f32[8,768]{1,0:T(8,128)S(1)} %shard_map.121.refs_1_), channel_id=1, source_target_pairs={{0,20},{1,17},{2,18},{3,19},{4,25},{5,21},{6,22},{7,23},{8,24},{9,... | collective-permute-start | bytes 73736 | tf_op jit(solution)/shard_map/ppermute | solution.py:364
  78.9 2.4 %collective-permute-done.28.refs_1_ = f32[8,768]{1,0:T(8,128)S(1)} collective-permute-done((f32[8,768]{1,0:T(8,128)S(1)}, f32[8,768]{1,0:T(8,128)S(1)}, u32[]{:S(2)}, u32[]{:S(2)}) %collective-permute-start.28) | collective-permute-done | bytes 24608 | tf_op jit(solution)/shard_map/ppermute | solution.py:364
  84.1 4.0 %collective-permute-start.34 = (f32[8,768]{1,0:T(8,128)S(1)}, f32[8,768]{1,0:T(8,128)S(1)}, u32[]{:S(2)}, u32[]{:S(2)}) collective-permute-start(f32[8,768]{1,0:T(8,128)S(1)} %shard_map.126.refs_0_), channel_id=1, source_target_pairs={{0,19},{1,18},{2,17},{3,16},{4,23},{5,22},{6,21},{7,20},{8,27},{9,... | collective-permute-start | bytes 73736 | tf_op jit(solution)/shard_map/ppermute | solution.py:364
  88.2 1.8 %collective-permute-done.34.refs_3_ = f32[8,768]{1,0:T(8,128)S(1)} collective-permute-done((f32[8,768]{1,0:T(8,128)S(1)}, f32[8,768]{1,0:T(8,128)S(1)}, u32[]{:S(2)}, u32[]{:S(2)}) %collective-permute-start.34) | collective-permute-done | bytes 24608 | tf_op jit(solution)/shard_map/ppermute | solution.py:364
  90.2 5.3 %collective-permute-start.36 = (f32[8,768]{1,0:T(8,128)S(1)}, f32[8,768]{1,0:T(8,128)S(1)}, u32[]{:S(2)}, u32[]{:S(2)}) collective-permute-start(f32[8,768]{1,0:T(8,128)S(1)} %shard_map.127.refs_0_), channel_id=1, source_target_pairs={{0,24},{1,25},{2,26},{3,27},{4,28},{5,29},{6,30},{7,31},{8,16},{9,... | collective-permute-start | bytes 73736 | tf_op jit(solution)/shard_map/ppermute | solution.py:364
  95.5 1.5 %collective-permute-done.36.refs_2_ = f32[8,768]{1,0:T(8,128)S(1)} collective-permute-done((f32[8,768]{1,0:T(8,128)S(1)}, f32[8,768]{1,0:T(8,128)S(1)}, u32[]{:S(2)}, u32[]{:S(2)}) %collective-permute-start.36) | collective-permute-done | bytes 24608 | tf_op jit(solution)/shard_map/ppermute | solution.py:364
  97.0 2.6 %collective-permute-done.37.refs_3_ = f32[8,768]{1,0:T(8,128)S(1)} collective-permute-done((f32[8,768]{1,0:T(8,128)S(1)}, f32[8,768]{1,0:T(8,128)S(1)}, u32[]{:S(2)}, u32[]{:S(2)}) %collective-permute-start.37) | collective-permute-done | bytes 24608 | tf_op jit(solution)/shard_map/ppermute | solution.py:364
  99.6 0.9 shard_map.128
  (93 shorter events, 17.9 us)
Async XLA Ops:
  5.3 1.9 %collective-permute-start.22 = (f32[128,768]{1,0:T(8,128)S(1)}, f32[128,768]{1,0:T(8,128)S(1)}, u32[]{:S(2)}, u32[]{:S(2)}) collective-permute-start(f32[128,768]{1,0:T(8,128)S(1)} %get-tuple-element.32), channel_id=1, source_target_pairs={{0,16},{1,17},{2,18},{3,19},{4,21},{5,20},{6,22},{7,23},{8,24},{9,... | collective-permute-start | bytes 1179656 | tf_op jit(solution)/shard_map/ppermute | solution.py:364
  5.8 1.9 %collective-permute-start.23 = (f32[128,768]{1,0:T(8,128)S(1)}, f32[128,768]{1,0:T(8,128)S(1)}, u32[]{:S(2)}, u32[]{:S(2)}) collective-permute-start(f32[128,768]{1,0:T(8,128)S(1)} %get-tuple-element.32), channel_id=1, source_target_pairs={{0,16},{1,17},{2,18},{3,19},{4,20},{5,21},{6,22},{7,23},{8,24},{9,... | collective-permute-start | bytes 1179656 | tf_op jit(solution)/shard_map/ppermute | solution.py:364
  7.8 68.0 %collective-permute-start.24 = (f32[128,768]{1,0:T(8,128)S(1)}, f32[128,768]{1,0:T(8,128)S(1)}, u32[]{:S(2)}, u32[]{:S(2)}) collective-permute-start(f32[128,768]{1,0:T(8,128)S(1)} %shard_map.119.mine_ref), channel_id=1, source_target_pairs={{0,16},{1,17},{2,18},{3,19},{4,20},{5,21},{6,22},{7,23},{8,24},{9,... | collective-permute-start | bytes 1179656 | tf_op jit(solution)/shard_map/ppermute | solution.py:364
  11.2 1.4 %collective-permute-start.3 = (f32[8,768]{1,0:T(8,128)}, f32[8,768]{1,0:T(8,128)S(1)}, u32[]{:S(2)}, u32[]{:S(2)}) collective-permute-start(f32[8,768]{1,0:T(8,128)} %shard_map.103.refs_2_), channel_id=1, source_target_pairs={{0,16},{1,17},{2,18},{3,19},{4,20},{5,21},{6,22},{7,23},{8,24},{9,... | collective-permute-start | bytes 73736 | tf_op jit(solution)/shard_map/ppermute | solution.py:364
  11.3 1.9 %collective-permute-start = (f32[8,768]{1,0:T(8,128)}, f32[8,768]{1,0:T(8,128)S(1)}, u32[]{:S(2)}, u32[]{:S(2)}) collective-permute-start(f32[8,768]{1,0:T(8,128)} %shard_map.103.refs_2_), channel_id=1, source_target_pairs={{0,16},{1,17},{2,18},{3,19},{4,20},{5,21},{6,22},{7,23},{8,24},{9,... | collective-permute-start | bytes 73736 | tf_op jit(solution)/shard_map/ppermute | solution.py:364
  11.7 1.5 %collective-permute-start.1 = (f32[8,768]{1,0:T(8,128)}, f32[8,768]{1,0:T(8,128)S(1)}, u32[]{:S(2)}, u32[]{:S(2)}) collective-permute-start(f32[8,768]{1,0:T(8,128)} %shard_map.103.refs_2_), channel_id=1, source_target_pairs={{0,16},{1,17},{2,18},{3,19},{4,20},{5,21},{6,22},{7,23},{8,24},{9,... | collective-permute-start | bytes 73736 | tf_op jit(solution)/shard_map/ppermute | solution.py:364
  13.6 1.5 %collective-permute-start.2 = (f32[8,768]{1,0:T(8,128)S(1)}, f32[8,768]{1,0:T(8,128)S(1)}, u32[]{:S(2)}, u32[]{:S(2)}) collective-permute-start(f32[8,768]{1,0:T(8,128)S(1)} %shard_map.105), channel_id=1, source_target_pairs={{0,16},{1,17},{2,18},{3,19},{4,20},{5,21},{6,22},{7,23},{8,28},{9,... | collective-permute-start | bytes 73736 | tf_op jit(solution)/shard_map/ppermute | solution.py:364
  19.6 24.8 %collective-permute-start.9 = (f32[8,768]{1,0:T(8,128)S(1)}, f32[8,768]{1,0:T(8,128)S(1)}, u32[]{:S(2)}, u32[]{:S(2)}) collective-permute-start(f32[8,768]{1,0:T(8,128)S(1)} %shard_map.111), channel_id=1, source_target_pairs={{0,20},{1,17},{2,18},{3,19},{4,16},{5,21},{6,22},{7,23},{8,24},{9,... | collective-permute-start | bytes 73736 | tf_op jit(solution)/shard_map/ppermute | solution.py:364
  44.7 5.8 %collective-permute-start.10 = (f32[8,768]{1,0:T(8,128)S(1)}, f32[8,768]{1,0:T(8,128)S(1)}, u32[]{:S(2)}, u32[]{:S(2)}) collective-permute-start(f32[8,768]{1,0:T(8,128)S(1)} %shard_map.112.refs_0_), channel_id=1, source_target_pairs={{0,20},{1,21},{2,22},{3,23},{4,16},{5,17},{6,18},{7,19},{8,28},{9,... | collective-permute-start | bytes 73736 | tf_op jit(solution)/shard_map/ppermute | solution.py:364
  46.4 4.1 %collective-permute-start.11 = (f32[8,768]{1,0:T(8,128)S(1)}, f32[8,768]{1,0:T(8,128)S(1)}, u32[]{:S(2)}, u32[]{:S(2)}) collective-permute-start(f32[8,768]{1,0:T(8,128)S(1)} %shard_map.112.refs_0_), channel_id=1, source_target_pairs={{0,24},{1,25},{2,26},{3,27},{4,28},{5,29},{6,30},{7,31},{8,16},{9,... | collective-permute-start | bytes 73736 | tf_op jit(solution)/shard_map/ppermute | solution.py:364
  46.4 4.2 %collective-permute-start.12 = (f32[8,768]{1,0:T(8,128)S(1)}, f32[8,768]{1,0:T(8,128)S(1)}, u32[]{:S(2)}, u32[]{:S(2)}) collective-permute-start(f32[8,768]{1,0:T(8,128)S(1)} %shard_map.112.refs_0_), channel_id=1, source_target_pairs={{0,28},{1,29},{2,30},{3,31},{4,24},{5,25},{6,26},{7,27},{8,20},{9,... | collective-permute-start | bytes 73736 | tf_op jit(solution)/shard_map/ppermute | solution.py:364
  51.5 5.5 %collective-permute-start.13 = (f32[8,2048]{1,0:T(8,128)S(1)}, f32[8,2048]{1,0:T(8,128)S(1)}, u32[]{:S(2)}, u32[]{:S(2)}) collective-permute-start(f32[8,2048]{1,0:T(8,128)S(1)} %get-tuple-element.25.refs_0_), channel_id=1, source_target_pairs={{0,1},{1,0},{2,3},{3,2},{4,5},{5,4},{6,7},{7,6},{8,9},{9,8},{10,11... | collective-permute-start | bytes 196616 | tf_op jit(solution)/shard_map/ppermute | solution.py:364
  51.5 8.7 %collective-permute-start.14 = (f32[8,2048]{1,0:T(8,128)S(1)}, f32[8,2048]{1,0:T(8,128)S(1)}, u32[]{:S(2)}, u32[]{:S(2)}) collective-permute-start(f32[8,2048]{1,0:T(8,128)S(1)} %get-tuple-element.25.refs_0_), channel_id=1, source_target_pairs={{0,2},{1,3},{2,0},{3,1},{4,6},{5,7},{6,4},{7,5},{8,10},{9,11},{10,... | collective-permute-start | bytes 196616 | tf_op jit(solution)/shard_map/ppermute | solution.py:364
  51.6 8.7 %collective-permute-start.15 = (f32[8,2048]{1,0:T(8,128)S(1)}, f32[8,2048]{1,0:T(8,128)S(1)}, u32[]{:S(2)}, u32[]{:S(2)}) collective-permute-start(f32[8,2048]{1,0:T(8,128)S(1)} %get-tuple-element.25.refs_0_), channel_id=1, source_target_pairs={{0,3},{1,2},{2,1},{3,0},{4,7},{5,6},{6,5},{7,4},{8,11},{9,10},{10,... | collective-permute-start | bytes 196616 | tf_op jit(solution)/shard_map/ppermute | solution.py:364
  62.0 1.2 %collective-permute-start.16 = (f32[8,768]{1,0:T(8,128)S(1)}, f32[8,768]{1,0:T(8,128)S(1)}, u32[]{:S(2)}, u32[]{:S(2)}) collective-permute-start(f32[8,768]{1,0:T(8,128)S(1)} %shard_map.115), channel_id=1, source_target_pairs={{0,16},{1,17},{2,18},{3,19},{4,20},{5,21},{6,22},{7,23},{8,24},{9,... | collective-permute-start | bytes 73736 | tf_op jit(solution)/shard_map/ppermute | solution.py:364
  63.3 3.5 %collective-permute-start.17 = (f32[8,768]{1,0:T(8,128)S(1)}, f32[8,768]{1,0:T(8,128)S(1)}, u32[]{:S(2)}, u32[]{:S(2)}) collective-permute-start(f32[8,768]{1,0:T(8,128)S(1)} %add.3.refs_0_), channel_id=1, source_target_pairs={{0,20},{1,21},{2,22},{3,23},{4,16},{5,17},{6,18},{7,19},{8,28},{9,... | collective-permute-start | bytes 73736 | tf_op jit(solution)/shard_map/ppermute | solution.py:364
  64.7 3.3 %collective-permute-start.18 = (f32[8,768]{1,0:T(8,128)S(1)}, f32[8,768]{1,0:T(8,128)S(1)}, u32[]{:S(2)}, u32[]{:S(2)}) collective-permute-start(f32[8,768]{1,0:T(8,128)S(1)} %add.3.refs_0_), channel_id=1, source_target_pairs={{0,24},{1,25},{2,26},{3,27},{4,28},{5,29},{6,30},{7,31},{8,16},{9,... | collective-permute-start | bytes 73736 | tf_op jit(solution)/shard_map/ppermute | solution.py:364
  65.1 4.2 %collective-permute-start.19 = (f32[8,768]{1,0:T(8,128)S(1)}, f32[8,768]{1,0:T(8,128)S(1)}, u32[]{:S(2)}, u32[]{:S(2)}) collective-permute-start(f32[8,768]{1,0:T(8,128)S(1)} %add.3.refs_0_), channel_id=1, source_target_pairs={{0,28},{1,29},{2,30},{3,31},{4,24},{5,25},{6,26},{7,27},{8,20},{9,... | collective-permute-start | bytes 73736 | tf_op jit(solution)/shard_map/ppermute | solution.py:364
  69.6 3.3 %collective-permute-start.25 = (f32[8,768]{1,0:T(8,128)S(1)}, f32[8,768]{1,0:T(8,128)S(1)}, u32[]{:S(2)}, u32[]{:S(2)}) collective-permute-start(f32[8,768]{1,0:T(8,128)S(1)} %get-tuple-element.28.refs_0_), channel_id=1, source_target_pairs={{0,24},{1,17},{2,18},{3,19},{4,20},{5,21},{6,22},{7,23},{8,16},{9,... | collective-permute-start | bytes 73736 | tf_op jit(solution)/shard_map/ppermute | solution.py:364
  70.9 4.2 %collective-permute-start.26 = (f32[8,768]{1,0:T(8,128)S(1)}, f32[8,768]{1,0:T(8,128)S(1)}, u32[]{:S(2)}, u32[]{:S(2)}) collective-permute-start(f32[8,768]{1,0:T(8,128)S(1)} %get-tuple-element.28.refs_0_), channel_id=1, source_target_pairs={{0,28},{1,17},{2,18},{3,19},{4,20},{5,21},{6,22},{7,23},{8,24},{9,... | collective-permute-start | bytes 73736 | tf_op jit(solution)/shard_map/ppermute | solution.py:364
  71.1 5.2 %collective-permute-start.20 = (f32[8,768]{1,0:T(8,128)S(1)}, f32[8,768]{1,0:T(8,128)S(1)}, u32[]{:S(2)}, u32[]{:S(2)}) collective-permute-start(f32[8,768]{1,0:T(8,128)S(1)} %get-tuple-element.28.refs_0_), channel_id=1, source_target_pairs={{0,20},{1,17},{2,18},{3,19},{4,16},{5,21},{6,22},{7,23},{8,24},{9,... | collective-permute-start | bytes 73736 | tf_op jit(solution)/shard_map/ppermute | solution.py:364
  71.7 4.7 %collective-permute-start.21 = (f32[8,768]{1,0:T(8,128)S(1)}, f32[8,768]{1,0:T(8,128)S(1)}, u32[]{:S(2)}, u32[]{:S(2)}) collective-permute-start(f32[8,768]{1,0:T(8,128)S(1)} %get-tuple-element.29), channel_id=1, source_target_pairs={{0,16},{1,17},{2,18},{3,19},{4,21},{5,20},{6,22},{7,23},{8,24},{9,... | collective-permute-start | bytes 73736 | tf_op jit(solution)/shard_map/ppermute | solution.py:364
  75.5 2.8 %collective-permute-start.27 = (f32[8,768]{1,0:T(8,128)S(1)}, f32[8,768]{1,0:T(8,128)S(1)}, u32[]{:S(2)}, u32[]{:S(2)}) collective-permute-start(f32[8,768]{1,0:T(8,128)S(1)} %shard_map.122), channel_id=1, source_target_pairs={{0,16},{1,24},{2,18},{3,19},{4,20},{5,28},{6,22},{7,23},{8,25},{9,... | collective-permute-start | bytes 73736 | tf_op jit(solution)/shard_map/ppermute | solution.py:364
  77.0 1.2 %collective-permute-start.29 = (f32[8,768]{1,0:T(8,128)S(1)}, f32[8,768]{1,0:T(8,128)S(1)}, u32[]{:S(2)}, u32[]{:S(2)}) collective-permute-start(f32[8,768]{1,0:T(8,128)S(1)} %shard_map.121.refs_1_), channel_id=1, source_target_pairs={{0,16},{1,17},{2,18},{3,19},{4,29},{5,21},{6,20},{7,23},{8,24},{9,... | collective-permute-start | bytes 73736 | tf_op jit(solution)/shard_map/ppermute | solution.py:364
  77.2 4.2 %collective-permute-start.28 = (f32[8,768]{1,0:T(8,128)S(1)}, f32[8,768]{1,0:T(8,128)S(1)}, u32[]{:S(2)}, u32[]{:S(2)}) collective-permute-start(f32[8,768]{1,0:T(8,128)S(1)} %shard_map.121.refs_1_), channel_id=1, source_target_pairs={{0,20},{1,17},{2,18},{3,19},{4,25},{5,21},{6,22},{7,23},{8,24},{9,... | collective-permute-start | bytes 73736 | tf_op jit(solution)/shard_map/ppermute | solution.py:364
  78.6 3.7 %collective-permute-start.30 = (f32[8,768]{1,0:T(8,128)S(1)}, f32[8,768]{1,0:T(8,128)S(1)}, u32[]{:S(2)}, u32[]{:S(2)}) collective-permute-start(f32[8,768]{1,0:T(8,128)S(1)} %shard_map.124), channel_id=1, source_target_pairs={{0,16},{1,17},{2,18},{3,19},{4,20},{5,21},{6,22},{7,23},{8,24},{9,... | collective-permute-start | bytes 73736 | tf_op jit(solution)/shard_map/ppermute | solution.py:364
  83.9 4.1 %collective-permute-start.32 = (f32[8,768]{1,0:T(8,128)S(1)}, f32[8,768]{1,0:T(8,128)S(1)}, u32[]{:S(2)}, u32[]{:S(2)}) collective-permute-start(f32[8,768]{1,0:T(8,128)S(1)} %shard_map.126.refs_0_), channel_id=1, source_target_pairs={{0,17},{1,16},{2,19},{3,18},{4,21},{5,20},{6,23},{7,22},{8,25},{9,... | collective-permute-start | bytes 73736 | tf_op jit(solution)/shard_map/ppermute | solution.py:364
  84.0 4.2 %collective-permute-start.33 = (f32[8,768]{1,0:T(8,128)S(1)}, f32[8,768]{1,0:T(8,128)S(1)}, u32[]{:S(2)}, u32[]{:S(2)}) collective-permute-start(f32[8,768]{1,0:T(8,128)S(1)} %shard_map.126.refs_0_), channel_id=1, source_target_pairs={{0,18},{1,19},{2,16},{3,17},{4,22},{5,23},{6,20},{7,21},{8,26},{9,... | collective-permute-start | bytes 73736 | tf_op jit(solution)/shard_map/ppermute | solution.py:364
  84.1 5.9 %collective-permute-start.34 = (f32[8,768]{1,0:T(8,128)S(1)}, f32[8,768]{1,0:T(8,128)S(1)}, u32[]{:S(2)}, u32[]{:S(2)}) collective-permute-start(f32[8,768]{1,0:T(8,128)S(1)} %shard_map.126.refs_0_), channel_id=1, source_target_pairs={{0,19},{1,18},{2,17},{3,16},{4,23},{5,22},{6,21},{7,20},{8,27},{9,... | collective-permute-start | bytes 73736 | tf_op jit(solution)/shard_map/ppermute | solution.py:364
  90.0 5.5 %collective-permute-start.35 = (f32[8,768]{1,0:T(8,128)S(1)}, f32[8,768]{1,0:T(8,128)S(1)}, u32[]{:S(2)}, u32[]{:S(2)}) collective-permute-start(f32[8,768]{1,0:T(8,128)S(1)} %shard_map.127.refs_0_), channel_id=1, source_target_pairs={{0,20},{1,21},{2,22},{3,23},{4,16},{5,17},{6,18},{7,19},{8,28},{9,... | collective-permute-start | bytes 73736 | tf_op jit(solution)/shard_map/ppermute | solution.py:364
  90.2 6.8 %collective-permute-start.36 = (f32[8,768]{1,0:T(8,128)S(1)}, f32[8,768]{1,0:T(8,128)S(1)}, u32[]{:S(2)}, u32[]{:S(2)}) collective-permute-start(f32[8,768]{1,0:T(8,128)S(1)} %shard_map.127.refs_0_), channel_id=1, source_target_pairs={{0,24},{1,25},{2,26},{3,27},{4,28},{5,29},{6,30},{7,31},{8,16},{9,... | collective-permute-start | bytes 73736 | tf_op jit(solution)/shard_map/ppermute | solution.py:364
  95.5 4.2 %collective-permute-start.37 = (f32[8,768]{1,0:T(8,128)S(1)}, f32[8,768]{1,0:T(8,128)S(1)}, u32[]{:S(2)}, u32[]{:S(2)}) collective-permute-start(f32[8,768]{1,0:T(8,128)S(1)} %shard_map.127.refs_0_), channel_id=1, source_target_pairs={{0,28},{1,29},{2,30},{3,31},{4,24},{5,25},{6,26},{7,27},{8,20},{9,... | collective-permute-start | bytes 73736 | tf_op jit(solution)/shard_map/ppermute | solution.py:364
  (17 other events, 163.1 us)
